TPU v7x, 128 devices: a whole 4x4x4 slice. The times are simulated.
128 devices in a mesh: pipe: 2 (over x_hi), seq: 16 (over x_lo, y, core), chan: 4 (over z).
Axes of the slice: x: 4 (x_hi: 2, x_lo: 2; x = x_hi * 2 + x_lo), y: 4, z: 4, core: 2. Of those that a mesh axis runs over, the one named last changes fastest.
Arguments:
- fwd_in: bfloat16 [2, 2048, 8192], P('pipe', 'seq', 'chan'), may hold values from -14 to 14
- saved_in: bfloat16 [2, 2048, 8192], P('pipe', 'seq', 'chan'), may hold values from -14 to 14
- saved_conv: bfloat16 [2, 2048, 8192], P('pipe', 'seq', 'chan'), may hold values from -5 to 5
- grad_out: bfloat16 [2, 2048, 8192], P('pipe', 'seq', 'chan'), may hold values from -14 to 14
- filters: bfloat16 [2, 2048, 8192], P('pipe', None, 'chan'), may hold values from -1.2 to 1.2
- mix_params: float32 [2, 7, 8192], P('pipe', None, 'chan'), may hold values from -1.5 to 1.5
- span_order: int32 [16], replicated, may hold values from 0 to 15, each once
Outputs:
- layer_out: bfloat16 [2, 2048, 8192], P('pipe', 'seq', 'chan')
- input_grad: bfloat16 [2, 2048, 8192], P('pipe', 'seq', 'chan')
- param_grad: float32 [2, 7, 8192], P('pipe', None, 'chan')
- received: bfloat16 [2, 2048, 8192], P('pipe', 'seq', 'chan')
Inputs may be any that keep to these rules, and one draw needn't show every extreme that they name: span_order holds each block position once.
All inputs are finite; a program needn't handle non-finite values.
Results may differ from a plain program's by a relative error of at most 0.015.
Values may be sent and summed in bfloat16 or wider, within the bound.
No kernel may reach another device: no remote copies, remote signals or barrier semaphores. Data moves between devices by JAX's collectives and lax.ppermute only.
A program may use at most 192 MiB of HBM per device.

v0:
```python
import functools

import jax
import jax.numpy as jnp
import ml_dtypes
import numpy as np
from jax import lax
from jax.experimental import pallas as pl
from jax.experimental.pallas import tpu as pltpu
from jax.sharding import PartitionSpec as P


D = 8192
EPSILON = 1e-05
BLOCK = 256
LANES = 128


def split_bf16(table):
    high = table.astype(np.float32).astype(ml_dtypes.bfloat16)
    low = (table - high.astype(np.float64)).astype(np.float32).astype(ml_dtypes.bfloat16)
    return high, low


def transform_tables():
    period = 2 * BLOCK
    freq = np.arange(BLOCK)[:, None]
    time = np.arange(BLOCK)[None, :]
    angle = 2.0 * np.pi / period * (freq * time % period)
    real, imag = np.cos(angle), -np.sin(angle)
    imag[0] = np.where(np.arange(BLOCK) % 2 == 0, 1.0, -1.0)
    enter = np.concatenate([real, imag], axis=0)
    angle = 2.0 * np.pi / period * (freq * (time + BLOCK) % period)
    real, imag = 2.0 * np.cos(angle), -2.0 * np.sin(angle)
    real[0] = 1.0
    imag[0] = np.where(np.arange(BLOCK) % 2 == 0, 1.0, -1.0)
    leave = np.concatenate([real, imag], axis=0).T / period
    return split_bf16(enter) + split_bf16(leave)


def rows_to_columns(rows):
    return jnp.concatenate([rows] * 16, axis=0).T


def columns_to_rows(columns):
    lane = lax.broadcasted_iota(jnp.int32, (128, 128), 1)
    square = jnp.zeros((128, 128), jnp.float32)
    for index, column in enumerate(columns):
        square = jnp.where(lane == index, column, square)
    return square.T[:8]


VMEM = pl.BlockSpec(memory_space=pltpu.VMEM)
SMEM = pl.BlockSpec(memory_space=pltpu.SMEM)


def in_vmem(array):
    return pltpu.with_memory_space_constraint(array, pltpu.VMEM)


HBM = pl.BlockSpec(memory_space=pl.ANY)


def in_hbm(array):
    return pltpu.with_memory_space_constraint(array, pltpu.HBM)


def lane_spec(rows, wide):
    return pl.BlockSpec((1, rows, wide), lambda step, *_: (0, 0, step))


def whole(shape):
    return pl.BlockSpec(shape, lambda step, *_: (0,) * len(shape))


def pack_kernel(fwd_ref, saved_ref, cot_ref, out_ref, squares_ref, acc):
    step = pl.program_id(0)
    rows = fwd_ref.shape[1]

    @pl.when(step == 0)
    def _():
        acc[...] = jnp.zeros_like(acc)

    totals = [acc[0], acc[1]]
    for group in range(fwd_ref.shape[2] // LANES):
        at = pl.ds(group * LANES, LANES)
        for index, ref in enumerate((fwd_ref, saved_ref, cot_ref)):
            value = ref[0, :, at]
            out_ref[group, index * rows : (index + 1) * rows, :] = value
            if index < 2:
                wide = value.astype(jnp.float32)
                totals[index] = totals[index] + wide * wide
    acc[0] = totals[0]
    acc[1] = totals[1]

    @pl.when(step == pl.num_programs(0) - 1)
    def _():
        squares_ref[...] = columns_to_rows(
            [jnp.sum(acc[index], axis=1, keepdims=True) for index in range(2)]
        )


def pack(fwd_in, saved_in, grad_out):
    rows, width = fwd_in.shape[1:]
    wide = 512
    return pl.pallas_call(
        pack_kernel,
        out_shape=(
            jax.ShapeDtypeStruct((width // LANES, 3 * rows, LANES), jnp.bfloat16),
            jax.ShapeDtypeStruct((8, 128), jnp.float32),
        ),
        grid=(width // wide,),
        in_specs=[lane_spec(rows, wide)] * 3,
        out_specs=(
            pl.BlockSpec((wide // LANES, 3 * rows, LANES), lambda step: (step, 0, 0)),
            whole((8, 128)),
        ),
        scratch_shapes=[pltpu.VMEM((2, rows, 128), jnp.float32)],
        name="pack",
        compiler_params=pltpu.CompilerParams(vmem_limit_bytes=16 << 20),
    )(in_hbm(fwd_in), in_hbm(saved_in), in_hbm(grad_out))


def over_chan(rows):
    count = lax.axis_size("chan")
    got = [rows]
    for apart in range(1, count):
        got.append(
            lax.ppermute(rows, "chan", [(low, (low + apart) % count) for low in range(count)])
        )
    return got


def across(rows, flip):
    count = lax.axis_size("seq")
    return lax.ppermute(rows, "seq", [(low, low ^ flip) for low in range(count)])


def round_ring(rows, apart):
    count = lax.axis_size("seq")
    place = lambda low: low // 8 * 8 + (low + 2 * apart) % 8
    return lax.ppermute(rows, "seq", [(low, place(low)) for low in range(count)])


def gather_order():
    own = lax.axis_index("seq").astype(jnp.int32)
    block = jnp.arange(16, dtype=jnp.int32)
    core = (block ^ own) & 1
    back = (own // 2 - block // 2) % 4
    side = (block // 8) ^ (own // 8)
    return side * 8 + back * 2 + core


def early_kernel(where_ref, inv_ref, saved_ref, sconv_ref, cot_ref, out_ref, inv):
    @pl.when(pl.program_id(0) == 0)
    def _():
        inv[...] = rows_to_columns(inv_ref[0:8, :])

    inv_saved = inv[:, 1:2]
    for group in range(saved_ref.shape[2] // LANES):
        at = pl.ds(group * LANES, LANES)
        normed = saved_ref[0, :, at].astype(jnp.float32) * inv_saved
        grad_query = cot_ref[0, :, at].astype(jnp.float32) * sconv_ref[0, :, at].astype(jnp.float32)
        out_ref[0:1, at] = jnp.sum(grad_query, axis=0, keepdims=True)
        out_ref[1:2, at] = jnp.sum(grad_query * normed, axis=0, keepdims=True)


def early(where, inv, saved_in, saved_conv, grad_out):
    rows, width = saved_in.shape[1:]
    wide = 512
    return pl.pallas_call(
        early_kernel,
        out_shape=jax.ShapeDtypeStruct((2, width), jnp.float32),
        grid_spec=pltpu.PrefetchScalarGridSpec(
            num_scalar_prefetch=1,
            grid=(width // wide,),
            in_specs=[VMEM] + [lane_spec(rows, wide)] * 3,
            out_specs=pl.BlockSpec((2, wide), lambda step, *_: (0, step)),
            scratch_shapes=[pltpu.VMEM((rows, 128), jnp.float32)],
        ),
        name="early",
        compiler_params=pltpu.CompilerParams(vmem_limit_bytes=12 << 20),
    )(where, inv, saved_in, saved_conv, grad_out)


def side_by_side(ref, index):
    at = 2 * index * BLOCK
    return jnp.concatenate([ref[at : at + BLOCK, :], ref[at + BLOCK : at + 2 * BLOCK, :]], axis=1)


def enter_transform(enter_hi, enter_lo, data):
    return jnp.dot(enter_hi[...], data, preferred_element_type=jnp.float32) + jnp.dot(
        enter_lo[...], data, preferred_element_type=jnp.float32
    )


def filter_kernel(where_ref, taps_ref, enter_hi, enter_lo, filt):
    del where_ref
    freq = lax.broadcasted_iota(jnp.int32, (2 * BLOCK, LANES), 0)
    parity = jnp.where(freq % 2 == 0, 1.0, -1.0)
    first = lax.broadcasted_iota(jnp.int32, (BLOCK, LANES), 0) == 0
    earlier = None
    for pair in range(filt.shape[0] // 2):
        pair_spectra = enter_transform(enter_hi, enter_lo, side_by_side(taps_ref.at[0], pair))
        for side in range(2):
            current = pair_spectra[:, side * LANES : (side + 1) * LANES]
            both = parity * current
            if earlier is not None:
                both = both + earlier
            earlier = current
            real, imag = both[:BLOCK], both[BLOCK:]
            index = 2 * pair + side
            filt[index, 0] = real
            filt[index, 1] = jnp.where(first, 0.0, imag)
            filt[index, 2] = jnp.where(first, imag, real)


def filter_spectra(where, filters, tables):
    length = filters.shape[1]
    shape = (length // BLOCK, 3, BLOCK, LANES)
    return pl.pallas_call(
        filter_kernel,
        out_shape=pltpu.VMEM(shape, jnp.float32),
        grid_spec=pltpu.PrefetchScalarGridSpec(
            num_scalar_prefetch=1,
            grid=(1,),
            in_specs=[pl.BlockSpec((1, length, LANES), lambda step, at: (0, 0, at[0]))]
            + [whole(table.shape) for table in tables[:2]],
            out_specs=VMEM,
        ),
        name="filter_spectra",
        compiler_params=pltpu.CompilerParams(vmem_limit_bytes=16 << 20),
    )(where, in_hbm(filters), *[in_hbm(table) for table in tables[:2]])


def fold(block):
    return jnp.sum(block.reshape(block.shape[0] // 8, 8, LANES), axis=0)


def conv_kernel(
    where_ref, order_ref, gathered_ref, inv_ref, params_ref, filt, raw_hbm, enter_hi_hbm,
    enter_lo_hbm, leave_hi_hbm, leave_lo_hbm, out_hbm, raw_ref, enter_hi, enter_lo, leave_hi,
    leave_lo, out_ref, ordered, spectra, product, inv_rows, inv, raw_sem, table_sem, out_sem,
):
    stored = raw_ref.shape[0]
    raw_copies = [
        pltpu.make_async_copy(raw_hbm.at[index], raw_ref.at[index], raw_sem.at[index])
        for index in range(stored)
    ]
    table_copies = [
        pltpu.make_async_copy(source, target, table_sem.at[index])
        for index, (source, target) in enumerate(
            (
                (enter_hi_hbm, enter_hi),
                (enter_lo_hbm, enter_lo),
                (leave_hi_hbm, leave_hi),
                (leave_lo_hbm, leave_lo),
            )
        )
    ]
    out_copies = [
        pltpu.make_async_copy(out_ref.at[index], out_hbm.at[index], out_sem.at[index])
        for index in range(stored)
    ]
    for copy in raw_copies + table_copies:
        copy.start()
    rows = raw_ref.shape[1] // 3
    blocks = stored * rows // BLOCK
    lanes = pl.ds(pl.multiple_of(where_ref[0] * LANES, LANES), LANES)
    p = [params_ref[0, row : row + 1, lanes] for row in range(7)]

    for index in range(stored):
        inv_rows[2 * index : 2 * index + 2, :] = inv_ref[pl.ds(2 * gathered_ref[index], 2), :]
    inv[...] = jnp.concatenate([inv_rows[...]] * (128 // (2 * stored)), axis=0).T
    for index in range(stored):
        raw_copies[index].wait()
        at = pl.multiple_of(order_ref[index] * rows, rows)
        inv_fwd = inv[:, 2 * index : 2 * index + 1]
        inv_saved = inv[:, 2 * index + 1 : 2 * index + 2]
        scaled = raw_ref[index, :rows, :].astype(jnp.float32) * inv_fwd * p[0]
        mixed = (scaled * p[3] + p[4]) * (scaled * p[5] + p[6])
        scaled = raw_ref[index, rows : 2 * rows, :].astype(jnp.float32) * inv_saved * p[0]
        cot = raw_ref[index, 2 * rows :, :].astype(jnp.float32)
        ordered[pl.ds(at, rows), :LANES] = mixed.astype(jnp.bfloat16)
        ordered[pl.ds(at, rows), LANES:] = (cot * (scaled * p[1] + p[2])).astype(jnp.bfloat16)

    table_copies[0].wait()
    table_copies[1].wait()
    for index in range(blocks):
        data = ordered[index * BLOCK : (index + 1) * BLOCK, :]
        spectra[index] = enter_transform(enter_hi, enter_lo, data)

    def products(tile, carry):
        low = pl.ds(pl.multiple_of(tile * 8, 8), 8)
        high = pl.ds(pl.multiple_of(BLOCK + tile * 8, 8), 8)
        f_re = [filt[d, 0, low, :] for d in range(blocks)]
        f_im = [filt[d, 1, low, :] for d in range(blocks)]
        f_nq = [filt[d, 2, low, :] for d in range(blocks)]
        for adjoint in (False, True):
            lanes = slice(LANES, 2 * LANES) if adjoint else slice(0, LANES)
            x_re = [spectra[j, low, lanes] for j in range(blocks)]
            x_im = [spectra[j, high, lanes] for j in range(blocks)]
            for i in range(blocks):
                re = im = None
                for j in range(i, blocks) if adjoint else range(i + 1):
                    d = abs(i - j)
                    a, b = f_re[d] * x_re[j], f_im[d] * x_im[j]
                    c, e = f_nq[d] * x_im[j], f_im[d] * x_re[j]
                    one = a + b if adjoint else a - b
                    two = c - e if adjoint else c + e
                    re = one if re is None else re + one
                    im = two if im is None else im + two
                product[i, low, lanes] = re
                product[i, high, lanes] = im
        return carry

    lax.fori_loop(0, BLOCK // 8, products, 0)

    table_copies[2].wait()
    table_copies[3].wait()
    for index in range(blocks):
        value = product[index]
        top = value.astype(jnp.bfloat16)
        rest = (value - top.astype(jnp.float32)).astype(jnp.bfloat16)
        left = (
            jnp.dot(leave_hi[...], top, preferred_element_type=jnp.float32)
            + jnp.dot(leave_lo[...], top, preferred_element_type=jnp.float32)
            + jnp.dot(leave_hi[...], rest, preferred_element_type=jnp.float32)
        )
        ordered[index * BLOCK : (index + 1) * BLOCK, :] = left.astype(jnp.bfloat16)

    sums = [jnp.zeros((8, LANES), jnp.float32)] * 3
    for index in range(stored):
        at = pl.multiple_of(order_ref[index] * rows, rows)
        block = ordered[pl.ds(at, rows), :]
        out_ref[index, :rows, :] = block
        grad_mixed = block[:, LANES:].astype(jnp.float32)
        inv_saved = inv[:, 2 * index + 1 : 2 * index + 2]
        normed = raw_ref[index, rows : 2 * rows, :].astype(jnp.float32) * inv_saved
        once = grad_mixed * normed
        for power, term in enumerate((grad_mixed, once, once * normed)):
            sums[power] = sums[power] + fold(term)

    sums = jnp.concatenate(
        [jnp.sum(total, axis=0, keepdims=True) for total in sums]
        + [jnp.zeros((5, LANES), jnp.float32)],
        axis=0,
    )
    top = sums.astype(jnp.bfloat16)
    rest = (sums - top.astype(jnp.float32)).astype(jnp.bfloat16)
    for index in range(stored):
        out_ref[index, rows : rows + 8, :LANES] = top
        out_ref[index, rows : rows + 8, LANES:] = rest
        out_copies[index].start()
    for copy in out_copies:
        copy.wait()


def convolve(where, order, gathered, raw, inv, params, spectra, tables):
    stored = raw.shape[0]
    rows = raw.shape[1] // 3
    length = stored * rows
    blocks = length // BLOCK
    return pl.pallas_call(
        conv_kernel,
        out_shape=pltpu.HBM((stored, rows + 8, 2 * LANES), jnp.bfloat16),
        in_specs=[SMEM] * 3 + [VMEM] * 3 + [HBM] * 5,
        out_specs=HBM,
        scratch_shapes=[
            pltpu.VMEM(raw.shape, jnp.bfloat16),
            *[pltpu.VMEM(table.shape, jnp.bfloat16) for table in tables],
            pltpu.VMEM((stored, rows + 8, 2 * LANES), jnp.bfloat16),
            pltpu.VMEM((length, 2 * LANES), jnp.bfloat16),
            pltpu.VMEM((blocks, 2 * BLOCK, 2 * LANES), jnp.float32),
            pltpu.VMEM((blocks, 2 * BLOCK, 2 * LANES), jnp.float32),
            pltpu.VMEM((2 * stored, 128), jnp.float32),
            pltpu.VMEM((128, 128), jnp.float32),
            pltpu.SemaphoreType.DMA((stored,)),
            pltpu.SemaphoreType.DMA((4,)),
            pltpu.SemaphoreType.DMA((stored,)),
        ],
        name="convolve",
        compiler_params=pltpu.CompilerParams(vmem_limit_bytes=28 << 20),
    )(
        where, order, gathered, inv, params, in_vmem(spectra), in_hbm(raw),
        *[in_hbm(table) for table in tables],
    )


def leave_kernel(
    pipe_ref, inv_ref, back_ref, known_ref, fwd_ref, saved_ref, sconv_ref, cot_ref, params_ref,
    layer_ref, send_ref, partial_ref, grads_ref, cross_ref, inv, acc,
):
    step = pl.program_id(0)
    rows = fwd_ref.shape[1]

    @pl.when(step == 0)
    def _():
        inv[...] = rows_to_columns(inv_ref[0:8, :])
        acc[...] = jnp.zeros_like(acc)

    inv_fwd = inv[:, 0:1]
    inv_saved = inv[:, 1:2]
    first = pipe_ref[0] == 0
    cross = acc[...]
    groups = fwd_ref.shape[2] // LANES
    for group in range(groups):
        at = pl.ds(group * LANES, LANES)
        p = [params_ref[0, row : row + 1, at] for row in range(7)]
        inputs = fwd_ref[0, :, at].astype(jnp.float32)
        query = inputs * inv_fwd * p[0] * p[1] + p[2]
        conv = back_ref[step * groups + group, :rows, :LANES].astype(jnp.float32)
        layer = inputs + query * conv
        layer_ref[0, :, at] = layer.astype(jnp.bfloat16)

        grad_mixed = back_ref[step * groups + group, :rows, LANES:].astype(jnp.float32)
        cot = cot_ref[0, :, at].astype(jnp.float32)
        normed = saved_ref[0, :, at].astype(jnp.float32) * inv_saved
        scaled = normed * p[0]
        grad_query = cot * sconv_ref[0, :, at].astype(jnp.float32)
        mixed_grad = (scaled * p[5] + p[6]) * p[3] + (scaled * p[3] + p[4]) * p[5]
        grad_normed = (grad_query * p[1] + grad_mixed * mixed_grad) * p[0]
        cross = cross + grad_normed * normed
        partial = cot + inv_saved * grad_normed
        partial_ref[0, :, at] = partial
        send_ref[0, :, at] = jnp.where(first, layer, partial).astype(jnp.bfloat16)

        extra = back_ref[step * groups + group, rows : rows + 8, :].astype(jnp.float32)
        extra = extra[:, :LANES] + extra[:, LANES:]
        m0, m1, m2 = extra[0:1], extra[1:2], extra[2:3]
        q0, q1 = known_ref[0:1, at], known_ref[1:2, at]
        key_normed = p[0] * p[5] * m2 + p[6] * m1
        value_normed = p[0] * p[3] * m2 + p[4] * m1
        grads = [
            p[1] * q1 + p[3] * key_normed + p[5] * value_normed,
            p[0] * q1,
            q0,
            p[0] * key_normed,
            p[0] * p[5] * m1 + p[6] * m0,
            p[0] * value_normed,
            p[0] * p[3] * m1 + p[4] * m0,
        ]
        grads_ref[0, :, at] = jnp.concatenate(grads, axis=0)
    acc[...] = cross

    @pl.when(step == pl.num_programs(0) - 1)
    def _():
        cross = columns_to_rows([jnp.sum(acc[...], axis=1, keepdims=True)])[0:1]
        cross_ref[...] = jnp.broadcast_to(cross, (8, 128))


def leave(pipe, inv, back, known, fwd_in, saved_in, saved_conv, grad_out, mix_params):
    rows, width = fwd_in.shape[1:]
    wide = 512
    spec, params = lane_spec(rows, wide), lane_spec(7, wide)
    return pl.pallas_call(
        leave_kernel,
        out_shape=(
            jax.ShapeDtypeStruct(fwd_in.shape, jnp.bfloat16),
            jax.ShapeDtypeStruct(fwd_in.shape, jnp.bfloat16),
            jax.ShapeDtypeStruct(fwd_in.shape, jnp.float32),
            jax.ShapeDtypeStruct(mix_params.shape, jnp.float32),
            jax.ShapeDtypeStruct((8, 128), jnp.float32),
        ),
        grid_spec=pltpu.PrefetchScalarGridSpec(
            num_scalar_prefetch=1,
            grid=(width // wide,),
            in_specs=[VMEM, VMEM, pl.BlockSpec((2, wide), lambda step, *_: (0, step))]
            + [spec] * 4
            + [params],
            out_specs=(spec, spec, spec, params, whole((8, 128))),
            scratch_shapes=[pltpu.VMEM((rows, 128), jnp.float32)] * 2,
        ),
        name="leave",
        compiler_params=pltpu.CompilerParams(vmem_limit_bytes=24 << 20),
    )(pipe, inv, in_vmem(back), known, fwd_in, saved_in, saved_conv, grad_out, mix_params)


def subtract_kernel(scale_ref, value_ref, saved_ref, out_ref, scale):
    @pl.when(pl.program_id(0) == 0)
    def _():
        scale[...] = rows_to_columns(scale_ref[...])

    factor = scale[:, 0:1]
    for at in range(0, out_ref.shape[2], LANES):
        at = pl.ds(at, LANES)
        value = value_ref[0, :, at].astype(jnp.float32)
        saved = saved_ref[0, :, at].astype(jnp.float32)
        out_ref[0, :, at] = (value - saved * factor).astype(jnp.bfloat16)


def subtract(scale_rows, value, saved, resident):
    rows, width = saved.shape[1:]
    wide = width if resident else 1024
    spec = lane_spec(rows, wide)
    if resident:
        value, saved = in_vmem(value), in_vmem(saved)
    return pl.pallas_call(
        subtract_kernel,
        out_shape=jax.ShapeDtypeStruct(saved.shape, jnp.bfloat16),
        grid=(width // wide,),
        in_specs=[VMEM] + [VMEM if resident else spec] * 2,
        out_specs=spec,
        scratch_shapes=[pltpu.VMEM((rows, 128), jnp.float32)],
        compiler_params=pltpu.CompilerParams(vmem_limit_bytes=16 << 20),
    )(scale_rows, value, saved)


def per_device(tables, fwd_in, saved_in, saved_conv, grad_out, filters, mix_params, span_order):
    where = lax.axis_index("seq").astype(jnp.int32).reshape(1)
    pipe = lax.axis_index("pipe").astype(jnp.int32).reshape(1)
    raw, sums = pack(fwd_in, saved_in, grad_out)
    raw = lax.all_to_all(raw, "seq", 0, 0)
    sums = sum(over_chan(sums))[:2]
    sums = jnp.concatenate([sums, across(sums, 1)], axis=0)
    sums = jnp.concatenate([sums] + [round_ring(sums, apart) for apart in (1, 2, 3)], axis=0)
    inv = lax.rsqrt(jnp.concatenate([sums, across(sums, 8)], axis=0) / D + EPSILON)
    spectra = filter_spectra(where, filters, tables)
    peer_saved = lax.ppermute(saved_in, "pipe", [(1, 0)])
    back = convolve(where, span_order, gather_order(), raw, inv, mix_params, spectra, tables)
    back = lax.all_to_all(back, "seq", 0, 0)
    known = early(where, inv, saved_in, saved_conv, grad_out)
    for flip in (1, 2, 4, 8):
        known = known + across(known, flip)
    layer_out, outgoing, partial, param_grad, cross = leave(
        pipe, inv, back, known, fwd_in, saved_in, saved_conv, grad_out, mix_params
    )
    incoming = lax.ppermute(outgoing, "pipe", [(0, 1), (1, 0)])
    crosses = over_chan(cross)
    scale = sum(crosses) * (inv[1:2] * inv[1:2] / D)
    peer_scale = lax.ppermute(scale, "pipe", [(1, 0)])
    input_grad = subtract(scale, partial, saved_in, False)
    received = subtract(peer_scale, incoming, peer_saved, True)
    return (layer_out, input_grad, param_grad, received)


def solution(mesh):
    tables = transform_tables()
    in_specs = (
        P("pipe", "seq", "chan"),
        P("pipe", "seq", "chan"),
        P("pipe", "seq", "chan"),
        P("pipe", "seq", "chan"),
        P("pipe", None, "chan"),
        P("pipe", None, "chan"),
        P(),
    )
    out_specs = (
        P("pipe", "seq", "chan"),
        P("pipe", "seq", "chan"),
        P("pipe", None, "chan"),
        P("pipe", "seq", "chan"),
    )
    return jax.shard_map(
        functools.partial(per_device, tuple(jnp.asarray(table) for table in tables)),
        mesh=mesh,
        in_specs=in_specs,
        out_specs=out_specs,
        check_vma=False,
    )
```

profile of v0, /device:TPU:0, one launch (start us, length us, event | category | flops | bytes accessed | tf_op | source)
XLA Modules:
  0.0 102.1 jit_solution(5408954586370374033)
XLA Ops:
  0.6 4.0 %pack.1 = (bf16[16,384,128]{2,1,0:T(8,128)(2,1)}, f32[8,128]{1,0:T(8,128)S(1)}) custom-call(bf16[1,128,2048]{2,1,0:T(8,128)(2,1)} %fwd_ref.3, bf16[1,128,2048]{2,1,0:T(8,128)(2,1)} %saved_ref.7, bf16[1,128,2048]{2,1,0:T(8,128)(2,1)} %cot_ref.5), custom_call_target="tpu_custom_call" | custom-call | tf_op jit(solution)/shard_map/pack/pallas_call | solution.py:106
  4.6 0.0 copy-start.5
  4.6 5.8 %all-to-all-start = ((bf16[16,384,128]{2,1,0:T(8,128)(2,1)}), bf16[16,384,128]{2,1,0:T(8,128)(2,1)}, u32[]{:S(2)}, u32[]{:S(2)}) async-start(bf16[16,384,128]{2,1,0:T(8,128)(2,1)} %get-tuple-element.12), calls=%async_computation | async-start | bytes 3145728 | tf_op jit(solution)/shard_map/all_to_all | solution.py:513
  10.4 2.0 %collective-permute-start = (f32[8,128]{1,0:T(8,128)S(1)}, f32[8,128]{1,0:T(8,128)S(1)}, u32[]{:S(2)}, u32[]{:S(2)}) collective-permute-start(f32[8,128]{1,0:T(8,128)S(1)} %get-tuple-element.11), channel_id=1, source_target_pairs={{0,1},{1,2},{2,3},{3,0},{4,5},{5,6},{6,7},{7,4},{8,9},{9,10},{10,1... | collective-permute-start | bytes 12296 | tf_op jit(solution)/shard_map/ppermute | solution.py:129
  12.4 3.6 %collective-permute-start.1 = (f32[8,128]{1,0:T(8,128)S(1)}, f32[8,128]{1,0:T(8,128)S(1)}, u32[]{:S(2)}, u32[]{:S(2)}) collective-permute-start(f32[8,128]{1,0:T(8,128)S(1)} %get-tuple-element.11), channel_id=1, source_target_pairs={{0,2},{1,3},{2,0},{3,1},{4,6},{5,7},{6,4},{7,5},{8,10},{9,11},{10,... | collective-permute-start | bytes 12296 | tf_op jit(solution)/shard_map/ppermute | solution.py:129
  16.0 1.0 collective-permute-start.2
  17.0 0.0 collective-permute-done
  17.0 0.6 collective-permute-done.1
  17.6 2.0 %collective-permute-done.2 = f32[8,128]{1,0:T(8,128)S(1)} collective-permute-done((f32[8,128]{1,0:T(8,128)S(1)}, f32[8,128]{1,0:T(8,128)S(1)}, u32[]{:S(2)}, u32[]{:S(2)}) %collective-permute-start.2) | collective-permute-done | bytes 4128 | tf_op jit(solution)/shard_map/ppermute | solution.py:129
  19.6 0.0 collective-permute-start.3
  19.6 1.2 %collective-permute-done.3 = f32[2,128]{1,0:T(2,128)S(1)} collective-permute-done((f32[2,128]{1,0:T(2,128)S(1)}, f32[2,128]{1,0:T(2,128)S(1)}, u32[]{:S(2)}, u32[]{:S(2)}) %collective-permute-start.3) | collective-permute-done | bytes 1056 | tf_op jit(solution)/shard_map/ppermute | solution.py:136
  20.8 1.8 %collective-permute-start.4 = (f32[4,128]{1,0:T(4,128)S(1)}, f32[4,128]{1,0:T(4,128)S(1)}, u32[]{:S(2)}, u32[]{:S(2)}) collective-permute-start(f32[4,128]{1,0:T(4,128)S(1)} %pad_maximum_fusion), channel_id=1, source_target_pairs={{0,8},{4,12},{8,16},{12,20},{16,24},{20,28},{24,0},{28,4},{32,40},... | collective-permute-start | bytes 6152 | tf_op jit(solution)/shard_map/ppermute | solution.py:142
  22.6 2.7 %collective-permute-start.5 = (f32[4,128]{1,0:T(4,128)S(1)}, f32[4,128]{1,0:T(4,128)S(1)}, u32[]{:S(2)}, u32[]{:S(2)}) collective-permute-start(f32[4,128]{1,0:T(4,128)S(1)} %pad_maximum_fusion), channel_id=1, source_target_pairs={{0,16},{4,20},{8,24},{12,28},{16,0},{20,4},{24,8},{28,12},{32,48},... | collective-permute-start | bytes 6152 | tf_op jit(solution)/shard_map/ppermute | solution.py:142
  25.3 1.5 %collective-permute-start.6 = (f32[4,128]{1,0:T(4,128)S(1)}, f32[4,128]{1,0:T(4,128)S(1)}, u32[]{:S(2)}, u32[]{:S(2)}) collective-permute-start(f32[4,128]{1,0:T(4,128)S(1)} %pad_maximum_fusion), channel_id=1, source_target_pairs={{0,24},{4,28},{8,0},{12,4},{16,8},{20,12},{24,16},{28,20},{32,56},... | collective-permute-start | bytes 6152 | tf_op jit(solution)/shard_map/ppermute | solution.py:142
  26.7 2.8 %collective-permute-done.4 = f32[4,128]{1,0:T(4,128)S(1)} collective-permute-done((f32[4,128]{1,0:T(4,128)S(1)}, f32[4,128]{1,0:T(4,128)S(1)}, u32[]{:S(2)}, u32[]{:S(2)}) %collective-permute-start.4) | collective-permute-done | bytes 2080 | tf_op jit(solution)/shard_map/ppermute | solution.py:142
  29.5 0.4 collective-permute-done.5
  29.8 0.0 collective-permute-done.6
  29.9 1.7 %collective-permute-start.7 = (f32[16,128]{1,0:T(8,128)S(1)}, f32[16,128]{1,0:T(8,128)S(1)}, u32[]{:S(2)}, u32[]{:S(2)}) collective-permute-start(f32[16,128]{1,0:T(8,128)S(1)} %concatenate.12), channel_id=1, source_target_pairs={{0,32},{4,36},{8,40},{12,44},{16,48},{20,52},{24,56},{28,60},{32,0... | collective-permute-start | bytes 24584 | tf_op jit(solution)/shard_map/ppermute | solution.py:136
  31.6 0.0 copy-done.5
  31.6 0.0 copy-start.4
  31.6 1.9 %filter_spectra.1.filt = f32[8,3,256,128]{3,2,1,0:T(8,128)S(1)} custom-call(s32[1]{0:T(128)} %bitcast.1.where_ref, bf16[1,2048,2048]{2,1,0:T(8,128)(2,1)} %taps_ref.1, bf16[512,256]{1,0:T(8,128)(2,1)} %constant.90.clone.enter_hi.enter_hi_hbm, bf16[512,256]{1,0:T(8,128)(2,1)} %constant.91.clone.enter_lo.enter_lo_hbm), custom_call_target="tpu_custom_call" | custom-call | tf_op jit(solution)/shard_map/filter_spectra/pallas_call | solution.py:221
  33.5 0.1 collective-permute-done.7
  33.7 0.0 all-to-all-done.raw_hbm
  33.7 0.0 copy-done.4
  33.7 10.7 %convolve.1 = bf16[16,136,256]{2,1,0:T(8,128)(2,1)} custom-call(s32[1]{0:T(128)} %bitcast.1.where_ref, s32[16]{0:T(128)S(1)} %copy-done.4, s32[16]{0:T(128)S(1)} %fusion.4.gathered_ref, f32[32,128]{1,0:T(8,128)S(1)} %add_rsqrt_fusion.inv_ref, f32[1,7,2048]{2,1,0:T(8,128)S(1)} %copy.15.params_ref, f32[8,3,256,128]{3,2,1,0:T(8,128)S(1)} %filter_spectra.1.filt, ...), custom_call_target="tpu_custom_call" | custom-call | tf_op jit(solution)/shard_map/convolve/pallas_call | solution.py:364
  44.4 0.0 copy-start
  44.4 0.0 copy-start.1
  44.4 0.0 copy-start.3
  44.4 0.0 copy-start.2
  44.4 6.2 %all-to-all-start.1 = ((bf16[16,136,256]{2,1,0:T(8,128)(2,1)}), bf16[16,136,256]{2,1,0:T(8,128)(2,1)S(1)}, u32[]{:S(2)}, u32[]{:S(2)}) async-start(bf16[16,136,256]{2,1,0:T(8,128)(2,1)} %convolve.1), calls=%async_computation.1 | async-start | bytes 2228224 | tf_op jit(solution)/shard_map/all_to_all | solution.py:521
  50.7 0.0 copy-done
  50.7 0.0 copy-done.1
  50.7 0.0 copy-done.3
  50.7 0.8 early.1
  51.4 0.5 collective-permute-start.8
  51.9 0.8 collective-permute-done.8
  52.8 1.9 %collective-permute-start.9 = (f32[2,2048]{1,0:T(2,128)S(1)}, f32[2,2048]{1,0:T(2,128)S(1)}, u32[]{:S(2)}, u32[]{:S(2)}) collective-permute-start(f32[2,2048]{1,0:T(2,128)S(1)} %add.60), channel_id=1, source_target_pairs={{0,8},{4,12},{8,0},{12,4},{16,24},{20,28},{24,16},{28,20},{32,40},... | collective-permute-start | bytes 49160 | tf_op jit(solution)/shard_map/ppermute | solution.py:136
  54.7 10.0 %collective-permute-done.9 = f32[2,2048]{1,0:T(2,128)S(1)} collective-permute-done((f32[2,2048]{1,0:T(2,128)S(1)}, f32[2,2048]{1,0:T(2,128)S(1)}, u32[]{:S(2)}, u32[]{:S(2)}) %collective-permute-start.9) | collective-permute-done | bytes 16416 | tf_op jit(solution)/shard_map/ppermute | solution.py:136
  64.8 4.0 %collective-permute-start.10 = (f32[2,2048]{1,0:T(2,128)S(1)}, f32[2,2048]{1,0:T(2,128)S(1)}, u32[]{:S(2)}, u32[]{:S(2)}) collective-permute-start(f32[2,2048]{1,0:T(2,128)S(1)} %add.61), channel_id=1, source_target_pairs={{0,16},{4,20},{8,24},{12,28},{16,0},{20,4},{24,8},{28,12},{32,48},... | collective-permute-start | bytes 49160 | tf_op jit(solution)/shard_map/ppermute | solution.py:136
  68.8 1.7 %collective-permute-done.10 = f32[2,2048]{1,0:T(2,128)S(1)} collective-permute-done((f32[2,2048]{1,0:T(2,128)S(1)}, f32[2,2048]{1,0:T(2,128)S(1)}, u32[]{:S(2)}, u32[]{:S(2)}) %collective-permute-start.10) | collective-permute-done | bytes 16416 | tf_op jit(solution)/shard_map/ppermute | solution.py:136
  70.5 2.3 %collective-permute-start.11 = (f32[2,2048]{1,0:T(2,128)S(1)}, f32[2,2048]{1,0:T(2,128)S(1)}, u32[]{:S(2)}, u32[]{:S(2)}) collective-permute-start(f32[2,2048]{1,0:T(2,128)S(1)} %add.62), channel_id=1, source_target_pairs={{0,32},{4,36},{8,40},{12,44},{16,48},{20,52},{24,56},{28,60},{32,0... | collective-permute-start | bytes 49160 | tf_op jit(solution)/shard_map/ppermute | solution.py:136
  72.9 1.3 %collective-permute-start.17 = (bf16[1,128,2048]{2,1,0:T(8,128)(2,1)S(1)}, bf16[1,128,2048]{2,1,0:T(8,128)(2,1)}, u32[]{:S(2)}, u32[]{:S(2)}) collective-permute-start(bf16[1,128,2048]{2,1,0:T(8,128)(2,1)S(1)} %copy-done), channel_id=1, source_target_pairs={{64,0},{65,1},{66,2},{67,3},{68,4},{69,5},{70,6},{71,7},{72,8},{73... | collective-permute-start | bytes 1572872 | tf_op jit(solution)/shard_map/ppermute | solution.py:519
  74.2 0.4 collective-permute-done.11
  74.6 0.0 all-to-all-done.1.back_ref
  74.6 0.0 copy-done.2
  74.6 2.9 %leave.1 = (bf16[1,128,2048]{2,1,0:T(8,128)(2,1)}, bf16[1,128,2048]{2,1,0:T(8,128)(2,1)S(1)}, f32[1,128,2048]{2,1,0:T(8,128)S(1)}, f32[1,7,2048]{2,1,0:T(8,128)S(1)}, f32[8,128]{1,0:T(8,128)S(1)}) custom-call(s32[1]{0:T(128)} %bitcast.pipe_ref, f32[32,128]{1,0:T(8,128)S(1)} %add_rsqrt_fusion.inv_ref, bf16[16,136,256]{2,1,0:T(8,128)(2,1)S(1)} %all-to-all-done.1.back_ref, ...), custom_call_target="tpu_custom_call" | custom-call | tf_op jit(solution)/shard_map/leave/pallas_call | solution.py:456
  77.5 4.5 %collective-permute-start.16 = (bf16[1,128,2048]{2,1,0:T(8,128)(2,1)S(1)}, bf16[1,128,2048]{2,1,0:T(8,128)(2,1)S(1)}, u32[]{:S(2)}, u32[]{:S(2)}) collective-permute-start(bf16[1,128,2048]{2,1,0:T(8,128)(2,1)S(1)} %get-tuple-element.17), channel_id=1, source_target_pairs={{0,64},{64,0},{1,65},{65,1},{2,66},{66,2},{3,67},{67,3},{4,68},{68... | collective-permute-start | bytes 1572872 | tf_op jit(solution)/shard_map/ppermute | solution.py:528
  82.1 1.9 %collective-permute-start.12 = (f32[8,128]{1,0:T(8,128)S(1)}, f32[8,128]{1,0:T(8,128)S(1)}, u32[]{:S(2)}, u32[]{:S(2)}) collective-permute-start(f32[8,128]{1,0:T(8,128)S(1)} %get-tuple-element.14), channel_id=1, source_target_pairs={{0,1},{1,2},{2,3},{3,0},{4,5},{5,6},{6,7},{7,4},{8,9},{9,10},{10,1... | collective-permute-start | bytes 12296 | tf_op jit(solution)/shard_map/ppermute | solution.py:129
  84.0 3.6 %collective-permute-start.13 = (f32[8,128]{1,0:T(8,128)S(1)}, f32[8,128]{1,0:T(8,128)S(1)}, u32[]{:S(2)}, u32[]{:S(2)}) collective-permute-start(f32[8,128]{1,0:T(8,128)S(1)} %get-tuple-element.14), channel_id=1, source_target_pairs={{0,2},{1,3},{2,0},{3,1},{4,6},{5,7},{6,4},{7,5},{8,10},{9,11},{10,... | collective-permute-start | bytes 12296 | tf_op jit(solution)/shard_map/ppermute | solution.py:129
  87.6 1.0 collective-permute-start.14
  88.6 0.0 collective-permute-done.12
  88.6 0.6 collective-permute-done.13
  89.2 2.0 %collective-permute-done.14 = f32[8,128]{1,0:T(8,128)S(1)} collective-permute-done((f32[8,128]{1,0:T(8,128)S(1)}, f32[8,128]{1,0:T(8,128)S(1)}, u32[]{:S(2)}, u32[]{:S(2)}) %collective-permute-start.14) | collective-permute-done | bytes 4128 | tf_op jit(solution)/shard_map/ppermute | solution.py:129
  91.2 1.3 %collective-permute-start.15 = (f32[8,128]{1,0:T(8,128)S(1)}, f32[8,128]{1,0:T(8,128)S(1)}, u32[]{:S(2)}, u32[]{:S(2)}) collective-permute-start(f32[8,128]{1,0:T(8,128)S(1)} %add_multiply_fusion.scale_ref), channel_id=1, source_target_pairs={{64,0},{65,1},{66,2},{67,3},{68,4},{69,5},{70,6},{71,7},{72,8},{73... | collective-permute-start | bytes 12296 | tf_op jit(solution)/shard_map/ppermute | solution.py:531
  92.5 0.7 copy.17
  93.1 1.2 %shard_map.138 = bf16[1,128,2048]{2,1,0:T(8,128)(2,1)} custom-call(f32[8,128]{1,0:T(8,128)S(1)} %add_multiply_fusion.scale_ref, f32[1,128,2048]{2,1,0:T(8,128)S(1)} %get-tuple-element.15.value_ref, bf16[1,128,2048]{2,1,0:T(8,128)(2,1)S(1)} %copy-done), custom_call_target="tpu_custom_call" | custom-call | tf_op jit(solution)/shard_map/pallas_call | solution.py:498
  94.4 0.0 collective-permute-done.17.saved_ref
  94.4 5.6 %collective-permute-done.15.scale_ref = f32[8,128]{1,0:T(8,128)S(1)} collective-permute-done((f32[8,128]{1,0:T(8,128)S(1)}, f32[8,128]{1,0:T(8,128)S(1)}, u32[]{:S(2)}, u32[]{:S(2)}) %collective-permute-start.15) | collective-permute-done | bytes 4128 | tf_op jit(solution)/shard_map/ppermute | solution.py:531
  100.0 0.0 collective-permute-done.16.value_ref
  100.0 2.1 %shard_map.139 = bf16[1,128,2048]{2,1,0:T(8,128)(2,1)} custom-call(f32[8,128]{1,0:T(8,128)S(1)} %collective-permute-done.15.scale_ref, bf16[1,128,2048]{2,1,0:T(8,128)(2,1)S(1)} %collective-permute-done.16.value_ref, bf16[1,128,2048]{2,1,0:T(8,128)(2,1)} %collective-permute-done.17.saved_ref), custom_call_target="tpu_custom_call" | custom-call | tf_op jit(solution)/shard_map/pallas_call | solution.py:498
  (14 shorter events, 0.2 us)
Async XLA Ops:
  4.6 27.0 %copy-start.5 = (f32[1,7,2048]{2,0,1:T(1,128)S(1)}, f32[1,7,2048]{2,0,1:T(1,128)}, u32[]{:S(2)}) copy-start(f32[1,7,2048]{2,0,1:T(1,128)} %param.16) | copy-start | bytes 172036
  4.6 29.1 %all-to-all-start = ((bf16[16,384,128]{2,1,0:T(8,128)(2,1)}), bf16[16,384,128]{2,1,0:T(8,128)(2,1)}, u32[]{:S(2)}, u32[]{:S(2)}) async-start(bf16[16,384,128]{2,1,0:T(8,128)(2,1)} %get-tuple-element.12), calls=%async_computation | async-start | bytes 3145728 | tf_op jit(solution)/shard_map/all_to_all | solution.py:513
  10.4 6.6 %collective-permute-start = (f32[8,128]{1,0:T(8,128)S(1)}, f32[8,128]{1,0:T(8,128)S(1)}, u32[]{:S(2)}, u32[]{:S(2)}) collective-permute-start(f32[8,128]{1,0:T(8,128)S(1)} %get-tuple-element.11), channel_id=1, source_target_pairs={{0,1},{1,2},{2,3},{3,0},{4,5},{5,6},{6,7},{7,4},{8,9},{9,10},{10,1... | collective-permute-start | bytes 12296 | tf_op jit(solution)/shard_map/ppermute | solution.py:129
  12.4 5.2 %collective-permute-start.1 = (f32[8,128]{1,0:T(8,128)S(1)}, f32[8,128]{1,0:T(8,128)S(1)}, u32[]{:S(2)}, u32[]{:S(2)}) collective-permute-start(f32[8,128]{1,0:T(8,128)S(1)} %get-tuple-element.11), channel_id=1, source_target_pairs={{0,2},{1,3},{2,0},{3,1},{4,6},{5,7},{6,4},{7,5},{8,10},{9,11},{10,... | collective-permute-start | bytes 12296 | tf_op jit(solution)/shard_map/ppermute | solution.py:129
  16.0 3.6 %collective-permute-start.2 = (f32[8,128]{1,0:T(8,128)S(1)}, f32[8,128]{1,0:T(8,128)S(1)}, u32[]{:S(2)}, u32[]{:S(2)}) collective-permute-start(f32[8,128]{1,0:T(8,128)S(1)} %get-tuple-element.11), channel_id=1, source_target_pairs={{0,3},{1,0},{2,1},{3,2},{4,7},{5,4},{6,5},{7,6},{8,11},{9,8},{10,9... | collective-permute-start | bytes 12296 | tf_op jit(solution)/shard_map/ppermute | solution.py:129
  19.6 1.2 %collective-permute-start.3 = (f32[2,128]{1,0:T(2,128)S(1)}, f32[2,128]{1,0:T(2,128)S(1)}, u32[]{:S(2)}, u32[]{:S(2)}) collective-permute-start(f32[2,128]{1,0:T(2,128)S(1)} %slice.7), channel_id=1, source_target_pairs={{0,4},{4,0},{8,12},{12,8},{16,20},{20,16},{24,28},{28,24},{32,36},... | collective-permute-start | bytes 3080 | tf_op jit(solution)/shard_map/ppermute | solution.py:136
  20.8 8.7 %collective-permute-start.4 = (f32[4,128]{1,0:T(4,128)S(1)}, f32[4,128]{1,0:T(4,128)S(1)}, u32[]{:S(2)}, u32[]{:S(2)}) collective-permute-start(f32[4,128]{1,0:T(4,128)S(1)} %pad_maximum_fusion), channel_id=1, source_target_pairs={{0,8},{4,12},{8,16},{12,20},{16,24},{20,28},{24,0},{28,4},{32,40},... | collective-permute-start | bytes 6152 | tf_op jit(solution)/shard_map/ppermute | solution.py:142
  22.6 7.3 %collective-permute-start.5 = (f32[4,128]{1,0:T(4,128)S(1)}, f32[4,128]{1,0:T(4,128)S(1)}, u32[]{:S(2)}, u32[]{:S(2)}) collective-permute-start(f32[4,128]{1,0:T(4,128)S(1)} %pad_maximum_fusion), channel_id=1, source_target_pairs={{0,16},{4,20},{8,24},{12,28},{16,0},{20,4},{24,8},{28,12},{32,48},... | collective-permute-start | bytes 6152 | tf_op jit(solution)/shard_map/ppermute | solution.py:142
  25.3 4.6 %collective-permute-start.6 = (f32[4,128]{1,0:T(4,128)S(1)}, f32[4,128]{1,0:T(4,128)S(1)}, u32[]{:S(2)}, u32[]{:S(2)}) collective-permute-start(f32[4,128]{1,0:T(4,128)S(1)} %pad_maximum_fusion), channel_id=1, source_target_pairs={{0,24},{4,28},{8,0},{12,4},{16,8},{20,12},{24,16},{28,20},{32,56},... | collective-permute-start | bytes 6152 | tf_op jit(solution)/shard_map/ppermute | solution.py:142
  29.9 3.7 %collective-permute-start.7 = (f32[16,128]{1,0:T(8,128)S(1)}, f32[16,128]{1,0:T(8,128)S(1)}, u32[]{:S(2)}, u32[]{:S(2)}) collective-permute-start(f32[16,128]{1,0:T(8,128)S(1)} %concatenate.12), channel_id=1, source_target_pairs={{0,32},{4,36},{8,40},{12,44},{16,48},{20,52},{24,56},{28,60},{32,0... | collective-permute-start | bytes 24584 | tf_op jit(solution)/shard_map/ppermute | solution.py:136
  31.6 2.1 %copy-start.4 = (s32[16]{0:T(128)S(1)}, s32[16]{0:T(128)}, u32[]{:S(2)}) copy-start(s32[16]{0:T(128)} %order_ref.1) | copy-start | bytes 196
  44.4 6.3 %copy-start = (bf16[1,128,2048]{2,1,0:T(8,128)(2,1)S(1)}, bf16[1,128,2048]{2,1,0:T(8,128)(2,1)}, u32[]{:S(2)}) copy-start(bf16[1,128,2048]{2,1,0:T(8,128)(2,1)} %saved_ref.7) | copy-start | bytes 1572868
  44.4 6.3 %copy-start.1 = (bf16[1,128,2048]{2,1,0:T(8,128)(2,1)S(1)}, bf16[1,128,2048]{2,1,0:T(8,128)(2,1)}, u32[]{:S(2)}) copy-start(bf16[1,128,2048]{2,1,0:T(8,128)(2,1)} %cot_ref.5) | copy-start | bytes 1572868
  44.4 6.3 %copy-start.3 = (bf16[1,128,2048]{2,1,0:T(8,128)(2,1)S(1)}, bf16[1,128,2048]{2,1,0:T(8,128)(2,1)}, u32[]{:S(2)}) copy-start(bf16[1,128,2048]{2,1,0:T(8,128)(2,1)} %sconv_ref.3) | copy-start | bytes 1572868
  44.4 30.2 %copy-start.2 = (bf16[1,128,2048]{2,1,0:T(8,128)(2,1)S(1)}, bf16[1,128,2048]{2,1,0:T(8,128)(2,1)}, u32[]{:S(2)}) copy-start(bf16[1,128,2048]{2,1,0:T(8,128)(2,1)} %fwd_ref.3) | copy-start | bytes 1572868
  44.4 30.2 %all-to-all-start.1 = ((bf16[16,136,256]{2,1,0:T(8,128)(2,1)}), bf16[16,136,256]{2,1,0:T(8,128)(2,1)S(1)}, u32[]{:S(2)}, u32[]{:S(2)}) async-start(bf16[16,136,256]{2,1,0:T(8,128)(2,1)} %convolve.1), calls=%async_computation.1 | async-start | bytes 2228224 | tf_op jit(solution)/shard_map/all_to_all | solution.py:521
  51.4 1.3 %collective-permute-start.8 = (f32[2,2048]{1,0:T(2,128)S(1)}, f32[2,2048]{1,0:T(2,128)S(1)}, u32[]{:S(2)}, u32[]{:S(2)}) collective-permute-start(f32[2,2048]{1,0:T(2,128)S(1)} %early.1), channel_id=1, source_target_pairs={{0,4},{4,0},{8,12},{12,8},{16,20},{20,16},{24,28},{28,24},{32,36},... | collective-permute-start | bytes 49160 | tf_op jit(solution)/shard_map/ppermute | solution.py:136
  52.8 12.0 %collective-permute-start.9 = (f32[2,2048]{1,0:T(2,128)S(1)}, f32[2,2048]{1,0:T(2,128)S(1)}, u32[]{:S(2)}, u32[]{:S(2)}) collective-permute-start(f32[2,2048]{1,0:T(2,128)S(1)} %add.60), channel_id=1, source_target_pairs={{0,8},{4,12},{8,0},{12,4},{16,24},{20,28},{24,16},{28,20},{32,40},... | collective-permute-start | bytes 49160 | tf_op jit(solution)/shard_map/ppermute | solution.py:136
  64.8 5.8 %collective-permute-start.10 = (f32[2,2048]{1,0:T(2,128)S(1)}, f32[2,2048]{1,0:T(2,128)S(1)}, u32[]{:S(2)}, u32[]{:S(2)}) collective-permute-start(f32[2,2048]{1,0:T(2,128)S(1)} %add.61), channel_id=1, source_target_pairs={{0,16},{4,20},{8,24},{12,28},{16,0},{20,4},{24,8},{28,12},{32,48},... | collective-permute-start | bytes 49160 | tf_op jit(solution)/shard_map/ppermute | solution.py:136
  70.5 4.0 %collective-permute-start.11 = (f32[2,2048]{1,0:T(2,128)S(1)}, f32[2,2048]{1,0:T(2,128)S(1)}, u32[]{:S(2)}, u32[]{:S(2)}) collective-permute-start(f32[2,2048]{1,0:T(2,128)S(1)} %add.62), channel_id=1, source_target_pairs={{0,32},{4,36},{8,40},{12,44},{16,48},{20,52},{24,56},{28,60},{32,0... | collective-permute-start | bytes 49160 | tf_op jit(solution)/shard_map/ppermute | solution.py:136
  72.9 21.5 %collective-permute-start.17 = (bf16[1,128,2048]{2,1,0:T(8,128)(2,1)S(1)}, bf16[1,128,2048]{2,1,0:T(8,128)(2,1)}, u32[]{:S(2)}, u32[]{:S(2)}) collective-permute-start(bf16[1,128,2048]{2,1,0:T(8,128)(2,1)S(1)} %copy-done), channel_id=1, source_target_pairs={{64,0},{65,1},{66,2},{67,3},{68,4},{69,5},{70,6},{71,7},{72,8},{73... | collective-permute-start | bytes 1572872 | tf_op jit(solution)/shard_map/ppermute | solution.py:519
  77.5 22.5 %collective-permute-start.16 = (bf16[1,128,2048]{2,1,0:T(8,128)(2,1)S(1)}, bf16[1,128,2048]{2,1,0:T(8,128)(2,1)S(1)}, u32[]{:S(2)}, u32[]{:S(2)}) collective-permute-start(bf16[1,128,2048]{2,1,0:T(8,128)(2,1)S(1)} %get-tuple-element.17), channel_id=1, source_target_pairs={{0,64},{64,0},{1,65},{65,1},{2,66},{66,2},{3,67},{67,3},{4,68},{68... | collective-permute-start | bytes 1572872 | tf_op jit(solution)/shard_map/ppermute | solution.py:528
  82.1 6.5 %collective-permute-start.12 = (f32[8,128]{1,0:T(8,128)S(1)}, f32[8,128]{1,0:T(8,128)S(1)}, u32[]{:S(2)}, u32[]{:S(2)}) collective-permute-start(f32[8,128]{1,0:T(8,128)S(1)} %get-tuple-element.14), channel_id=1, source_target_pairs={{0,1},{1,2},{2,3},{3,0},{4,5},{5,6},{6,7},{7,4},{8,9},{9,10},{10,1... | collective-permute-start | bytes 12296 | tf_op jit(solution)/shard_map/ppermute | solution.py:129
  84.0 5.2 %collective-permute-start.13 = (f32[8,128]{1,0:T(8,128)S(1)}, f32[8,128]{1,0:T(8,128)S(1)}, u32[]{:S(2)}, u32[]{:S(2)}) collective-permute-start(f32[8,128]{1,0:T(8,128)S(1)} %get-tuple-element.14), channel_id=1, source_target_pairs={{0,2},{1,3},{2,0},{3,1},{4,6},{5,7},{6,4},{7,5},{8,10},{9,11},{10,... | collective-permute-start | bytes 12296 | tf_op jit(solution)/shard_map/ppermute | solution.py:129
  87.6 3.6 %collective-permute-start.14 = (f32[8,128]{1,0:T(8,128)S(1)}, f32[8,128]{1,0:T(8,128)S(1)}, u32[]{:S(2)}, u32[]{:S(2)}) collective-permute-start(f32[8,128]{1,0:T(8,128)S(1)} %get-tuple-element.14), channel_id=1, source_target_pairs={{0,3},{1,0},{2,1},{3,2},{4,7},{5,4},{6,5},{7,6},{8,11},{9,8},{10,9... | collective-permute-start | bytes 12296 | tf_op jit(solution)/shard_map/ppermute | solution.py:129
  91.2 8.8 %collective-permute-start.15 = (f32[8,128]{1,0:T(8,128)S(1)}, f32[8,128]{1,0:T(8,128)S(1)}, u32[]{:S(2)}, u32[]{:S(2)}) collective-permute-start(f32[8,128]{1,0:T(8,128)S(1)} %add_multiply_fusion.scale_ref), channel_id=1, source_target_pairs={{64,0},{65,1},{66,2},{67,3},{68,4},{69,5},{70,6},{71,7},{72,8},{73... | collective-permute-start | bytes 12296 | tf_op jit(solution)/shard_map/ppermute | solution.py:531
where the time goes:
time: 103 us; the launch traced here: 102 us
  starting transfers between devices  48.6 us (47%)
  waiting for transfers between devices  28.2 us (27%)
  Pallas kernels  23.6 us (23%)
    ppermute x6, waiting for transfers between devices, across(): lax.ppermute(rows, 'seq', [(low, low ^ flip) for low in range(count)])  14.2 us
    ppermute x6, starting transfers between devices, over_chan(): lax.ppermute(rows, 'chan', [(low, (low + apart) % count) for low in range...  13.1 us
    pallas_call x1, Pallas kernels, convolve(): pl.pallas_call(conv_kernel, out_shape=pltpu.HBM((stored, rows + 8, 2 * LA...  10.7 us
    ppermute x6, starting transfers between devices, across(): lax.ppermute(rows, 'seq', [(low, low ^ flip) for low in range(count)])  10.4 us
    all_to_all x1, starting transfers between devices, per_device(): back = lax.all_to_all(back, 'seq', 0, 0)  6.21 us
    ppermute x3, starting transfers between devices, round_ring(): lax.ppermute(rows, 'seq', [(low, place(low)) for low in range(count)])  5.95 us
    all_to_all x1, starting transfers between devices, per_device(): raw = lax.all_to_all(raw, 'seq', 0, 0)  5.79 us
    ppermute x1, waiting for transfers between devices, per_device(): peer_scale = lax.ppermute(scale, 'pipe', [(1, 0)])  5.63 us
  transfers between devices with their start and end apart: 20, of which 12 were waited for; matrix products, arithmetic and copies ran while one was open for 1% of the time, Pallas kernels for 7%

commit v1 on v0

--- a/solution.py
+++ b/solution.py
@@ -73,49 +73,62 @@
     return pl.BlockSpec(shape, lambda step, *_: (0,) * len(shape))
 
 
-def pack_kernel(fwd_ref, saved_ref, cot_ref, out_ref, squares_ref, acc):
-    step = pl.program_id(0)
-    rows = fwd_ref.shape[1]
-
-    @pl.when(step == 0)
-    def _():
-        acc[...] = jnp.zeros_like(acc)
-
-    totals = [acc[0], acc[1]]
-    for group in range(fwd_ref.shape[2] // LANES):
-        at = pl.ds(group * LANES, LANES)
-        for index, ref in enumerate((fwd_ref, saved_ref, cot_ref)):
-            value = ref[0, :, at]
-            out_ref[group, index * rows : (index + 1) * rows, :] = value
-            if index < 2:
-                wide = value.astype(jnp.float32)
-                totals[index] = totals[index] + wide * wide
-    acc[0] = totals[0]
-    acc[1] = totals[1]
-
-    @pl.when(step == pl.num_programs(0) - 1)
-    def _():
-        squares_ref[...] = columns_to_rows(
-            [jnp.sum(acc[index], axis=1, keepdims=True) for index in range(2)]
-        )
+def pack_kernel(fwd_hbm, saved_hbm, cot_hbm, out_hbm, squares_ref, held, in_sem, out_sem):
+    rows, width = held.shape[1:]
+    steps = in_sem.shape[1]
+    wide = width // steps
+    sources = (fwd_hbm, saved_hbm, cot_hbm)
+    arriving = [
+        [
+            pltpu.make_async_copy(
+                source.at[0, :, pl.ds(step * wide, wide)],
+                held.at[index, :, pl.ds(step * wide, wide)],
+                in_sem.at[index, step],
+            )
+            for index, source in enumerate(sources)
+        ]
+        for step in range(steps)
+    ]
+    for copies in arriving:
+        for copy in copies:
+            copy.start()
+    leaving = []
+    totals = [jnp.zeros((rows, LANES), jnp.float32)] * 2
+    for step, copies in enumerate(arriving):
+        for index, copy in enumerate(copies):
+            copy.wait()
+            for group in range(step * wide // LANES, (step + 1) * wide // LANES):
+                out = pltpu.make_async_copy(
+                    held.at[index, :, pl.ds(group * LANES, LANES)],
+                    out_hbm.at[group, pl.ds(index * rows, rows), :],
+                    out_sem.at[index, group],
+                )
+                out.start()
+                leaving.append(out)
+        for index in range(2):
+            for group in range(step * wide // LANES, (step + 1) * wide // LANES):
+                value = held[index, :, group * LANES : (group + 1) * LANES].astype(jnp.float32)
+                totals[index] = totals[index] + value * value
+    squares_ref[...] = columns_to_rows([jnp.sum(total, axis=1, keepdims=True) for total in totals])
+    for copy in leaving:
+        copy.wait()
 
 
 def pack(fwd_in, saved_in, grad_out):
     rows, width = fwd_in.shape[1:]
-    wide = 512
     return pl.pallas_call(
         pack_kernel,
         out_shape=(
-            jax.ShapeDtypeStruct((width // LANES, 3 * rows, LANES), jnp.bfloat16),
+            pltpu.HBM((width // LANES, 3 * rows, LANES), jnp.bfloat16),
             jax.ShapeDtypeStruct((8, 128), jnp.float32),
         ),
-        grid=(width // wide,),
-        in_specs=[lane_spec(rows, wide)] * 3,
-        out_specs=(
-            pl.BlockSpec((wide // LANES, 3 * rows, LANES), lambda step: (step, 0, 0)),
-            whole((8, 128)),
-        ),
-        scratch_shapes=[pltpu.VMEM((2, rows, 128), jnp.float32)],
+        in_specs=[HBM] * 3,
+        out_specs=(HBM, VMEM),
+        scratch_shapes=[
+            pltpu.VMEM((3, rows, width), jnp.bfloat16),
+            pltpu.SemaphoreType.DMA((3, 4)),
+            pltpu.SemaphoreType.DMA((3, width // LANES)),
+        ],
         name="pack",
         compiler_params=pltpu.CompilerParams(vmem_limit_bytes=16 << 20),
     )(in_hbm(fwd_in), in_hbm(saved_in), in_hbm(grad_out))
@@ -151,36 +164,38 @@
     return side * 8 + back * 2 + core
 
 
-def early_kernel(where_ref, inv_ref, saved_ref, sconv_ref, cot_ref, out_ref, inv):
-    @pl.when(pl.program_id(0) == 0)
+def early_kernel(sums_ref, saved_ref, sconv_ref, cot_ref, out_ref, inv):
+    step = pl.program_id(0)
+
+    @pl.when(step == 0)
     def _():
-        inv[...] = rows_to_columns(inv_ref[0:8, :])
+        inv[...] = rows_to_columns(lax.rsqrt(sums_ref[...] / D + EPSILON))
 
     inv_saved = inv[:, 1:2]
-    for group in range(saved_ref.shape[2] // LANES):
-        at = pl.ds(group * LANES, LANES)
+    pairs = saved_ref.shape[2] // (2 * LANES)
+    half = out_ref.shape[0] // 2
+    for pair in range(pairs):
+        at = pl.ds(pair * 2 * LANES, 2 * LANES)
         normed = saved_ref[0, :, at].astype(jnp.float32) * inv_saved
         grad_query = cot_ref[0, :, at].astype(jnp.float32) * sconv_ref[0, :, at].astype(jnp.float32)
-        out_ref[0:1, at] = jnp.sum(grad_query, axis=0, keepdims=True)
-        out_ref[1:2, at] = jnp.sum(grad_query * normed, axis=0, keepdims=True)
-
-
-def early(where, inv, saved_in, saved_conv, grad_out):
+        row = step * pairs + pair
+        out_ref[pl.ds(row, 1), :] = jnp.sum(grad_query, axis=0, keepdims=True)
+        out_ref[pl.ds(row + half, 1), :] = jnp.sum(grad_query * normed, axis=0, keepdims=True)
+
+
+def early(sums, saved_in, saved_conv, grad_out):
     rows, width = saved_in.shape[1:]
     wide = 512
     return pl.pallas_call(
         early_kernel,
-        out_shape=jax.ShapeDtypeStruct((2, width), jnp.float32),
-        grid_spec=pltpu.PrefetchScalarGridSpec(
-            num_scalar_prefetch=1,
-            grid=(width // wide,),
-            in_specs=[VMEM] + [lane_spec(rows, wide)] * 3,
-            out_specs=pl.BlockSpec((2, wide), lambda step, *_: (0, step)),
-            scratch_shapes=[pltpu.VMEM((rows, 128), jnp.float32)],
-        ),
+        out_shape=jax.ShapeDtypeStruct((width // LANES, 2 * LANES), jnp.float32),
+        grid=(width // wide,),
+        in_specs=[VMEM] + [lane_spec(rows, wide)] * 3,
+        out_specs=whole((width // LANES, 2 * LANES)),
+        scratch_shapes=[pltpu.VMEM((rows, 128), jnp.float32)],
         name="early",
         compiler_params=pltpu.CompilerParams(vmem_limit_bytes=12 << 20),
-    )(where, inv, saved_in, saved_conv, grad_out)
+    )(sums, in_hbm(saved_in), in_hbm(saved_conv), in_hbm(grad_out))
 
 
 def side_by_side(ref, index):
@@ -238,7 +253,7 @@
 
 
 def conv_kernel(
-    where_ref, order_ref, gathered_ref, inv_ref, params_ref, filt, raw_hbm, enter_hi_hbm,
+    where_ref, order_ref, gathered_ref, inv_ref, known_ref, params_ref, filt, raw_hbm, enter_hi_hbm,
     enter_lo_hbm, leave_hi_hbm, leave_lo_hbm, out_hbm, raw_ref, enter_hi, enter_lo, leave_hi,
     leave_lo, out_ref, ordered, spectra, product, inv_rows, inv, raw_sem, table_sem, out_sem,
 ):
@@ -346,30 +361,32 @@
         + [jnp.zeros((5, LANES), jnp.float32)],
         axis=0,
     )
+    known = known_ref[...].astype(jnp.bfloat16)
     top = sums.astype(jnp.bfloat16)
     rest = (sums - top.astype(jnp.float32)).astype(jnp.bfloat16)
     for index in range(stored):
-        out_ref[index, rows : rows + 8, :LANES] = top
-        out_ref[index, rows : rows + 8, LANES:] = rest
+        out_ref[index, rows : rows + 16, :] = known
+        out_ref[index, rows + 16 :, :LANES] = top
+        out_ref[index, rows + 16 :, LANES:] = rest
         out_copies[index].start()
     for copy in out_copies:
         copy.wait()
 
 
-def convolve(where, order, gathered, raw, inv, params, spectra, tables):
+def convolve(where, order, gathered, raw, inv, known, params, spectra, tables):
     stored = raw.shape[0]
     rows = raw.shape[1] // 3
     length = stored * rows
     blocks = length // BLOCK
     return pl.pallas_call(
         conv_kernel,
-        out_shape=pltpu.HBM((stored, rows + 8, 2 * LANES), jnp.bfloat16),
-        in_specs=[SMEM] * 3 + [VMEM] * 3 + [HBM] * 5,
+        out_shape=pltpu.HBM((stored, rows + 24, 2 * LANES), jnp.bfloat16),
+        in_specs=[SMEM] * 3 + [VMEM] * 4 + [HBM] * 5,
         out_specs=HBM,
         scratch_shapes=[
             pltpu.VMEM(raw.shape, jnp.bfloat16),
             *[pltpu.VMEM(table.shape, jnp.bfloat16) for table in tables],
-            pltpu.VMEM((stored, rows + 8, 2 * LANES), jnp.bfloat16),
+            pltpu.VMEM((stored, rows + 24, 2 * LANES), jnp.bfloat16),
             pltpu.VMEM((length, 2 * LANES), jnp.bfloat16),
             pltpu.VMEM((blocks, 2 * BLOCK, 2 * LANES), jnp.float32),
             pltpu.VMEM((blocks, 2 * BLOCK, 2 * LANES), jnp.float32),
@@ -382,14 +399,14 @@
         name="convolve",
         compiler_params=pltpu.CompilerParams(vmem_limit_bytes=28 << 20),
     )(
-        where, order, gathered, inv, params, in_vmem(spectra), in_hbm(raw),
+        where, order, gathered, inv, known, params, in_vmem(spectra), in_hbm(raw),
         *[in_hbm(table) for table in tables],
     )
 
 
 def leave_kernel(
-    pipe_ref, inv_ref, back_ref, known_ref, fwd_ref, saved_ref, sconv_ref, cot_ref, params_ref,
-    layer_ref, send_ref, partial_ref, grads_ref, cross_ref, inv, acc,
+    pipe_ref, inv_ref, back_ref, fwd_ref, saved_ref, sconv_ref, cot_ref, params_ref,
+    layer_ref, send_ref, partial_ref, grads_ref, cross_ref, inv, acc, known,
 ):
     step = pl.program_id(0)
     rows = fwd_ref.shape[1]
@@ -398,6 +415,11 @@
     def _():
         inv[...] = rows_to_columns(inv_ref[0:8, :])
         acc[...] = jnp.zeros_like(acc)
+        total = back_ref[0, rows : rows + 16, :].astype(jnp.float32)
+        for index in range(1, back_ref.shape[0]):
+            total = total + back_ref[index, rows : rows + 16, :].astype(jnp.float32)
+        for row in range(16):
+            known[row] = total[row : row + 1, :]
 
     inv_fwd = inv[:, 0:1]
     inv_saved = inv[:, 1:2]
@@ -425,10 +447,12 @@
         partial_ref[0, :, at] = partial
         send_ref[0, :, at] = jnp.where(first, layer, partial).astype(jnp.bfloat16)
 
-        extra = back_ref[step * groups + group, rows : rows + 8, :].astype(jnp.float32)
+        extra = back_ref[step * groups + group, rows + 16 :, :].astype(jnp.float32)
         extra = extra[:, :LANES] + extra[:, LANES:]
         m0, m1, m2 = extra[0:1], extra[1:2], extra[2:3]
-        q0, q1 = known_ref[0:1, at], known_ref[1:2, at]
+        row = step * (groups // 2) + group // 2
+        side = slice(group % 2 * LANES, (group % 2 + 1) * LANES)
+        q0, q1 = known[row, :, side], known[row + 8, :, side]
         key_normed = p[0] * p[5] * m2 + p[6] * m1
         value_normed = p[0] * p[3] * m2 + p[4] * m1
         grads = [
@@ -445,11 +469,11 @@
 
     @pl.when(step == pl.num_programs(0) - 1)
     def _():
-        cross = columns_to_rows([jnp.sum(acc[...], axis=1, keepdims=True)])[0:1]
-        cross_ref[...] = jnp.broadcast_to(cross, (8, 128))
-
-
-def leave(pipe, inv, back, known, fwd_in, saved_in, saved_conv, grad_out, mix_params):
+        cross = columns_to_rows([jnp.sum(acc[...], axis=1, keepdims=True)])
+        cross_ref[...] = cross * (inv_ref[1:2, :] * inv_ref[1:2, :] / D)
+
+
+def leave(pipe, inv, back, fwd_in, saved_in, saved_conv, grad_out, mix_params):
     rows, width = fwd_in.shape[1:]
     wide = 512
     spec, params = lane_spec(rows, wide), lane_spec(7, wide)
@@ -465,72 +489,76 @@
         grid_spec=pltpu.PrefetchScalarGridSpec(
             num_scalar_prefetch=1,
             grid=(width // wide,),
-            in_specs=[VMEM, VMEM, pl.BlockSpec((2, wide), lambda step, *_: (0, step))]
+            in_specs=[VMEM, VMEM]
             + [spec] * 4
             + [params],
             out_specs=(spec, spec, spec, params, whole((8, 128))),
-            scratch_shapes=[pltpu.VMEM((rows, 128), jnp.float32)] * 2,
+            scratch_shapes=[pltpu.VMEM((rows, 128), jnp.float32)] * 2
+            + [pltpu.VMEM((16, 1, 2 * LANES), jnp.float32)],
         ),
         name="leave",
         compiler_params=pltpu.CompilerParams(vmem_limit_bytes=24 << 20),
-    )(pipe, inv, in_vmem(back), known, fwd_in, saved_in, saved_conv, grad_out, mix_params)
-
-
-def subtract_kernel(scale_ref, value_ref, saved_ref, out_ref, scale):
-    @pl.when(pl.program_id(0) == 0)
+    )(pipe, inv, in_vmem(back), fwd_in, saved_in, saved_conv, grad_out, mix_params)
+
+
+def subtract_kernel(row, s0, s1, s2, s3, value_ref, saved_ref, out_ref, scale):
+    step = pl.program_id(0)
+
+    @pl.when(step == 0)
     def _():
-        scale[...] = rows_to_columns(scale_ref[...])
-
-    factor = scale[:, 0:1]
-    for at in range(0, out_ref.shape[2], LANES):
-        at = pl.ds(at, LANES)
-        value = value_ref[0, :, at].astype(jnp.float32)
-        saved = saved_ref[0, :, at].astype(jnp.float32)
-        out_ref[0, :, at] = (value - saved * factor).astype(jnp.bfloat16)
-
-
-def subtract(scale_rows, value, saved, resident):
+        scale[...] = rows_to_columns(s0[...] + s1[...] + s2[...] + s3[...])
+
+    factor = scale[:, row : row + 1]
+    wide = out_ref.shape[2]
+    for at in range(0, wide, LANES):
+        source = pl.ds(at, LANES)
+        if value_ref.shape[2] != wide:
+            source = pl.ds(pl.multiple_of(step * wide + at, LANES), LANES)
+        value = value_ref[0, :, source].astype(jnp.float32)
+        saved = saved_ref[0, :, source].astype(jnp.float32)
+        out_ref[0, :, pl.ds(at, LANES)] = (value - saved * factor).astype(jnp.bfloat16)
+
+
+def subtract(row, scales, value, saved, resident):
     rows, width = saved.shape[1:]
-    wide = width if resident else 1024
+    wide = 512
     spec = lane_spec(rows, wide)
     if resident:
         value, saved = in_vmem(value), in_vmem(saved)
     return pl.pallas_call(
-        subtract_kernel,
+        functools.partial(subtract_kernel, row),
         out_shape=jax.ShapeDtypeStruct(saved.shape, jnp.bfloat16),
         grid=(width // wide,),
-        in_specs=[VMEM] + [VMEM if resident else spec] * 2,
+        in_specs=[VMEM] * 4 + [VMEM if resident else spec] * 2,
         out_specs=spec,
         scratch_shapes=[pltpu.VMEM((rows, 128), jnp.float32)],
         compiler_params=pltpu.CompilerParams(vmem_limit_bytes=16 << 20),
-    )(scale_rows, value, saved)
+    )(*scales, value, saved)
 
 
 def per_device(tables, fwd_in, saved_in, saved_conv, grad_out, filters, mix_params, span_order):
     where = lax.axis_index("seq").astype(jnp.int32).reshape(1)
     pipe = lax.axis_index("pipe").astype(jnp.int32).reshape(1)
+    peer_saved = lax.ppermute(saved_in, "pipe", [(1, 0)])
     raw, sums = pack(fwd_in, saved_in, grad_out)
     raw = lax.all_to_all(raw, "seq", 0, 0)
-    sums = sum(over_chan(sums))[:2]
+    own_sums = sum(over_chan(sums))
+    sums = own_sums[:2]
     sums = jnp.concatenate([sums, across(sums, 1)], axis=0)
     sums = jnp.concatenate([sums] + [round_ring(sums, apart) for apart in (1, 2, 3)], axis=0)
     inv = lax.rsqrt(jnp.concatenate([sums, across(sums, 8)], axis=0) / D + EPSILON)
     spectra = filter_spectra(where, filters, tables)
-    peer_saved = lax.ppermute(saved_in, "pipe", [(1, 0)])
-    back = convolve(where, span_order, gather_order(), raw, inv, mix_params, spectra, tables)
+    known = early(own_sums, saved_in, saved_conv, grad_out)
+    back = convolve(where, span_order, gather_order(), raw, inv, known, mix_params, spectra, tables)
     back = lax.all_to_all(back, "seq", 0, 0)
-    known = early(where, inv, saved_in, saved_conv, grad_out)
-    for flip in (1, 2, 4, 8):
-        known = known + across(known, flip)
     layer_out, outgoing, partial, param_grad, cross = leave(
-        pipe, inv, back, known, fwd_in, saved_in, saved_conv, grad_out, mix_params
-    )
+        pipe, inv, back, fwd_in, saved_in, saved_conv, grad_out, mix_params
+    )
+    peer_cross = lax.ppermute(cross, "pipe", [(1, 0)])
     incoming = lax.ppermute(outgoing, "pipe", [(0, 1), (1, 0)])
-    crosses = over_chan(cross)
-    scale = sum(crosses) * (inv[1:2] * inv[1:2] / D)
-    peer_scale = lax.ppermute(scale, "pipe", [(1, 0)])
-    input_grad = subtract(scale, partial, saved_in, False)
-    received = subtract(peer_scale, incoming, peer_saved, True)
+    scales = over_chan(jnp.concatenate([cross[:1], peer_cross[:1], cross[:6]], axis=0))
+    input_grad = subtract(0, scales, partial, saved_in, False)
+    received = subtract(1, scales, incoming, peer_saved, True)
     return (layer_out, input_grad, param_grad, received)
 
 

time: 103 us -> 106 us (1.029)
  waiting for transfers between devices: 28.2 us -> 41.1 us
  starting transfers between devices: 48.6 us -> 37 us
  Pallas kernels: 23.6 us -> 25.6 us
    all_to_all x1, waiting for transfers between devices: 0.01 us -> 17.4 us  [per_device(): back = lax.all_to_all(back, 'seq', 0, 0)]
    ppermute x6 -> x2, waiting for transfers between devices: 14.2 us -> 1.16 us  [across(): lax.ppermute(rows, 'seq', [(low, low ^ flip) for low in range(count)])]
    ppermute x6 -> x2, starting transfers between devices: 10.4 us -> 1.66 us  [across(): lax.ppermute(rows, 'seq', [(low, low ^ flip) for low in range(count)])]
    ppermute x1, waiting for transfers between devices: 5.63 us -> 14 us  [per_device(): peer_cross = lax.ppermute(cross, 'pipe', [(1, 0)])]
    pallas_call x5, Pallas kernels: 18.8 us -> 20.8 us  [the longest x1 10.7 us: convolve(): pl.pallas_call(conv_kernel, out_shape=pltpu.HBM((stored, rows + 24, 2 * L...]
    ppermute x1, starting transfers between devices: 4.52 us -> 3.3 us  [per_device(): incoming = lax.ppermute(outgoing, 'pipe', [(0, 1), (1, 0)])]
  transfers between devices with their start and end apart: 20 -> 16, of which waited for: 12 -> 9; matrix products, arithmetic and copies ran while one was open for 1% -> 1% of each run, Pallas kernels for 7% -> 9%
where the time goes in v1:
time: 106 us; the launch traced here: 105 us
  waiting for transfers between devices  41.1 us (39%)
  starting transfers between devices  37 us (35%)
  Pallas kernels  25.6 us (24%)
    all_to_all x1, waiting for transfers between devices, per_device(): back = lax.all_to_all(back, 'seq', 0, 0)  17.4 us
    ppermute x1, waiting for transfers between devices, per_device(): peer_cross = lax.ppermute(cross, 'pipe', [(1, 0)])  14 us
    ppermute x6, starting transfers between devices, over_chan(): lax.ppermute(rows, 'chan', [(low, (low + apart) % count) for low in range...  12.6 us
    pallas_call x1, Pallas kernels, convolve(): pl.pallas_call(conv_kernel, out_shape=pltpu.HBM((stored, rows + 24, 2 * L...  10.7 us
    ppermute x3, starting transfers between devices, round_ring(): lax.ppermute(rows, 'seq', [(low, place(low)) for low in range(count)])  5.95 us
    all_to_all x1, starting transfers between devices, per_device(): raw = lax.all_to_all(raw, 'seq', 0, 0)  5.8 us
    ppermute x6, waiting for transfers between devices, over_chan(): lax.ppermute(rows, 'chan', [(low, (low + apart) % count) for low in range...  5.42 us
    all_to_all x1, starting transfers between devices, per_device(): back = lax.all_to_all(back, 'seq', 0, 0)  5.18 us
  transfers between devices with their start and end apart: 16, of which 9 were waited for; matrix products, arithmetic and copies ran while one was open for 1% of the time, Pallas kernels for 9%

profile of v1, /device:TPU:0, one launch (start us, length us, event | category | flops | bytes accessed | tf_op | source)
XLA Modules:
  0.0 105.4 jit_solution(13026901929509187435)
XLA Ops:
  0.6 2.7 %pack.1 = (bf16[16,384,128]{2,1,0:T(8,128)(2,1)}, f32[8,128]{1,0:T(8,128)S(1)}) custom-call(bf16[1,128,2048]{2,1,0:T(8,128)(2,1)} %fwd_ref.1, bf16[1,128,2048]{2,1,0:T(8,128)(2,1)} %saved_ref.5, bf16[1,128,2048]{2,1,0:T(8,128)(2,1)} %cot_ref.3), custom_call_target="tpu_custom_call" | custom-call | tf_op jit(solution)/shard_map/pack/pallas_call | solution.py:119
  3.3 0.0 copy-start.5
  3.4 5.8 %all-to-all-start = ((bf16[16,384,128]{2,1,0:T(8,128)(2,1)}), bf16[16,384,128]{2,1,0:T(8,128)(2,1)}, u32[]{:S(2)}, u32[]{:S(2)}) async-start(bf16[16,384,128]{2,1,0:T(8,128)(2,1)} %get-tuple-element.12), calls=%async_computation | async-start | bytes 3145728 | tf_op jit(solution)/shard_map/all_to_all | solution.py:544
  9.2 2.0 %collective-permute-start = (f32[8,128]{1,0:T(8,128)S(1)}, f32[8,128]{1,0:T(8,128)S(1)}, u32[]{:S(2)}, u32[]{:S(2)}) collective-permute-start(f32[8,128]{1,0:T(8,128)S(1)} %get-tuple-element.11), channel_id=1, source_target_pairs={{0,1},{1,2},{2,3},{3,0},{4,5},{5,6},{6,7},{7,4},{8,9},{9,10},{10,1... | collective-permute-start | bytes 12296 | tf_op jit(solution)/shard_map/ppermute | solution.py:142
  11.2 3.6 %collective-permute-start.1 = (f32[8,128]{1,0:T(8,128)S(1)}, f32[8,128]{1,0:T(8,128)S(1)}, u32[]{:S(2)}, u32[]{:S(2)}) collective-permute-start(f32[8,128]{1,0:T(8,128)S(1)} %get-tuple-element.11), channel_id=1, source_target_pairs={{0,2},{1,3},{2,0},{3,1},{4,6},{5,7},{6,4},{7,5},{8,10},{9,11},{10,... | collective-permute-start | bytes 12296 | tf_op jit(solution)/shard_map/ppermute | solution.py:142
  14.7 1.0 collective-permute-start.2
  15.7 0.0 collective-permute-done
  15.7 0.6 collective-permute-done.1
  16.4 2.0 %collective-permute-done.2 = f32[8,128]{1,0:T(8,128)S(1)} collective-permute-done((f32[8,128]{1,0:T(8,128)S(1)}, f32[8,128]{1,0:T(8,128)S(1)}, u32[]{:S(2)}, u32[]{:S(2)}) %collective-permute-start.2) | collective-permute-done | bytes 4128 | tf_op jit(solution)/shard_map/ppermute | solution.py:142
  18.4 0.0 collective-permute-start.3
  18.4 1.2 %collective-permute-done.3 = f32[2,128]{1,0:T(2,128)S(1)} collective-permute-done((f32[2,128]{1,0:T(2,128)S(1)}, f32[2,128]{1,0:T(2,128)S(1)}, u32[]{:S(2)}, u32[]{:S(2)}) %collective-permute-start.3) | collective-permute-done | bytes 1056 | tf_op jit(solution)/shard_map/ppermute | solution.py:149
  19.5 1.8 %collective-permute-start.4 = (f32[4,128]{1,0:T(4,128)S(1)}, f32[4,128]{1,0:T(4,128)S(1)}, u32[]{:S(2)}, u32[]{:S(2)}) collective-permute-start(f32[4,128]{1,0:T(4,128)S(1)} %pad_maximum_fusion.1), channel_id=1, source_target_pairs={{0,8},{4,12},{8,16},{12,20},{16,24},{20,28},{24,0},{28,4},{32,40},... | collective-permute-start | bytes 6152 | tf_op jit(solution)/shard_map/ppermute | solution.py:155
  21.3 2.7 %collective-permute-start.5 = (f32[4,128]{1,0:T(4,128)S(1)}, f32[4,128]{1,0:T(4,128)S(1)}, u32[]{:S(2)}, u32[]{:S(2)}) collective-permute-start(f32[4,128]{1,0:T(4,128)S(1)} %pad_maximum_fusion.1), channel_id=1, source_target_pairs={{0,16},{4,20},{8,24},{12,28},{16,0},{20,4},{24,8},{28,12},{32,48},... | collective-permute-start | bytes 6152 | tf_op jit(solution)/shard_map/ppermute | solution.py:155
  24.0 1.5 %collective-permute-start.6 = (f32[4,128]{1,0:T(4,128)S(1)}, f32[4,128]{1,0:T(4,128)S(1)}, u32[]{:S(2)}, u32[]{:S(2)}) collective-permute-start(f32[4,128]{1,0:T(4,128)S(1)} %pad_maximum_fusion.1), channel_id=1, source_target_pairs={{0,24},{4,28},{8,0},{12,4},{16,8},{20,12},{24,16},{28,20},{32,56},... | collective-permute-start | bytes 6152 | tf_op jit(solution)/shard_map/ppermute | solution.py:155
  25.5 2.8 %collective-permute-done.4 = f32[4,128]{1,0:T(4,128)S(1)} collective-permute-done((f32[4,128]{1,0:T(4,128)S(1)}, f32[4,128]{1,0:T(4,128)S(1)}, u32[]{:S(2)}, u32[]{:S(2)}) %collective-permute-start.4) | collective-permute-done | bytes 2080 | tf_op jit(solution)/shard_map/ppermute | solution.py:155
  28.2 0.4 collective-permute-done.5
  28.6 0.0 collective-permute-done.6
  28.6 1.7 %collective-permute-start.7 = (f32[16,128]{1,0:T(8,128)S(1)}, f32[16,128]{1,0:T(8,128)S(1)}, u32[]{:S(2)}, u32[]{:S(2)}) collective-permute-start(f32[16,128]{1,0:T(8,128)S(1)} %concatenate.15), channel_id=1, source_target_pairs={{0,32},{4,36},{8,40},{12,44},{16,48},{20,52},{24,56},{28,60},{32,0... | collective-permute-start | bytes 24584 | tf_op jit(solution)/shard_map/ppermute | solution.py:149
  30.3 0.0 copy-done.5
  30.4 1.9 %filter_spectra.1.filt = f32[8,3,256,128]{3,2,1,0:T(8,128)S(1)} custom-call(s32[1]{0:T(128)} %bitcast.1.where_ref, bf16[1,2048,2048]{2,1,0:T(8,128)(2,1)} %taps_ref.1, bf16[512,256]{1,0:T(8,128)(2,1)} %constant.88.clone.enter_hi.enter_hi_hbm, bf16[512,256]{1,0:T(8,128)(2,1)} %constant.89.clone.enter_lo.enter_lo_hbm), custom_call_target="tpu_custom_call" | custom-call | tf_op jit(solution)/shard_map/filter_spectra/pallas_call | solution.py:236
  32.3 0.0 copy-start.4
  32.3 2.6 %early.1.known_ref = f32[16,256]{1,0:T(8,128)S(1)} custom-call(f32[8,128]{1,0:T(8,128)S(1)} %add_add_fusion.sums_ref, bf16[1,128,2048]{2,1,0:T(8,128)(2,1)} %saved_ref.5, bf16[1,128,2048]{2,1,0:T(8,128)(2,1)} %sconv_ref.3, bf16[1,128,2048]{2,1,0:T(8,128)(2,1)} %cot_ref.3), custom_call_target="tpu_custom_call" | custom-call | tf_op jit(solution)/shard_map/early/pallas_call | solution.py:189
  35.0 0.0 collective-permute-done.7
  35.0 0.0 all-to-all-done.raw_hbm
  35.0 0.0 copy-done.4
  35.0 10.7 %convolve.1 = bf16[16,152,256]{2,1,0:T(8,128)(2,1)} custom-call(s32[1]{0:T(128)} %bitcast.1.where_ref, s32[16]{0:T(128)S(1)} %copy-done.4, s32[16]{0:T(128)S(1)} %fusion.4.gathered_ref, f32[32,128]{1,0:T(8,128)S(1)} %add_rsqrt_fusion.inv_ref, f32[16,256]{1,0:T(8,128)S(1)} %early.1.known_ref, f32[1,7,2048]{2,1,0:T(8,128)S(1)} %copy.15.params_ref, ...), custom_call_target="tpu_custom_call" | custom-call | tf_op jit(solution)/shard_map/convolve/pallas_call | solution.py:381
  45.8 0.0 copy-start
  45.8 0.0 copy-start.1
  45.8 0.0 copy-start.2
  45.8 0.0 copy-start.3
  45.9 5.2 %all-to-all-start.1 = ((bf16[16,152,256]{2,1,0:T(8,128)(2,1)}), bf16[16,152,256]{2,1,0:T(8,128)(2,1)S(1)}, u32[]{:S(2)}, u32[]{:S(2)}) async-start(bf16[16,152,256]{2,1,0:T(8,128)(2,1)} %convolve.1), calls=%async_computation.1 | async-start | bytes 2490368 | tf_op jit(solution)/shard_map/all_to_all | solution.py:553
  51.0 0.0 copy-done
  51.1 1.3 %collective-permute-start.13 = (bf16[1,128,2048]{2,1,0:T(8,128)(2,1)S(1)}, bf16[1,128,2048]{2,1,0:T(8,128)(2,1)}, u32[]{:S(2)}, u32[]{:S(2)}) collective-permute-start(bf16[1,128,2048]{2,1,0:T(8,128)(2,1)S(1)} %copy-done), channel_id=1, source_target_pairs={{64,0},{65,1},{66,2},{67,3},{68,4},{69,5},{70,6},{71,7},{72,8},{73... | collective-permute-start | bytes 1572872 | tf_op jit(solution)/shard_map/ppermute | solution.py:542
  52.4 17.4 %all-to-all-done.1.back_ref = bf16[16,152,256]{2,1,0:T(8,128)(2,1)S(1)} async-done(((bf16[16,152,256]{2,1,0:T(8,128)(2,1)}), bf16[16,152,256]{2,1,0:T(8,128)(2,1)S(1)}, u32[]{:S(2)}, u32[]{:S(2)}) %all-to-all-start.1) | async-done | bytes 1245216 | tf_op jit(solution)/shard_map/all_to_all | solution.py:553
  69.7 0.0 copy-done.1
  69.7 0.0 copy-done.2
  69.7 0.0 copy-done.3
  69.7 2.9 %leave.1 = (bf16[1,128,2048]{2,1,0:T(8,128)(2,1)}, bf16[1,128,2048]{2,1,0:T(8,128)(2,1)S(1)}, f32[1,128,2048]{2,1,0:T(8,128)S(1)}, f32[1,7,2048]{2,1,0:T(8,128)S(1)}, f32[8,128]{1,0:T(8,128)S(1)}) custom-call(s32[1]{0:T(128)} %bitcast.pipe_ref, f32[32,128]{1,0:T(8,128)S(1)} %add_rsqrt_fusion.inv_ref, bf16[16,152,256]{2,1,0:T(8,128)(2,1)S(1)} %all-to-all-done.1.back_ref, ...), custom_call_target="tpu_custom_call" | custom-call | tf_op jit(solution)/shard_map/leave/pallas_call | solution.py:480
  72.7 3.3 %collective-permute-start.12 = (bf16[1,128,2048]{2,1,0:T(8,128)(2,1)S(1)}, bf16[1,128,2048]{2,1,0:T(8,128)(2,1)S(1)}, u32[]{:S(2)}, u32[]{:S(2)}) collective-permute-start(bf16[1,128,2048]{2,1,0:T(8,128)(2,1)S(1)} %get-tuple-element.17), channel_id=1, source_target_pairs={{0,64},{64,0},{1,65},{65,1},{2,66},{66,2},{3,67},{67,3},{4,68},{68... | collective-permute-start | bytes 1572872 | tf_op jit(solution)/shard_map/ppermute | solution.py:558
  76.0 1.3 %collective-permute-start.8 = (f32[8,128]{1,0:T(8,128)S(1)}, f32[8,128]{1,0:T(8,128)S(1)}, u32[]{:S(2)}, u32[]{:S(2)}) collective-permute-start(f32[8,128]{1,0:T(8,128)S(1)} %get-tuple-element.14), channel_id=1, source_target_pairs={{64,0},{65,1},{66,2},{67,3},{68,4},{69,5},{70,6},{71,7},{72,8},{73... | collective-permute-start | bytes 12296 | tf_op jit(solution)/shard_map/ppermute | solution.py:557
  77.3 14.0 %collective-permute-done.8 = f32[8,128]{1,0:T(8,128)S(1)} collective-permute-done((f32[8,128]{1,0:T(8,128)S(1)}, f32[8,128]{1,0:T(8,128)S(1)}, u32[]{:S(2)}, u32[]{:S(2)}) %collective-permute-start.8) | collective-permute-done | bytes 4128 | tf_op jit(solution)/shard_map/ppermute | solution.py:557
  91.2 4.0 %collective-permute-start.10 = (f32[8,128]{1,0:T(8,128)S(1)}, f32[8,128]{1,0:T(8,128)S(1)}, u32[]{:S(2)}, u32[]{:S(2)}) collective-permute-start(f32[8,128]{1,0:T(8,128)S(1)} %pad_maximum_fusion.s0), channel_id=1, source_target_pairs={{0,2},{1,3},{2,0},{3,1},{4,6},{5,7},{6,4},{7,5},{8,10},{9,11},{10,... | collective-permute-start | bytes 12296 | tf_op jit(solution)/shard_map/ppermute | solution.py:142
  95.2 0.7 collective-permute-start.11
  95.9 1.3 %collective-permute-start.9 = (f32[8,128]{1,0:T(8,128)S(1)}, f32[8,128]{1,0:T(8,128)S(1)}, u32[]{:S(2)}, u32[]{:S(2)}) collective-permute-start(f32[8,128]{1,0:T(8,128)S(1)} %pad_maximum_fusion.s0), channel_id=1, source_target_pairs={{0,1},{1,2},{2,3},{3,0},{4,5},{5,6},{6,7},{7,4},{8,9},{9,10},{10,1... | collective-permute-start | bytes 12296 | tf_op jit(solution)/shard_map/ppermute | solution.py:142
  97.2 0.7 copy.17
  97.9 0.0 collective-permute-done.10.s2
  97.9 0.9 collective-permute-done.11.s3
  98.8 1.9 %collective-permute-done.9.s1 = f32[8,128]{1,0:T(8,128)S(1)} collective-permute-done((f32[8,128]{1,0:T(8,128)S(1)}, f32[8,128]{1,0:T(8,128)S(1)}, u32[]{:S(2)}, u32[]{:S(2)}) %collective-permute-start.9) | collective-permute-done | bytes 4128 | tf_op jit(solution)/shard_map/ppermute | solution.py:142
  100.7 1.8 %shard_map.138 = bf16[1,128,2048]{2,1,0:T(8,128)(2,1)} custom-call(f32[8,128]{1,0:T(8,128)S(1)} %pad_maximum_fusion.s0, f32[8,128]{1,0:T(8,128)S(1)} %collective-permute-done.9.s1, f32[8,128]{1,0:T(8,128)S(1)} %collective-permute-done.10.s2, f32[8,128]{1,0:T(8,128)S(1)} %collective-permute-done.11.s3, f32[1,128,2048]{2,1,0:T(8,128)S(1)} %get-tuple-element.15.value_ref, ...), custom_call_target="tpu_custom_call" | custom-call | tf_op jit(solution)/shard_map/pallas_call | solution.py:528
  102.6 0.0 collective-permute-done.13.saved_ref
  102.6 0.0 collective-permute-done.12.value_ref
  102.6 2.8 %shard_map.139 = bf16[1,128,2048]{2,1,0:T(8,128)(2,1)} custom-call(f32[8,128]{1,0:T(8,128)S(1)} %pad_maximum_fusion.s0, f32[8,128]{1,0:T(8,128)S(1)} %collective-permute-done.9.s1, f32[8,128]{1,0:T(8,128)S(1)} %collective-permute-done.10.s2, f32[8,128]{1,0:T(8,128)S(1)} %collective-permute-done.11.s3, ...), custom_call_target="tpu_custom_call" | custom-call | tf_op jit(solution)/shard_map/pallas_call | solution.py:528
  (11 shorter events, 0.2 us)
Async XLA Ops:
  3.3 27.0 %copy-start.5 = (f32[1,7,2048]{2,0,1:T(1,128)S(1)}, f32[1,7,2048]{2,0,1:T(1,128)}, u32[]{:S(2)}) copy-start(f32[1,7,2048]{2,0,1:T(1,128)} %param.16) | copy-start | bytes 172036
  3.4 31.7 %all-to-all-start = ((bf16[16,384,128]{2,1,0:T(8,128)(2,1)}), bf16[16,384,128]{2,1,0:T(8,128)(2,1)}, u32[]{:S(2)}, u32[]{:S(2)}) async-start(bf16[16,384,128]{2,1,0:T(8,128)(2,1)} %get-tuple-element.12), calls=%async_computation | async-start | bytes 3145728 | tf_op jit(solution)/shard_map/all_to_all | solution.py:544
  9.2 6.6 %collective-permute-start = (f32[8,128]{1,0:T(8,128)S(1)}, f32[8,128]{1,0:T(8,128)S(1)}, u32[]{:S(2)}, u32[]{:S(2)}) collective-permute-start(f32[8,128]{1,0:T(8,128)S(1)} %get-tuple-element.11), channel_id=1, source_target_pairs={{0,1},{1,2},{2,3},{3,0},{4,5},{5,6},{6,7},{7,4},{8,9},{9,10},{10,1... | collective-permute-start | bytes 12296 | tf_op jit(solution)/shard_map/ppermute | solution.py:142
  11.2 5.2 %collective-permute-start.1 = (f32[8,128]{1,0:T(8,128)S(1)}, f32[8,128]{1,0:T(8,128)S(1)}, u32[]{:S(2)}, u32[]{:S(2)}) collective-permute-start(f32[8,128]{1,0:T(8,128)S(1)} %get-tuple-element.11), channel_id=1, source_target_pairs={{0,2},{1,3},{2,0},{3,1},{4,6},{5,7},{6,4},{7,5},{8,10},{9,11},{10,... | collective-permute-start | bytes 12296 | tf_op jit(solution)/shard_map/ppermute | solution.py:142
  14.7 3.6 %collective-permute-start.2 = (f32[8,128]{1,0:T(8,128)S(1)}, f32[8,128]{1,0:T(8,128)S(1)}, u32[]{:S(2)}, u32[]{:S(2)}) collective-permute-start(f32[8,128]{1,0:T(8,128)S(1)} %get-tuple-element.11), channel_id=1, source_target_pairs={{0,3},{1,0},{2,1},{3,2},{4,7},{5,4},{6,5},{7,6},{8,11},{9,8},{10,9... | collective-permute-start | bytes 12296 | tf_op jit(solution)/shard_map/ppermute | solution.py:142
  18.4 1.2 %collective-permute-start.3 = (f32[2,128]{1,0:T(2,128)S(1)}, f32[2,128]{1,0:T(2,128)S(1)}, u32[]{:S(2)}, u32[]{:S(2)}) collective-permute-start(f32[2,128]{1,0:T(2,128)S(1)} %slice.12), channel_id=1, source_target_pairs={{0,4},{4,0},{8,12},{12,8},{16,20},{20,16},{24,28},{28,24},{32,36},... | collective-permute-start | bytes 3080 | tf_op jit(solution)/shard_map/ppermute | solution.py:149
  19.5 8.7 %collective-permute-start.4 = (f32[4,128]{1,0:T(4,128)S(1)}, f32[4,128]{1,0:T(4,128)S(1)}, u32[]{:S(2)}, u32[]{:S(2)}) collective-permute-start(f32[4,128]{1,0:T(4,128)S(1)} %pad_maximum_fusion.1), channel_id=1, source_target_pairs={{0,8},{4,12},{8,16},{12,20},{16,24},{20,28},{24,0},{28,4},{32,40},... | collective-permute-start | bytes 6152 | tf_op jit(solution)/shard_map/ppermute | solution.py:155
  21.3 7.3 %collective-permute-start.5 = (f32[4,128]{1,0:T(4,128)S(1)}, f32[4,128]{1,0:T(4,128)S(1)}, u32[]{:S(2)}, u32[]{:S(2)}) collective-permute-start(f32[4,128]{1,0:T(4,128)S(1)} %pad_maximum_fusion.1), channel_id=1, source_target_pairs={{0,16},{4,20},{8,24},{12,28},{16,0},{20,4},{24,8},{28,12},{32,48},... | collective-permute-start | bytes 6152 | tf_op jit(solution)/shard_map/ppermute | solution.py:155
  24.0 4.6 %collective-permute-start.6 = (f32[4,128]{1,0:T(4,128)S(1)}, f32[4,128]{1,0:T(4,128)S(1)}, u32[]{:S(2)}, u32[]{:S(2)}) collective-permute-start(f32[4,128]{1,0:T(4,128)S(1)} %pad_maximum_fusion.1), channel_id=1, source_target_pairs={{0,24},{4,28},{8,0},{12,4},{16,8},{20,12},{24,16},{28,20},{32,56},... | collective-permute-start | bytes 6152 | tf_op jit(solution)/shard_map/ppermute | solution.py:155
  28.6 6.3 %collective-permute-start.7 = (f32[16,128]{1,0:T(8,128)S(1)}, f32[16,128]{1,0:T(8,128)S(1)}, u32[]{:S(2)}, u32[]{:S(2)}) collective-permute-start(f32[16,128]{1,0:T(8,128)S(1)} %concatenate.15), channel_id=1, source_target_pairs={{0,32},{4,36},{8,40},{12,44},{16,48},{20,52},{24,56},{28,60},{32,0... | collective-permute-start | bytes 24584 | tf_op jit(solution)/shard_map/ppermute | solution.py:149
  32.3 2.7 %copy-start.4 = (s32[16]{0:T(128)S(1)}, s32[16]{0:T(128)}, u32[]{:S(2)}) copy-start(s32[16]{0:T(128)} %order_ref.1) | copy-start | bytes 196
  45.8 5.2 %copy-start = (bf16[1,128,2048]{2,1,0:T(8,128)(2,1)S(1)}, bf16[1,128,2048]{2,1,0:T(8,128)(2,1)}, u32[]{:S(2)}) copy-start(bf16[1,128,2048]{2,1,0:T(8,128)(2,1)} %saved_ref.5) | copy-start | bytes 1572868
  45.8 23.9 %copy-start.1 = (bf16[1,128,2048]{2,1,0:T(8,128)(2,1)S(1)}, bf16[1,128,2048]{2,1,0:T(8,128)(2,1)}, u32[]{:S(2)}) copy-start(bf16[1,128,2048]{2,1,0:T(8,128)(2,1)} %cot_ref.3) | copy-start | bytes 1572868
  45.8 23.9 %copy-start.2 = (bf16[1,128,2048]{2,1,0:T(8,128)(2,1)S(1)}, bf16[1,128,2048]{2,1,0:T(8,128)(2,1)}, u32[]{:S(2)}) copy-start(bf16[1,128,2048]{2,1,0:T(8,128)(2,1)} %fwd_ref.1) | copy-start | bytes 1572868
  45.8 23.9 %copy-start.3 = (bf16[1,128,2048]{2,1,0:T(8,128)(2,1)S(1)}, bf16[1,128,2048]{2,1,0:T(8,128)(2,1)}, u32[]{:S(2)}) copy-start(bf16[1,128,2048]{2,1,0:T(8,128)(2,1)} %sconv_ref.3) | copy-start | bytes 1572868
  45.9 23.9 %all-to-all-start.1 = ((bf16[16,152,256]{2,1,0:T(8,128)(2,1)}), bf16[16,152,256]{2,1,0:T(8,128)(2,1)S(1)}, u32[]{:S(2)}, u32[]{:S(2)}) async-start(bf16[16,152,256]{2,1,0:T(8,128)(2,1)} %convolve.1), calls=%async_computation.1 | async-start | bytes 2490368 | tf_op jit(solution)/shard_map/all_to_all | solution.py:553
  51.1 51.5 %collective-permute-start.13 = (bf16[1,128,2048]{2,1,0:T(8,128)(2,1)S(1)}, bf16[1,128,2048]{2,1,0:T(8,128)(2,1)}, u32[]{:S(2)}, u32[]{:S(2)}) collective-permute-start(bf16[1,128,2048]{2,1,0:T(8,128)(2,1)S(1)} %copy-done), channel_id=1, source_target_pairs={{64,0},{65,1},{66,2},{67,3},{68,4},{69,5},{70,6},{71,7},{72,8},{73... | collective-permute-start | bytes 1572872 | tf_op jit(solution)/shard_map/ppermute | solution.py:542
  72.7 29.9 %collective-permute-start.12 = (bf16[1,128,2048]{2,1,0:T(8,128)(2,1)S(1)}, bf16[1,128,2048]{2,1,0:T(8,128)(2,1)S(1)}, u32[]{:S(2)}, u32[]{:S(2)}) collective-permute-start(bf16[1,128,2048]{2,1,0:T(8,128)(2,1)S(1)} %get-tuple-element.17), channel_id=1, source_target_pairs={{0,64},{64,0},{1,65},{65,1},{2,66},{66,2},{3,67},{67,3},{4,68},{68... | collective-permute-start | bytes 1572872 | tf_op jit(solution)/shard_map/ppermute | solution.py:558
  76.0 15.3 %collective-permute-start.8 = (f32[8,128]{1,0:T(8,128)S(1)}, f32[8,128]{1,0:T(8,128)S(1)}, u32[]{:S(2)}, u32[]{:S(2)}) collective-permute-start(f32[8,128]{1,0:T(8,128)S(1)} %get-tuple-element.14), channel_id=1, source_target_pairs={{64,0},{65,1},{66,2},{67,3},{68,4},{69,5},{70,6},{71,7},{72,8},{73... | collective-permute-start | bytes 12296 | tf_op jit(solution)/shard_map/ppermute | solution.py:557
  91.2 6.7 %collective-permute-start.10 = (f32[8,128]{1,0:T(8,128)S(1)}, f32[8,128]{1,0:T(8,128)S(1)}, u32[]{:S(2)}, u32[]{:S(2)}) collective-permute-start(f32[8,128]{1,0:T(8,128)S(1)} %pad_maximum_fusion.s0), channel_id=1, source_target_pairs={{0,2},{1,3},{2,0},{3,1},{4,6},{5,7},{6,4},{7,5},{8,10},{9,11},{10,... | collective-permute-start | bytes 12296 | tf_op jit(solution)/shard_map/ppermute | solution.py:142
  95.2 3.6 %collective-permute-start.11 = (f32[8,128]{1,0:T(8,128)S(1)}, f32[8,128]{1,0:T(8,128)S(1)}, u32[]{:S(2)}, u32[]{:S(2)}) collective-permute-start(f32[8,128]{1,0:T(8,128)S(1)} %pad_maximum_fusion.s0), channel_id=1, source_target_pairs={{0,3},{1,0},{2,1},{3,2},{4,7},{5,4},{6,5},{7,6},{8,11},{9,8},{10,9... | collective-permute-start | bytes 12296 | tf_op jit(solution)/shard_map/ppermute | solution.py:142
  95.9 4.8 %collective-permute-start.9 = (f32[8,128]{1,0:T(8,128)S(1)}, f32[8,128]{1,0:T(8,128)S(1)}, u32[]{:S(2)}, u32[]{:S(2)}) collective-permute-start(f32[8,128]{1,0:T(8,128)S(1)} %pad_maximum_fusion.s0), channel_id=1, source_target_pairs={{0,1},{1,2},{2,3},{3,0},{4,5},{5,6},{6,7},{7,4},{8,9},{9,10},{10,1... | collective-permute-start | bytes 12296 | tf_op jit(solution)/shard_map/ppermute | solution.py:142

commit v2 on v1

--- a/solution.py
+++ b/solution.py
@@ -35,7 +35,7 @@
     real[0] = 1.0
     imag[0] = np.where(np.arange(BLOCK) % 2 == 0, 1.0, -1.0)
     leave = np.concatenate([real, imag], axis=0).T / period
-    return split_bf16(enter) + split_bf16(leave)
+    return tuple(np.concatenate(split_bf16(table), axis=1) for table in (enter, leave))
 
 
 def rows_to_columns(rows):
@@ -134,34 +134,9 @@
     )(in_hbm(fwd_in), in_hbm(saved_in), in_hbm(grad_out))
 
 
-def over_chan(rows):
-    count = lax.axis_size("chan")
-    got = [rows]
-    for apart in range(1, count):
-        got.append(
-            lax.ppermute(rows, "chan", [(low, (low + apart) % count) for low in range(count)])
-        )
-    return got
-
-
-def across(rows, flip):
-    count = lax.axis_size("seq")
-    return lax.ppermute(rows, "seq", [(low, low ^ flip) for low in range(count)])
-
-
-def round_ring(rows, apart):
-    count = lax.axis_size("seq")
-    place = lambda low: low // 8 * 8 + (low + 2 * apart) % 8
-    return lax.ppermute(rows, "seq", [(low, place(low)) for low in range(count)])
-
-
-def gather_order():
-    own = lax.axis_index("seq").astype(jnp.int32)
-    block = jnp.arange(16, dtype=jnp.int32)
-    core = (block ^ own) & 1
-    back = (own // 2 - block // 2) % 4
-    side = (block // 8) ^ (own // 8)
-    return side * 8 + back * 2 + core
+def across(rows, axis, flip):
+    count = lax.axis_size(axis)
+    return lax.ppermute(rows, axis, [(low, low ^ flip) for low in range(count)])
 
 
 def early_kernel(sums_ref, saved_ref, sconv_ref, cot_ref, out_ref, inv):
@@ -203,20 +178,20 @@
     return jnp.concatenate([ref[at : at + BLOCK, :], ref[at + BLOCK : at + 2 * BLOCK, :]], axis=1)
 
 
-def enter_transform(enter_hi, enter_lo, data):
-    return jnp.dot(enter_hi[...], data, preferred_element_type=jnp.float32) + jnp.dot(
-        enter_lo[...], data, preferred_element_type=jnp.float32
-    )
-
-
-def filter_kernel(where_ref, taps_ref, enter_hi, enter_lo, filt):
+def table_dot(table, data):
+    return jnp.dot(
+        table[...], jnp.concatenate([data, data], axis=0), preferred_element_type=jnp.float32
+    )
+
+
+def filter_kernel(where_ref, taps_ref, enter, filt):
     del where_ref
     freq = lax.broadcasted_iota(jnp.int32, (2 * BLOCK, LANES), 0)
     parity = jnp.where(freq % 2 == 0, 1.0, -1.0)
     first = lax.broadcasted_iota(jnp.int32, (BLOCK, LANES), 0) == 0
     earlier = None
     for pair in range(filt.shape[0] // 2):
-        pair_spectra = enter_transform(enter_hi, enter_lo, side_by_side(taps_ref.at[0], pair))
+        pair_spectra = table_dot(enter, side_by_side(taps_ref.at[0], pair))
         for side in range(2):
             current = pair_spectra[:, side * LANES : (side + 1) * LANES]
             both = parity * current
@@ -240,12 +215,12 @@
             num_scalar_prefetch=1,
             grid=(1,),
             in_specs=[pl.BlockSpec((1, length, LANES), lambda step, at: (0, 0, at[0]))]
-            + [whole(table.shape) for table in tables[:2]],
+            + [whole(tables[0].shape)],
             out_specs=VMEM,
         ),
         name="filter_spectra",
         compiler_params=pltpu.CompilerParams(vmem_limit_bytes=16 << 20),
-    )(where, in_hbm(filters), *[in_hbm(table) for table in tables[:2]])
+    )(where, in_hbm(filters), in_hbm(tables[0]))
 
 
 def fold(block):
@@ -253,9 +228,8 @@
 
 
 def conv_kernel(
-    where_ref, order_ref, gathered_ref, inv_ref, known_ref, params_ref, filt, raw_hbm, enter_hi_hbm,
-    enter_lo_hbm, leave_hi_hbm, leave_lo_hbm, out_hbm, raw_ref, enter_hi, enter_lo, leave_hi,
-    leave_lo, out_ref, ordered, spectra, product, inv_rows, inv, raw_sem, table_sem, out_sem,
+    where_ref, order_ref, gathered_ref, inv_ref, known_ref, params_ref, filt, raw_hbm, enter_hbm,
+    leave_hbm, out_hbm, raw_ref, enter, leave, out_ref, ordered, spectra, product, inv_rows, inv, raw_sem, table_sem, out_sem,
 ):
     stored = raw_ref.shape[0]
     raw_copies = [
@@ -264,14 +238,7 @@
     ]
     table_copies = [
         pltpu.make_async_copy(source, target, table_sem.at[index])
-        for index, (source, target) in enumerate(
-            (
-                (enter_hi_hbm, enter_hi),
-                (enter_lo_hbm, enter_lo),
-                (leave_hi_hbm, leave_hi),
-                (leave_lo_hbm, leave_lo),
-            )
-        )
+        for index, (source, target) in enumerate(((enter_hbm, enter), (leave_hbm, leave)))
     ]
     out_copies = [
         pltpu.make_async_copy(out_ref.at[index], out_hbm.at[index], out_sem.at[index])
@@ -284,6 +251,7 @@
     lanes = pl.ds(pl.multiple_of(where_ref[0] * LANES, LANES), LANES)
     p = [params_ref[0, row : row + 1, lanes] for row in range(7)]
 
+    gains = [p[0] * p[1], p[0] * p[3], p[0] * p[5]]
     for index in range(stored):
         inv_rows[2 * index : 2 * index + 2, :] = inv_ref[pl.ds(2 * gathered_ref[index], 2), :]
     inv[...] = jnp.concatenate([inv_rows[...]] * (128 // (2 * stored)), axis=0).T
@@ -292,18 +260,17 @@
         at = pl.multiple_of(order_ref[index] * rows, rows)
         inv_fwd = inv[:, 2 * index : 2 * index + 1]
         inv_saved = inv[:, 2 * index + 1 : 2 * index + 2]
-        scaled = raw_ref[index, :rows, :].astype(jnp.float32) * inv_fwd * p[0]
-        mixed = (scaled * p[3] + p[4]) * (scaled * p[5] + p[6])
-        scaled = raw_ref[index, rows : 2 * rows, :].astype(jnp.float32) * inv_saved * p[0]
+        normed = raw_ref[index, :rows, :].astype(jnp.float32) * inv_fwd
+        mixed = (normed * gains[1] + p[4]) * (normed * gains[2] + p[6])
+        normed = raw_ref[index, rows : 2 * rows, :].astype(jnp.float32) * inv_saved
         cot = raw_ref[index, 2 * rows :, :].astype(jnp.float32)
         ordered[pl.ds(at, rows), :LANES] = mixed.astype(jnp.bfloat16)
-        ordered[pl.ds(at, rows), LANES:] = (cot * (scaled * p[1] + p[2])).astype(jnp.bfloat16)
+        ordered[pl.ds(at, rows), LANES:] = (cot * (normed * gains[0] + p[2])).astype(jnp.bfloat16)
 
     table_copies[0].wait()
-    table_copies[1].wait()
     for index in range(blocks):
         data = ordered[index * BLOCK : (index + 1) * BLOCK, :]
-        spectra[index] = enter_transform(enter_hi, enter_lo, data)
+        spectra[index] = table_dot(enter, data)
 
     def products(tile, carry):
         low = pl.ds(pl.multiple_of(tile * 8, 8), 8)
@@ -331,17 +298,9 @@
 
     lax.fori_loop(0, BLOCK // 8, products, 0)
 
-    table_copies[2].wait()
-    table_copies[3].wait()
+    table_copies[1].wait()
     for index in range(blocks):
-        value = product[index]
-        top = value.astype(jnp.bfloat16)
-        rest = (value - top.astype(jnp.float32)).astype(jnp.bfloat16)
-        left = (
-            jnp.dot(leave_hi[...], top, preferred_element_type=jnp.float32)
-            + jnp.dot(leave_lo[...], top, preferred_element_type=jnp.float32)
-            + jnp.dot(leave_hi[...], rest, preferred_element_type=jnp.float32)
-        )
+        left = table_dot(leave, product[index].astype(jnp.bfloat16))
         ordered[index * BLOCK : (index + 1) * BLOCK, :] = left.astype(jnp.bfloat16)
 
     sums = [jnp.zeros((8, LANES), jnp.float32)] * 3
@@ -381,7 +340,7 @@
     return pl.pallas_call(
         conv_kernel,
         out_shape=pltpu.HBM((stored, rows + 24, 2 * LANES), jnp.bfloat16),
-        in_specs=[SMEM] * 3 + [VMEM] * 4 + [HBM] * 5,
+        in_specs=[SMEM] * 3 + [VMEM] * 4 + [HBM] * 3,
         out_specs=HBM,
         scratch_shapes=[
             pltpu.VMEM(raw.shape, jnp.bfloat16),
@@ -393,7 +352,7 @@
             pltpu.VMEM((2 * stored, 128), jnp.float32),
             pltpu.VMEM((128, 128), jnp.float32),
             pltpu.SemaphoreType.DMA((stored,)),
-            pltpu.SemaphoreType.DMA((4,)),
+            pltpu.SemaphoreType.DMA((2,)),
             pltpu.SemaphoreType.DMA((stored,)),
         ],
         name="convolve",
@@ -470,7 +429,8 @@
     @pl.when(step == pl.num_programs(0) - 1)
     def _():
         cross = columns_to_rows([jnp.sum(acc[...], axis=1, keepdims=True)])
-        cross_ref[...] = cross * (inv_ref[1:2, :] * inv_ref[1:2, :] / D)
+        cross = cross[0:1] * (inv_ref[1:2, :] * inv_ref[1:2, :] / D)
+        cross_ref[...] = jnp.broadcast_to(cross, (8, 128))
 
 
 def leave(pipe, inv, back, fwd_in, saved_in, saved_conv, grad_out, mix_params):
@@ -501,22 +461,22 @@
     )(pipe, inv, in_vmem(back), fwd_in, saved_in, saved_conv, grad_out, mix_params)
 
 
-def subtract_kernel(row, s0, s1, s2, s3, value_ref, saved_ref, out_ref, scale):
+def subtract_kernel(row, first, second, value_ref, saved_ref, out_ref, scale):
     step = pl.program_id(0)
 
     @pl.when(step == 0)
     def _():
-        scale[...] = rows_to_columns(s0[...] + s1[...] + s2[...] + s3[...])
+        scale[...] = rows_to_columns(first[...] + second[...])
 
     factor = scale[:, row : row + 1]
     wide = out_ref.shape[2]
     for at in range(0, wide, LANES):
-        source = pl.ds(at, LANES)
+        own = source = pl.ds(at, LANES)
         if value_ref.shape[2] != wide:
             source = pl.ds(pl.multiple_of(step * wide + at, LANES), LANES)
         value = value_ref[0, :, source].astype(jnp.float32)
-        saved = saved_ref[0, :, source].astype(jnp.float32)
-        out_ref[0, :, pl.ds(at, LANES)] = (value - saved * factor).astype(jnp.bfloat16)
+        saved = saved_ref[0, :, own].astype(jnp.float32)
+        out_ref[0, :, own] = (value - saved * factor).astype(jnp.bfloat16)
 
 
 def subtract(row, scales, value, saved, resident):
@@ -524,12 +484,12 @@
     wide = 512
     spec = lane_spec(rows, wide)
     if resident:
-        value, saved = in_vmem(value), in_vmem(saved)
+        value, saved = in_vmem(value), in_hbm(saved)
     return pl.pallas_call(
         functools.partial(subtract_kernel, row),
         out_shape=jax.ShapeDtypeStruct(saved.shape, jnp.bfloat16),
         grid=(width // wide,),
-        in_specs=[VMEM] * 4 + [VMEM if resident else spec] * 2,
+        in_specs=[VMEM] * 2 + [VMEM if resident else spec, spec],
         out_specs=spec,
         scratch_shapes=[pltpu.VMEM((rows, 128), jnp.float32)],
         compiler_params=pltpu.CompilerParams(vmem_limit_bytes=16 << 20),
@@ -539,24 +499,30 @@
 def per_device(tables, fwd_in, saved_in, saved_conv, grad_out, filters, mix_params, span_order):
     where = lax.axis_index("seq").astype(jnp.int32).reshape(1)
     pipe = lax.axis_index("pipe").astype(jnp.int32).reshape(1)
-    peer_saved = lax.ppermute(saved_in, "pipe", [(1, 0)])
+    gathered = jnp.arange(lax.axis_size("seq"), dtype=jnp.int32) ^ where
     raw, sums = pack(fwd_in, saved_in, grad_out)
     raw = lax.all_to_all(raw, "seq", 0, 0)
-    own_sums = sum(over_chan(sums))
-    sums = own_sums[:2]
-    sums = jnp.concatenate([sums, across(sums, 1)], axis=0)
-    sums = jnp.concatenate([sums] + [round_ring(sums, apart) for apart in (1, 2, 3)], axis=0)
-    inv = lax.rsqrt(jnp.concatenate([sums, across(sums, 8)], axis=0) / D + EPSILON)
+    for flip in (1, 2):
+        sums = sums + across(sums, "chan", flip)
+    own_sums, sums = sums, sums[:2]
+    for flip in (1, 2, 4):
+        sums = jnp.concatenate([sums, across(sums, "seq", flip)], axis=0)
+    sums = jnp.concatenate([sums, across(sums, "seq", 8)], axis=0)
+    inv = lax.rsqrt(sums / D + EPSILON)
+    peer_saved = lax.ppermute(saved_in, "pipe", [(1, 0)])
+    known = early(own_sums, saved_in, saved_conv, grad_out)
     spectra = filter_spectra(where, filters, tables)
-    known = early(own_sums, saved_in, saved_conv, grad_out)
-    back = convolve(where, span_order, gather_order(), raw, inv, known, mix_params, spectra, tables)
+    back = convolve(where, span_order, gathered, raw, inv, known, mix_params, spectra, tables)
     back = lax.all_to_all(back, "seq", 0, 0)
     layer_out, outgoing, partial, param_grad, cross = leave(
         pipe, inv, back, fwd_in, saved_in, saved_conv, grad_out, mix_params
     )
     peer_cross = lax.ppermute(cross, "pipe", [(1, 0)])
     incoming = lax.ppermute(outgoing, "pipe", [(0, 1), (1, 0)])
-    scales = over_chan(jnp.concatenate([cross[:1], peer_cross[:1], cross[:6]], axis=0))
+    own_row = lax.broadcasted_iota(jnp.int32, cross.shape, 0) == 0
+    scale = jnp.where(own_row, cross, peer_cross)
+    scale = scale + across(scale, "chan", 1)
+    scales = (scale, across(scale, "chan", 2))
     input_grad = subtract(0, scales, partial, saved_in, False)
     received = subtract(1, scales, incoming, peer_saved, True)
     return (layer_out, input_grad, param_grad, received)

time: 106 us -> 110 us (1.038)
  waiting for transfers between devices: 41.1 us -> 46.7 us
  starting transfers between devices: 37 us -> 35.6 us
    ppermute x11 -> x8, waiting for transfers between devices: 9.7 us -> 15.3 us  [across(): return lax.ppermute(rows, axis, [(low, low ^ flip) for low in range(count)])]
    ppermute x11 -> x8, starting transfers between devices: 20.2 us -> 19 us  [across(): return lax.ppermute(rows, axis, [(low, low ^ flip) for low in range(count)])]
  transfers between devices with their start and end apart: 16 -> 13, of which waited for: 9 -> 9; matrix products, arithmetic and copies ran while one was open for 1% -> 1% of each run, Pallas kernels for 9% -> 9%
where the time goes in v2:
time: 110 us
  waiting for transfers between devices  46.7 us (42%)
  starting transfers between devices  35.6 us (32%)
  Pallas kernels  25.7 us (23%)
    ppermute x8, starting transfers between devices, across(): return lax.ppermute(rows, axis, [(low, low ^ flip) for low in range(count)])  19 us
    all_to_all x1, waiting for transfers between devices, per_device(): back = lax.all_to_all(back, 'seq', 0, 0)  17.4 us
    ppermute x8, waiting for transfers between devices, across(): return lax.ppermute(rows, axis, [(low, low ^ flip) for low in range(count)])  15.3 us
    ppermute x1, waiting for transfers between devices, per_device(): peer_cross = lax.ppermute(cross, 'pipe', [(1, 0)])  14 us
    pallas_call x1, Pallas kernels, convolve(): pl.pallas_call(conv_kernel, out_shape=pltpu.HBM((stored, rows + 24, 2 * L...  10.2 us
    all_to_all x1, starting transfers between devices, per_device(): raw = lax.all_to_all(raw, 'seq', 0, 0)  5.8 us
    pallas_call x2, Pallas kernels, subtract(): pl.pallas_call(functools.partial(subtract_kernel, row), out_shape=jax.Sha...  5.31 us
    all_to_all x1, starting transfers between devices, per_device(): back = lax.all_to_all(back, 'seq', 0, 0)  4.99 us
  transfers between devices with their start and end apart: 13, of which 9 were waited for; matrix products, arithmetic and copies ran while one was open for 1% of the time, Pallas kernels for 9%

profile of v2, /device:TPU:0, one launch (start us, length us, event | category | flops | bytes accessed | tf_op | source)
XLA Modules:
  0.0 109.7 jit_solution(5744805200345313546)
XLA Ops:
  0.6 2.7 %pack.1 = (bf16[16,384,128]{2,1,0:T(8,128)(2,1)}, f32[8,128]{1,0:T(8,128)S(1)}) custom-call(bf16[1,128,2048]{2,1,0:T(8,128)(2,1)} %fwd_ref.1, bf16[1,128,2048]{2,1,0:T(8,128)(2,1)} %saved_ref.5, bf16[1,128,2048]{2,1,0:T(8,128)(2,1)} %cot_ref.3), custom_call_target="tpu_custom_call" | custom-call | tf_op jit(solution)/shard_map/pack/pallas_call | solution.py:119
  3.3 0.0 copy-start.5
  3.3 5.8 %all-to-all-start = ((bf16[16,384,128]{2,1,0:T(8,128)(2,1)}), bf16[16,384,128]{2,1,0:T(8,128)(2,1)}, u32[]{:S(2)}, u32[]{:S(2)}) async-start(bf16[16,384,128]{2,1,0:T(8,128)(2,1)} %get-tuple-element.12), calls=%async_computation | async-start | bytes 3145728 | tf_op jit(solution)/shard_map/all_to_all | solution.py:504
  9.2 2.0 %collective-permute-start = (f32[8,128]{1,0:T(8,128)S(1)}, f32[8,128]{1,0:T(8,128)S(1)}, u32[]{:S(2)}, u32[]{:S(2)}) collective-permute-start(f32[8,128]{1,0:T(8,128)S(1)} %get-tuple-element.11), channel_id=1, source_target_pairs={{0,1},{1,0},{2,3},{3,2},{4,5},{5,4},{6,7},{7,6},{8,9},{9,8},{10,11... | collective-permute-start | bytes 12296 | tf_op jit(solution)/shard_map/ppermute | solution.py:139
  11.2 1.7 %collective-permute-done = f32[8,128]{1,0:T(8,128)S(1)} collective-permute-done((f32[8,128]{1,0:T(8,128)S(1)}, f32[8,128]{1,0:T(8,128)S(1)}, u32[]{:S(2)}, u32[]{:S(2)}) %collective-permute-start) | collective-permute-done | bytes 4128 | tf_op jit(solution)/shard_map/ppermute | solution.py:139
  12.8 3.9 %collective-permute-start.1 = (f32[8,128]{1,0:T(8,128)S(1)}, f32[8,128]{1,0:T(8,128)S(1)}, u32[]{:S(2)}, u32[]{:S(2)}) collective-permute-start(f32[8,128]{1,0:T(8,128)S(1)} %add.15), channel_id=1, source_target_pairs={{0,2},{1,3},{2,0},{3,1},{4,6},{5,7},{6,4},{7,5},{8,10},{9,11},{10,... | collective-permute-start | bytes 12296 | tf_op jit(solution)/shard_map/ppermute | solution.py:139
  16.7 1.6 %collective-permute-done.1 = f32[8,128]{1,0:T(8,128)S(1)} collective-permute-done((f32[8,128]{1,0:T(8,128)S(1)}, f32[8,128]{1,0:T(8,128)S(1)}, u32[]{:S(2)}, u32[]{:S(2)}) %collective-permute-start.1) | collective-permute-done | bytes 4128 | tf_op jit(solution)/shard_map/ppermute | solution.py:139
  18.3 0.0 collective-permute-start.2
  18.3 1.2 %collective-permute-done.2 = f32[2,128]{1,0:T(2,128)S(1)} collective-permute-done((f32[2,128]{1,0:T(2,128)S(1)}, f32[2,128]{1,0:T(2,128)S(1)}, u32[]{:S(2)}, u32[]{:S(2)}) %collective-permute-start.2) | collective-permute-done | bytes 1056 | tf_op jit(solution)/shard_map/ppermute | solution.py:139
  19.5 1.8 %collective-permute-start.3 = (f32[4,128]{1,0:T(4,128)S(1)}, f32[4,128]{1,0:T(4,128)S(1)}, u32[]{:S(2)}, u32[]{:S(2)}) collective-permute-start(f32[4,128]{1,0:T(4,128)S(1)} %pad_maximum_fusion.2), channel_id=1, source_target_pairs={{0,8},{4,12},{8,0},{12,4},{16,24},{20,28},{24,16},{28,20},{32,40},... | collective-permute-start | bytes 6152 | tf_op jit(solution)/shard_map/ppermute | solution.py:139
  21.3 6.7 %collective-permute-done.3 = f32[4,128]{1,0:T(4,128)S(1)} collective-permute-done((f32[4,128]{1,0:T(4,128)S(1)}, f32[4,128]{1,0:T(4,128)S(1)}, u32[]{:S(2)}, u32[]{:S(2)}) %collective-permute-start.3) | collective-permute-done | bytes 2080 | tf_op jit(solution)/shard_map/ppermute | solution.py:139
  28.0 3.9 %collective-permute-start.4 = (f32[8,128]{1,0:T(8,128)S(1)}, f32[8,128]{1,0:T(8,128)S(1)}, u32[]{:S(2)}, u32[]{:S(2)}) collective-permute-start(f32[8,128]{1,0:T(8,128)S(1)} %pad_maximum_fusion.1), channel_id=1, source_target_pairs={{0,16},{4,20},{8,24},{12,28},{16,0},{20,4},{24,8},{28,12},{32,48},... | collective-permute-start | bytes 12296 | tf_op jit(solution)/shard_map/ppermute | solution.py:139
  31.9 1.6 %collective-permute-done.4 = f32[8,128]{1,0:T(8,128)S(1)} collective-permute-done((f32[8,128]{1,0:T(8,128)S(1)}, f32[8,128]{1,0:T(8,128)S(1)}, u32[]{:S(2)}, u32[]{:S(2)}) %collective-permute-start.4) | collective-permute-done | bytes 4128 | tf_op jit(solution)/shard_map/ppermute | solution.py:139
  33.5 1.6 %collective-permute-start.5 = (f32[16,128]{1,0:T(8,128)S(1)}, f32[16,128]{1,0:T(8,128)S(1)}, u32[]{:S(2)}, u32[]{:S(2)}) collective-permute-start(f32[16,128]{1,0:T(8,128)S(1)} %pad_maximum_fusion), channel_id=1, source_target_pairs={{0,32},{4,36},{8,40},{12,44},{16,48},{20,52},{24,56},{28,60},{32,0... | collective-permute-start | bytes 24584 | tf_op jit(solution)/shard_map/ppermute | solution.py:139
  35.1 0.0 copy-done.5
  35.1 1.9 %filter_spectra.1.filt = f32[8,3,256,128]{3,2,1,0:T(8,128)S(1)} custom-call(s32[1]{0:T(128)} %bitcast.1.where_ref, bf16[1,2048,2048]{2,1,0:T(8,128)(2,1)} %taps_ref.1, bf16[512,512]{1,0:T(8,128)(2,1)} %constant.23.clone.enter.enter_hbm), custom_call_target="tpu_custom_call" | custom-call | tf_op jit(solution)/shard_map/filter_spectra/pallas_call | solution.py:211
  37.1 0.0 copy-start.4
  37.1 2.6 %early.1.known_ref = f32[16,256]{1,0:T(8,128)S(1)} custom-call(f32[8,128]{1,0:T(8,128)S(1)} %add.16.sums_ref, bf16[1,128,2048]{2,1,0:T(8,128)(2,1)} %saved_ref.5, bf16[1,128,2048]{2,1,0:T(8,128)(2,1)} %sconv_ref.3, bf16[1,128,2048]{2,1,0:T(8,128)(2,1)} %cot_ref.3), custom_call_target="tpu_custom_call" | custom-call | tf_op jit(solution)/shard_map/early/pallas_call | solution.py:164
  39.8 0.0 collective-permute-done.5
  39.8 0.0 all-to-all-done.raw_hbm
  39.8 0.0 copy-done.4
  39.8 10.2 %convolve.1 = bf16[16,152,256]{2,1,0:T(8,128)(2,1)} custom-call(s32[1]{0:T(128)} %bitcast.1.where_ref, s32[16]{0:T(128)S(1)} %copy-done.4, s32[16]{0:T(128)S(1)} %iota_xor_fusion.gathered_ref, f32[32,128]{1,0:T(8,128)S(1)} %add_rsqrt_fusion.inv_ref, f32[16,256]{1,0:T(8,128)S(1)} %early.1.known_ref, f32[1,7,2048]{2,1,0:T(8,128)S(1)} %copy.13.params_ref, ...), custom_call_target="tpu_custom_call" | custom-call | tf_op jit(solution)/shard_map/convolve/pallas_call | solution.py:340
  50.0 0.0 copy-start
  50.0 0.0 copy-start.1
  50.0 0.0 copy-start.2
  50.1 0.0 copy-start.3
  50.1 5.0 %all-to-all-start.1 = ((bf16[16,152,256]{2,1,0:T(8,128)(2,1)}), bf16[16,152,256]{2,1,0:T(8,128)(2,1)S(1)}, u32[]{:S(2)}, u32[]{:S(2)}) async-start(bf16[16,152,256]{2,1,0:T(8,128)(2,1)} %convolve.1), calls=%async_computation.1 | async-start | bytes 2490368 | tf_op jit(solution)/shard_map/all_to_all | solution.py:516
  55.1 0.0 copy-done
  55.1 1.3 %collective-permute-start.10 = (bf16[1,128,2048]{2,1,0:T(8,128)(2,1)S(1)}, bf16[1,128,2048]{2,1,0:T(8,128)(2,1)}, u32[]{:S(2)}, u32[]{:S(2)}) collective-permute-start(bf16[1,128,2048]{2,1,0:T(8,128)(2,1)S(1)} %copy-done), channel_id=1, source_target_pairs={{64,0},{65,1},{66,2},{67,3},{68,4},{69,5},{70,6},{71,7},{72,8},{73... | collective-permute-start | bytes 1572872 | tf_op jit(solution)/shard_map/ppermute | solution.py:512
  56.4 17.4 %all-to-all-done.1.back_ref = bf16[16,152,256]{2,1,0:T(8,128)(2,1)S(1)} async-done(((bf16[16,152,256]{2,1,0:T(8,128)(2,1)}), bf16[16,152,256]{2,1,0:T(8,128)(2,1)S(1)}, u32[]{:S(2)}, u32[]{:S(2)}) %all-to-all-start.1) | async-done | bytes 1245216 | tf_op jit(solution)/shard_map/all_to_all | solution.py:516
  73.8 0.0 copy-done.1
  73.8 0.0 copy-done.2
  73.8 0.0 copy-done.3
  73.8 2.9 %leave.1 = (bf16[1,128,2048]{2,1,0:T(8,128)(2,1)}, bf16[1,128,2048]{2,1,0:T(8,128)(2,1)S(1)}, f32[1,128,2048]{2,1,0:T(8,128)S(1)}, f32[1,7,2048]{2,1,0:T(8,128)S(1)}, f32[8,128]{1,0:T(8,128)S(1)}) custom-call(s32[1]{0:T(128)} %bitcast.pipe_ref, f32[32,128]{1,0:T(8,128)S(1)} %add_rsqrt_fusion.inv_ref, bf16[16,152,256]{2,1,0:T(8,128)(2,1)S(1)} %all-to-all-done.1.back_ref, ...), custom_call_target="tpu_custom_call" | custom-call | tf_op jit(solution)/shard_map/leave/pallas_call | solution.py:440
  76.7 3.3 %collective-permute-start.9 = (bf16[1,128,2048]{2,1,0:T(8,128)(2,1)S(1)}, bf16[1,128,2048]{2,1,0:T(8,128)(2,1)S(1)}, u32[]{:S(2)}, u32[]{:S(2)}) collective-permute-start(bf16[1,128,2048]{2,1,0:T(8,128)(2,1)S(1)} %get-tuple-element.17), channel_id=1, source_target_pairs={{0,64},{64,0},{1,65},{65,1},{2,66},{66,2},{3,67},{67,3},{4,68},{68... | collective-permute-start | bytes 1572872 | tf_op jit(solution)/shard_map/ppermute | solution.py:521
  80.0 1.3 %collective-permute-start.6 = (f32[8,128]{1,0:T(8,128)S(1)}, f32[8,128]{1,0:T(8,128)S(1)}, u32[]{:S(2)}, u32[]{:S(2)}) collective-permute-start(f32[8,128]{1,0:T(8,128)S(1)} %get-tuple-element.14), channel_id=1, source_target_pairs={{64,0},{65,1},{66,2},{67,3},{68,4},{69,5},{70,6},{71,7},{72,8},{73... | collective-permute-start | bytes 12296 | tf_op jit(solution)/shard_map/ppermute | solution.py:520
  81.3 14.0 %collective-permute-done.6 = f32[8,128]{1,0:T(8,128)S(1)} collective-permute-done((f32[8,128]{1,0:T(8,128)S(1)}, f32[8,128]{1,0:T(8,128)S(1)}, u32[]{:S(2)}, u32[]{:S(2)}) %collective-permute-start.6) | collective-permute-done | bytes 4128 | tf_op jit(solution)/shard_map/ppermute | solution.py:520
  95.2 0.1 broadcast_select_fusion
  95.3 1.9 %collective-permute-start.7 = (f32[8,128]{1,0:T(8,128)S(1)}, f32[8,128]{1,0:T(8,128)S(1)}, u32[]{:S(2)}, u32[]{:S(2)}) collective-permute-start(f32[8,128]{1,0:T(8,128)S(1)} %broadcast_select_fusion), channel_id=1, source_target_pairs={{0,1},{1,0},{2,3},{3,2},{4,5},{5,4},{6,7},{7,6},{8,9},{9,8},{10,11... | collective-permute-start | bytes 12296 | tf_op jit(solution)/shard_map/ppermute | solution.py:139
  97.2 1.7 %collective-permute-done.7 = f32[8,128]{1,0:T(8,128)S(1)} collective-permute-done((f32[8,128]{1,0:T(8,128)S(1)}, f32[8,128]{1,0:T(8,128)S(1)}, u32[]{:S(2)}, u32[]{:S(2)}) %collective-permute-start.7) | collective-permute-done | bytes 4128 | tf_op jit(solution)/shard_map/ppermute | solution.py:139
  98.9 3.9 %collective-permute-start.8 = (f32[8,128]{1,0:T(8,128)S(1)}, f32[8,128]{1,0:T(8,128)S(1)}, u32[]{:S(2)}, u32[]{:S(2)}) collective-permute-start(f32[8,128]{1,0:T(8,128)S(1)} %add.19.first), channel_id=1, source_target_pairs={{0,2},{1,3},{2,0},{3,1},{4,6},{5,7},{6,4},{7,5},{8,10},{9,11},{10,... | collective-permute-start | bytes 12296 | tf_op jit(solution)/shard_map/ppermute | solution.py:139
  102.8 0.7 copy.15
  103.5 0.9 collective-permute-done.8.second
  104.4 1.8 %shard_map.120 = bf16[1,128,2048]{2,1,0:T(8,128)(2,1)} custom-call(f32[8,128]{1,0:T(8,128)S(1)} %add.19.first, f32[8,128]{1,0:T(8,128)S(1)} %collective-permute-done.8.second, f32[1,128,2048]{2,1,0:T(8,128)S(1)} %get-tuple-element.15.value_ref, bf16[1,128,2048]{2,1,0:T(8,128)(2,1)S(1)} %copy-done), custom_call_target="tpu_custom_call" | custom-call | tf_op jit(solution)/shard_map/pallas_call | solution.py:488
  106.2 0.0 collective-permute-done.10.saved_ref
  106.2 0.0 collective-permute-done.9.value_ref
  106.2 3.5 %shard_map.121 = bf16[1,128,2048]{2,1,0:T(8,128)(2,1)} custom-call(f32[8,128]{1,0:T(8,128)S(1)} %add.19.first, f32[8,128]{1,0:T(8,128)S(1)} %collective-permute-done.8.second, bf16[1,128,2048]{2,1,0:T(8,128)(2,1)S(1)} %collective-permute-done.9.value_ref, bf16[1,128,2048]{2,1,0:T(8,128)(2,1)} %collective-permute-done.10.saved_ref), custom_call_target="tpu_custom_call" | custom-call | tf_op jit(solution)/shard_map/pallas_call | solution.py:488
  (12 shorter events, 0.1 us)
Async XLA Ops:
  3.3 31.8 %copy-start.5 = (f32[1,7,2048]{2,0,1:T(1,128)S(1)}, f32[1,7,2048]{2,0,1:T(1,128)}, u32[]{:S(2)}) copy-start(f32[1,7,2048]{2,0,1:T(1,128)} %param.14) | copy-start | bytes 172036
  3.3 36.5 %all-to-all-start = ((bf16[16,384,128]{2,1,0:T(8,128)(2,1)}), bf16[16,384,128]{2,1,0:T(8,128)(2,1)}, u32[]{:S(2)}, u32[]{:S(2)}) async-start(bf16[16,384,128]{2,1,0:T(8,128)(2,1)} %get-tuple-element.12), calls=%async_computation | async-start | bytes 3145728 | tf_op jit(solution)/shard_map/all_to_all | solution.py:504
  9.2 3.7 %collective-permute-start = (f32[8,128]{1,0:T(8,128)S(1)}, f32[8,128]{1,0:T(8,128)S(1)}, u32[]{:S(2)}, u32[]{:S(2)}) collective-permute-start(f32[8,128]{1,0:T(8,128)S(1)} %get-tuple-element.11), channel_id=1, source_target_pairs={{0,1},{1,0},{2,3},{3,2},{4,5},{5,4},{6,7},{7,6},{8,9},{9,8},{10,11... | collective-permute-start | bytes 12296 | tf_op jit(solution)/shard_map/ppermute | solution.py:139
  12.8 5.5 %collective-permute-start.1 = (f32[8,128]{1,0:T(8,128)S(1)}, f32[8,128]{1,0:T(8,128)S(1)}, u32[]{:S(2)}, u32[]{:S(2)}) collective-permute-start(f32[8,128]{1,0:T(8,128)S(1)} %add.15), channel_id=1, source_target_pairs={{0,2},{1,3},{2,0},{3,1},{4,6},{5,7},{6,4},{7,5},{8,10},{9,11},{10,... | collective-permute-start | bytes 12296 | tf_op jit(solution)/shard_map/ppermute | solution.py:139
  18.3 1.2 %collective-permute-start.2 = (f32[2,128]{1,0:T(2,128)S(1)}, f32[2,128]{1,0:T(2,128)S(1)}, u32[]{:S(2)}, u32[]{:S(2)}) collective-permute-start(f32[2,128]{1,0:T(2,128)S(1)} %slice.3), channel_id=1, source_target_pairs={{0,4},{4,0},{8,12},{12,8},{16,20},{20,16},{24,28},{28,24},{32,36},... | collective-permute-start | bytes 3080 | tf_op jit(solution)/shard_map/ppermute | solution.py:139
  19.5 8.5 %collective-permute-start.3 = (f32[4,128]{1,0:T(4,128)S(1)}, f32[4,128]{1,0:T(4,128)S(1)}, u32[]{:S(2)}, u32[]{:S(2)}) collective-permute-start(f32[4,128]{1,0:T(4,128)S(1)} %pad_maximum_fusion.2), channel_id=1, source_target_pairs={{0,8},{4,12},{8,0},{12,4},{16,24},{20,28},{24,16},{28,20},{32,40},... | collective-permute-start | bytes 6152 | tf_op jit(solution)/shard_map/ppermute | solution.py:139
  28.0 5.5 %collective-permute-start.4 = (f32[8,128]{1,0:T(8,128)S(1)}, f32[8,128]{1,0:T(8,128)S(1)}, u32[]{:S(2)}, u32[]{:S(2)}) collective-permute-start(f32[8,128]{1,0:T(8,128)S(1)} %pad_maximum_fusion.1), channel_id=1, source_target_pairs={{0,16},{4,20},{8,24},{12,28},{16,0},{20,4},{24,8},{28,12},{32,48},... | collective-permute-start | bytes 12296 | tf_op jit(solution)/shard_map/ppermute | solution.py:139
  33.5 6.3 %collective-permute-start.5 = (f32[16,128]{1,0:T(8,128)S(1)}, f32[16,128]{1,0:T(8,128)S(1)}, u32[]{:S(2)}, u32[]{:S(2)}) collective-permute-start(f32[16,128]{1,0:T(8,128)S(1)} %pad_maximum_fusion), channel_id=1, source_target_pairs={{0,32},{4,36},{8,40},{12,44},{16,48},{20,52},{24,56},{28,60},{32,0... | collective-permute-start | bytes 24584 | tf_op jit(solution)/shard_map/ppermute | solution.py:139
  37.1 2.7 %copy-start.4 = (s32[16]{0:T(128)S(1)}, s32[16]{0:T(128)}, u32[]{:S(2)}) copy-start(s32[16]{0:T(128)} %order_ref.1) | copy-start | bytes 196
  50.0 5.0 %copy-start = (bf16[1,128,2048]{2,1,0:T(8,128)(2,1)S(1)}, bf16[1,128,2048]{2,1,0:T(8,128)(2,1)}, u32[]{:S(2)}) copy-start(bf16[1,128,2048]{2,1,0:T(8,128)(2,1)} %saved_ref.5) | copy-start | bytes 1572868
  50.0 23.7 %copy-start.1 = (bf16[1,128,2048]{2,1,0:T(8,128)(2,1)S(1)}, bf16[1,128,2048]{2,1,0:T(8,128)(2,1)}, u32[]{:S(2)}) copy-start(bf16[1,128,2048]{2,1,0:T(8,128)(2,1)} %cot_ref.3) | copy-start | bytes 1572868
  50.0 23.7 %copy-start.2 = (bf16[1,128,2048]{2,1,0:T(8,128)(2,1)S(1)}, bf16[1,128,2048]{2,1,0:T(8,128)(2,1)}, u32[]{:S(2)}) copy-start(bf16[1,128,2048]{2,1,0:T(8,128)(2,1)} %fwd_ref.1) | copy-start | bytes 1572868
  50.1 23.7 %copy-start.3 = (bf16[1,128,2048]{2,1,0:T(8,128)(2,1)S(1)}, bf16[1,128,2048]{2,1,0:T(8,128)(2,1)}, u32[]{:S(2)}) copy-start(bf16[1,128,2048]{2,1,0:T(8,128)(2,1)} %sconv_ref.3) | copy-start | bytes 1572868
  50.1 23.7 %all-to-all-start.1 = ((bf16[16,152,256]{2,1,0:T(8,128)(2,1)}), bf16[16,152,256]{2,1,0:T(8,128)(2,1)S(1)}, u32[]{:S(2)}, u32[]{:S(2)}) async-start(bf16[16,152,256]{2,1,0:T(8,128)(2,1)} %convolve.1), calls=%async_computation.1 | async-start | bytes 2490368 | tf_op jit(solution)/shard_map/all_to_all | solution.py:516
  55.1 51.2 %collective-permute-start.10 = (bf16[1,128,2048]{2,1,0:T(8,128)(2,1)S(1)}, bf16[1,128,2048]{2,1,0:T(8,128)(2,1)}, u32[]{:S(2)}, u32[]{:S(2)}) collective-permute-start(bf16[1,128,2048]{2,1,0:T(8,128)(2,1)S(1)} %copy-done), channel_id=1, source_target_pairs={{64,0},{65,1},{66,2},{67,3},{68,4},{69,5},{70,6},{71,7},{72,8},{73... | collective-permute-start | bytes 1572872 | tf_op jit(solution)/shard_map/ppermute | solution.py:512
  76.7 29.6 %collective-permute-start.9 = (bf16[1,128,2048]{2,1,0:T(8,128)(2,1)S(1)}, bf16[1,128,2048]{2,1,0:T(8,128)(2,1)S(1)}, u32[]{:S(2)}, u32[]{:S(2)}) collective-permute-start(bf16[1,128,2048]{2,1,0:T(8,128)(2,1)S(1)} %get-tuple-element.17), channel_id=1, source_target_pairs={{0,64},{64,0},{1,65},{65,1},{2,66},{66,2},{3,67},{67,3},{4,68},{68... | collective-permute-start | bytes 1572872 | tf_op jit(solution)/shard_map/ppermute | solution.py:521
  80.0 15.3 %collective-permute-start.6 = (f32[8,128]{1,0:T(8,128)S(1)}, f32[8,128]{1,0:T(8,128)S(1)}, u32[]{:S(2)}, u32[]{:S(2)}) collective-permute-start(f32[8,128]{1,0:T(8,128)S(1)} %get-tuple-element.14), channel_id=1, source_target_pairs={{64,0},{65,1},{66,2},{67,3},{68,4},{69,5},{70,6},{71,7},{72,8},{73... | collective-permute-start | bytes 12296 | tf_op jit(solution)/shard_map/ppermute | solution.py:520
  95.3 3.6 %collective-permute-start.7 = (f32[8,128]{1,0:T(8,128)S(1)}, f32[8,128]{1,0:T(8,128)S(1)}, u32[]{:S(2)}, u32[]{:S(2)}) collective-permute-start(f32[8,128]{1,0:T(8,128)S(1)} %broadcast_select_fusion), channel_id=1, source_target_pairs={{0,1},{1,0},{2,3},{3,2},{4,5},{5,4},{6,7},{7,6},{8,9},{9,8},{10,11... | collective-permute-start | bytes 12296 | tf_op jit(solution)/shard_map/ppermute | solution.py:139
  98.9 5.5 %collective-permute-start.8 = (f32[8,128]{1,0:T(8,128)S(1)}, f32[8,128]{1,0:T(8,128)S(1)}, u32[]{:S(2)}, u32[]{:S(2)}) collective-permute-start(f32[8,128]{1,0:T(8,128)S(1)} %add.19.first), channel_id=1, source_target_pairs={{0,2},{1,3},{2,0},{3,1},{4,6},{5,7},{6,4},{7,5},{8,10},{9,11},{10,... | collective-permute-start | bytes 12296 | tf_op jit(solution)/shard_map/ppermute | solution.py:139

commit v3 on v1

--- a/solution.py
+++ b/solution.py
@@ -35,7 +35,7 @@
     real[0] = 1.0
     imag[0] = np.where(np.arange(BLOCK) % 2 == 0, 1.0, -1.0)
     leave = np.concatenate([real, imag], axis=0).T / period
-    return split_bf16(enter) + split_bf16(leave)
+    return (np.concatenate(split_bf16(enter), axis=1), split_bf16(leave)[0])
 
 
 def rows_to_columns(rows):
@@ -203,20 +203,20 @@
     return jnp.concatenate([ref[at : at + BLOCK, :], ref[at + BLOCK : at + 2 * BLOCK, :]], axis=1)
 
 
-def enter_transform(enter_hi, enter_lo, data):
-    return jnp.dot(enter_hi[...], data, preferred_element_type=jnp.float32) + jnp.dot(
-        enter_lo[...], data, preferred_element_type=jnp.float32
-    )
-
-
-def filter_kernel(where_ref, taps_ref, enter_hi, enter_lo, filt):
+def table_dot(table, data):
+    return jnp.dot(
+        table[...], jnp.concatenate([data, data], axis=0), preferred_element_type=jnp.float32
+    )
+
+
+def filter_kernel(where_ref, taps_ref, enter, filt, edge):
     del where_ref
     freq = lax.broadcasted_iota(jnp.int32, (2 * BLOCK, LANES), 0)
     parity = jnp.where(freq % 2 == 0, 1.0, -1.0)
-    first = lax.broadcasted_iota(jnp.int32, (BLOCK, LANES), 0) == 0
+    first = lax.broadcasted_iota(jnp.int32, (8, LANES), 0) == 0
     earlier = None
     for pair in range(filt.shape[0] // 2):
-        pair_spectra = enter_transform(enter_hi, enter_lo, side_by_side(taps_ref.at[0], pair))
+        pair_spectra = table_dot(enter, side_by_side(taps_ref.at[0], pair))
         for side in range(2):
             current = pair_spectra[:, side * LANES : (side + 1) * LANES]
             both = parity * current
@@ -226,26 +226,29 @@
             real, imag = both[:BLOCK], both[BLOCK:]
             index = 2 * pair + side
             filt[index, 0] = real
-            filt[index, 1] = jnp.where(first, 0.0, imag)
-            filt[index, 2] = jnp.where(first, imag, real)
+            filt[index, 1] = imag - real
+            filt[index, 2] = imag + real
+            edge[index, 0] = jnp.where(first, 0.0, imag[:8])
+            edge[index, 1] = jnp.where(first, imag[:8], real[:8])
 
 
 def filter_spectra(where, filters, tables):
     length = filters.shape[1]
     shape = (length // BLOCK, 3, BLOCK, LANES)
+    edge_shape = (length // BLOCK, 2, 8, LANES)
     return pl.pallas_call(
         filter_kernel,
-        out_shape=pltpu.VMEM(shape, jnp.float32),
+        out_shape=(pltpu.VMEM(shape, jnp.float32), pltpu.VMEM(edge_shape, jnp.float32)),
         grid_spec=pltpu.PrefetchScalarGridSpec(
             num_scalar_prefetch=1,
             grid=(1,),
             in_specs=[pl.BlockSpec((1, length, LANES), lambda step, at: (0, 0, at[0]))]
-            + [whole(table.shape) for table in tables[:2]],
-            out_specs=VMEM,
+            + [whole(tables[0].shape)],
+            out_specs=(VMEM, VMEM),
         ),
         name="filter_spectra",
         compiler_params=pltpu.CompilerParams(vmem_limit_bytes=16 << 20),
-    )(where, in_hbm(filters), *[in_hbm(table) for table in tables[:2]])
+    )(where, in_hbm(filters), in_hbm(tables[0]))
 
 
 def fold(block):
@@ -253,9 +256,8 @@
 
 
 def conv_kernel(
-    where_ref, order_ref, gathered_ref, inv_ref, known_ref, params_ref, filt, raw_hbm, enter_hi_hbm,
-    enter_lo_hbm, leave_hi_hbm, leave_lo_hbm, out_hbm, raw_ref, enter_hi, enter_lo, leave_hi,
-    leave_lo, out_ref, ordered, spectra, product, inv_rows, inv, raw_sem, table_sem, out_sem,
+    where_ref, order_ref, gathered_ref, inv_ref, known_ref, params_ref, filt, edge, raw_hbm, enter_hbm,
+    leave_hbm, out_hbm, raw_ref, enter, leave, out_ref, ordered, spectra, product, inv_rows, inv, raw_sem, table_sem, out_sem,
 ):
     stored = raw_ref.shape[0]
     raw_copies = [
@@ -264,14 +266,7 @@
     ]
     table_copies = [
         pltpu.make_async_copy(source, target, table_sem.at[index])
-        for index, (source, target) in enumerate(
-            (
-                (enter_hi_hbm, enter_hi),
-                (enter_lo_hbm, enter_lo),
-                (leave_hi_hbm, leave_hi),
-                (leave_lo_hbm, leave_lo),
-            )
-        )
+        for index, (source, target) in enumerate(((enter_hbm.at[:, pl.ds(0, BLOCK)], enter), (leave_hbm, leave)))
     ]
     out_copies = [
         pltpu.make_async_copy(out_ref.at[index], out_hbm.at[index], out_sem.at[index])
@@ -284,63 +279,86 @@
     lanes = pl.ds(pl.multiple_of(where_ref[0] * LANES, LANES), LANES)
     p = [params_ref[0, row : row + 1, lanes] for row in range(7)]
 
+    gains = [p[0] * p[1], p[0] * p[3], p[0] * p[5]]
     for index in range(stored):
         inv_rows[2 * index : 2 * index + 2, :] = inv_ref[pl.ds(2 * gathered_ref[index], 2), :]
     inv[...] = jnp.concatenate([inv_rows[...]] * (128 // (2 * stored)), axis=0).T
     for index in range(stored):
-        raw_copies[index].wait()
+        if index % 4 == 0:
+            for copy in raw_copies[index : index + 4]:
+                copy.wait()
         at = pl.multiple_of(order_ref[index] * rows, rows)
         inv_fwd = inv[:, 2 * index : 2 * index + 1]
         inv_saved = inv[:, 2 * index + 1 : 2 * index + 2]
-        scaled = raw_ref[index, :rows, :].astype(jnp.float32) * inv_fwd * p[0]
-        mixed = (scaled * p[3] + p[4]) * (scaled * p[5] + p[6])
-        scaled = raw_ref[index, rows : 2 * rows, :].astype(jnp.float32) * inv_saved * p[0]
+        normed = raw_ref[index, :rows, :].astype(jnp.float32) * inv_fwd
+        mixed = (normed * gains[1] + p[4]) * (normed * gains[2] + p[6])
+        normed = raw_ref[index, rows : 2 * rows, :].astype(jnp.float32) * inv_saved
         cot = raw_ref[index, 2 * rows :, :].astype(jnp.float32)
         ordered[pl.ds(at, rows), :LANES] = mixed.astype(jnp.bfloat16)
-        ordered[pl.ds(at, rows), LANES:] = (cot * (scaled * p[1] + p[2])).astype(jnp.bfloat16)
+        ordered[pl.ds(at, rows), LANES:] = (cot * (normed * gains[0] + p[2])).astype(jnp.bfloat16)
 
     table_copies[0].wait()
-    table_copies[1].wait()
     for index in range(blocks):
         data = ordered[index * BLOCK : (index + 1) * BLOCK, :]
-        spectra[index] = enter_transform(enter_hi, enter_lo, data)
-
-    def products(tile, carry):
-        low = pl.ds(pl.multiple_of(tile * 8, 8), 8)
-        high = pl.ds(pl.multiple_of(BLOCK + tile * 8, 8), 8)
-        f_re = [filt[d, 0, low, :] for d in range(blocks)]
-        f_im = [filt[d, 1, low, :] for d in range(blocks)]
-        f_nq = [filt[d, 2, low, :] for d in range(blocks)]
+        spectra[index] = jnp.dot(enter[...], data, preferred_element_type=jnp.float32)
+
+    def forward_and_adjoint(low, high, one_product):
         for adjoint in (False, True):
             lanes = slice(LANES, 2 * LANES) if adjoint else slice(0, LANES)
             x_re = [spectra[j, low, lanes] for j in range(blocks)]
             x_im = [spectra[j, high, lanes] for j in range(blocks)]
             for i in range(blocks):
-                re = im = None
-                for j in range(i, blocks) if adjoint else range(i + 1):
-                    d = abs(i - j)
-                    a, b = f_re[d] * x_re[j], f_im[d] * x_im[j]
-                    c, e = f_nq[d] * x_im[j], f_im[d] * x_re[j]
-                    one = a + b if adjoint else a - b
-                    two = c - e if adjoint else c + e
-                    re = one if re is None else re + one
-                    im = two if im is None else im + two
+                terms = range(i, blocks) if adjoint else range(i + 1)
+                re, im = one_product(adjoint, x_re, x_im, [(abs(i - j), j) for j in terms])
                 product[i, low, lanes] = re
                 product[i, high, lanes] = im
+
+    def total(terms):
+        terms = list(terms)
+        return functools.reduce(lambda one, two: one + two, terms)
+
+    def first_tile(adjoint, x_re, x_im, terms):
+        f_re = [filt[d, 0, 0:8, :] for d in range(blocks)]
+        f_im = [edge[d, 0] for d in range(blocks)]
+        f_nq = [edge[d, 1] for d in range(blocks)]
+        direct = total(f_re[d] * x_re[j] for d, j in terms)
+        crossed = total(f_im[d] * x_im[j] for d, j in terms)
+        straight = total(f_nq[d] * x_im[j] for d, j in terms)
+        turned = total(f_im[d] * x_re[j] for d, j in terms)
+        if adjoint:
+            return direct + crossed, straight - turned
+        return direct - crossed, straight + turned
+
+    forward_and_adjoint(slice(0, 8), slice(BLOCK, BLOCK + 8), first_tile)
+
+    def products(tile, carry):
+        low = pl.ds(pl.multiple_of(tile * 8, 8), 8)
+        high = pl.ds(pl.multiple_of(BLOCK + tile * 8, 8), 8)
+        f_re = [filt[d, 0, low, :] for d in range(blocks)]
+        f_less = [filt[d, 1, low, :] for d in range(blocks)]
+        f_more = [filt[d, 2, low, :] for d in range(blocks)]
+
+        def other_tile(adjoint, x_re, x_im, terms):
+            both = total(f_re[d] * (x_re[j] + x_im[j]) for d, j in terms)
+            if adjoint:
+                return (
+                    both + total(f_less[d] * x_im[j] for d, j in terms),
+                    both - total(f_more[d] * x_re[j] for d, j in terms),
+                )
+            return (
+                both - total(f_more[d] * x_im[j] for d, j in terms),
+                both + total(f_less[d] * x_re[j] for d, j in terms),
+            )
+
+        forward_and_adjoint(low, high, other_tile)
         return carry
 
-    lax.fori_loop(0, BLOCK // 8, products, 0)
-
-    table_copies[2].wait()
-    table_copies[3].wait()
+    lax.fori_loop(1, BLOCK // 8, products, 0)
+
+    table_copies[1].wait()
     for index in range(blocks):
-        value = product[index]
-        top = value.astype(jnp.bfloat16)
-        rest = (value - top.astype(jnp.float32)).astype(jnp.bfloat16)
-        left = (
-            jnp.dot(leave_hi[...], top, preferred_element_type=jnp.float32)
-            + jnp.dot(leave_lo[...], top, preferred_element_type=jnp.float32)
-            + jnp.dot(leave_hi[...], rest, preferred_element_type=jnp.float32)
+        left = jnp.dot(
+            leave[...], product[index].astype(jnp.bfloat16), preferred_element_type=jnp.float32
         )
         ordered[index * BLOCK : (index + 1) * BLOCK, :] = left.astype(jnp.bfloat16)
 
@@ -374,6 +392,7 @@
 
 
 def convolve(where, order, gathered, raw, inv, known, params, spectra, tables):
+    filt, edge = spectra
     stored = raw.shape[0]
     rows = raw.shape[1] // 3
     length = stored * rows
@@ -381,11 +400,12 @@
     return pl.pallas_call(
         conv_kernel,
         out_shape=pltpu.HBM((stored, rows + 24, 2 * LANES), jnp.bfloat16),
-        in_specs=[SMEM] * 3 + [VMEM] * 4 + [HBM] * 5,
+        in_specs=[SMEM] * 3 + [VMEM] * 5 + [HBM] * 3,
         out_specs=HBM,
         scratch_shapes=[
             pltpu.VMEM(raw.shape, jnp.bfloat16),
-            *[pltpu.VMEM(table.shape, jnp.bfloat16) for table in tables],
+            pltpu.VMEM((2 * BLOCK, BLOCK), jnp.bfloat16),
+            pltpu.VMEM((BLOCK, 2 * BLOCK), jnp.bfloat16),
             pltpu.VMEM((stored, rows + 24, 2 * LANES), jnp.bfloat16),
             pltpu.VMEM((length, 2 * LANES), jnp.bfloat16),
             pltpu.VMEM((blocks, 2 * BLOCK, 2 * LANES), jnp.float32),
@@ -393,61 +413,120 @@
             pltpu.VMEM((2 * stored, 128), jnp.float32),
             pltpu.VMEM((128, 128), jnp.float32),
             pltpu.SemaphoreType.DMA((stored,)),
-            pltpu.SemaphoreType.DMA((4,)),
+            pltpu.SemaphoreType.DMA((2,)),
             pltpu.SemaphoreType.DMA((stored,)),
         ],
         name="convolve",
         compiler_params=pltpu.CompilerParams(vmem_limit_bytes=28 << 20),
     )(
-        where, order, gathered, inv, known, params, in_vmem(spectra), in_hbm(raw),
+        where, order, gathered, inv, known, params, in_vmem(filt), in_vmem(edge), in_hbm(raw),
         *[in_hbm(table) for table in tables],
     )
+
+
+def forward_terms(at, inputs, conv, params_ref, inv_fwd):
+    p = [params_ref[0, row : row + 1, at] for row in range(3)]
+    query = inputs * inv_fwd * (p[0] * p[1]) + p[2]
+    return inputs + query * conv
+
+
+def backward_terms(at, saved, sconv, cot, grad_mixed, params_ref, inv_saved):
+    p = [params_ref[0, row : row + 1, at] for row in range(7)]
+    normed = saved * inv_saved
+    mixed_grad = normed * (2.0 * p[0] * p[3] * p[5] * p[0]) + p[0] * (p[6] * p[3] + p[4] * p[5])
+    grad_normed = cot * sconv * (p[1] * p[0]) + grad_mixed * mixed_grad
+    return cot + inv_saved * grad_normed, grad_normed * normed
 
 
 def leave_kernel(
     pipe_ref, inv_ref, back_ref, fwd_ref, saved_ref, sconv_ref, cot_ref, params_ref,
-    layer_ref, send_ref, partial_ref, grads_ref, cross_ref, inv, acc, known,
+    send_ref, cross_ref, inv, acc,
 ):
+    rows, width = fwd_ref.shape[1:]
+    inv[...] = rows_to_columns(inv_ref[0:8, :])
+    inv_fwd = inv[:, 0:1]
+    inv_saved = inv[:, 1:2]
+
+    def backward(send):
+        cross = jnp.zeros((rows, LANES), jnp.float32)
+        for group in range(width // LANES):
+            at = pl.ds(group * LANES, LANES)
+            partial, term = backward_terms(
+                at,
+                saved_ref[0, :, at].astype(jnp.float32),
+                sconv_ref[0, :, at].astype(jnp.float32),
+                cot_ref[0, :, at].astype(jnp.float32),
+                back_ref[group, :rows, LANES:].astype(jnp.float32),
+                params_ref,
+                inv_saved,
+            )
+            cross = cross + term
+            if send:
+                send_ref[0, :, at] = partial.astype(jnp.bfloat16)
+        acc[...] = cross
+
+    @pl.when(pipe_ref[0] == 0)
+    def _():
+        for group in range(width // LANES):
+            at = pl.ds(group * LANES, LANES)
+            inputs = fwd_ref[0, :, at].astype(jnp.float32)
+            conv = back_ref[group, :rows, :LANES].astype(jnp.float32)
+            layer = forward_terms(at, inputs, conv, params_ref, inv_fwd)
+            send_ref[0, :, at] = layer.astype(jnp.bfloat16)
+        backward(False)
+
+    @pl.when(pipe_ref[0] != 0)
+    def _():
+        backward(True)
+
+    cross = columns_to_rows([jnp.sum(acc[...], axis=1, keepdims=True)])
+    cross_ref[...] = cross * (inv_ref[1:2, :] * inv_ref[1:2, :] / D)
+
+
+def leave(pipe, inv, back, fwd_in, saved_in, saved_conv, grad_out, mix_params):
+    return pl.pallas_call(
+        leave_kernel,
+        out_shape=(
+            pltpu.VMEM(fwd_in.shape, jnp.bfloat16),
+            pltpu.VMEM((8, 128), jnp.float32),
+        ),
+        in_specs=[SMEM] + [VMEM] * 7,
+        out_specs=(VMEM, VMEM),
+        scratch_shapes=[pltpu.VMEM((fwd_in.shape[1], 128), jnp.float32)] * 2,
+        name="leave",
+        compiler_params=pltpu.CompilerParams(vmem_limit_bytes=24 << 20),
+    )(
+        pipe, inv, in_vmem(back),
+        *[in_vmem(a) for a in (fwd_in, saved_in, saved_conv, grad_out)], mix_params,
+    )
+
+
+def forward_kernel(inv_ref, back_ref, fwd_ref, params_ref, layer_ref, grads_ref, known, inv):
     step = pl.program_id(0)
     rows = fwd_ref.shape[1]
 
     @pl.when(step == 0)
     def _():
         inv[...] = rows_to_columns(inv_ref[0:8, :])
-        acc[...] = jnp.zeros_like(acc)
         total = back_ref[0, rows : rows + 16, :].astype(jnp.float32)
         for index in range(1, back_ref.shape[0]):
             total = total + back_ref[index, rows : rows + 16, :].astype(jnp.float32)
         for row in range(16):
             known[row] = total[row : row + 1, :]
 
-    inv_fwd = inv[:, 0:1]
-    inv_saved = inv[:, 1:2]
-    first = pipe_ref[0] == 0
-    cross = acc[...]
-    groups = fwd_ref.shape[2] // LANES
+    wide = layer_ref.shape[2]
+    groups = wide // LANES
     for group in range(groups):
-        at = pl.ds(group * LANES, LANES)
-        p = [params_ref[0, row : row + 1, at] for row in range(7)]
+        own = pl.ds(group * LANES, LANES)
+        at = pl.ds(pl.multiple_of(step * wide + group * LANES, LANES), LANES)
+        block = step * groups + group
+        conv = back_ref[block, :rows, :LANES].astype(jnp.float32)
         inputs = fwd_ref[0, :, at].astype(jnp.float32)
-        query = inputs * inv_fwd * p[0] * p[1] + p[2]
-        conv = back_ref[step * groups + group, :rows, :LANES].astype(jnp.float32)
-        layer = inputs + query * conv
-        layer_ref[0, :, at] = layer.astype(jnp.bfloat16)
-
-        grad_mixed = back_ref[step * groups + group, :rows, LANES:].astype(jnp.float32)
-        cot = cot_ref[0, :, at].astype(jnp.float32)
-        normed = saved_ref[0, :, at].astype(jnp.float32) * inv_saved
-        scaled = normed * p[0]
-        grad_query = cot * sconv_ref[0, :, at].astype(jnp.float32)
-        mixed_grad = (scaled * p[5] + p[6]) * p[3] + (scaled * p[3] + p[4]) * p[5]
-        grad_normed = (grad_query * p[1] + grad_mixed * mixed_grad) * p[0]
-        cross = cross + grad_normed * normed
-        partial = cot + inv_saved * grad_normed
-        partial_ref[0, :, at] = partial
-        send_ref[0, :, at] = jnp.where(first, layer, partial).astype(jnp.bfloat16)
-
-        extra = back_ref[step * groups + group, rows + 16 :, :].astype(jnp.float32)
+        layer = forward_terms(own, inputs, conv, params_ref, inv[:, 0:1])
+        layer_ref[0, :, own] = layer.astype(jnp.bfloat16)
+
+        p = [params_ref[0, row : row + 1, own] for row in range(7)]
+        extra = back_ref[block, rows + 16 :, :].astype(jnp.float32)
         extra = extra[:, :LANES] + extra[:, LANES:]
         m0, m1, m2 = extra[0:1], extra[1:2], extra[2:3]
         row = step * (groups // 2) + group // 2
@@ -464,82 +543,107 @@
             p[0] * value_normed,
             p[0] * p[3] * m1 + p[4] * m0,
         ]
-        grads_ref[0, :, at] = jnp.concatenate(grads, axis=0)
-    acc[...] = cross
-
-    @pl.when(step == pl.num_programs(0) - 1)
-    def _():
-        cross = columns_to_rows([jnp.sum(acc[...], axis=1, keepdims=True)])
-        cross_ref[...] = cross * (inv_ref[1:2, :] * inv_ref[1:2, :] / D)
-
-
-def leave(pipe, inv, back, fwd_in, saved_in, saved_conv, grad_out, mix_params):
+        grads_ref[0, :, own] = jnp.concatenate(grads, axis=0)
+
+
+def finish_forward(inv, back, fwd_in, mix_params):
     rows, width = fwd_in.shape[1:]
     wide = 512
-    spec, params = lane_spec(rows, wide), lane_spec(7, wide)
-    return pl.pallas_call(
-        leave_kernel,
+    return pl.pallas_call(
+        forward_kernel,
         out_shape=(
             jax.ShapeDtypeStruct(fwd_in.shape, jnp.bfloat16),
-            jax.ShapeDtypeStruct(fwd_in.shape, jnp.bfloat16),
-            jax.ShapeDtypeStruct(fwd_in.shape, jnp.float32),
             jax.ShapeDtypeStruct(mix_params.shape, jnp.float32),
-            jax.ShapeDtypeStruct((8, 128), jnp.float32),
         ),
-        grid_spec=pltpu.PrefetchScalarGridSpec(
-            num_scalar_prefetch=1,
-            grid=(width // wide,),
-            in_specs=[VMEM, VMEM]
-            + [spec] * 4
-            + [params],
-            out_specs=(spec, spec, spec, params, whole((8, 128))),
-            scratch_shapes=[pltpu.VMEM((rows, 128), jnp.float32)] * 2
-            + [pltpu.VMEM((16, 1, 2 * LANES), jnp.float32)],
-        ),
-        name="leave",
-        compiler_params=pltpu.CompilerParams(vmem_limit_bytes=24 << 20),
-    )(pipe, inv, in_vmem(back), fwd_in, saved_in, saved_conv, grad_out, mix_params)
-
-
-def subtract_kernel(row, s0, s1, s2, s3, value_ref, saved_ref, out_ref, scale):
+        grid=(width // wide,),
+        in_specs=[VMEM] * 3 + [lane_spec(7, wide)],
+        out_specs=(lane_spec(rows, wide), lane_spec(7, wide)),
+        scratch_shapes=[
+            pltpu.VMEM((16, 1, 2 * LANES), jnp.float32),
+            pltpu.VMEM((rows, 128), jnp.float32),
+        ],
+        name="finish_forward",
+        compiler_params=pltpu.CompilerParams(vmem_limit_bytes=16 << 20),
+    )(inv, in_vmem(back), in_vmem(fwd_in), mix_params)
+
+
+def backward_kernel(
+    s0, s1, s2, s3, inv_ref, back_ref, saved_ref, sconv_ref, cot_ref, params_ref, peer_ref,
+    grad_ref, term_ref, scale, inv,
+):
     step = pl.program_id(0)
 
     @pl.when(step == 0)
     def _():
         scale[...] = rows_to_columns(s0[...] + s1[...] + s2[...] + s3[...])
-
-    factor = scale[:, row : row + 1]
+        inv[...] = rows_to_columns(inv_ref[0:8, :])
+
+    rows, wide = grad_ref.shape[1:]
+    for group in range(wide // LANES):
+        own = pl.ds(group * LANES, LANES)
+        at = pl.ds(pl.multiple_of(step * wide + group * LANES, LANES), LANES)
+        saved = saved_ref[0, :, at].astype(jnp.float32)
+        partial, _ = backward_terms(
+            own,
+            saved,
+            sconv_ref[0, :, at].astype(jnp.float32),
+            cot_ref[0, :, at].astype(jnp.float32),
+            back_ref[step * (wide // LANES) + group, :rows, LANES:].astype(jnp.float32),
+            params_ref,
+            inv[:, 1:2],
+        )
+        grad_ref[0, :, own] = (partial - saved * scale[:, 0:1]).astype(jnp.bfloat16)
+        term_ref[:, at] = peer_ref[0, :, own].astype(jnp.float32) * scale[:, 1:2]
+
+
+def finish_backward(scales, inv, back, saved_in, saved_conv, grad_out, mix_params, peer_saved):
+    rows, width = saved_in.shape[1:]
+    wide = 512
+    spec = lane_spec(rows, wide)
+    return pl.pallas_call(
+        backward_kernel,
+        out_shape=(
+            jax.ShapeDtypeStruct(saved_in.shape, jnp.bfloat16),
+            pltpu.VMEM((rows, width), jnp.float32),
+        ),
+        grid=(width // wide,),
+        in_specs=[VMEM] * 9 + [lane_spec(7, wide), spec],
+        out_specs=(spec, VMEM),
+        scratch_shapes=[pltpu.VMEM((rows, 128), jnp.float32)] * 2,
+        name="finish_backward",
+        compiler_params=pltpu.CompilerParams(vmem_limit_bytes=16 << 20),
+    )(
+        *scales, inv, in_vmem(back),
+        *[in_vmem(a) for a in (saved_in, saved_conv, grad_out)], mix_params, in_hbm(peer_saved),
+    )
+
+
+def received_kernel(value_ref, term_ref, out_ref):
     wide = out_ref.shape[2]
     for at in range(0, wide, LANES):
-        source = pl.ds(at, LANES)
-        if value_ref.shape[2] != wide:
-            source = pl.ds(pl.multiple_of(step * wide + at, LANES), LANES)
+        own = pl.ds(at, LANES)
+        source = pl.ds(pl.multiple_of(pl.program_id(0) * wide + at, LANES), LANES)
         value = value_ref[0, :, source].astype(jnp.float32)
-        saved = saved_ref[0, :, source].astype(jnp.float32)
-        out_ref[0, :, pl.ds(at, LANES)] = (value - saved * factor).astype(jnp.bfloat16)
-
-
-def subtract(row, scales, value, saved, resident):
-    rows, width = saved.shape[1:]
+        out_ref[0, :, own] = (value - term_ref[:, source]).astype(jnp.bfloat16)
+
+
+def finish_received(value, term):
+    rows, width = term.shape
     wide = 512
-    spec = lane_spec(rows, wide)
-    if resident:
-        value, saved = in_vmem(value), in_vmem(saved)
-    return pl.pallas_call(
-        functools.partial(subtract_kernel, row),
-        out_shape=jax.ShapeDtypeStruct(saved.shape, jnp.bfloat16),
+    return pl.pallas_call(
+        received_kernel,
+        out_shape=jax.ShapeDtypeStruct(value.shape, jnp.bfloat16),
         grid=(width // wide,),
-        in_specs=[VMEM] * 4 + [VMEM if resident else spec] * 2,
-        out_specs=spec,
-        scratch_shapes=[pltpu.VMEM((rows, 128), jnp.float32)],
-        compiler_params=pltpu.CompilerParams(vmem_limit_bytes=16 << 20),
-    )(*scales, value, saved)
+        in_specs=[VMEM, VMEM],
+        out_specs=lane_spec(rows, wide),
+        name="received",
+        compiler_params=pltpu.CompilerParams(vmem_limit_bytes=8 << 20),
+    )(in_vmem(value), in_vmem(term))
 
 
 def per_device(tables, fwd_in, saved_in, saved_conv, grad_out, filters, mix_params, span_order):
     where = lax.axis_index("seq").astype(jnp.int32).reshape(1)
     pipe = lax.axis_index("pipe").astype(jnp.int32).reshape(1)
-    peer_saved = lax.ppermute(saved_in, "pipe", [(1, 0)])
     raw, sums = pack(fwd_in, saved_in, grad_out)
     raw = lax.all_to_all(raw, "seq", 0, 0)
     own_sums = sum(over_chan(sums))
@@ -547,18 +651,20 @@
     sums = jnp.concatenate([sums, across(sums, 1)], axis=0)
     sums = jnp.concatenate([sums] + [round_ring(sums, apart) for apart in (1, 2, 3)], axis=0)
     inv = lax.rsqrt(jnp.concatenate([sums, across(sums, 8)], axis=0) / D + EPSILON)
+    peer_saved = lax.ppermute(saved_in, "pipe", [(1, 0)])
     spectra = filter_spectra(where, filters, tables)
     known = early(own_sums, saved_in, saved_conv, grad_out)
     back = convolve(where, span_order, gather_order(), raw, inv, known, mix_params, spectra, tables)
     back = lax.all_to_all(back, "seq", 0, 0)
-    layer_out, outgoing, partial, param_grad, cross = leave(
-        pipe, inv, back, fwd_in, saved_in, saved_conv, grad_out, mix_params
-    )
+    outgoing, cross = leave(pipe, inv, back, fwd_in, saved_in, saved_conv, grad_out, mix_params)
     peer_cross = lax.ppermute(cross, "pipe", [(1, 0)])
     incoming = lax.ppermute(outgoing, "pipe", [(0, 1), (1, 0)])
     scales = over_chan(jnp.concatenate([cross[:1], peer_cross[:1], cross[:6]], axis=0))
-    input_grad = subtract(0, scales, partial, saved_in, False)
-    received = subtract(1, scales, incoming, peer_saved, True)
+    layer_out, param_grad = finish_forward(inv, back, fwd_in, mix_params)
+    input_grad, term = finish_backward(
+        scales, inv, back, saved_in, saved_conv, grad_out, mix_params, peer_saved
+    )
+    received = finish_received(incoming, term)
     return (layer_out, input_grad, param_grad, received)
 
 

time: 106 us -> 104 us (0.981)
  Pallas kernels: 25.6 us -> 24.1 us
    pallas_call x1, Pallas kernels: 10.7 us -> 7.99 us  [convolve(): pl.pallas_call(conv_kernel, out_shape=pltpu.HBM((stored, rows + 24, 2 * L...]
    ppermute x6, waiting for transfers between devices: 5.42 us -> 3.5 us  [over_chan(): lax.ppermute(rows, 'chan', [(low, (low + apart) % count) for low in range...]
    ppermute x1, waiting for transfers between devices: 14 us -> 15.6 us  [per_device(): peer_cross = lax.ppermute(cross, 'pipe', [(1, 0)])]
    pallas_call x4 -> x5, Pallas kernels: 9.52 us -> 10.7 us  [the longest x1 3.82 us: finish_backward(): pl.pallas_call(backward_kernel, out_shape=(jax.ShapeDtypeStruct(saved_in....]
  transfers between devices with their start and end apart: 16 -> 16, of which waited for: 9 -> 8; matrix products, arithmetic and copies ran while one was open for 1% -> 1% of each run, Pallas kernels for 9% -> 11%
where the time goes in v3:
time: 104 us; the launch traced here: 103 us
  waiting for transfers between devices  40.8 us (39%)
  starting transfers between devices  36.8 us (35%)
  Pallas kernels  24.1 us (23%)
    all_to_all x1, waiting for transfers between devices, per_device(): back = lax.all_to_all(back, 'seq', 0, 0)  17.4 us
    ppermute x1, waiting for transfers between devices, per_device(): peer_cross = lax.ppermute(cross, 'pipe', [(1, 0)])  15.6 us
    ppermute x6, starting transfers between devices, over_chan(): lax.ppermute(rows, 'chan', [(low, (low + apart) % count) for low in range...  12.6 us
    pallas_call x1, Pallas kernels, convolve(): pl.pallas_call(conv_kernel, out_shape=pltpu.HBM((stored, rows + 24, 2 * L...  7.99 us
    ppermute x3, starting transfers between devices, round_ring(): lax.ppermute(rows, 'seq', [(low, place(low)) for low in range(count)])  5.95 us
    all_to_all x1, starting transfers between devices, per_device(): raw = lax.all_to_all(raw, 'seq', 0, 0)  5.8 us
    all_to_all x1, starting transfers between devices, per_device(): back = lax.all_to_all(back, 'seq', 0, 0)  5.18 us
    pallas_call x1, Pallas kernels, finish_backward(): pl.pallas_call(backward_kernel, out_shape=(jax.ShapeDtypeStruct(saved_in....  3.82 us
  transfers between devices with their start and end apart: 16, of which 8 were waited for; matrix products, arithmetic and copies ran while one was open for 1% of the time, Pallas kernels for 11%

profile of v3, /device:TPU:0, one launch (start us, length us, event | category | flops | bytes accessed | tf_op | source)
XLA Modules:
  0.0 103.4 jit_solution(9742521383426297973)
XLA Ops:
  0.6 2.7 %pack.1 = (bf16[16,384,128]{2,1,0:T(8,128)(2,1)}, f32[8,128]{1,0:T(8,128)S(1)}) custom-call(bf16[1,128,2048]{2,1,0:T(8,128)(2,1)} %fwd_ref.3, bf16[1,128,2048]{2,1,0:T(8,128)(2,1)} %saved_ref.5, bf16[1,128,2048]{2,1,0:T(8,128)(2,1)} %cot_ref.5), custom_call_target="tpu_custom_call" | custom-call | tf_op jit(solution)/shard_map/pack/pallas_call | solution.py:119
  3.3 0.0 copy-start.5
  3.4 5.8 %all-to-all-start = ((bf16[16,384,128]{2,1,0:T(8,128)(2,1)}), bf16[16,384,128]{2,1,0:T(8,128)(2,1)}, u32[]{:S(2)}, u32[]{:S(2)}) async-start(bf16[16,384,128]{2,1,0:T(8,128)(2,1)} %get-tuple-element.17), calls=%async_computation | async-start | bytes 3145728 | tf_op jit(solution)/shard_map/all_to_all | solution.py:648
  9.2 2.0 %collective-permute-start = (f32[8,128]{1,0:T(8,128)S(1)}, f32[8,128]{1,0:T(8,128)S(1)}, u32[]{:S(2)}, u32[]{:S(2)}) collective-permute-start(f32[8,128]{1,0:T(8,128)S(1)} %get-tuple-element.14), channel_id=1, source_target_pairs={{0,1},{1,2},{2,3},{3,0},{4,5},{5,6},{6,7},{7,4},{8,9},{9,10},{10,1... | collective-permute-start | bytes 12296 | tf_op jit(solution)/shard_map/ppermute | solution.py:142
  11.1 3.6 %collective-permute-start.1 = (f32[8,128]{1,0:T(8,128)S(1)}, f32[8,128]{1,0:T(8,128)S(1)}, u32[]{:S(2)}, u32[]{:S(2)}) collective-permute-start(f32[8,128]{1,0:T(8,128)S(1)} %get-tuple-element.14), channel_id=1, source_target_pairs={{0,2},{1,3},{2,0},{3,1},{4,6},{5,7},{6,4},{7,5},{8,10},{9,11},{10,... | collective-permute-start | bytes 12296 | tf_op jit(solution)/shard_map/ppermute | solution.py:142
  14.7 1.0 collective-permute-start.2
  15.7 0.0 collective-permute-done
  15.7 0.6 collective-permute-done.1
  16.4 2.0 %collective-permute-done.2 = f32[8,128]{1,0:T(8,128)S(1)} collective-permute-done((f32[8,128]{1,0:T(8,128)S(1)}, f32[8,128]{1,0:T(8,128)S(1)}, u32[]{:S(2)}, u32[]{:S(2)}) %collective-permute-start.2) | collective-permute-done | bytes 4128 | tf_op jit(solution)/shard_map/ppermute | solution.py:142
  18.4 0.0 collective-permute-start.3
  18.4 1.2 %collective-permute-done.3 = f32[2,128]{1,0:T(2,128)S(1)} collective-permute-done((f32[2,128]{1,0:T(2,128)S(1)}, f32[2,128]{1,0:T(2,128)S(1)}, u32[]{:S(2)}, u32[]{:S(2)}) %collective-permute-start.3) | collective-permute-done | bytes 1056 | tf_op jit(solution)/shard_map/ppermute | solution.py:149
  19.5 1.8 %collective-permute-start.4 = (f32[4,128]{1,0:T(4,128)S(1)}, f32[4,128]{1,0:T(4,128)S(1)}, u32[]{:S(2)}, u32[]{:S(2)}) collective-permute-start(f32[4,128]{1,0:T(4,128)S(1)} %pad_maximum_fusion.1), channel_id=1, source_target_pairs={{0,8},{4,12},{8,16},{12,20},{16,24},{20,28},{24,0},{28,4},{32,40},... | collective-permute-start | bytes 6152 | tf_op jit(solution)/shard_map/ppermute | solution.py:155
  21.3 2.7 %collective-permute-start.5 = (f32[4,128]{1,0:T(4,128)S(1)}, f32[4,128]{1,0:T(4,128)S(1)}, u32[]{:S(2)}, u32[]{:S(2)}) collective-permute-start(f32[4,128]{1,0:T(4,128)S(1)} %pad_maximum_fusion.1), channel_id=1, source_target_pairs={{0,16},{4,20},{8,24},{12,28},{16,0},{20,4},{24,8},{28,12},{32,48},... | collective-permute-start | bytes 6152 | tf_op jit(solution)/shard_map/ppermute | solution.py:155
  24.0 1.5 %collective-permute-start.6 = (f32[4,128]{1,0:T(4,128)S(1)}, f32[4,128]{1,0:T(4,128)S(1)}, u32[]{:S(2)}, u32[]{:S(2)}) collective-permute-start(f32[4,128]{1,0:T(4,128)S(1)} %pad_maximum_fusion.1), channel_id=1, source_target_pairs={{0,24},{4,28},{8,0},{12,4},{16,8},{20,12},{24,16},{28,20},{32,56},... | collective-permute-start | bytes 6152 | tf_op jit(solution)/shard_map/ppermute | solution.py:155
  25.5 2.8 %collective-permute-done.4 = f32[4,128]{1,0:T(4,128)S(1)} collective-permute-done((f32[4,128]{1,0:T(4,128)S(1)}, f32[4,128]{1,0:T(4,128)S(1)}, u32[]{:S(2)}, u32[]{:S(2)}) %collective-permute-start.4) | collective-permute-done | bytes 2080 | tf_op jit(solution)/shard_map/ppermute | solution.py:155
  28.2 0.4 collective-permute-done.5
  28.6 0.0 collective-permute-done.6
  28.6 1.7 %collective-permute-start.7 = (f32[16,128]{1,0:T(8,128)S(1)}, f32[16,128]{1,0:T(8,128)S(1)}, u32[]{:S(2)}, u32[]{:S(2)}) collective-permute-start(f32[16,128]{1,0:T(8,128)S(1)} %concatenate.15), channel_id=1, source_target_pairs={{0,32},{4,36},{8,40},{12,44},{16,48},{20,52},{24,56},{28,60},{32,0... | collective-permute-start | bytes 24584 | tf_op jit(solution)/shard_map/ppermute | solution.py:149
  30.3 0.0 copy-done.5
  30.4 2.0 %filter_spectra.1 = (f32[8,3,256,128]{3,2,1,0:T(8,128)S(1)}, f32[8,2,8,128]{3,2,1,0:T(8,128)S(1)}) custom-call(s32[1]{0:T(128)} %bitcast.where_ref, bf16[1,2048,2048]{2,1,0:T(8,128)(2,1)} %taps_ref.1, bf16[512,512]{1,0:T(8,128)(2,1)} %constant.84.clone.enter.enter_hbm), custom_call_target="tpu_custom_call" | custom-call | tf_op jit(solution)/shard_map/filter_spectra/pallas_call | solution.py:239
  32.3 0.0 copy-start.4
  32.3 2.6 %early.1.known_ref = f32[16,256]{1,0:T(8,128)S(1)} custom-call(f32[8,128]{1,0:T(8,128)S(1)} %add_add_fusion.sums_ref, bf16[1,128,2048]{2,1,0:T(8,128)(2,1)} %saved_ref.5, bf16[1,128,2048]{2,1,0:T(8,128)(2,1)} %sconv_ref.5, bf16[1,128,2048]{2,1,0:T(8,128)(2,1)} %cot_ref.5), custom_call_target="tpu_custom_call" | custom-call | tf_op jit(solution)/shard_map/early/pallas_call | solution.py:189
  35.0 0.0 collective-permute-done.7
  35.1 0.0 all-to-all-done.raw_hbm
  35.1 0.0 copy-done.4
  35.1 8.0 %convolve.1 = bf16[16,152,256]{2,1,0:T(8,128)(2,1)} custom-call(s32[1]{0:T(128)} %bitcast.where_ref, s32[16]{0:T(128)S(1)} %copy-done.4, s32[16]{0:T(128)S(1)} %fusion.4.gathered_ref, f32[32,128]{1,0:T(8,128)S(1)} %add_rsqrt_fusion.inv_ref, f32[16,256]{1,0:T(8,128)S(1)} %early.1.known_ref, f32[1,7,2048]{2,1,0:T(8,128)S(1)} %copy.13.params_ref, ...), custom_call_target="tpu_custom_call" | custom-call | tf_op jit(solution)/shard_map/convolve/pallas_call | solution.py:400
  43.1 0.0 copy-start
  43.1 0.0 copy-start.1
  43.1 0.0 copy-start.2
  43.1 0.0 copy-start.3
  43.1 5.2 %all-to-all-start.1 = ((bf16[16,152,256]{2,1,0:T(8,128)(2,1)}), bf16[16,152,256]{2,1,0:T(8,128)(2,1)S(1)}, u32[]{:S(2)}, u32[]{:S(2)}) async-start(bf16[16,152,256]{2,1,0:T(8,128)(2,1)} %convolve.1), calls=%async_computation.1 | async-start | bytes 2490368 | tf_op jit(solution)/shard_map/all_to_all | solution.py:658
  48.3 0.0 copy-done
  48.3 1.3 %collective-permute-start.12 = (bf16[1,128,2048]{2,1,0:T(8,128)(2,1)S(1)}, bf16[1,128,2048]{2,1,0:T(8,128)(2,1)}, u32[]{:S(2)}, u32[]{:S(2)}) collective-permute-start(bf16[1,128,2048]{2,1,0:T(8,128)(2,1)S(1)} %copy-done), channel_id=1, source_target_pairs={{64,0},{65,1},{66,2},{67,3},{68,4},{69,5},{70,6},{71,7},{72,8},{73... | collective-permute-start | bytes 1572872 | tf_op jit(solution)/shard_map/ppermute | solution.py:654
  49.6 17.4 %all-to-all-done.1.back_ref = bf16[16,152,256]{2,1,0:T(8,128)(2,1)S(1)} async-done(((bf16[16,152,256]{2,1,0:T(8,128)(2,1)}), bf16[16,152,256]{2,1,0:T(8,128)(2,1)S(1)}, u32[]{:S(2)}, u32[]{:S(2)}) %all-to-all-start.1) | async-done | bytes 1245216 | tf_op jit(solution)/shard_map/all_to_all | solution.py:658
  67.0 0.0 copy-done.1
  67.0 0.0 copy-done.2
  67.0 0.0 copy-done.3
  67.0 1.5 %leave.1 = (bf16[1,128,2048]{2,1,0:T(8,128)(2,1)S(1)}, f32[8,128]{1,0:T(8,128)S(1)}) custom-call(s32[1]{0:T(128)} %bitcast.1.pipe_ref, f32[32,128]{1,0:T(8,128)S(1)} %add_rsqrt_fusion.inv_ref, bf16[16,152,256]{2,1,0:T(8,128)(2,1)S(1)} %all-to-all-done.1.back_ref, bf16[1,128,2048]{2,1,0:T(8,128)(2,1)S(1)} %copy-done.2, bf16[1,128,2048]{2,1,0:T(8,128)(2,1)S(1)} %copy-done, ...), custom_call_target="tpu_custom_call" | custom-call | tf_op jit(solution)/shard_map/leave/pallas_call | solution.py:487
  68.5 3.1 %collective-permute-start.13 = (bf16[1,128,2048]{2,1,0:T(8,128)(2,1)S(1)}, bf16[1,128,2048]{2,1,0:T(8,128)(2,1)S(1)}, u32[]{:S(2)}, u32[]{:S(2)}) collective-permute-start(bf16[1,128,2048]{2,1,0:T(8,128)(2,1)S(1)} %get-tuple-element.22), channel_id=1, source_target_pairs={{0,64},{64,0},{1,65},{65,1},{2,66},{66,2},{3,67},{67,3},{4,68},{68... | collective-permute-start | bytes 1572872 | tf_op jit(solution)/shard_map/ppermute | solution.py:661
  71.6 1.3 %collective-permute-start.8 = (f32[8,128]{1,0:T(8,128)S(1)}, f32[8,128]{1,0:T(8,128)S(1)}, u32[]{:S(2)}, u32[]{:S(2)}) collective-permute-start(f32[8,128]{1,0:T(8,128)S(1)} %get-tuple-element.19), channel_id=1, source_target_pairs={{64,0},{65,1},{66,2},{67,3},{68,4},{69,5},{70,6},{71,7},{72,8},{73... | collective-permute-start | bytes 12296 | tf_op jit(solution)/shard_map/ppermute | solution.py:660
  72.9 15.6 %collective-permute-done.8 = f32[8,128]{1,0:T(8,128)S(1)} collective-permute-done((f32[8,128]{1,0:T(8,128)S(1)}, f32[8,128]{1,0:T(8,128)S(1)}, u32[]{:S(2)}, u32[]{:S(2)}) %collective-permute-start.8) | collective-permute-done | bytes 4128 | tf_op jit(solution)/shard_map/ppermute | solution.py:660
  88.5 4.0 %collective-permute-start.10 = (f32[8,128]{1,0:T(8,128)S(1)}, f32[8,128]{1,0:T(8,128)S(1)}, u32[]{:S(2)}, u32[]{:S(2)}) collective-permute-start(f32[8,128]{1,0:T(8,128)S(1)} %pad_maximum_fusion.s0), channel_id=1, source_target_pairs={{0,2},{1,3},{2,0},{3,1},{4,6},{5,7},{6,4},{7,5},{8,10},{9,11},{10,... | collective-permute-start | bytes 12296 | tf_op jit(solution)/shard_map/ppermute | solution.py:142
  92.5 0.7 collective-permute-start.11
  93.2 1.3 %collective-permute-start.9 = (f32[8,128]{1,0:T(8,128)S(1)}, f32[8,128]{1,0:T(8,128)S(1)}, u32[]{:S(2)}, u32[]{:S(2)}) collective-permute-start(f32[8,128]{1,0:T(8,128)S(1)} %pad_maximum_fusion.s0), channel_id=1, source_target_pairs={{0,1},{1,2},{2,3},{3,0},{4,5},{5,6},{6,7},{7,4},{8,9},{9,10},{10,1... | collective-permute-start | bytes 12296 | tf_op jit(solution)/shard_map/ppermute | solution.py:142
  94.5 1.9 %finish_forward.1 = (bf16[1,128,2048]{2,1,0:T(8,128)(2,1)}, f32[1,7,2048]{2,1,0:T(8,128)S(1)}) custom-call(f32[32,128]{1,0:T(8,128)S(1)} %add_rsqrt_fusion.inv_ref, bf16[16,152,256]{2,1,0:T(8,128)(2,1)S(1)} %all-to-all-done.1.back_ref, bf16[1,128,2048]{2,1,0:T(8,128)(2,1)S(1)} %copy-done.2, f32[1,7,2048]{2,1,0:T(8,128)S(1)} %copy.13.params_ref), custom_call_target="tpu_custom_call" | custom-call | tf_op jit(solution)/shard_map/finish_forward/pallas_call | solution.py:552
  96.4 0.7 copy.17
  97.1 0.0 collective-permute-done.12.peer_ref
  97.1 0.0 collective-permute-done.10.s2
  97.1 0.0 collective-permute-done.11.s3
  97.1 0.9 collective-permute-done.9.s1
  98.0 3.8 %finish_backward.1 = (bf16[1,128,2048]{2,1,0:T(8,128)(2,1)}, f32[128,2048]{1,0:T(8,128)S(1)}) custom-call(f32[8,128]{1,0:T(8,128)S(1)} %pad_maximum_fusion.s0, f32[8,128]{1,0:T(8,128)S(1)} %collective-permute-done.9.s1, f32[8,128]{1,0:T(8,128)S(1)} %collective-permute-done.10.s2, f32[8,128]{1,0:T(8,128)S(1)} %collective-permute-done.11.s3, ...), custom_call_target="tpu_custom_call" | custom-call | tf_op jit(solution)/shard_map/finish_backward/pallas_call | solution.py:603
  101.8 0.0 collective-permute-done.13.value_ref
  101.8 1.5 %received.1 = bf16[1,128,2048]{2,1,0:T(8,128)(2,1)} custom-call(bf16[1,128,2048]{2,1,0:T(8,128)(2,1)S(1)} %collective-permute-done.13.value_ref, f32[128,2048]{1,0:T(8,128)S(1)} %get-tuple-element.23.term_ref), custom_call_target="tpu_custom_call" | custom-call | tf_op jit(solution)/shard_map/received/pallas_call | solution.py:633
  (11 shorter events, 0.2 us)
Async XLA Ops:
  3.3 27.0 %copy-start.5 = (f32[1,7,2048]{2,0,1:T(1,128)S(1)}, f32[1,7,2048]{2,0,1:T(1,128)}, u32[]{:S(2)}) copy-start(f32[1,7,2048]{2,0,1:T(1,128)} %param.14) | copy-start | bytes 172036
  3.4 31.7 %all-to-all-start = ((bf16[16,384,128]{2,1,0:T(8,128)(2,1)}), bf16[16,384,128]{2,1,0:T(8,128)(2,1)}, u32[]{:S(2)}, u32[]{:S(2)}) async-start(bf16[16,384,128]{2,1,0:T(8,128)(2,1)} %get-tuple-element.17), calls=%async_computation | async-start | bytes 3145728 | tf_op jit(solution)/shard_map/all_to_all | solution.py:648
  9.2 6.6 %collective-permute-start = (f32[8,128]{1,0:T(8,128)S(1)}, f32[8,128]{1,0:T(8,128)S(1)}, u32[]{:S(2)}, u32[]{:S(2)}) collective-permute-start(f32[8,128]{1,0:T(8,128)S(1)} %get-tuple-element.14), channel_id=1, source_target_pairs={{0,1},{1,2},{2,3},{3,0},{4,5},{5,6},{6,7},{7,4},{8,9},{9,10},{10,1... | collective-permute-start | bytes 12296 | tf_op jit(solution)/shard_map/ppermute | solution.py:142
  11.1 5.2 %collective-permute-start.1 = (f32[8,128]{1,0:T(8,128)S(1)}, f32[8,128]{1,0:T(8,128)S(1)}, u32[]{:S(2)}, u32[]{:S(2)}) collective-permute-start(f32[8,128]{1,0:T(8,128)S(1)} %get-tuple-element.14), channel_id=1, source_target_pairs={{0,2},{1,3},{2,0},{3,1},{4,6},{5,7},{6,4},{7,5},{8,10},{9,11},{10,... | collective-permute-start | bytes 12296 | tf_op jit(solution)/shard_map/ppermute | solution.py:142
  14.7 3.6 %collective-permute-start.2 = (f32[8,128]{1,0:T(8,128)S(1)}, f32[8,128]{1,0:T(8,128)S(1)}, u32[]{:S(2)}, u32[]{:S(2)}) collective-permute-start(f32[8,128]{1,0:T(8,128)S(1)} %get-tuple-element.14), channel_id=1, source_target_pairs={{0,3},{1,0},{2,1},{3,2},{4,7},{5,4},{6,5},{7,6},{8,11},{9,8},{10,9... | collective-permute-start | bytes 12296 | tf_op jit(solution)/shard_map/ppermute | solution.py:142
  18.4 1.2 %collective-permute-start.3 = (f32[2,128]{1,0:T(2,128)S(1)}, f32[2,128]{1,0:T(2,128)S(1)}, u32[]{:S(2)}, u32[]{:S(2)}) collective-permute-start(f32[2,128]{1,0:T(2,128)S(1)} %slice.12), channel_id=1, source_target_pairs={{0,4},{4,0},{8,12},{12,8},{16,20},{20,16},{24,28},{28,24},{32,36},... | collective-permute-start | bytes 3080 | tf_op jit(solution)/shard_map/ppermute | solution.py:149
  19.5 8.7 %collective-permute-start.4 = (f32[4,128]{1,0:T(4,128)S(1)}, f32[4,128]{1,0:T(4,128)S(1)}, u32[]{:S(2)}, u32[]{:S(2)}) collective-permute-start(f32[4,128]{1,0:T(4,128)S(1)} %pad_maximum_fusion.1), channel_id=1, source_target_pairs={{0,8},{4,12},{8,16},{12,20},{16,24},{20,28},{24,0},{28,4},{32,40},... | collective-permute-start | bytes 6152 | tf_op jit(solution)/shard_map/ppermute | solution.py:155
  21.3 7.3 %collective-permute-start.5 = (f32[4,128]{1,0:T(4,128)S(1)}, f32[4,128]{1,0:T(4,128)S(1)}, u32[]{:S(2)}, u32[]{:S(2)}) collective-permute-start(f32[4,128]{1,0:T(4,128)S(1)} %pad_maximum_fusion.1), channel_id=1, source_target_pairs={{0,16},{4,20},{8,24},{12,28},{16,0},{20,4},{24,8},{28,12},{32,48},... | collective-permute-start | bytes 6152 | tf_op jit(solution)/shard_map/ppermute | solution.py:155
  24.0 4.6 %collective-permute-start.6 = (f32[4,128]{1,0:T(4,128)S(1)}, f32[4,128]{1,0:T(4,128)S(1)}, u32[]{:S(2)}, u32[]{:S(2)}) collective-permute-start(f32[4,128]{1,0:T(4,128)S(1)} %pad_maximum_fusion.1), channel_id=1, source_target_pairs={{0,24},{4,28},{8,0},{12,4},{16,8},{20,12},{24,16},{28,20},{32,56},... | collective-permute-start | bytes 6152 | tf_op jit(solution)/shard_map/ppermute | solution.py:155
  28.6 6.4 %collective-permute-start.7 = (f32[16,128]{1,0:T(8,128)S(1)}, f32[16,128]{1,0:T(8,128)S(1)}, u32[]{:S(2)}, u32[]{:S(2)}) collective-permute-start(f32[16,128]{1,0:T(8,128)S(1)} %concatenate.15), channel_id=1, source_target_pairs={{0,32},{4,36},{8,40},{12,44},{16,48},{20,52},{24,56},{28,60},{32,0... | collective-permute-start | bytes 24584 | tf_op jit(solution)/shard_map/ppermute | solution.py:149
  32.3 2.7 %copy-start.4 = (s32[16]{0:T(128)S(1)}, s32[16]{0:T(128)}, u32[]{:S(2)}) copy-start(s32[16]{0:T(128)} %order_ref.1) | copy-start | bytes 196
  43.1 5.2 %copy-start = (bf16[1,128,2048]{2,1,0:T(8,128)(2,1)S(1)}, bf16[1,128,2048]{2,1,0:T(8,128)(2,1)}, u32[]{:S(2)}) copy-start(bf16[1,128,2048]{2,1,0:T(8,128)(2,1)} %saved_ref.5) | copy-start | bytes 1572868
  43.1 23.9 %copy-start.1 = (bf16[1,128,2048]{2,1,0:T(8,128)(2,1)S(1)}, bf16[1,128,2048]{2,1,0:T(8,128)(2,1)}, u32[]{:S(2)}) copy-start(bf16[1,128,2048]{2,1,0:T(8,128)(2,1)} %cot_ref.5) | copy-start | bytes 1572868
  43.1 23.9 %copy-start.2 = (bf16[1,128,2048]{2,1,0:T(8,128)(2,1)S(1)}, bf16[1,128,2048]{2,1,0:T(8,128)(2,1)}, u32[]{:S(2)}) copy-start(bf16[1,128,2048]{2,1,0:T(8,128)(2,1)} %fwd_ref.3) | copy-start | bytes 1572868
  43.1 23.9 %copy-start.3 = (bf16[1,128,2048]{2,1,0:T(8,128)(2,1)S(1)}, bf16[1,128,2048]{2,1,0:T(8,128)(2,1)}, u32[]{:S(2)}) copy-start(bf16[1,128,2048]{2,1,0:T(8,128)(2,1)} %sconv_ref.5) | copy-start | bytes 1572868
  43.1 23.9 %all-to-all-start.1 = ((bf16[16,152,256]{2,1,0:T(8,128)(2,1)}), bf16[16,152,256]{2,1,0:T(8,128)(2,1)S(1)}, u32[]{:S(2)}, u32[]{:S(2)}) async-start(bf16[16,152,256]{2,1,0:T(8,128)(2,1)} %convolve.1), calls=%async_computation.1 | async-start | bytes 2490368 | tf_op jit(solution)/shard_map/all_to_all | solution.py:658
  48.3 48.8 %collective-permute-start.12 = (bf16[1,128,2048]{2,1,0:T(8,128)(2,1)S(1)}, bf16[1,128,2048]{2,1,0:T(8,128)(2,1)}, u32[]{:S(2)}, u32[]{:S(2)}) collective-permute-start(bf16[1,128,2048]{2,1,0:T(8,128)(2,1)S(1)} %copy-done), channel_id=1, source_target_pairs={{64,0},{65,1},{66,2},{67,3},{68,4},{69,5},{70,6},{71,7},{72,8},{73... | collective-permute-start | bytes 1572872 | tf_op jit(solution)/shard_map/ppermute | solution.py:654
  68.5 33.3 %collective-permute-start.13 = (bf16[1,128,2048]{2,1,0:T(8,128)(2,1)S(1)}, bf16[1,128,2048]{2,1,0:T(8,128)(2,1)S(1)}, u32[]{:S(2)}, u32[]{:S(2)}) collective-permute-start(bf16[1,128,2048]{2,1,0:T(8,128)(2,1)S(1)} %get-tuple-element.22), channel_id=1, source_target_pairs={{0,64},{64,0},{1,65},{65,1},{2,66},{66,2},{3,67},{67,3},{4,68},{68... | collective-permute-start | bytes 1572872 | tf_op jit(solution)/shard_map/ppermute | solution.py:661
  71.6 16.9 %collective-permute-start.8 = (f32[8,128]{1,0:T(8,128)S(1)}, f32[8,128]{1,0:T(8,128)S(1)}, u32[]{:S(2)}, u32[]{:S(2)}) collective-permute-start(f32[8,128]{1,0:T(8,128)S(1)} %get-tuple-element.19), channel_id=1, source_target_pairs={{64,0},{65,1},{66,2},{67,3},{68,4},{69,5},{70,6},{71,7},{72,8},{73... | collective-permute-start | bytes 12296 | tf_op jit(solution)/shard_map/ppermute | solution.py:660
  88.5 8.6 %collective-permute-start.10 = (f32[8,128]{1,0:T(8,128)S(1)}, f32[8,128]{1,0:T(8,128)S(1)}, u32[]{:S(2)}, u32[]{:S(2)}) collective-permute-start(f32[8,128]{1,0:T(8,128)S(1)} %pad_maximum_fusion.s0), channel_id=1, source_target_pairs={{0,2},{1,3},{2,0},{3,1},{4,6},{5,7},{6,4},{7,5},{8,10},{9,11},{10,... | collective-permute-start | bytes 12296 | tf_op jit(solution)/shard_map/ppermute | solution.py:142
  92.5 4.6 %collective-permute-start.11 = (f32[8,128]{1,0:T(8,128)S(1)}, f32[8,128]{1,0:T(8,128)S(1)}, u32[]{:S(2)}, u32[]{:S(2)}) collective-permute-start(f32[8,128]{1,0:T(8,128)S(1)} %pad_maximum_fusion.s0), channel_id=1, source_target_pairs={{0,3},{1,0},{2,1},{3,2},{4,7},{5,4},{6,5},{7,6},{8,11},{9,8},{10,9... | collective-permute-start | bytes 12296 | tf_op jit(solution)/shard_map/ppermute | solution.py:142
  93.2 4.8 %collective-permute-start.9 = (f32[8,128]{1,0:T(8,128)S(1)}, f32[8,128]{1,0:T(8,128)S(1)}, u32[]{:S(2)}, u32[]{:S(2)}) collective-permute-start(f32[8,128]{1,0:T(8,128)S(1)} %pad_maximum_fusion.s0), channel_id=1, source_target_pairs={{0,1},{1,2},{2,3},{3,0},{4,5},{5,6},{6,7},{7,4},{8,9},{9,10},{10,1... | collective-permute-start | bytes 12296 | tf_op jit(solution)/shard_map/ppermute | solution.py:142

commit v4 on v3

--- a/solution.py
+++ b/solution.py
@@ -14,12 +14,6 @@
 EPSILON = 1e-05
 BLOCK = 256
 LANES = 128
-
-
-def split_bf16(table):
-    high = table.astype(np.float32).astype(ml_dtypes.bfloat16)
-    low = (table - high.astype(np.float64)).astype(np.float32).astype(ml_dtypes.bfloat16)
-    return high, low
 
 
 def transform_tables():
@@ -35,7 +29,7 @@
     real[0] = 1.0
     imag[0] = np.where(np.arange(BLOCK) % 2 == 0, 1.0, -1.0)
     leave = np.concatenate([real, imag], axis=0).T / period
-    return (np.concatenate(split_bf16(enter), axis=1), split_bf16(leave)[0])
+    return tuple(table.astype(np.float32).astype(ml_dtypes.bfloat16) for table in (enter, leave))
 
 
 def rows_to_columns(rows):
@@ -149,9 +143,9 @@
     return lax.ppermute(rows, "seq", [(low, low ^ flip) for low in range(count)])
 
 
-def round_ring(rows, apart):
+def from_chip(rows, side, back):
     count = lax.axis_size("seq")
-    place = lambda low: low // 8 * 8 + (low + 2 * apart) % 8
+    place = lambda low: (low // 8 ^ side) * 8 + (low + 2 * back) % 8
     return lax.ppermute(rows, "seq", [(low, place(low)) for low in range(count)])
 
 
@@ -203,48 +197,37 @@
     return jnp.concatenate([ref[at : at + BLOCK, :], ref[at + BLOCK : at + 2 * BLOCK, :]], axis=1)
 
 
-def table_dot(table, data):
-    return jnp.dot(
-        table[...], jnp.concatenate([data, data], axis=0), preferred_element_type=jnp.float32
-    )
-
-
-def filter_kernel(where_ref, taps_ref, enter, filt, edge):
+def filter_kernel(where_ref, taps_ref, enter, filt):
     del where_ref
     freq = lax.broadcasted_iota(jnp.int32, (2 * BLOCK, LANES), 0)
     parity = jnp.where(freq % 2 == 0, 1.0, -1.0)
-    first = lax.broadcasted_iota(jnp.int32, (8, LANES), 0) == 0
     earlier = None
     for pair in range(filt.shape[0] // 2):
-        pair_spectra = table_dot(enter, side_by_side(taps_ref.at[0], pair))
+        pair_spectra = jnp.dot(
+            enter[...], side_by_side(taps_ref.at[0], pair), preferred_element_type=jnp.float32
+        )
         for side in range(2):
             current = pair_spectra[:, side * LANES : (side + 1) * LANES]
             both = parity * current
             if earlier is not None:
                 both = both + earlier
             earlier = current
-            real, imag = both[:BLOCK], both[BLOCK:]
-            index = 2 * pair + side
-            filt[index, 0] = real
-            filt[index, 1] = imag - real
-            filt[index, 2] = imag + real
-            edge[index, 0] = jnp.where(first, 0.0, imag[:8])
-            edge[index, 1] = jnp.where(first, imag[:8], real[:8])
+            filt[2 * pair + side, 0] = both[:BLOCK]
+            filt[2 * pair + side, 1] = both[BLOCK:]
 
 
 def filter_spectra(where, filters, tables):
     length = filters.shape[1]
-    shape = (length // BLOCK, 3, BLOCK, LANES)
-    edge_shape = (length // BLOCK, 2, 8, LANES)
+    shape = (length // BLOCK, 2, BLOCK, LANES)
     return pl.pallas_call(
         filter_kernel,
-        out_shape=(pltpu.VMEM(shape, jnp.float32), pltpu.VMEM(edge_shape, jnp.float32)),
+        out_shape=pltpu.VMEM(shape, jnp.float32),
         grid_spec=pltpu.PrefetchScalarGridSpec(
             num_scalar_prefetch=1,
             grid=(1,),
             in_specs=[pl.BlockSpec((1, length, LANES), lambda step, at: (0, 0, at[0]))]
             + [whole(tables[0].shape)],
-            out_specs=(VMEM, VMEM),
+            out_specs=VMEM,
         ),
         name="filter_spectra",
         compiler_params=pltpu.CompilerParams(vmem_limit_bytes=16 << 20),
@@ -256,7 +239,7 @@
 
 
 def conv_kernel(
-    where_ref, order_ref, gathered_ref, inv_ref, known_ref, params_ref, filt, edge, raw_hbm, enter_hbm,
+    where_ref, order_ref, gathered_ref, inv_ref, known_ref, params_ref, filt, raw_hbm, enter_hbm,
     leave_hbm, out_hbm, raw_ref, enter, leave, out_ref, ordered, spectra, product, inv_rows, inv, raw_sem, table_sem, out_sem,
 ):
     stored = raw_ref.shape[0]
@@ -266,7 +249,7 @@
     ]
     table_copies = [
         pltpu.make_async_copy(source, target, table_sem.at[index])
-        for index, (source, target) in enumerate(((enter_hbm.at[:, pl.ds(0, BLOCK)], enter), (leave_hbm, leave)))
+        for index, (source, target) in enumerate(((enter_hbm, enter), (leave_hbm, leave)))
     ]
     out_copies = [
         pltpu.make_async_copy(out_ref.at[index], out_hbm.at[index], out_sem.at[index])
@@ -319,8 +302,10 @@
 
     def first_tile(adjoint, x_re, x_im, terms):
         f_re = [filt[d, 0, 0:8, :] for d in range(blocks)]
-        f_im = [edge[d, 0] for d in range(blocks)]
-        f_nq = [edge[d, 1] for d in range(blocks)]
+        first = lax.broadcasted_iota(jnp.int32, (8, LANES), 0) == 0
+        imag = [filt[d, 1, 0:8, :] for d in range(blocks)]
+        f_im = [jnp.where(first, 0.0, value) for value in imag]
+        f_nq = [jnp.where(first, value, f_re[d]) for d, value in enumerate(imag)]
         direct = total(f_re[d] * x_re[j] for d, j in terms)
         crossed = total(f_im[d] * x_im[j] for d, j in terms)
         straight = total(f_nq[d] * x_im[j] for d, j in terms)
@@ -335,8 +320,9 @@
         low = pl.ds(pl.multiple_of(tile * 8, 8), 8)
         high = pl.ds(pl.multiple_of(BLOCK + tile * 8, 8), 8)
         f_re = [filt[d, 0, low, :] for d in range(blocks)]
-        f_less = [filt[d, 1, low, :] for d in range(blocks)]
-        f_more = [filt[d, 2, low, :] for d in range(blocks)]
+        f_im = [filt[d, 1, low, :] for d in range(blocks)]
+        f_less = [f_im[d] - f_re[d] for d in range(blocks)]
+        f_more = [f_im[d] + f_re[d] for d in range(blocks)]
 
         def other_tile(adjoint, x_re, x_im, terms):
             both = total(f_re[d] * (x_re[j] + x_im[j]) for d, j in terms)
@@ -392,7 +378,6 @@
 
 
 def convolve(where, order, gathered, raw, inv, known, params, spectra, tables):
-    filt, edge = spectra
     stored = raw.shape[0]
     rows = raw.shape[1] // 3
     length = stored * rows
@@ -400,7 +385,7 @@
     return pl.pallas_call(
         conv_kernel,
         out_shape=pltpu.HBM((stored, rows + 24, 2 * LANES), jnp.bfloat16),
-        in_specs=[SMEM] * 3 + [VMEM] * 5 + [HBM] * 3,
+        in_specs=[SMEM] * 3 + [VMEM] * 4 + [HBM] * 3,
         out_specs=HBM,
         scratch_shapes=[
             pltpu.VMEM(raw.shape, jnp.bfloat16),
@@ -419,7 +404,7 @@
         name="convolve",
         compiler_params=pltpu.CompilerParams(vmem_limit_bytes=28 << 20),
     )(
-        where, order, gathered, inv, known, params, in_vmem(filt), in_vmem(edge), in_hbm(raw),
+        where, order, gathered, inv, known, params, in_vmem(spectra), in_hbm(raw),
         *[in_hbm(table) for table in tables],
     )
 
@@ -649,8 +634,9 @@
     own_sums = sum(over_chan(sums))
     sums = own_sums[:2]
     sums = jnp.concatenate([sums, across(sums, 1)], axis=0)
-    sums = jnp.concatenate([sums] + [round_ring(sums, apart) for apart in (1, 2, 3)], axis=0)
-    inv = lax.rsqrt(jnp.concatenate([sums, across(sums, 8)], axis=0) / D + EPSILON)
+    chips = [(side, back) for side in range(2) for back in range(4)]
+    far = [from_chip(sums, *chip) if any(chip) else sums for chip in chips]
+    inv = lax.rsqrt(jnp.concatenate(far, axis=0) / D + EPSILON)
     peer_saved = lax.ppermute(saved_in, "pipe", [(1, 0)])
     spectra = filter_spectra(where, filters, tables)
     known = early(own_sums, saved_in, saved_conv, grad_out)

time: 104 us -> 107 us (1.029)
  starting transfers between devices: 36.8 us -> 39.9 us
    ppermute x3 -> x7, starting transfers between devices: 5.95 us -> 10.7 us  [from_chip(): lax.ppermute(rows, 'seq', [(low, place(low)) for low in range(count)])]
    ppermute x2 -> x1, starting transfers between devices: 1.66 us -> 0.01 us  [across(): lax.ppermute(rows, 'seq', [(low, low ^ flip) for low in range(count)])]
    ppermute x3 -> x7, waiting for transfers between devices: 3.13 us -> 4.17 us  [from_chip(): lax.ppermute(rows, 'seq', [(low, place(low)) for low in range(count)])]
  transfers between devices with their start and end apart: 16 -> 19, of which waited for: 8 -> 6; matrix products, arithmetic and copies ran while one was open for 1% -> 1% of each run, Pallas kernels for 11% -> 11%
where the time goes in v4:
time: 107 us; the launch traced here: 106 us
  waiting for transfers between devices  40.9 us (38%)
  starting transfers between devices  39.9 us (37%)
  Pallas kernels  23.6 us (22%)
    all_to_all x1, waiting for transfers between devices, per_device(): back = lax.all_to_all(back, 'seq', 0, 0)  17.4 us
    ppermute x1, waiting for transfers between devices, per_device(): peer_cross = lax.ppermute(cross, 'pipe', [(1, 0)])  15.6 us
    ppermute x6, starting transfers between devices, over_chan(): lax.ppermute(rows, 'chan', [(low, (low + apart) % count) for low in range...  13.2 us
    ppermute x7, starting transfers between devices, from_chip(): lax.ppermute(rows, 'seq', [(low, place(low)) for low in range(count)])  10.7 us
    pallas_call x1, Pallas kernels, convolve(): pl.pallas_call(conv_kernel, out_shape=pltpu.HBM((stored, rows + 24, 2 * L...  7.9 us
    all_to_all x1, starting transfers between devices, per_device(): raw = lax.all_to_all(raw, 'seq', 0, 0)  5.8 us
    all_to_all x1, starting transfers between devices, per_device(): back = lax.all_to_all(back, 'seq', 0, 0)  4.52 us
    ppermute x7, waiting for transfers between devices, from_chip(): lax.ppermute(rows, 'seq', [(low, place(low)) for low in range(count)])  4.17 us
  transfers between devices with their start and end apart: 19, of which 6 were waited for; matrix products, arithmetic and copies ran while one was open for 1% of the time, Pallas kernels for 11%

profile of v4, /device:TPU:0, one launch (start us, length us, event | category | flops | bytes accessed | tf_op | source)
XLA Modules:
  0.0 106.1 jit_solution(714208476887318012)
XLA Ops:
  0.6 2.7 %pack.1 = (bf16[16,384,128]{2,1,0:T(8,128)(2,1)}, f32[8,128]{1,0:T(8,128)S(1)}) custom-call(bf16[1,128,2048]{2,1,0:T(8,128)(2,1)} %fwd_ref.3, bf16[1,128,2048]{2,1,0:T(8,128)(2,1)} %saved_ref.5, bf16[1,128,2048]{2,1,0:T(8,128)(2,1)} %cot_ref.5), custom_call_target="tpu_custom_call" | custom-call | tf_op jit(solution)/shard_map/pack/pallas_call | solution.py:113
  3.3 0.0 copy-start.5
  3.3 5.8 %all-to-all-start = ((bf16[16,384,128]{2,1,0:T(8,128)(2,1)}), bf16[16,384,128]{2,1,0:T(8,128)(2,1)}, u32[]{:S(2)}, u32[]{:S(2)}) async-start(bf16[16,384,128]{2,1,0:T(8,128)(2,1)} %get-tuple-element.13), calls=%async_computation | async-start | bytes 3145728 | tf_op jit(solution)/shard_map/all_to_all | solution.py:633
  9.1 2.0 %collective-permute-start = (f32[8,128]{1,0:T(8,128)S(1)}, f32[8,128]{1,0:T(8,128)S(1)}, u32[]{:S(2)}, u32[]{:S(2)}) collective-permute-start(f32[8,128]{1,0:T(8,128)S(1)} %get-tuple-element.12), channel_id=1, source_target_pairs={{0,1},{1,2},{2,3},{3,0},{4,5},{5,6},{6,7},{7,4},{8,9},{9,10},{10,1... | collective-permute-start | bytes 12296 | tf_op jit(solution)/shard_map/ppermute | solution.py:136
  11.1 3.6 %collective-permute-start.1 = (f32[8,128]{1,0:T(8,128)S(1)}, f32[8,128]{1,0:T(8,128)S(1)}, u32[]{:S(2)}, u32[]{:S(2)}) collective-permute-start(f32[8,128]{1,0:T(8,128)S(1)} %get-tuple-element.12), channel_id=1, source_target_pairs={{0,2},{1,3},{2,0},{3,1},{4,6},{5,7},{6,4},{7,5},{8,10},{9,11},{10,... | collective-permute-start | bytes 12296 | tf_op jit(solution)/shard_map/ppermute | solution.py:136
  14.7 1.0 collective-permute-start.2
  15.7 0.0 collective-permute-done
  15.7 0.6 collective-permute-done.1
  16.3 2.0 %collective-permute-done.2 = f32[8,128]{1,0:T(8,128)S(1)} collective-permute-done((f32[8,128]{1,0:T(8,128)S(1)}, f32[8,128]{1,0:T(8,128)S(1)}, u32[]{:S(2)}, u32[]{:S(2)}) %collective-permute-start.2) | collective-permute-done | bytes 4128 | tf_op jit(solution)/shard_map/ppermute | solution.py:136
  18.3 0.0 collective-permute-start.3
  18.3 1.2 %collective-permute-done.3 = f32[2,128]{1,0:T(2,128)S(1)} collective-permute-done((f32[2,128]{1,0:T(2,128)S(1)}, f32[2,128]{1,0:T(2,128)S(1)}, u32[]{:S(2)}, u32[]{:S(2)}) %collective-permute-start.3) | collective-permute-done | bytes 1056 | tf_op jit(solution)/shard_map/ppermute | solution.py:143
  19.5 3.9 %collective-permute-start.10 = (f32[4,128]{1,0:T(4,128)S(1)}, f32[4,128]{1,0:T(4,128)S(1)}, u32[]{:S(2)}, u32[]{:S(2)}) collective-permute-start(f32[4,128]{1,0:T(4,128)S(1)} %pad_maximum_fusion.1), channel_id=1, source_target_pairs={{0,56},{4,60},{8,32},{12,36},{16,40},{20,44},{24,48},{28,52},{32,2... | collective-permute-start | bytes 6152 | tf_op jit(solution)/shard_map/ppermute | solution.py:149
  23.4 0.0 collective-permute-start.4
  23.4 2.3 %collective-permute-start.5 = (f32[4,128]{1,0:T(4,128)S(1)}, f32[4,128]{1,0:T(4,128)S(1)}, u32[]{:S(2)}, u32[]{:S(2)}) collective-permute-start(f32[4,128]{1,0:T(4,128)S(1)} %pad_maximum_fusion.1), channel_id=1, source_target_pairs={{0,16},{4,20},{8,24},{12,28},{16,0},{20,4},{24,8},{28,12},{32,48},... | collective-permute-start | bytes 6152 | tf_op jit(solution)/shard_map/ppermute | solution.py:149
  25.8 1.2 %collective-permute-start.6 = (f32[4,128]{1,0:T(4,128)S(1)}, f32[4,128]{1,0:T(4,128)S(1)}, u32[]{:S(2)}, u32[]{:S(2)}) collective-permute-start(f32[4,128]{1,0:T(4,128)S(1)} %pad_maximum_fusion.1), channel_id=1, source_target_pairs={{0,24},{4,28},{8,0},{12,4},{16,8},{20,12},{24,16},{28,20},{32,56},... | collective-permute-start | bytes 6152 | tf_op jit(solution)/shard_map/ppermute | solution.py:149
  26.9 0.6 collective-permute-start.7
  27.5 4.2 %collective-permute-done.10 = f32[4,128]{1,0:T(4,128)S(1)} collective-permute-done((f32[4,128]{1,0:T(4,128)S(1)}, f32[4,128]{1,0:T(4,128)S(1)}, u32[]{:S(2)}, u32[]{:S(2)}) %collective-permute-start.10) | collective-permute-done | bytes 2080 | tf_op jit(solution)/shard_map/ppermute | solution.py:149
  31.6 0.5 collective-permute-start.8
  32.1 0.0 collective-permute-done.4
  32.1 2.3 %collective-permute-start.9 = (f32[4,128]{1,0:T(4,128)S(1)}, f32[4,128]{1,0:T(4,128)S(1)}, u32[]{:S(2)}, u32[]{:S(2)}) collective-permute-start(f32[4,128]{1,0:T(4,128)S(1)} %pad_maximum_fusion.1), channel_id=1, source_target_pairs={{0,48},{4,52},{8,56},{12,60},{16,32},{20,36},{24,40},{28,44},{32,1... | collective-permute-start | bytes 6152 | tf_op jit(solution)/shard_map/ppermute | solution.py:149
  34.4 0.0 copy-done.5
  34.5 1.6 %filter_spectra.1.filt = f32[8,2,256,128]{3,2,1,0:T(8,128)S(1)} custom-call(s32[1]{0:T(128)} %bitcast.where_ref, bf16[1,2048,2048]{2,1,0:T(8,128)(2,1)} %taps_ref.1, bf16[512,256]{1,0:T(8,128)(2,1)} %constant.84.clone.enter.enter_hbm), custom_call_target="tpu_custom_call" | custom-call | tf_op jit(solution)/shard_map/filter_spectra/pallas_call | solution.py:222
  36.1 0.0 copy-start.4
  36.1 2.6 %early.1.known_ref = f32[16,256]{1,0:T(8,128)S(1)} custom-call(f32[8,128]{1,0:T(8,128)S(1)} %add_add_fusion.sums_ref, bf16[1,128,2048]{2,1,0:T(8,128)(2,1)} %saved_ref.5, bf16[1,128,2048]{2,1,0:T(8,128)(2,1)} %sconv_ref.5, bf16[1,128,2048]{2,1,0:T(8,128)(2,1)} %cot_ref.5), custom_call_target="tpu_custom_call" | custom-call | tf_op jit(solution)/shard_map/early/pallas_call | solution.py:183
  38.7 0.0 collective-permute-done.5
  38.7 0.0 collective-permute-done.6
  38.7 0.0 collective-permute-done.7
  38.8 0.0 collective-permute-done.8
  38.8 0.0 collective-permute-done.9
  38.8 0.1 concatenate.11
  38.9 0.0 all-to-all-done.raw_hbm
  38.9 0.0 copy-done.4
  38.9 7.9 %convolve.1 = bf16[16,152,256]{2,1,0:T(8,128)(2,1)} custom-call(s32[1]{0:T(128)} %bitcast.where_ref, s32[16]{0:T(128)S(1)} %copy-done.4, s32[16]{0:T(128)S(1)} %fusion.4.gathered_ref, f32[32,128]{1,0:T(8,128)S(1)} %add_rsqrt_fusion.inv_ref, f32[16,256]{1,0:T(8,128)S(1)} %early.1.known_ref, f32[1,7,2048]{2,1,0:T(8,128)S(1)} %copy.13.params_ref, ...), custom_call_target="tpu_custom_call" | custom-call | tf_op jit(solution)/shard_map/convolve/pallas_call | solution.py:385
  46.8 0.0 copy-start
  46.8 0.0 copy-start.1
  46.8 0.0 copy-start.2
  46.8 0.0 copy-start.3
  46.8 4.5 %all-to-all-start.1 = ((bf16[16,152,256]{2,1,0:T(8,128)(2,1)}), bf16[16,152,256]{2,1,0:T(8,128)(2,1)S(1)}, u32[]{:S(2)}, u32[]{:S(2)}) async-start(bf16[16,152,256]{2,1,0:T(8,128)(2,1)} %convolve.1), calls=%async_computation.1 | async-start | bytes 2490368 | tf_op jit(solution)/shard_map/all_to_all | solution.py:644
  51.4 0.0 copy-done
  51.4 1.3 %collective-permute-start.15 = (bf16[1,128,2048]{2,1,0:T(8,128)(2,1)S(1)}, bf16[1,128,2048]{2,1,0:T(8,128)(2,1)}, u32[]{:S(2)}, u32[]{:S(2)}) collective-permute-start(bf16[1,128,2048]{2,1,0:T(8,128)(2,1)S(1)} %copy-done), channel_id=1, source_target_pairs={{64,0},{65,1},{66,2},{67,3},{68,4},{69,5},{70,6},{71,7},{72,8},{73... | collective-permute-start | bytes 1572872 | tf_op jit(solution)/shard_map/ppermute | solution.py:640
  52.7 17.4 %all-to-all-done.1.back_ref = bf16[16,152,256]{2,1,0:T(8,128)(2,1)S(1)} async-done(((bf16[16,152,256]{2,1,0:T(8,128)(2,1)}), bf16[16,152,256]{2,1,0:T(8,128)(2,1)S(1)}, u32[]{:S(2)}, u32[]{:S(2)}) %all-to-all-start.1) | async-done | bytes 1245216 | tf_op jit(solution)/shard_map/all_to_all | solution.py:644
  70.1 0.0 copy-done.1
  70.1 0.0 copy-done.2
  70.1 0.0 copy-done.3
  70.1 1.5 %leave.1 = (bf16[1,128,2048]{2,1,0:T(8,128)(2,1)S(1)}, f32[8,128]{1,0:T(8,128)S(1)}) custom-call(s32[1]{0:T(128)} %bitcast.1.pipe_ref, f32[32,128]{1,0:T(8,128)S(1)} %add_rsqrt_fusion.inv_ref, bf16[16,152,256]{2,1,0:T(8,128)(2,1)S(1)} %all-to-all-done.1.back_ref, bf16[1,128,2048]{2,1,0:T(8,128)(2,1)S(1)} %copy-done.2, bf16[1,128,2048]{2,1,0:T(8,128)(2,1)S(1)} %copy-done, ...), custom_call_target="tpu_custom_call" | custom-call | tf_op jit(solution)/shard_map/leave/pallas_call | solution.py:472
  71.6 3.1 %collective-permute-start.16 = (bf16[1,128,2048]{2,1,0:T(8,128)(2,1)S(1)}, bf16[1,128,2048]{2,1,0:T(8,128)(2,1)S(1)}, u32[]{:S(2)}, u32[]{:S(2)}) collective-permute-start(bf16[1,128,2048]{2,1,0:T(8,128)(2,1)S(1)} %get-tuple-element.18), channel_id=1, source_target_pairs={{0,64},{64,0},{1,65},{65,1},{2,66},{66,2},{3,67},{67,3},{4,68},{68... | collective-permute-start | bytes 1572872 | tf_op jit(solution)/shard_map/ppermute | solution.py:647
  74.6 1.3 %collective-permute-start.11 = (f32[8,128]{1,0:T(8,128)S(1)}, f32[8,128]{1,0:T(8,128)S(1)}, u32[]{:S(2)}, u32[]{:S(2)}) collective-permute-start(f32[8,128]{1,0:T(8,128)S(1)} %get-tuple-element.15), channel_id=1, source_target_pairs={{64,0},{65,1},{66,2},{67,3},{68,4},{69,5},{70,6},{71,7},{72,8},{73... | collective-permute-start | bytes 12296 | tf_op jit(solution)/shard_map/ppermute | solution.py:646
  75.9 15.6 %collective-permute-done.11 = f32[8,128]{1,0:T(8,128)S(1)} collective-permute-done((f32[8,128]{1,0:T(8,128)S(1)}, f32[8,128]{1,0:T(8,128)S(1)}, u32[]{:S(2)}, u32[]{:S(2)}) %collective-permute-start.11) | collective-permute-done | bytes 4128 | tf_op jit(solution)/shard_map/ppermute | solution.py:646
  91.6 2.0 %collective-permute-start.12 = (f32[8,128]{1,0:T(8,128)S(1)}, f32[8,128]{1,0:T(8,128)S(1)}, u32[]{:S(2)}, u32[]{:S(2)}) collective-permute-start(f32[8,128]{1,0:T(8,128)S(1)} %pad_maximum_fusion.s0), channel_id=1, source_target_pairs={{0,1},{1,2},{2,3},{3,0},{4,5},{5,6},{6,7},{7,4},{8,9},{9,10},{10,1... | collective-permute-start | bytes 12296 | tf_op jit(solution)/shard_map/ppermute | solution.py:136
  93.5 3.6 %collective-permute-start.13 = (f32[8,128]{1,0:T(8,128)S(1)}, f32[8,128]{1,0:T(8,128)S(1)}, u32[]{:S(2)}, u32[]{:S(2)}) collective-permute-start(f32[8,128]{1,0:T(8,128)S(1)} %pad_maximum_fusion.s0), channel_id=1, source_target_pairs={{0,2},{1,3},{2,0},{3,1},{4,6},{5,7},{6,4},{7,5},{8,10},{9,11},{10,... | collective-permute-start | bytes 12296 | tf_op jit(solution)/shard_map/ppermute | solution.py:136
  97.1 1.0 collective-permute-start.14
  98.1 1.9 %finish_forward.1 = (bf16[1,128,2048]{2,1,0:T(8,128)(2,1)}, f32[1,7,2048]{2,1,0:T(8,128)S(1)}) custom-call(f32[32,128]{1,0:T(8,128)S(1)} %add_rsqrt_fusion.inv_ref, bf16[16,152,256]{2,1,0:T(8,128)(2,1)S(1)} %all-to-all-done.1.back_ref, bf16[1,128,2048]{2,1,0:T(8,128)(2,1)S(1)} %copy-done.2, f32[1,7,2048]{2,1,0:T(8,128)S(1)} %copy.13.params_ref), custom_call_target="tpu_custom_call" | custom-call | tf_op jit(solution)/shard_map/finish_forward/pallas_call | solution.py:537
  100.1 0.7 copy.17
  100.7 0.0 collective-permute-done.15.peer_ref
  100.7 0.0 collective-permute-done.12.s1
  100.7 0.0 collective-permute-done.13.s2
  100.7 0.0 collective-permute-done.14.s3
  100.8 3.8 %finish_backward.1 = (bf16[1,128,2048]{2,1,0:T(8,128)(2,1)}, f32[128,2048]{1,0:T(8,128)S(1)}) custom-call(f32[8,128]{1,0:T(8,128)S(1)} %pad_maximum_fusion.s0, f32[8,128]{1,0:T(8,128)S(1)} %collective-permute-done.12.s1, f32[8,128]{1,0:T(8,128)S(1)} %collective-permute-done.13.s2, f32[8,128]{1,0:T(8,128)S(1)} %collective-permute-done.14.s3, ...), custom_call_target="tpu_custom_call" | custom-call | tf_op jit(solution)/shard_map/finish_backward/pallas_call | solution.py:588
  104.6 0.0 collective-permute-done.16.value_ref
  104.6 1.5 %received.1 = bf16[1,128,2048]{2,1,0:T(8,128)(2,1)} custom-call(bf16[1,128,2048]{2,1,0:T(8,128)(2,1)S(1)} %collective-permute-done.16.value_ref, f32[128,2048]{1,0:T(8,128)S(1)} %get-tuple-element.19.term_ref), custom_call_target="tpu_custom_call" | custom-call | tf_op jit(solution)/shard_map/received/pallas_call | solution.py:618
  (9 shorter events, 0.1 us)
Async XLA Ops:
  3.3 31.1 %copy-start.5 = (f32[1,7,2048]{2,0,1:T(1,128)S(1)}, f32[1,7,2048]{2,0,1:T(1,128)}, u32[]{:S(2)}) copy-start(f32[1,7,2048]{2,0,1:T(1,128)} %param.14) | copy-start | bytes 172036
  3.3 35.5 %all-to-all-start = ((bf16[16,384,128]{2,1,0:T(8,128)(2,1)}), bf16[16,384,128]{2,1,0:T(8,128)(2,1)}, u32[]{:S(2)}, u32[]{:S(2)}) async-start(bf16[16,384,128]{2,1,0:T(8,128)(2,1)} %get-tuple-element.13), calls=%async_computation | async-start | bytes 3145728 | tf_op jit(solution)/shard_map/all_to_all | solution.py:633
  9.1 6.6 %collective-permute-start = (f32[8,128]{1,0:T(8,128)S(1)}, f32[8,128]{1,0:T(8,128)S(1)}, u32[]{:S(2)}, u32[]{:S(2)}) collective-permute-start(f32[8,128]{1,0:T(8,128)S(1)} %get-tuple-element.12), channel_id=1, source_target_pairs={{0,1},{1,2},{2,3},{3,0},{4,5},{5,6},{6,7},{7,4},{8,9},{9,10},{10,1... | collective-permute-start | bytes 12296 | tf_op jit(solution)/shard_map/ppermute | solution.py:136
  11.1 5.2 %collective-permute-start.1 = (f32[8,128]{1,0:T(8,128)S(1)}, f32[8,128]{1,0:T(8,128)S(1)}, u32[]{:S(2)}, u32[]{:S(2)}) collective-permute-start(f32[8,128]{1,0:T(8,128)S(1)} %get-tuple-element.12), channel_id=1, source_target_pairs={{0,2},{1,3},{2,0},{3,1},{4,6},{5,7},{6,4},{7,5},{8,10},{9,11},{10,... | collective-permute-start | bytes 12296 | tf_op jit(solution)/shard_map/ppermute | solution.py:136
  14.7 3.6 %collective-permute-start.2 = (f32[8,128]{1,0:T(8,128)S(1)}, f32[8,128]{1,0:T(8,128)S(1)}, u32[]{:S(2)}, u32[]{:S(2)}) collective-permute-start(f32[8,128]{1,0:T(8,128)S(1)} %get-tuple-element.12), channel_id=1, source_target_pairs={{0,3},{1,0},{2,1},{3,2},{4,7},{5,4},{6,5},{7,6},{8,11},{9,8},{10,9... | collective-permute-start | bytes 12296 | tf_op jit(solution)/shard_map/ppermute | solution.py:136
  18.3 1.2 %collective-permute-start.3 = (f32[2,128]{1,0:T(2,128)S(1)}, f32[2,128]{1,0:T(2,128)S(1)}, u32[]{:S(2)}, u32[]{:S(2)}) collective-permute-start(f32[2,128]{1,0:T(2,128)S(1)} %slice.12), channel_id=1, source_target_pairs={{0,4},{4,0},{8,12},{12,8},{16,20},{20,16},{24,28},{28,24},{32,36},... | collective-permute-start | bytes 3080 | tf_op jit(solution)/shard_map/ppermute | solution.py:143
  19.5 12.1 %collective-permute-start.10 = (f32[4,128]{1,0:T(4,128)S(1)}, f32[4,128]{1,0:T(4,128)S(1)}, u32[]{:S(2)}, u32[]{:S(2)}) collective-permute-start(f32[4,128]{1,0:T(4,128)S(1)} %pad_maximum_fusion.1), channel_id=1, source_target_pairs={{0,56},{4,60},{8,32},{12,36},{16,40},{20,44},{24,48},{28,52},{32,2... | collective-permute-start | bytes 6152 | tf_op jit(solution)/shard_map/ppermute | solution.py:149
  23.4 8.7 %collective-permute-start.4 = (f32[4,128]{1,0:T(4,128)S(1)}, f32[4,128]{1,0:T(4,128)S(1)}, u32[]{:S(2)}, u32[]{:S(2)}) collective-permute-start(f32[4,128]{1,0:T(4,128)S(1)} %pad_maximum_fusion.1), channel_id=1, source_target_pairs={{0,8},{4,12},{8,16},{12,20},{16,24},{20,28},{24,0},{28,4},{32,40},... | collective-permute-start | bytes 6152 | tf_op jit(solution)/shard_map/ppermute | solution.py:149
  23.4 15.3 %collective-permute-start.5 = (f32[4,128]{1,0:T(4,128)S(1)}, f32[4,128]{1,0:T(4,128)S(1)}, u32[]{:S(2)}, u32[]{:S(2)}) collective-permute-start(f32[4,128]{1,0:T(4,128)S(1)} %pad_maximum_fusion.1), channel_id=1, source_target_pairs={{0,16},{4,20},{8,24},{12,28},{16,0},{20,4},{24,8},{28,12},{32,48},... | collective-permute-start | bytes 6152 | tf_op jit(solution)/shard_map/ppermute | solution.py:149
  25.8 13.0 %collective-permute-start.6 = (f32[4,128]{1,0:T(4,128)S(1)}, f32[4,128]{1,0:T(4,128)S(1)}, u32[]{:S(2)}, u32[]{:S(2)}) collective-permute-start(f32[4,128]{1,0:T(4,128)S(1)} %pad_maximum_fusion.1), channel_id=1, source_target_pairs={{0,24},{4,28},{8,0},{12,4},{16,8},{20,12},{24,16},{28,20},{32,56},... | collective-permute-start | bytes 6152 | tf_op jit(solution)/shard_map/ppermute | solution.py:149
  26.9 11.8 %collective-permute-start.7 = (f32[4,128]{1,0:T(4,128)S(1)}, f32[4,128]{1,0:T(4,128)S(1)}, u32[]{:S(2)}, u32[]{:S(2)}) collective-permute-start(f32[4,128]{1,0:T(4,128)S(1)} %pad_maximum_fusion.1), channel_id=1, source_target_pairs={{0,32},{4,36},{8,40},{12,44},{16,48},{20,52},{24,56},{28,60},{32,0... | collective-permute-start | bytes 6152 | tf_op jit(solution)/shard_map/ppermute | solution.py:149
  31.6 7.1 %collective-permute-start.8 = (f32[4,128]{1,0:T(4,128)S(1)}, f32[4,128]{1,0:T(4,128)S(1)}, u32[]{:S(2)}, u32[]{:S(2)}) collective-permute-start(f32[4,128]{1,0:T(4,128)S(1)} %pad_maximum_fusion.1), channel_id=1, source_target_pairs={{0,40},{4,44},{8,48},{12,52},{16,56},{20,60},{24,32},{28,36},{32,8... | collective-permute-start | bytes 6152 | tf_op jit(solution)/shard_map/ppermute | solution.py:149
  32.1 6.7 %collective-permute-start.9 = (f32[4,128]{1,0:T(4,128)S(1)}, f32[4,128]{1,0:T(4,128)S(1)}, u32[]{:S(2)}, u32[]{:S(2)}) collective-permute-start(f32[4,128]{1,0:T(4,128)S(1)} %pad_maximum_fusion.1), channel_id=1, source_target_pairs={{0,48},{4,52},{8,56},{12,60},{16,32},{20,36},{24,40},{28,44},{32,1... | collective-permute-start | bytes 6152 | tf_op jit(solution)/shard_map/ppermute | solution.py:149
  36.1 2.8 %copy-start.4 = (s32[16]{0:T(128)S(1)}, s32[16]{0:T(128)}, u32[]{:S(2)}) copy-start(s32[16]{0:T(128)} %order_ref.1) | copy-start | bytes 196
  46.8 4.6 %copy-start = (bf16[1,128,2048]{2,1,0:T(8,128)(2,1)S(1)}, bf16[1,128,2048]{2,1,0:T(8,128)(2,1)}, u32[]{:S(2)}) copy-start(bf16[1,128,2048]{2,1,0:T(8,128)(2,1)} %saved_ref.5) | copy-start | bytes 1572868
  46.8 23.3 %copy-start.1 = (bf16[1,128,2048]{2,1,0:T(8,128)(2,1)S(1)}, bf16[1,128,2048]{2,1,0:T(8,128)(2,1)}, u32[]{:S(2)}) copy-start(bf16[1,128,2048]{2,1,0:T(8,128)(2,1)} %cot_ref.5) | copy-start | bytes 1572868
  46.8 23.2 %copy-start.2 = (bf16[1,128,2048]{2,1,0:T(8,128)(2,1)S(1)}, bf16[1,128,2048]{2,1,0:T(8,128)(2,1)}, u32[]{:S(2)}) copy-start(bf16[1,128,2048]{2,1,0:T(8,128)(2,1)} %fwd_ref.3) | copy-start | bytes 1572868
  46.8 23.2 %copy-start.3 = (bf16[1,128,2048]{2,1,0:T(8,128)(2,1)S(1)}, bf16[1,128,2048]{2,1,0:T(8,128)(2,1)}, u32[]{:S(2)}) copy-start(bf16[1,128,2048]{2,1,0:T(8,128)(2,1)} %sconv_ref.5) | copy-start | bytes 1572868
  46.8 23.2 %all-to-all-start.1 = ((bf16[16,152,256]{2,1,0:T(8,128)(2,1)}), bf16[16,152,256]{2,1,0:T(8,128)(2,1)S(1)}, u32[]{:S(2)}, u32[]{:S(2)}) async-start(bf16[16,152,256]{2,1,0:T(8,128)(2,1)} %convolve.1), calls=%async_computation.1 | async-start | bytes 2490368 | tf_op jit(solution)/shard_map/all_to_all | solution.py:644
  51.4 49.4 %collective-permute-start.15 = (bf16[1,128,2048]{2,1,0:T(8,128)(2,1)S(1)}, bf16[1,128,2048]{2,1,0:T(8,128)(2,1)}, u32[]{:S(2)}, u32[]{:S(2)}) collective-permute-start(bf16[1,128,2048]{2,1,0:T(8,128)(2,1)S(1)} %copy-done), channel_id=1, source_target_pairs={{64,0},{65,1},{66,2},{67,3},{68,4},{69,5},{70,6},{71,7},{72,8},{73... | collective-permute-start | bytes 1572872 | tf_op jit(solution)/shard_map/ppermute | solution.py:640
  71.6 33.0 %collective-permute-start.16 = (bf16[1,128,2048]{2,1,0:T(8,128)(2,1)S(1)}, bf16[1,128,2048]{2,1,0:T(8,128)(2,1)S(1)}, u32[]{:S(2)}, u32[]{:S(2)}) collective-permute-start(bf16[1,128,2048]{2,1,0:T(8,128)(2,1)S(1)} %get-tuple-element.18), channel_id=1, source_target_pairs={{0,64},{64,0},{1,65},{65,1},{2,66},{66,2},{3,67},{67,3},{4,68},{68... | collective-permute-start | bytes 1572872 | tf_op jit(solution)/shard_map/ppermute | solution.py:647
  74.6 16.9 %collective-permute-start.11 = (f32[8,128]{1,0:T(8,128)S(1)}, f32[8,128]{1,0:T(8,128)S(1)}, u32[]{:S(2)}, u32[]{:S(2)}) collective-permute-start(f32[8,128]{1,0:T(8,128)S(1)} %get-tuple-element.15), channel_id=1, source_target_pairs={{64,0},{65,1},{66,2},{67,3},{68,4},{69,5},{70,6},{71,7},{72,8},{73... | collective-permute-start | bytes 12296 | tf_op jit(solution)/shard_map/ppermute | solution.py:646
  91.6 9.2 %collective-permute-start.12 = (f32[8,128]{1,0:T(8,128)S(1)}, f32[8,128]{1,0:T(8,128)S(1)}, u32[]{:S(2)}, u32[]{:S(2)}) collective-permute-start(f32[8,128]{1,0:T(8,128)S(1)} %pad_maximum_fusion.s0), channel_id=1, source_target_pairs={{0,1},{1,2},{2,3},{3,0},{4,5},{5,6},{6,7},{7,4},{8,9},{9,10},{10,1... | collective-permute-start | bytes 12296 | tf_op jit(solution)/shard_map/ppermute | solution.py:136
  93.5 7.2 %collective-permute-start.13 = (f32[8,128]{1,0:T(8,128)S(1)}, f32[8,128]{1,0:T(8,128)S(1)}, u32[]{:S(2)}, u32[]{:S(2)}) collective-permute-start(f32[8,128]{1,0:T(8,128)S(1)} %pad_maximum_fusion.s0), channel_id=1, source_target_pairs={{0,2},{1,3},{2,0},{3,1},{4,6},{5,7},{6,4},{7,5},{8,10},{9,11},{10,... | collective-permute-start | bytes 12296 | tf_op jit(solution)/shard_map/ppermute | solution.py:136
  97.1 3.6 %collective-permute-start.14 = (f32[8,128]{1,0:T(8,128)S(1)}, f32[8,128]{1,0:T(8,128)S(1)}, u32[]{:S(2)}, u32[]{:S(2)}) collective-permute-start(f32[8,128]{1,0:T(8,128)S(1)} %pad_maximum_fusion.s0), channel_id=1, source_target_pairs={{0,3},{1,0},{2,1},{3,2},{4,7},{5,4},{6,5},{7,6},{8,11},{9,8},{10,9... | collective-permute-start | bytes 12296 | tf_op jit(solution)/shard_map/ppermute | solution.py:136

commit v5 on v4

--- a/solution.py
+++ b/solution.py
@@ -143,9 +143,9 @@
     return lax.ppermute(rows, "seq", [(low, low ^ flip) for low in range(count)])
 
 
-def from_chip(rows, side, back):
+def round_ring(rows, apart):
     count = lax.axis_size("seq")
-    place = lambda low: (low // 8 ^ side) * 8 + (low + 2 * back) % 8
+    place = lambda low: low // 8 * 8 + (low + 2 * apart) % 8
     return lax.ppermute(rows, "seq", [(low, place(low)) for low in range(count)])
 
 
@@ -424,15 +424,17 @@
 
 
 def leave_kernel(
-    pipe_ref, inv_ref, back_ref, fwd_ref, saved_ref, sconv_ref, cot_ref, params_ref,
-    send_ref, cross_ref, inv, acc,
+    pipe_ref, inv_ref, back_ref, fwd_hbm, saved_ref, sconv_ref, cot_ref, params_ref,
+    send_ref, keep_ref, cross_ref, inv, acc, fwd_ref, fwd_sem,
 ):
     rows, width = fwd_ref.shape[1:]
+    fwd_copy = pltpu.make_async_copy(fwd_hbm, fwd_ref, fwd_sem)
+    fwd_copy.start()
     inv[...] = rows_to_columns(inv_ref[0:8, :])
     inv_fwd = inv[:, 0:1]
     inv_saved = inv[:, 1:2]
 
-    def backward(send):
+    def both(layer_ref, partial_ref):
         cross = jnp.zeros((rows, LANES), jnp.float32)
         for group in range(width // LANES):
             at = pl.ds(group * LANES, LANES)
@@ -446,23 +448,23 @@
                 inv_saved,
             )
             cross = cross + term
-            if send:
-                send_ref[0, :, at] = partial.astype(jnp.bfloat16)
+            partial_ref[0, :, at] = partial.astype(jnp.bfloat16)
         acc[...] = cross
-
-    @pl.when(pipe_ref[0] == 0)
-    def _():
+        fwd_copy.wait()
         for group in range(width // LANES):
             at = pl.ds(group * LANES, LANES)
             inputs = fwd_ref[0, :, at].astype(jnp.float32)
             conv = back_ref[group, :rows, :LANES].astype(jnp.float32)
             layer = forward_terms(at, inputs, conv, params_ref, inv_fwd)
-            send_ref[0, :, at] = layer.astype(jnp.bfloat16)
-        backward(False)
+            layer_ref[0, :, at] = layer.astype(jnp.bfloat16)
+
+    @pl.when(pipe_ref[0] == 0)
+    def _():
+        both(send_ref, keep_ref)
 
     @pl.when(pipe_ref[0] != 0)
     def _():
-        backward(True)
+        both(keep_ref, send_ref)
 
     cross = columns_to_rows([jnp.sum(acc[...], axis=1, keepdims=True)])
     cross_ref[...] = cross * (inv_ref[1:2, :] * inv_ref[1:2, :] / D)
@@ -473,45 +475,59 @@
         leave_kernel,
         out_shape=(
             pltpu.VMEM(fwd_in.shape, jnp.bfloat16),
+            pltpu.VMEM(fwd_in.shape, jnp.bfloat16),
             pltpu.VMEM((8, 128), jnp.float32),
         ),
-        in_specs=[SMEM] + [VMEM] * 7,
-        out_specs=(VMEM, VMEM),
-        scratch_shapes=[pltpu.VMEM((fwd_in.shape[1], 128), jnp.float32)] * 2,
+        in_specs=[SMEM] + [VMEM] * 2 + [HBM] + [VMEM] * 4,
+        out_specs=(VMEM, VMEM, VMEM),
+        scratch_shapes=[pltpu.VMEM((fwd_in.shape[1], 128), jnp.float32)] * 2
+        + [pltpu.VMEM(fwd_in.shape, jnp.bfloat16), pltpu.SemaphoreType.DMA],
         name="leave",
         compiler_params=pltpu.CompilerParams(vmem_limit_bytes=24 << 20),
     )(
-        pipe, inv, in_vmem(back),
-        *[in_vmem(a) for a in (fwd_in, saved_in, saved_conv, grad_out)], mix_params,
-    )
-
-
-def forward_kernel(inv_ref, back_ref, fwd_ref, params_ref, layer_ref, grads_ref, known, inv):
+        pipe, inv, in_vmem(back), in_hbm(fwd_in),
+        *[in_vmem(a) for a in (saved_in, saved_conv, grad_out)], mix_params,
+    )
+
+
+def finish_kernel(
+    pipe_ref, s0, s1, s2, s3, back_ref, send_ref, keep_ref, saved_ref, params_ref, peer_ref,
+    layer_hbm, grad_ref, grads_ref, term_ref, scale, known, layer_sem,
+):
     step = pl.program_id(0)
-    rows = fwd_ref.shape[1]
+    first = pipe_ref[0] == 0
+    rows, wide = grad_ref.shape[1:]
+    sent = pltpu.make_async_copy(send_ref, layer_hbm, layer_sem)
+    kept = pltpu.make_async_copy(keep_ref, layer_hbm, layer_sem)
 
     @pl.when(step == 0)
     def _():
-        inv[...] = rows_to_columns(inv_ref[0:8, :])
+        @pl.when(first)
+        def _():
+            sent.start()
+
+        @pl.when(jnp.logical_not(first))
+        def _():
+            kept.start()
+
+        scale[...] = rows_to_columns(s0[...] + s1[...] + s2[...] + s3[...])
         total = back_ref[0, rows : rows + 16, :].astype(jnp.float32)
         for index in range(1, back_ref.shape[0]):
             total = total + back_ref[index, rows : rows + 16, :].astype(jnp.float32)
         for row in range(16):
             known[row] = total[row : row + 1, :]
 
-    wide = layer_ref.shape[2]
     groups = wide // LANES
     for group in range(groups):
         own = pl.ds(group * LANES, LANES)
         at = pl.ds(pl.multiple_of(step * wide + group * LANES, LANES), LANES)
-        block = step * groups + group
-        conv = back_ref[block, :rows, :LANES].astype(jnp.float32)
-        inputs = fwd_ref[0, :, at].astype(jnp.float32)
-        layer = forward_terms(own, inputs, conv, params_ref, inv[:, 0:1])
-        layer_ref[0, :, own] = layer.astype(jnp.bfloat16)
+        partial = jnp.where(first, keep_ref[0, :, at], send_ref[0, :, at]).astype(jnp.float32)
+        saved = saved_ref[0, :, at].astype(jnp.float32)
+        grad_ref[0, :, own] = (partial - saved * scale[:, 0:1]).astype(jnp.bfloat16)
+        term_ref[:, at] = peer_ref[0, :, own].astype(jnp.float32) * scale[:, 1:2]
 
         p = [params_ref[0, row : row + 1, own] for row in range(7)]
-        extra = back_ref[block, rows + 16 :, :].astype(jnp.float32)
+        extra = back_ref[step * groups + group, rows + 16 :, :].astype(jnp.float32)
         extra = extra[:, :LANES] + extra[:, LANES:]
         m0, m1, m2 = extra[0:1], extra[1:2], extra[2:3]
         row = step * (groups // 2) + group // 2
@@ -530,76 +546,42 @@
         ]
         grads_ref[0, :, own] = jnp.concatenate(grads, axis=0)
 
-
-def finish_forward(inv, back, fwd_in, mix_params):
-    rows, width = fwd_in.shape[1:]
-    wide = 512
-    return pl.pallas_call(
-        forward_kernel,
-        out_shape=(
-            jax.ShapeDtypeStruct(fwd_in.shape, jnp.bfloat16),
-            jax.ShapeDtypeStruct(mix_params.shape, jnp.float32),
-        ),
-        grid=(width // wide,),
-        in_specs=[VMEM] * 3 + [lane_spec(7, wide)],
-        out_specs=(lane_spec(rows, wide), lane_spec(7, wide)),
-        scratch_shapes=[
-            pltpu.VMEM((16, 1, 2 * LANES), jnp.float32),
-            pltpu.VMEM((rows, 128), jnp.float32),
-        ],
-        name="finish_forward",
-        compiler_params=pltpu.CompilerParams(vmem_limit_bytes=16 << 20),
-    )(inv, in_vmem(back), in_vmem(fwd_in), mix_params)
-
-
-def backward_kernel(
-    s0, s1, s2, s3, inv_ref, back_ref, saved_ref, sconv_ref, cot_ref, params_ref, peer_ref,
-    grad_ref, term_ref, scale, inv,
-):
-    step = pl.program_id(0)
-
-    @pl.when(step == 0)
+    @pl.when(step == pl.num_programs(0) - 1)
     def _():
-        scale[...] = rows_to_columns(s0[...] + s1[...] + s2[...] + s3[...])
-        inv[...] = rows_to_columns(inv_ref[0:8, :])
-
-    rows, wide = grad_ref.shape[1:]
-    for group in range(wide // LANES):
-        own = pl.ds(group * LANES, LANES)
-        at = pl.ds(pl.multiple_of(step * wide + group * LANES, LANES), LANES)
-        saved = saved_ref[0, :, at].astype(jnp.float32)
-        partial, _ = backward_terms(
-            own,
-            saved,
-            sconv_ref[0, :, at].astype(jnp.float32),
-            cot_ref[0, :, at].astype(jnp.float32),
-            back_ref[step * (wide // LANES) + group, :rows, LANES:].astype(jnp.float32),
-            params_ref,
-            inv[:, 1:2],
-        )
-        grad_ref[0, :, own] = (partial - saved * scale[:, 0:1]).astype(jnp.bfloat16)
-        term_ref[:, at] = peer_ref[0, :, own].astype(jnp.float32) * scale[:, 1:2]
-
-
-def finish_backward(scales, inv, back, saved_in, saved_conv, grad_out, mix_params, peer_saved):
+        @pl.when(first)
+        def _():
+            sent.wait()
+
+        @pl.when(jnp.logical_not(first))
+        def _():
+            kept.wait()
+
+
+def finish(pipe, scales, back, send, keep, saved_in, mix_params, peer_saved):
     rows, width = saved_in.shape[1:]
     wide = 512
-    spec = lane_spec(rows, wide)
+    spec, params = lane_spec(rows, wide), lane_spec(7, wide)
     return pl.pallas_call(
-        backward_kernel,
+        finish_kernel,
         out_shape=(
+            pltpu.HBM(saved_in.shape, jnp.bfloat16),
             jax.ShapeDtypeStruct(saved_in.shape, jnp.bfloat16),
+            jax.ShapeDtypeStruct(mix_params.shape, jnp.float32),
             pltpu.VMEM((rows, width), jnp.float32),
         ),
         grid=(width // wide,),
-        in_specs=[VMEM] * 9 + [lane_spec(7, wide), spec],
-        out_specs=(spec, VMEM),
-        scratch_shapes=[pltpu.VMEM((rows, 128), jnp.float32)] * 2,
-        name="finish_backward",
+        in_specs=[SMEM] + [VMEM] * 8 + [params, spec],
+        out_specs=(HBM, spec, params, VMEM),
+        scratch_shapes=[
+            pltpu.VMEM((rows, 128), jnp.float32),
+            pltpu.VMEM((16, 1, 2 * LANES), jnp.float32),
+            pltpu.SemaphoreType.DMA,
+        ],
+        name="finish",
         compiler_params=pltpu.CompilerParams(vmem_limit_bytes=16 << 20),
     )(
-        *scales, inv, in_vmem(back),
-        *[in_vmem(a) for a in (saved_in, saved_conv, grad_out)], mix_params, in_hbm(peer_saved),
+        pipe, *scales, in_vmem(back), in_vmem(send), in_vmem(keep), in_vmem(saved_in),
+        mix_params, in_hbm(peer_saved),
     )
 
 
@@ -634,21 +616,21 @@
     own_sums = sum(over_chan(sums))
     sums = own_sums[:2]
     sums = jnp.concatenate([sums, across(sums, 1)], axis=0)
-    chips = [(side, back) for side in range(2) for back in range(4)]
-    far = [from_chip(sums, *chip) if any(chip) else sums for chip in chips]
-    inv = lax.rsqrt(jnp.concatenate(far, axis=0) / D + EPSILON)
+    sums = jnp.concatenate([sums] + [round_ring(sums, apart) for apart in (1, 2, 3)], axis=0)
+    inv = lax.rsqrt(jnp.concatenate([sums, across(sums, 8)], axis=0) / D + EPSILON)
     peer_saved = lax.ppermute(saved_in, "pipe", [(1, 0)])
     spectra = filter_spectra(where, filters, tables)
     known = early(own_sums, saved_in, saved_conv, grad_out)
     back = convolve(where, span_order, gather_order(), raw, inv, known, mix_params, spectra, tables)
     back = lax.all_to_all(back, "seq", 0, 0)
-    outgoing, cross = leave(pipe, inv, back, fwd_in, saved_in, saved_conv, grad_out, mix_params)
+    outgoing, keep, cross = leave(
+        pipe, inv, back, fwd_in, saved_in, saved_conv, grad_out, mix_params
+    )
     peer_cross = lax.ppermute(cross, "pipe", [(1, 0)])
     incoming = lax.ppermute(outgoing, "pipe", [(0, 1), (1, 0)])
     scales = over_chan(jnp.concatenate([cross[:1], peer_cross[:1], cross[:6]], axis=0))
-    layer_out, param_grad = finish_forward(inv, back, fwd_in, mix_params)
-    input_grad, term = finish_backward(
-        scales, inv, back, saved_in, saved_conv, grad_out, mix_params, peer_saved
+    layer_out, input_grad, param_grad, term = finish(
+        pipe, scales, back, outgoing, keep, saved_in, mix_params, peer_saved
     )
     received = finish_received(incoming, term)
     return (layer_out, input_grad, param_grad, received)

time: 107 us -> 104 us (0.972)
  starting transfers between devices: 39.9 us -> 37.1 us
  waiting for transfers between devices: 40.9 us -> 42.9 us
  Pallas kernels: 23.6 us -> 21.7 us
    ppermute x7 -> x3, starting transfers between devices: 10.7 us -> 5.95 us  [round_ring(): lax.ppermute(rows, 'seq', [(low, place(low)) for low in range(count)])]
    ppermute x6, waiting for transfers between devices: 2.61 us -> 6.09 us  [over_chan(): lax.ppermute(rows, 'chan', [(low, (low + apart) % count) for low in range...]
    pallas_call x2 -> x1, Pallas kernels: 5.75 us -> 3.7 us  [finish(): pl.pallas_call(finish_kernel, out_shape=(pltpu.HBM(saved_in.shape, jnp.bf...]
    ppermute x1 -> x2, starting transfers between devices: 0.01 us -> 1.66 us  [across(): lax.ppermute(rows, 'seq', [(low, low ^ flip) for low in range(count)])]
    ppermute x7 -> x3, waiting for transfers between devices: 4.17 us -> 3.13 us  [round_ring(): lax.ppermute(rows, 'seq', [(low, place(low)) for low in range(count)])]
  transfers between devices with their start and end apart: 19 -> 16, of which waited for: 6 -> 9; matrix products, arithmetic and copies ran while one was open for 1% -> 1% of each run, Pallas kernels for 11% -> 9%
where the time goes in v5:
time: 104 us; the launch traced here: 103 us
  waiting for transfers between devices  42.9 us (41%)
  starting transfers between devices  37.1 us (36%)
  Pallas kernels  21.7 us (21%)
    all_to_all x1, waiting for transfers between devices, per_device(): back = lax.all_to_all(back, 'seq', 0, 0)  17.4 us
    ppermute x1, waiting for transfers between devices, per_device(): peer_cross = lax.ppermute(cross, 'pipe', [(1, 0)])  15.2 us
    ppermute x6, starting transfers between devices, over_chan(): lax.ppermute(rows, 'chan', [(low, (low + apart) % count) for low in range...  12.6 us
    pallas_call x1, Pallas kernels, convolve(): pl.pallas_call(conv_kernel, out_shape=pltpu.HBM((stored, rows + 24, 2 * L...  7.9 us
    ppermute x6, waiting for transfers between devices, over_chan(): lax.ppermute(rows, 'chan', [(low, (low + apart) % count) for low in range...  6.09 us
    ppermute x3, starting transfers between devices, round_ring(): lax.ppermute(rows, 'seq', [(low, place(low)) for low in range(count)])  5.95 us
    all_to_all x1, starting transfers between devices, per_device(): raw = lax.all_to_all(raw, 'seq', 0, 0)  5.8 us
    all_to_all x1, starting transfers between devices, per_device(): back = lax.all_to_all(back, 'seq', 0, 0)  5.18 us
  transfers between devices with their start and end apart: 16, of which 9 were waited for; matrix products, arithmetic and copies ran while one was open for 1% of the time, Pallas kernels for 9%

profile of v5, /device:TPU:0, one launch (start us, length us, event | category | flops | bytes accessed | tf_op | source)
XLA Modules:
  0.0 103.4 jit_solution(6224502670614083954)
XLA Ops:
  0.6 2.7 %pack.1 = (bf16[16,384,128]{2,1,0:T(8,128)(2,1)}, f32[8,128]{1,0:T(8,128)S(1)}) custom-call(bf16[1,128,2048]{2,1,0:T(8,128)(2,1)} %fwd_hbm.3, bf16[1,128,2048]{2,1,0:T(8,128)(2,1)} %saved_ref.5, bf16[1,128,2048]{2,1,0:T(8,128)(2,1)} %cot_ref.3), custom_call_target="tpu_custom_call" | custom-call | tf_op jit(solution)/shard_map/pack/pallas_call | solution.py:113
  3.3 0.0 copy-start.5
  3.3 5.8 %all-to-all-start = ((bf16[16,384,128]{2,1,0:T(8,128)(2,1)}), bf16[16,384,128]{2,1,0:T(8,128)(2,1)}, u32[]{:S(2)}, u32[]{:S(2)}) async-start(bf16[16,384,128]{2,1,0:T(8,128)(2,1)} %get-tuple-element.14), calls=%async_computation | async-start | bytes 3145728 | tf_op jit(solution)/shard_map/all_to_all | solution.py:615
  9.2 2.0 %collective-permute-start = (f32[8,128]{1,0:T(8,128)S(1)}, f32[8,128]{1,0:T(8,128)S(1)}, u32[]{:S(2)}, u32[]{:S(2)}) collective-permute-start(f32[8,128]{1,0:T(8,128)S(1)} %get-tuple-element.13), channel_id=1, source_target_pairs={{0,1},{1,2},{2,3},{3,0},{4,5},{5,6},{6,7},{7,4},{8,9},{9,10},{10,1... | collective-permute-start | bytes 12296 | tf_op jit(solution)/shard_map/ppermute | solution.py:136
  11.1 3.6 %collective-permute-start.1 = (f32[8,128]{1,0:T(8,128)S(1)}, f32[8,128]{1,0:T(8,128)S(1)}, u32[]{:S(2)}, u32[]{:S(2)}) collective-permute-start(f32[8,128]{1,0:T(8,128)S(1)} %get-tuple-element.13), channel_id=1, source_target_pairs={{0,2},{1,3},{2,0},{3,1},{4,6},{5,7},{6,4},{7,5},{8,10},{9,11},{10,... | collective-permute-start | bytes 12296 | tf_op jit(solution)/shard_map/ppermute | solution.py:136
  14.7 1.0 collective-permute-start.2
  15.7 0.0 collective-permute-done
  15.7 0.6 collective-permute-done.1
  16.4 2.0 %collective-permute-done.2 = f32[8,128]{1,0:T(8,128)S(1)} collective-permute-done((f32[8,128]{1,0:T(8,128)S(1)}, f32[8,128]{1,0:T(8,128)S(1)}, u32[]{:S(2)}, u32[]{:S(2)}) %collective-permute-start.2) | collective-permute-done | bytes 4128 | tf_op jit(solution)/shard_map/ppermute | solution.py:136
  18.3 0.0 collective-permute-start.3
  18.4 1.2 %collective-permute-done.3 = f32[2,128]{1,0:T(2,128)S(1)} collective-permute-done((f32[2,128]{1,0:T(2,128)S(1)}, f32[2,128]{1,0:T(2,128)S(1)}, u32[]{:S(2)}, u32[]{:S(2)}) %collective-permute-start.3) | collective-permute-done | bytes 1056 | tf_op jit(solution)/shard_map/ppermute | solution.py:143
  19.5 1.8 %collective-permute-start.4 = (f32[4,128]{1,0:T(4,128)S(1)}, f32[4,128]{1,0:T(4,128)S(1)}, u32[]{:S(2)}, u32[]{:S(2)}) collective-permute-start(f32[4,128]{1,0:T(4,128)S(1)} %pad_maximum_fusion.1), channel_id=1, source_target_pairs={{0,8},{4,12},{8,16},{12,20},{16,24},{20,28},{24,0},{28,4},{32,40},... | collective-permute-start | bytes 6152 | tf_op jit(solution)/shard_map/ppermute | solution.py:149
  21.3 2.7 %collective-permute-start.5 = (f32[4,128]{1,0:T(4,128)S(1)}, f32[4,128]{1,0:T(4,128)S(1)}, u32[]{:S(2)}, u32[]{:S(2)}) collective-permute-start(f32[4,128]{1,0:T(4,128)S(1)} %pad_maximum_fusion.1), channel_id=1, source_target_pairs={{0,16},{4,20},{8,24},{12,28},{16,0},{20,4},{24,8},{28,12},{32,48},... | collective-permute-start | bytes 6152 | tf_op jit(solution)/shard_map/ppermute | solution.py:149
  24.0 1.5 %collective-permute-start.6 = (f32[4,128]{1,0:T(4,128)S(1)}, f32[4,128]{1,0:T(4,128)S(1)}, u32[]{:S(2)}, u32[]{:S(2)}) collective-permute-start(f32[4,128]{1,0:T(4,128)S(1)} %pad_maximum_fusion.1), channel_id=1, source_target_pairs={{0,24},{4,28},{8,0},{12,4},{16,8},{20,12},{24,16},{28,20},{32,56},... | collective-permute-start | bytes 6152 | tf_op jit(solution)/shard_map/ppermute | solution.py:149
  25.5 2.8 %collective-permute-done.4 = f32[4,128]{1,0:T(4,128)S(1)} collective-permute-done((f32[4,128]{1,0:T(4,128)S(1)}, f32[4,128]{1,0:T(4,128)S(1)}, u32[]{:S(2)}, u32[]{:S(2)}) %collective-permute-start.4) | collective-permute-done | bytes 2080 | tf_op jit(solution)/shard_map/ppermute | solution.py:149
  28.2 0.4 collective-permute-done.5
  28.6 0.0 collective-permute-done.6
  28.6 1.7 %collective-permute-start.7 = (f32[16,128]{1,0:T(8,128)S(1)}, f32[16,128]{1,0:T(8,128)S(1)}, u32[]{:S(2)}, u32[]{:S(2)}) collective-permute-start(f32[16,128]{1,0:T(8,128)S(1)} %concatenate.15), channel_id=1, source_target_pairs={{0,32},{4,36},{8,40},{12,44},{16,48},{20,52},{24,56},{28,60},{32,0... | collective-permute-start | bytes 24584 | tf_op jit(solution)/shard_map/ppermute | solution.py:143
  30.3 0.0 copy-done.5
  30.4 1.6 %filter_spectra.1.filt = f32[8,2,256,128]{3,2,1,0:T(8,128)S(1)} custom-call(s32[1]{0:T(128)} %bitcast.1.where_ref, bf16[1,2048,2048]{2,1,0:T(8,128)(2,1)} %taps_ref.1, bf16[512,256]{1,0:T(8,128)(2,1)} %constant.84.clone.enter.enter_hbm), custom_call_target="tpu_custom_call" | custom-call | tf_op jit(solution)/shard_map/filter_spectra/pallas_call | solution.py:222
  31.9 0.0 copy-start.3
  31.9 2.6 %early.1.known_ref = f32[16,256]{1,0:T(8,128)S(1)} custom-call(f32[8,128]{1,0:T(8,128)S(1)} %add_add_fusion.sums_ref, bf16[1,128,2048]{2,1,0:T(8,128)(2,1)} %saved_ref.5, bf16[1,128,2048]{2,1,0:T(8,128)(2,1)} %sconv_ref.3, bf16[1,128,2048]{2,1,0:T(8,128)(2,1)} %cot_ref.3), custom_call_target="tpu_custom_call" | custom-call | tf_op jit(solution)/shard_map/early/pallas_call | solution.py:183
  34.6 0.0 collective-permute-done.7
  34.7 0.0 all-to-all-done.raw_hbm
  34.7 0.0 copy-done.3
  34.7 7.9 %convolve.1 = bf16[16,152,256]{2,1,0:T(8,128)(2,1)} custom-call(s32[1]{0:T(128)} %bitcast.1.where_ref, s32[16]{0:T(128)S(1)} %copy-done.3, s32[16]{0:T(128)S(1)} %fusion.4.gathered_ref, f32[32,128]{1,0:T(8,128)S(1)} %add_rsqrt_fusion.inv_ref, f32[16,256]{1,0:T(8,128)S(1)} %early.1.known_ref, f32[1,7,2048]{2,1,0:T(8,128)S(1)} %copy.13.params_ref, ...), custom_call_target="tpu_custom_call" | custom-call | tf_op jit(solution)/shard_map/convolve/pallas_call | solution.py:385
  42.6 0.0 copy-start
  42.6 0.0 copy-start.1
  42.6 0.0 copy-start.2
  42.6 5.2 %all-to-all-start.1 = ((bf16[16,152,256]{2,1,0:T(8,128)(2,1)}), bf16[16,152,256]{2,1,0:T(8,128)(2,1)S(1)}, u32[]{:S(2)}, u32[]{:S(2)}) async-start(bf16[16,152,256]{2,1,0:T(8,128)(2,1)} %convolve.1), calls=%async_computation.1 | async-start | bytes 2490368 | tf_op jit(solution)/shard_map/all_to_all | solution.py:625
  47.8 0.0 copy-done
  47.8 1.3 %collective-permute-start.12 = (bf16[1,128,2048]{2,1,0:T(8,128)(2,1)S(1)}, bf16[1,128,2048]{2,1,0:T(8,128)(2,1)S(1)}, u32[]{:S(2)}, u32[]{:S(2)}) collective-permute-start(bf16[1,128,2048]{2,1,0:T(8,128)(2,1)S(1)} %copy-done), channel_id=1, source_target_pairs={{64,0},{65,1},{66,2},{67,3},{68,4},{69,5},{70,6},{71,7},{72,8},{73... | collective-permute-start | bytes 1572872 | tf_op jit(solution)/shard_map/ppermute | solution.py:621
  49.1 17.4 %all-to-all-done.1.back_ref = bf16[16,152,256]{2,1,0:T(8,128)(2,1)S(1)} async-done(((bf16[16,152,256]{2,1,0:T(8,128)(2,1)}), bf16[16,152,256]{2,1,0:T(8,128)(2,1)S(1)}, u32[]{:S(2)}, u32[]{:S(2)}) %all-to-all-start.1) | async-done | bytes 1245216 | tf_op jit(solution)/shard_map/all_to_all | solution.py:625
  66.5 0.0 copy-done.1
  66.5 0.0 copy-done.2
  66.5 1.6 %leave.1 = (bf16[1,128,2048]{2,1,0:T(8,128)(2,1)S(1)}, bf16[1,128,2048]{2,1,0:T(8,128)(2,1)S(1)}, f32[8,128]{1,0:T(8,128)S(1)}) custom-call(s32[1]{0:T(128)} %bitcast.pipe_ref, f32[32,128]{1,0:T(8,128)S(1)} %add_rsqrt_fusion.inv_ref, bf16[16,152,256]{2,1,0:T(8,128)(2,1)S(1)} %all-to-all-done.1.back_ref, bf16[1,128,2048]{2,1,0:T(8,128)(2,1)} %fwd_hbm.3, ...), custom_call_target="tpu_custom_call" | custom-call | tf_op jit(solution)/shard_map/leave/pallas_call | solution.py:474
  68.1 3.4 %collective-permute-start.13 = (bf16[1,128,2048]{2,1,0:T(8,128)(2,1)S(1)}, bf16[1,128,2048]{2,1,0:T(8,128)(2,1)S(1)}, u32[]{:S(2)}, u32[]{:S(2)}) collective-permute-start(bf16[1,128,2048]{2,1,0:T(8,128)(2,1)S(1)} %get-tuple-element.16.send_ref), channel_id=1, source_target_pairs={{0,64},{64,0},{1,65},{65,1},{2,66},{66,2},{3,67},{67,3},{4,68},{68... | collective-permute-start | bytes 1572872 | tf_op jit(solution)/shard_map/ppermute | solution.py:630
  71.5 1.3 %collective-permute-start.8 = (f32[8,128]{1,0:T(8,128)S(1)}, f32[8,128]{1,0:T(8,128)S(1)}, u32[]{:S(2)}, u32[]{:S(2)}) collective-permute-start(f32[8,128]{1,0:T(8,128)S(1)} %get-tuple-element.15), channel_id=1, source_target_pairs={{64,0},{65,1},{66,2},{67,3},{68,4},{69,5},{70,6},{71,7},{72,8},{73... | collective-permute-start | bytes 12296 | tf_op jit(solution)/shard_map/ppermute | solution.py:629
  72.8 15.2 %collective-permute-done.8 = f32[8,128]{1,0:T(8,128)S(1)} collective-permute-done((f32[8,128]{1,0:T(8,128)S(1)}, f32[8,128]{1,0:T(8,128)S(1)}, u32[]{:S(2)}, u32[]{:S(2)}) %collective-permute-start.8) | collective-permute-done | bytes 4128 | tf_op jit(solution)/shard_map/ppermute | solution.py:629
  88.0 4.0 %collective-permute-start.10 = (f32[8,128]{1,0:T(8,128)S(1)}, f32[8,128]{1,0:T(8,128)S(1)}, u32[]{:S(2)}, u32[]{:S(2)}) collective-permute-start(f32[8,128]{1,0:T(8,128)S(1)} %pad_maximum_fusion.s0), channel_id=1, source_target_pairs={{0,2},{1,3},{2,0},{3,1},{4,6},{5,7},{6,4},{7,5},{8,10},{9,11},{10,... | collective-permute-start | bytes 12296 | tf_op jit(solution)/shard_map/ppermute | solution.py:136
  92.0 0.7 collective-permute-start.11
  92.7 1.3 %collective-permute-start.9 = (f32[8,128]{1,0:T(8,128)S(1)}, f32[8,128]{1,0:T(8,128)S(1)}, u32[]{:S(2)}, u32[]{:S(2)}) collective-permute-start(f32[8,128]{1,0:T(8,128)S(1)} %pad_maximum_fusion.s0), channel_id=1, source_target_pairs={{0,1},{1,2},{2,3},{3,0},{4,5},{5,6},{6,7},{7,4},{8,9},{9,10},{10,1... | collective-permute-start | bytes 12296 | tf_op jit(solution)/shard_map/ppermute | solution.py:136
  94.0 0.0 collective-permute-done.12.peer_ref
  94.0 0.0 copy-start.4
  94.0 0.0 collective-permute-done.10.s2
  94.0 1.6 %collective-permute-done.11.s3 = f32[8,128]{1,0:T(8,128)S(1)} collective-permute-done((f32[8,128]{1,0:T(8,128)S(1)}, f32[8,128]{1,0:T(8,128)S(1)}, u32[]{:S(2)}, u32[]{:S(2)}) %collective-permute-start.11) | collective-permute-done | bytes 4128 | tf_op jit(solution)/shard_map/ppermute | solution.py:136
  95.6 1.9 %collective-permute-done.9.s1 = f32[8,128]{1,0:T(8,128)S(1)} collective-permute-done((f32[8,128]{1,0:T(8,128)S(1)}, f32[8,128]{1,0:T(8,128)S(1)}, u32[]{:S(2)}, u32[]{:S(2)}) %collective-permute-start.9) | collective-permute-done | bytes 4128 | tf_op jit(solution)/shard_map/ppermute | solution.py:136
  97.5 0.0 copy-done.4
  97.5 3.7 %finish.1 = (bf16[1,128,2048]{2,1,0:T(8,128)(2,1)}, bf16[1,128,2048]{2,1,0:T(8,128)(2,1)}, f32[1,7,2048]{2,1,0:T(8,128)S(1)}, f32[128,2048]{1,0:T(8,128)S(1)}) custom-call(s32[1]{0:T(128)} %bitcast.pipe_ref, f32[8,128]{1,0:T(8,128)S(1)} %pad_maximum_fusion.s0, f32[8,128]{1,0:T(8,128)S(1)} %collective-permute-done.9.s1, ...), custom_call_target="tpu_custom_call" | custom-call | tf_op jit(solution)/shard_map/finish/pallas_call | solution.py:564
  101.2 0.7 copy.16
  101.9 0.0 collective-permute-done.13.value_ref
  101.9 1.5 %received.1 = bf16[1,128,2048]{2,1,0:T(8,128)(2,1)} custom-call(bf16[1,128,2048]{2,1,0:T(8,128)(2,1)S(1)} %collective-permute-done.13.value_ref, f32[128,2048]{1,0:T(8,128)S(1)} %get-tuple-element.21.term_ref), custom_call_target="tpu_custom_call" | custom-call | tf_op jit(solution)/shard_map/received/pallas_call | solution.py:600
  (11 shorter events, 0.2 us)
Async XLA Ops:
  3.3 27.0 %copy-start.5 = (f32[1,7,2048]{2,0,1:T(1,128)S(1)}, f32[1,7,2048]{2,0,1:T(1,128)}, u32[]{:S(2)}) copy-start(f32[1,7,2048]{2,0,1:T(1,128)} %param.14) | copy-start | bytes 172036
  3.3 31.3 %all-to-all-start = ((bf16[16,384,128]{2,1,0:T(8,128)(2,1)}), bf16[16,384,128]{2,1,0:T(8,128)(2,1)}, u32[]{:S(2)}, u32[]{:S(2)}) async-start(bf16[16,384,128]{2,1,0:T(8,128)(2,1)} %get-tuple-element.14), calls=%async_computation | async-start | bytes 3145728 | tf_op jit(solution)/shard_map/all_to_all | solution.py:615
  9.2 6.6 %collective-permute-start = (f32[8,128]{1,0:T(8,128)S(1)}, f32[8,128]{1,0:T(8,128)S(1)}, u32[]{:S(2)}, u32[]{:S(2)}) collective-permute-start(f32[8,128]{1,0:T(8,128)S(1)} %get-tuple-element.13), channel_id=1, source_target_pairs={{0,1},{1,2},{2,3},{3,0},{4,5},{5,6},{6,7},{7,4},{8,9},{9,10},{10,1... | collective-permute-start | bytes 12296 | tf_op jit(solution)/shard_map/ppermute | solution.py:136
  11.1 5.2 %collective-permute-start.1 = (f32[8,128]{1,0:T(8,128)S(1)}, f32[8,128]{1,0:T(8,128)S(1)}, u32[]{:S(2)}, u32[]{:S(2)}) collective-permute-start(f32[8,128]{1,0:T(8,128)S(1)} %get-tuple-element.13), channel_id=1, source_target_pairs={{0,2},{1,3},{2,0},{3,1},{4,6},{5,7},{6,4},{7,5},{8,10},{9,11},{10,... | collective-permute-start | bytes 12296 | tf_op jit(solution)/shard_map/ppermute | solution.py:136
  14.7 3.6 %collective-permute-start.2 = (f32[8,128]{1,0:T(8,128)S(1)}, f32[8,128]{1,0:T(8,128)S(1)}, u32[]{:S(2)}, u32[]{:S(2)}) collective-permute-start(f32[8,128]{1,0:T(8,128)S(1)} %get-tuple-element.13), channel_id=1, source_target_pairs={{0,3},{1,0},{2,1},{3,2},{4,7},{5,4},{6,5},{7,6},{8,11},{9,8},{10,9... | collective-permute-start | bytes 12296 | tf_op jit(solution)/shard_map/ppermute | solution.py:136
  18.3 1.2 %collective-permute-start.3 = (f32[2,128]{1,0:T(2,128)S(1)}, f32[2,128]{1,0:T(2,128)S(1)}, u32[]{:S(2)}, u32[]{:S(2)}) collective-permute-start(f32[2,128]{1,0:T(2,128)S(1)} %slice.12), channel_id=1, source_target_pairs={{0,4},{4,0},{8,12},{12,8},{16,20},{20,16},{24,28},{28,24},{32,36},... | collective-permute-start | bytes 3080 | tf_op jit(solution)/shard_map/ppermute | solution.py:143
  19.5 8.7 %collective-permute-start.4 = (f32[4,128]{1,0:T(4,128)S(1)}, f32[4,128]{1,0:T(4,128)S(1)}, u32[]{:S(2)}, u32[]{:S(2)}) collective-permute-start(f32[4,128]{1,0:T(4,128)S(1)} %pad_maximum_fusion.1), channel_id=1, source_target_pairs={{0,8},{4,12},{8,16},{12,20},{16,24},{20,28},{24,0},{28,4},{32,40},... | collective-permute-start | bytes 6152 | tf_op jit(solution)/shard_map/ppermute | solution.py:149
  21.3 7.3 %collective-permute-start.5 = (f32[4,128]{1,0:T(4,128)S(1)}, f32[4,128]{1,0:T(4,128)S(1)}, u32[]{:S(2)}, u32[]{:S(2)}) collective-permute-start(f32[4,128]{1,0:T(4,128)S(1)} %pad_maximum_fusion.1), channel_id=1, source_target_pairs={{0,16},{4,20},{8,24},{12,28},{16,0},{20,4},{24,8},{28,12},{32,48},... | collective-permute-start | bytes 6152 | tf_op jit(solution)/shard_map/ppermute | solution.py:149
  24.0 4.6 %collective-permute-start.6 = (f32[4,128]{1,0:T(4,128)S(1)}, f32[4,128]{1,0:T(4,128)S(1)}, u32[]{:S(2)}, u32[]{:S(2)}) collective-permute-start(f32[4,128]{1,0:T(4,128)S(1)} %pad_maximum_fusion.1), channel_id=1, source_target_pairs={{0,24},{4,28},{8,0},{12,4},{16,8},{20,12},{24,16},{28,20},{32,56},... | collective-permute-start | bytes 6152 | tf_op jit(solution)/shard_map/ppermute | solution.py:149
  28.6 6.0 %collective-permute-start.7 = (f32[16,128]{1,0:T(8,128)S(1)}, f32[16,128]{1,0:T(8,128)S(1)}, u32[]{:S(2)}, u32[]{:S(2)}) collective-permute-start(f32[16,128]{1,0:T(8,128)S(1)} %concatenate.15), channel_id=1, source_target_pairs={{0,32},{4,36},{8,40},{12,44},{16,48},{20,52},{24,56},{28,60},{32,0... | collective-permute-start | bytes 24584 | tf_op jit(solution)/shard_map/ppermute | solution.py:143
  31.9 2.7 %copy-start.3 = (s32[16]{0:T(128)S(1)}, s32[16]{0:T(128)}, u32[]{:S(2)}) copy-start(s32[16]{0:T(128)} %order_ref.1) | copy-start | bytes 196
  42.6 5.2 %copy-start = (bf16[1,128,2048]{2,1,0:T(8,128)(2,1)S(1)}, bf16[1,128,2048]{2,1,0:T(8,128)(2,1)}, u32[]{:S(2)}) copy-start(bf16[1,128,2048]{2,1,0:T(8,128)(2,1)} %saved_ref.5) | copy-start | bytes 1572868
  42.6 23.9 %copy-start.1 = (bf16[1,128,2048]{2,1,0:T(8,128)(2,1)S(1)}, bf16[1,128,2048]{2,1,0:T(8,128)(2,1)}, u32[]{:S(2)}) copy-start(bf16[1,128,2048]{2,1,0:T(8,128)(2,1)} %cot_ref.3) | copy-start | bytes 1572868
  42.6 23.9 %copy-start.2 = (bf16[1,128,2048]{2,1,0:T(8,128)(2,1)S(1)}, bf16[1,128,2048]{2,1,0:T(8,128)(2,1)}, u32[]{:S(2)}) copy-start(bf16[1,128,2048]{2,1,0:T(8,128)(2,1)} %sconv_ref.3) | copy-start | bytes 1572868
  42.6 23.9 %all-to-all-start.1 = ((bf16[16,152,256]{2,1,0:T(8,128)(2,1)}), bf16[16,152,256]{2,1,0:T(8,128)(2,1)S(1)}, u32[]{:S(2)}, u32[]{:S(2)}) async-start(bf16[16,152,256]{2,1,0:T(8,128)(2,1)} %convolve.1), calls=%async_computation.1 | async-start | bytes 2490368 | tf_op jit(solution)/shard_map/all_to_all | solution.py:625
  47.8 46.2 %collective-permute-start.12 = (bf16[1,128,2048]{2,1,0:T(8,128)(2,1)S(1)}, bf16[1,128,2048]{2,1,0:T(8,128)(2,1)S(1)}, u32[]{:S(2)}, u32[]{:S(2)}) collective-permute-start(bf16[1,128,2048]{2,1,0:T(8,128)(2,1)S(1)} %copy-done), channel_id=1, source_target_pairs={{64,0},{65,1},{66,2},{67,3},{68,4},{69,5},{70,6},{71,7},{72,8},{73... | collective-permute-start | bytes 1572872 | tf_op jit(solution)/shard_map/ppermute | solution.py:621
  68.1 33.7 %collective-permute-start.13 = (bf16[1,128,2048]{2,1,0:T(8,128)(2,1)S(1)}, bf16[1,128,2048]{2,1,0:T(8,128)(2,1)S(1)}, u32[]{:S(2)}, u32[]{:S(2)}) collective-permute-start(bf16[1,128,2048]{2,1,0:T(8,128)(2,1)S(1)} %get-tuple-element.16.send_ref), channel_id=1, source_target_pairs={{0,64},{64,0},{1,65},{65,1},{2,66},{66,2},{3,67},{67,3},{4,68},{68... | collective-permute-start | bytes 1572872 | tf_op jit(solution)/shard_map/ppermute | solution.py:630
  71.5 16.5 %collective-permute-start.8 = (f32[8,128]{1,0:T(8,128)S(1)}, f32[8,128]{1,0:T(8,128)S(1)}, u32[]{:S(2)}, u32[]{:S(2)}) collective-permute-start(f32[8,128]{1,0:T(8,128)S(1)} %get-tuple-element.15), channel_id=1, source_target_pairs={{64,0},{65,1},{66,2},{67,3},{68,4},{69,5},{70,6},{71,7},{72,8},{73... | collective-permute-start | bytes 12296 | tf_op jit(solution)/shard_map/ppermute | solution.py:629
  88.0 6.0 %collective-permute-start.10 = (f32[8,128]{1,0:T(8,128)S(1)}, f32[8,128]{1,0:T(8,128)S(1)}, u32[]{:S(2)}, u32[]{:S(2)}) collective-permute-start(f32[8,128]{1,0:T(8,128)S(1)} %pad_maximum_fusion.s0), channel_id=1, source_target_pairs={{0,2},{1,3},{2,0},{3,1},{4,6},{5,7},{6,4},{7,5},{8,10},{9,11},{10,... | collective-permute-start | bytes 12296 | tf_op jit(solution)/shard_map/ppermute | solution.py:136
  92.0 3.6 %collective-permute-start.11 = (f32[8,128]{1,0:T(8,128)S(1)}, f32[8,128]{1,0:T(8,128)S(1)}, u32[]{:S(2)}, u32[]{:S(2)}) collective-permute-start(f32[8,128]{1,0:T(8,128)S(1)} %pad_maximum_fusion.s0), channel_id=1, source_target_pairs={{0,3},{1,0},{2,1},{3,2},{4,7},{5,4},{6,5},{7,6},{8,11},{9,8},{10,9... | collective-permute-start | bytes 12296 | tf_op jit(solution)/shard_map/ppermute | solution.py:136
  92.7 4.8 %collective-permute-start.9 = (f32[8,128]{1,0:T(8,128)S(1)}, f32[8,128]{1,0:T(8,128)S(1)}, u32[]{:S(2)}, u32[]{:S(2)}) collective-permute-start(f32[8,128]{1,0:T(8,128)S(1)} %pad_maximum_fusion.s0), channel_id=1, source_target_pairs={{0,1},{1,2},{2,3},{3,0},{4,5},{5,6},{6,7},{7,4},{8,9},{9,10},{10,1... | collective-permute-start | bytes 12296 | tf_op jit(solution)/shard_map/ppermute | solution.py:136
  94.0 3.5 %copy-start.4 = (bf16[1,128,2048]{2,1,0:T(8,128)(2,1)}, bf16[1,128,2048]{2,1,0:T(8,128)(2,1)S(1)}, u32[]{:S(2)}) copy-start(bf16[1,128,2048]{2,1,0:T(8,128)(2,1)S(1)} %collective-permute-done.12.peer_ref) | copy-start | bytes 1572868

commit v6 on v5

--- a/solution.py
+++ b/solution.py
@@ -221,13 +221,13 @@
     shape = (length // BLOCK, 2, BLOCK, LANES)
     return pl.pallas_call(
         filter_kernel,
-        out_shape=pltpu.VMEM(shape, jnp.float32),
+        out_shape=pltpu.HBM(shape, jnp.float32),
         grid_spec=pltpu.PrefetchScalarGridSpec(
             num_scalar_prefetch=1,
             grid=(1,),
             in_specs=[pl.BlockSpec((1, length, LANES), lambda step, at: (0, 0, at[0]))]
             + [whole(tables[0].shape)],
-            out_specs=VMEM,
+            out_specs=whole(shape),
         ),
         name="filter_spectra",
         compiler_params=pltpu.CompilerParams(vmem_limit_bytes=16 << 20),
@@ -239,8 +239,8 @@
 
 
 def conv_kernel(
-    where_ref, order_ref, gathered_ref, inv_ref, known_ref, params_ref, filt, raw_hbm, enter_hbm,
-    leave_hbm, out_hbm, raw_ref, enter, leave, out_ref, ordered, spectra, product, inv_rows, inv, raw_sem, table_sem, out_sem,
+    where_ref, order_ref, gathered_ref, inv_ref, known_ref, params_ref, filt_hbm, raw_hbm, enter_hbm,
+    leave_hbm, out_hbm, raw_ref, filt, enter, leave, out_ref, ordered, spectra, product, inv_rows, inv, raw_sem, table_sem, out_sem,
 ):
     stored = raw_ref.shape[0]
     raw_copies = [
@@ -249,7 +249,9 @@
     ]
     table_copies = [
         pltpu.make_async_copy(source, target, table_sem.at[index])
-        for index, (source, target) in enumerate(((enter_hbm, enter), (leave_hbm, leave)))
+        for index, (source, target) in enumerate(
+            ((enter_hbm, enter), (leave_hbm, leave), (filt_hbm, filt))
+        )
     ]
     out_copies = [
         pltpu.make_async_copy(out_ref.at[index], out_hbm.at[index], out_sem.at[index])
@@ -285,6 +287,8 @@
         data = ordered[index * BLOCK : (index + 1) * BLOCK, :]
         spectra[index] = jnp.dot(enter[...], data, preferred_element_type=jnp.float32)
 
+    table_copies[2].wait()
+
     def forward_and_adjoint(low, high, one_product):
         for adjoint in (False, True):
             lanes = slice(LANES, 2 * LANES) if adjoint else slice(0, LANES)
@@ -385,10 +389,11 @@
     return pl.pallas_call(
         conv_kernel,
         out_shape=pltpu.HBM((stored, rows + 24, 2 * LANES), jnp.bfloat16),
-        in_specs=[SMEM] * 3 + [VMEM] * 4 + [HBM] * 3,
+        in_specs=[SMEM] * 3 + [VMEM] * 3 + [HBM] * 4,
         out_specs=HBM,
         scratch_shapes=[
             pltpu.VMEM(raw.shape, jnp.bfloat16),
+            pltpu.VMEM(spectra.shape, jnp.float32),
             pltpu.VMEM((2 * BLOCK, BLOCK), jnp.bfloat16),
             pltpu.VMEM((BLOCK, 2 * BLOCK), jnp.bfloat16),
             pltpu.VMEM((stored, rows + 24, 2 * LANES), jnp.bfloat16),
@@ -398,13 +403,13 @@
             pltpu.VMEM((2 * stored, 128), jnp.float32),
             pltpu.VMEM((128, 128), jnp.float32),
             pltpu.SemaphoreType.DMA((stored,)),
-            pltpu.SemaphoreType.DMA((2,)),
+            pltpu.SemaphoreType.DMA((3,)),
             pltpu.SemaphoreType.DMA((stored,)),
         ],
         name="convolve",
         compiler_params=pltpu.CompilerParams(vmem_limit_bytes=28 << 20),
     )(
-        where, order, gathered, inv, known, params, in_vmem(spectra), in_hbm(raw),
+        where, order, gathered, inv, known, params, in_hbm(spectra), in_hbm(raw),
         *[in_hbm(table) for table in tables],
     )
 
@@ -490,49 +495,33 @@
     )
 
 
-def finish_kernel(
-    pipe_ref, s0, s1, s2, s3, back_ref, send_ref, keep_ref, saved_ref, params_ref, peer_ref,
-    layer_hbm, grad_ref, grads_ref, term_ref, scale, known, layer_sem,
+def rows_kernel(
+    pipe_ref, back_ref, send_ref, keep_ref, params_ref, layer_hbm, grads_ref, layer_sem
 ):
-    step = pl.program_id(0)
     first = pipe_ref[0] == 0
-    rows, wide = grad_ref.shape[1:]
+    stored, rows = back_ref.shape[0], send_ref.shape[1]
     sent = pltpu.make_async_copy(send_ref, layer_hbm, layer_sem)
     kept = pltpu.make_async_copy(keep_ref, layer_hbm, layer_sem)
 
-    @pl.when(step == 0)
-    def _():
-        @pl.when(first)
-        def _():
-            sent.start()
-
-        @pl.when(jnp.logical_not(first))
-        def _():
-            kept.start()
-
-        scale[...] = rows_to_columns(s0[...] + s1[...] + s2[...] + s3[...])
-        total = back_ref[0, rows : rows + 16, :].astype(jnp.float32)
-        for index in range(1, back_ref.shape[0]):
-            total = total + back_ref[index, rows : rows + 16, :].astype(jnp.float32)
-        for row in range(16):
-            known[row] = total[row : row + 1, :]
-
-    groups = wide // LANES
-    for group in range(groups):
+    @pl.when(first)
+    def _():
+        sent.start()
+
+    @pl.when(jnp.logical_not(first))
+    def _():
+        kept.start()
+
+    known = back_ref[0, rows : rows + 16, :].astype(jnp.float32)
+    for index in range(1, stored):
+        known = known + back_ref[index, rows : rows + 16, :].astype(jnp.float32)
+    for group in range(stored):
         own = pl.ds(group * LANES, LANES)
-        at = pl.ds(pl.multiple_of(step * wide + group * LANES, LANES), LANES)
-        partial = jnp.where(first, keep_ref[0, :, at], send_ref[0, :, at]).astype(jnp.float32)
-        saved = saved_ref[0, :, at].astype(jnp.float32)
-        grad_ref[0, :, own] = (partial - saved * scale[:, 0:1]).astype(jnp.bfloat16)
-        term_ref[:, at] = peer_ref[0, :, own].astype(jnp.float32) * scale[:, 1:2]
-
         p = [params_ref[0, row : row + 1, own] for row in range(7)]
-        extra = back_ref[step * groups + group, rows + 16 :, :].astype(jnp.float32)
+        extra = back_ref[group, rows + 16 :, :].astype(jnp.float32)
         extra = extra[:, :LANES] + extra[:, LANES:]
         m0, m1, m2 = extra[0:1], extra[1:2], extra[2:3]
-        row = step * (groups // 2) + group // 2
-        side = slice(group % 2 * LANES, (group % 2 + 1) * LANES)
-        q0, q1 = known[row, :, side], known[row + 8, :, side]
+        row, side = group // 2, slice(group % 2 * LANES, (group % 2 + 1) * LANES)
+        q0, q1 = known[row : row + 1, side], known[row + 8 : row + 9, side]
         key_normed = p[0] * p[5] * m2 + p[6] * m1
         value_normed = p[0] * p[3] * m2 + p[4] * m1
         grads = [
@@ -546,43 +535,67 @@
         ]
         grads_ref[0, :, own] = jnp.concatenate(grads, axis=0)
 
-    @pl.when(step == pl.num_programs(0) - 1)
-    def _():
-        @pl.when(first)
-        def _():
-            sent.wait()
-
-        @pl.when(jnp.logical_not(first))
-        def _():
-            kept.wait()
-
-
-def finish(pipe, scales, back, send, keep, saved_in, mix_params, peer_saved):
+    @pl.when(first)
+    def _():
+        sent.wait()
+
+    @pl.when(jnp.logical_not(first))
+    def _():
+        kept.wait()
+
+
+def finish_rows(pipe, back, send, keep, mix_params):
+    return pl.pallas_call(
+        rows_kernel,
+        out_shape=(
+            pltpu.HBM(send.shape, jnp.bfloat16),
+            jax.ShapeDtypeStruct(mix_params.shape, jnp.float32),
+        ),
+        in_specs=[SMEM] + [VMEM] * 4,
+        out_specs=(HBM, VMEM),
+        scratch_shapes=[pltpu.SemaphoreType.DMA],
+        name="finish_rows",
+        compiler_params=pltpu.CompilerParams(vmem_limit_bytes=8 << 20),
+    )(pipe, in_vmem(back), in_vmem(send), in_vmem(keep), mix_params)
+
+
+def cross_kernel(
+    pipe_ref, s0, s1, s2, s3, send_ref, keep_ref, saved_ref, peer_ref, grad_ref, term_ref, scale
+):
+    step = pl.program_id(0)
+    first = pipe_ref[0] == 0
+
+    @pl.when(step == 0)
+    def _():
+        scale[...] = rows_to_columns(s0[...] + s1[...] + s2[...] + s3[...])
+
+    wide = grad_ref.shape[2]
+    for group in range(wide // LANES):
+        own = pl.ds(group * LANES, LANES)
+        at = pl.ds(pl.multiple_of(step * wide + group * LANES, LANES), LANES)
+        partial = jnp.where(first, keep_ref[0, :, at], send_ref[0, :, at]).astype(jnp.float32)
+        saved = saved_ref[0, :, at].astype(jnp.float32)
+        grad_ref[0, :, own] = (partial - saved * scale[:, 0:1]).astype(jnp.bfloat16)
+        term_ref[:, at] = peer_ref[0, :, at].astype(jnp.float32) * scale[:, 1:2]
+
+
+def finish_cross(pipe, scales, send, keep, saved_in, peer_saved):
     rows, width = saved_in.shape[1:]
     wide = 512
-    spec, params = lane_spec(rows, wide), lane_spec(7, wide)
-    return pl.pallas_call(
-        finish_kernel,
+    spec = lane_spec(rows, wide)
+    return pl.pallas_call(
+        cross_kernel,
         out_shape=(
-            pltpu.HBM(saved_in.shape, jnp.bfloat16),
             jax.ShapeDtypeStruct(saved_in.shape, jnp.bfloat16),
-            jax.ShapeDtypeStruct(mix_params.shape, jnp.float32),
             pltpu.VMEM((rows, width), jnp.float32),
         ),
         grid=(width // wide,),
-        in_specs=[SMEM] + [VMEM] * 8 + [params, spec],
-        out_specs=(HBM, spec, params, VMEM),
-        scratch_shapes=[
-            pltpu.VMEM((rows, 128), jnp.float32),
-            pltpu.VMEM((16, 1, 2 * LANES), jnp.float32),
-            pltpu.SemaphoreType.DMA,
-        ],
-        name="finish",
-        compiler_params=pltpu.CompilerParams(vmem_limit_bytes=16 << 20),
-    )(
-        pipe, *scales, in_vmem(back), in_vmem(send), in_vmem(keep), in_vmem(saved_in),
-        mix_params, in_hbm(peer_saved),
-    )
+        in_specs=[SMEM] + [VMEM] * 8,
+        out_specs=(spec, VMEM),
+        scratch_shapes=[pltpu.VMEM((rows, 128), jnp.float32)],
+        name="finish_cross",
+        compiler_params=pltpu.CompilerParams(vmem_limit_bytes=8 << 20),
+    )(pipe, *scales, in_vmem(send), in_vmem(keep), in_vmem(saved_in), in_vmem(peer_saved))
 
 
 def received_kernel(value_ref, term_ref, out_ref):
@@ -629,9 +642,8 @@
     peer_cross = lax.ppermute(cross, "pipe", [(1, 0)])
     incoming = lax.ppermute(outgoing, "pipe", [(0, 1), (1, 0)])
     scales = over_chan(jnp.concatenate([cross[:1], peer_cross[:1], cross[:6]], axis=0))
-    layer_out, input_grad, param_grad, term = finish(
-        pipe, scales, back, outgoing, keep, saved_in, mix_params, peer_saved
-    )
+    layer_out, param_grad = finish_rows(pipe, back, outgoing, keep, mix_params)
+    input_grad, term = finish_cross(pipe, scales, outgoing, keep, saved_in, peer_saved)
     received = finish_received(incoming, term)
     return (layer_out, input_grad, param_grad, received)
 

time: 104 us -> 104 us (level)
  waiting for transfers between devices: 42.9 us -> 41.4 us
  local copies, waits for them, and re-layouts: 0.84 us -> 1.95 us
    ppermute x6, waiting for transfers between devices: 6.09 us -> 4.61 us  [over_chan(): lax.ppermute(rows, 'chan', [(low, (low + apart) % count) for low in range...]
    unnamed x14, local copies, waits for them, and re-layouts: 0.74 us -> 1.86 us
    pallas_call x2 -> x3, Pallas kernels: 5.27 us -> 5.76 us  [the longest x1 2.9 us: filter_spectra(): pl.pallas_call(filter_kernel, out_shape=pltpu.HBM(shape, jnp.float32), gr...]
  transfers between devices with their start and end apart: 16 -> 16, of which waited for: 9 -> 9; matrix products, arithmetic and copies ran while one was open for 1% -> 1% of each run, Pallas kernels for 9% -> 10%
where the time goes in v6:
time: 104 us
  waiting for transfers between devices  41.4 us (40%)
  starting transfers between devices  37.1 us (36%)
  Pallas kernels  22.2 us (21%)
  local copies, waits for them, and re-layouts  1.95 us (2%)
    all_to_all x1, waiting for transfers between devices, per_device(): back = lax.all_to_all(back, 'seq', 0, 0)  17.4 us
    ppermute x1, waiting for transfers between devices, per_device(): peer_cross = lax.ppermute(cross, 'pipe', [(1, 0)])  15.2 us
    ppermute x6, starting transfers between devices, over_chan(): lax.ppermute(rows, 'chan', [(low, (low + apart) % count) for low in range...  12.6 us
    pallas_call x1, Pallas kernels, convolve(): pl.pallas_call(conv_kernel, out_shape=pltpu.HBM((stored, rows + 24, 2 * L...  7.95 us
    ppermute x3, starting transfers between devices, round_ring(): lax.ppermute(rows, 'seq', [(low, place(low)) for low in range(count)])  5.99 us
    all_to_all x1, starting transfers between devices, per_device(): raw = lax.all_to_all(raw, 'seq', 0, 0)  5.76 us
    all_to_all x1, starting transfers between devices, per_device(): back = lax.all_to_all(back, 'seq', 0, 0)  5.18 us
    ppermute x6, waiting for transfers between devices, over_chan(): lax.ppermute(rows, 'chan', [(low, (low + apart) % count) for low in range...  4.61 us
  transfers between devices with their start and end apart: 16, of which 9 were waited for; matrix products, arithmetic and copies ran while one was open for 1% of the time, Pallas kernels for 10%

profile of v6, /device:TPU:0, one launch (start us, length us, event | category | flops | bytes accessed | tf_op | source)
XLA Modules:
  0.0 103.6 jit_solution(3489990473646506548)
XLA Ops:
  0.6 2.7 %pack.1 = (bf16[16,384,128]{2,1,0:T(8,128)(2,1)}, f32[8,128]{1,0:T(8,128)S(1)}) custom-call(bf16[1,128,2048]{2,1,0:T(8,128)(2,1)} %fwd_hbm.3, bf16[1,128,2048]{2,1,0:T(8,128)(2,1)} %saved_ref.5, bf16[1,128,2048]{2,1,0:T(8,128)(2,1)} %cot_ref.3), custom_call_target="tpu_custom_call" | custom-call | tf_op jit(solution)/shard_map/pack/pallas_call | solution.py:113
  3.3 0.0 copy-start.5
  3.3 5.8 %all-to-all-start = ((bf16[16,384,128]{2,1,0:T(8,128)(2,1)}), bf16[16,384,128]{2,1,0:T(8,128)(2,1)S(1)}, u32[]{:S(2)}, u32[]{:S(2)}) async-start(bf16[16,384,128]{2,1,0:T(8,128)(2,1)} %get-tuple-element.14), calls=%async_computation | async-start | bytes 3145728 | tf_op jit(solution)/shard_map/all_to_all | solution.py:628
  9.1 2.0 %collective-permute-start = (f32[8,128]{1,0:T(8,128)S(1)}, f32[8,128]{1,0:T(8,128)S(1)}, u32[]{:S(2)}, u32[]{:S(2)}) collective-permute-start(f32[8,128]{1,0:T(8,128)S(1)} %get-tuple-element.13), channel_id=1, source_target_pairs={{0,1},{1,2},{2,3},{3,0},{4,5},{5,6},{6,7},{7,4},{8,9},{9,10},{10,1... | collective-permute-start | bytes 12296 | tf_op jit(solution)/shard_map/ppermute | solution.py:136
  11.1 3.6 %collective-permute-start.1 = (f32[8,128]{1,0:T(8,128)S(1)}, f32[8,128]{1,0:T(8,128)S(1)}, u32[]{:S(2)}, u32[]{:S(2)}) collective-permute-start(f32[8,128]{1,0:T(8,128)S(1)} %get-tuple-element.13), channel_id=1, source_target_pairs={{0,2},{1,3},{2,0},{3,1},{4,6},{5,7},{6,4},{7,5},{8,10},{9,11},{10,... | collective-permute-start | bytes 12296 | tf_op jit(solution)/shard_map/ppermute | solution.py:136
  14.7 1.0 collective-permute-start.2
  15.7 0.0 collective-permute-done
  15.7 0.6 collective-permute-done.1
  16.3 2.0 %collective-permute-done.2 = f32[8,128]{1,0:T(8,128)S(1)} collective-permute-done((f32[8,128]{1,0:T(8,128)S(1)}, f32[8,128]{1,0:T(8,128)S(1)}, u32[]{:S(2)}, u32[]{:S(2)}) %collective-permute-start.2) | collective-permute-done | bytes 4128 | tf_op jit(solution)/shard_map/ppermute | solution.py:136
  18.3 0.0 collective-permute-start.3
  18.3 1.2 %collective-permute-done.3 = f32[2,128]{1,0:T(2,128)S(1)} collective-permute-done((f32[2,128]{1,0:T(2,128)S(1)}, f32[2,128]{1,0:T(2,128)S(1)}, u32[]{:S(2)}, u32[]{:S(2)}) %collective-permute-start.3) | collective-permute-done | bytes 1056 | tf_op jit(solution)/shard_map/ppermute | solution.py:143
  19.5 1.9 %collective-permute-start.4 = (f32[4,128]{1,0:T(4,128)S(1)}, f32[4,128]{1,0:T(4,128)S(1)}, u32[]{:S(2)}, u32[]{:S(2)}) collective-permute-start(f32[4,128]{1,0:T(4,128)S(1)} %pad_maximum_fusion.1), channel_id=1, source_target_pairs={{0,8},{4,12},{8,16},{12,20},{16,24},{20,28},{24,0},{28,4},{32,40},... | collective-permute-start | bytes 6152 | tf_op jit(solution)/shard_map/ppermute | solution.py:149
  21.3 2.7 %collective-permute-start.5 = (f32[4,128]{1,0:T(4,128)S(1)}, f32[4,128]{1,0:T(4,128)S(1)}, u32[]{:S(2)}, u32[]{:S(2)}) collective-permute-start(f32[4,128]{1,0:T(4,128)S(1)} %pad_maximum_fusion.1), channel_id=1, source_target_pairs={{0,16},{4,20},{8,24},{12,28},{16,0},{20,4},{24,8},{28,12},{32,48},... | collective-permute-start | bytes 6152 | tf_op jit(solution)/shard_map/ppermute | solution.py:149
  24.0 1.5 %collective-permute-start.6 = (f32[4,128]{1,0:T(4,128)S(1)}, f32[4,128]{1,0:T(4,128)S(1)}, u32[]{:S(2)}, u32[]{:S(2)}) collective-permute-start(f32[4,128]{1,0:T(4,128)S(1)} %pad_maximum_fusion.1), channel_id=1, source_target_pairs={{0,24},{4,28},{8,0},{12,4},{16,8},{20,12},{24,16},{28,20},{32,56},... | collective-permute-start | bytes 6152 | tf_op jit(solution)/shard_map/ppermute | solution.py:149
  25.5 2.8 %collective-permute-done.4 = f32[4,128]{1,0:T(4,128)S(1)} collective-permute-done((f32[4,128]{1,0:T(4,128)S(1)}, f32[4,128]{1,0:T(4,128)S(1)}, u32[]{:S(2)}, u32[]{:S(2)}) %collective-permute-start.4) | collective-permute-done | bytes 2080 | tf_op jit(solution)/shard_map/ppermute | solution.py:149
  28.2 0.4 collective-permute-done.5
  28.6 0.0 collective-permute-done.6
  28.6 1.7 %collective-permute-start.7 = (f32[16,128]{1,0:T(8,128)S(1)}, f32[16,128]{1,0:T(8,128)S(1)}, u32[]{:S(2)}, u32[]{:S(2)}) collective-permute-start(f32[16,128]{1,0:T(8,128)S(1)} %concatenate.15), channel_id=1, source_target_pairs={{0,32},{4,36},{8,40},{12,44},{16,48},{20,52},{24,56},{28,60},{32,0... | collective-permute-start | bytes 24584 | tf_op jit(solution)/shard_map/ppermute | solution.py:143
  30.3 0.0 copy-done.5
  30.3 2.9 %filter_spectra.1.filt_hbm = f32[8,2,256,128]{3,2,1,0:T(8,128)} custom-call(s32[1]{0:T(128)} %bitcast.1.where_ref, bf16[1,2048,2048]{2,1,0:T(8,128)(2,1)} %taps_ref.1, bf16[512,256]{1,0:T(8,128)(2,1)} %constant.84.clone.enter.enter_hbm), custom_call_target="tpu_custom_call" | custom-call | tf_op jit(solution)/shard_map/filter_spectra/pallas_call | solution.py:222
  33.2 0.0 copy-start.3
  33.2 2.6 %early.1.known_ref = f32[16,256]{1,0:T(8,128)S(1)} custom-call(f32[8,128]{1,0:T(8,128)S(1)} %add_add_fusion.sums_ref, bf16[1,128,2048]{2,1,0:T(8,128)(2,1)} %saved_ref.5, bf16[1,128,2048]{2,1,0:T(8,128)(2,1)} %sconv_ref.3, bf16[1,128,2048]{2,1,0:T(8,128)(2,1)} %cot_ref.3), custom_call_target="tpu_custom_call" | custom-call | tf_op jit(solution)/shard_map/early/pallas_call | solution.py:183
  35.9 0.0 collective-permute-done.7
  36.0 0.0 all-to-all-done.raw_hbm
  36.0 0.0 copy-start.4
  36.0 1.1 %copy-done.4 = bf16[16,384,128]{2,1,0:T(8,128)(2,1)} copy-done((bf16[16,384,128]{2,1,0:T(8,128)(2,1)}, bf16[16,384,128]{2,1,0:T(8,128)(2,1)S(1)}, u32[]{:S(2)}) %copy-start.4) | copy-done | bytes 1572888
  37.1 0.0 copy-done.3
  37.1 7.9 %convolve.1 = bf16[16,152,256]{2,1,0:T(8,128)(2,1)} custom-call(s32[1]{0:T(128)} %bitcast.1.where_ref, s32[16]{0:T(128)S(1)} %copy-done.3, s32[16]{0:T(128)S(1)} %fusion.4.gathered_ref, f32[32,128]{1,0:T(8,128)S(1)} %add_rsqrt_fusion.inv_ref, f32[16,256]{1,0:T(8,128)S(1)} %early.1.known_ref, f32[1,7,2048]{2,1,0:T(8,128)S(1)} %copy.13.params_ref, ...), custom_call_target="tpu_custom_call" | custom-call | tf_op jit(solution)/shard_map/convolve/pallas_call | solution.py:389
  45.1 0.0 copy-start
  45.1 0.0 copy-start.1
  45.1 0.0 copy-start.2
  45.1 5.2 %all-to-all-start.1 = ((bf16[16,152,256]{2,1,0:T(8,128)(2,1)}), bf16[16,152,256]{2,1,0:T(8,128)(2,1)S(1)}, u32[]{:S(2)}, u32[]{:S(2)}) async-start(bf16[16,152,256]{2,1,0:T(8,128)(2,1)} %convolve.1), calls=%async_computation.1 | async-start | bytes 2490368 | tf_op jit(solution)/shard_map/all_to_all | solution.py:638
  50.3 0.0 copy-done
  50.3 1.3 %collective-permute-start.12 = (bf16[1,128,2048]{2,1,0:T(8,128)(2,1)S(1)}, bf16[1,128,2048]{2,1,0:T(8,128)(2,1)S(1)}, u32[]{:S(2)}, u32[]{:S(2)}) collective-permute-start(bf16[1,128,2048]{2,1,0:T(8,128)(2,1)S(1)} %copy-done), channel_id=1, source_target_pairs={{64,0},{65,1},{66,2},{67,3},{68,4},{69,5},{70,6},{71,7},{72,8},{73... | collective-permute-start | bytes 1572872 | tf_op jit(solution)/shard_map/ppermute | solution.py:634
  51.6 17.4 %all-to-all-done.1.back_ref = bf16[16,152,256]{2,1,0:T(8,128)(2,1)S(1)} async-done(((bf16[16,152,256]{2,1,0:T(8,128)(2,1)}), bf16[16,152,256]{2,1,0:T(8,128)(2,1)S(1)}, u32[]{:S(2)}, u32[]{:S(2)}) %all-to-all-start.1) | async-done | bytes 1245216 | tf_op jit(solution)/shard_map/all_to_all | solution.py:638
  69.0 0.0 copy-done.1
  69.0 0.0 copy-done.2
  69.0 1.6 %leave.1 = (bf16[1,128,2048]{2,1,0:T(8,128)(2,1)S(1)}, bf16[1,128,2048]{2,1,0:T(8,128)(2,1)S(1)}, f32[8,128]{1,0:T(8,128)S(1)}) custom-call(s32[1]{0:T(128)} %bitcast.pipe_ref, f32[32,128]{1,0:T(8,128)S(1)} %add_rsqrt_fusion.inv_ref, bf16[16,152,256]{2,1,0:T(8,128)(2,1)S(1)} %all-to-all-done.1.back_ref, bf16[1,128,2048]{2,1,0:T(8,128)(2,1)} %fwd_hbm.3, ...), custom_call_target="tpu_custom_call" | custom-call | tf_op jit(solution)/shard_map/leave/pallas_call | solution.py:479
  70.6 3.4 %collective-permute-start.13 = (bf16[1,128,2048]{2,1,0:T(8,128)(2,1)S(1)}, bf16[1,128,2048]{2,1,0:T(8,128)(2,1)S(1)}, u32[]{:S(2)}, u32[]{:S(2)}) collective-permute-start(bf16[1,128,2048]{2,1,0:T(8,128)(2,1)S(1)} %get-tuple-element.15.send_ref), channel_id=1, source_target_pairs={{0,64},{64,0},{1,65},{65,1},{2,66},{66,2},{3,67},{67,3},{4,68},{68... | collective-permute-start | bytes 1572872 | tf_op jit(solution)/shard_map/ppermute | solution.py:643
  74.0 1.3 %collective-permute-start.8 = (f32[8,128]{1,0:T(8,128)S(1)}, f32[8,128]{1,0:T(8,128)S(1)}, u32[]{:S(2)}, u32[]{:S(2)}) collective-permute-start(f32[8,128]{1,0:T(8,128)S(1)} %get-tuple-element.18), channel_id=1, source_target_pairs={{64,0},{65,1},{66,2},{67,3},{68,4},{69,5},{70,6},{71,7},{72,8},{73... | collective-permute-start | bytes 12296 | tf_op jit(solution)/shard_map/ppermute | solution.py:642
  75.3 15.2 %collective-permute-done.8 = f32[8,128]{1,0:T(8,128)S(1)} collective-permute-done((f32[8,128]{1,0:T(8,128)S(1)}, f32[8,128]{1,0:T(8,128)S(1)}, u32[]{:S(2)}, u32[]{:S(2)}) %collective-permute-start.8) | collective-permute-done | bytes 4128 | tf_op jit(solution)/shard_map/ppermute | solution.py:642
  90.5 4.0 %collective-permute-start.10 = (f32[8,128]{1,0:T(8,128)S(1)}, f32[8,128]{1,0:T(8,128)S(1)}, u32[]{:S(2)}, u32[]{:S(2)}) collective-permute-start(f32[8,128]{1,0:T(8,128)S(1)} %pad_maximum_fusion.s0), channel_id=1, source_target_pairs={{0,2},{1,3},{2,0},{3,1},{4,6},{5,7},{6,4},{7,5},{8,10},{9,11},{10,... | collective-permute-start | bytes 12296 | tf_op jit(solution)/shard_map/ppermute | solution.py:136
  94.4 0.7 collective-permute-start.11
  95.2 1.3 %collective-permute-start.9 = (f32[8,128]{1,0:T(8,128)S(1)}, f32[8,128]{1,0:T(8,128)S(1)}, u32[]{:S(2)}, u32[]{:S(2)}) collective-permute-start(f32[8,128]{1,0:T(8,128)S(1)} %pad_maximum_fusion.s0), channel_id=1, source_target_pairs={{0,1},{1,2},{2,3},{3,0},{4,5},{5,6},{6,7},{7,4},{8,9},{9,10},{10,1... | collective-permute-start | bytes 12296 | tf_op jit(solution)/shard_map/ppermute | solution.py:136
  96.5 0.8 finish_rows.1
  97.3 0.7 copy.16
  98.0 0.0 collective-permute-done.12.peer_ref
  98.0 0.0 collective-permute-done.10.s2
  98.0 0.1 collective-permute-done.11.s3
  98.0 1.9 %collective-permute-done.9.s1 = f32[8,128]{1,0:T(8,128)S(1)} collective-permute-done((f32[8,128]{1,0:T(8,128)S(1)}, f32[8,128]{1,0:T(8,128)S(1)}, u32[]{:S(2)}, u32[]{:S(2)}) %collective-permute-start.9) | collective-permute-done | bytes 4128 | tf_op jit(solution)/shard_map/ppermute | solution.py:136
  100.0 2.1 %finish_cross.1 = (bf16[1,128,2048]{2,1,0:T(8,128)(2,1)}, f32[128,2048]{1,0:T(8,128)S(1)}) custom-call(s32[1]{0:T(128)} %bitcast.pipe_ref, f32[8,128]{1,0:T(8,128)S(1)} %pad_maximum_fusion.s0, f32[8,128]{1,0:T(8,128)S(1)} %collective-permute-done.9.s1, f32[8,128]{1,0:T(8,128)S(1)} %collective-permute-done.10.s2, f32[8,128]{1,0:T(8,128)S(1)} %collective-permute-done.11.s3, ...), custom_call_target="tpu_custom_call" | custom-call | tf_op jit(solution)/shard_map/finish_cross/pallas_call | solution.py:586
  102.0 0.0 collective-permute-done.13.value_ref
  102.0 1.5 %received.1 = bf16[1,128,2048]{2,1,0:T(8,128)(2,1)} custom-call(bf16[1,128,2048]{2,1,0:T(8,128)(2,1)S(1)} %collective-permute-done.13.value_ref, f32[128,2048]{1,0:T(8,128)S(1)} %get-tuple-element.21.term_ref), custom_call_target="tpu_custom_call" | custom-call | tf_op jit(solution)/shard_map/received/pallas_call | solution.py:613
  (11 shorter events, 0.2 us)
Async XLA Ops:
  3.3 27.0 %copy-start.5 = (f32[1,7,2048]{2,0,1:T(1,128)S(1)}, f32[1,7,2048]{2,0,1:T(1,128)}, u32[]{:S(2)}) copy-start(f32[1,7,2048]{2,0,1:T(1,128)} %param.14) | copy-start | bytes 172036
  3.3 32.6 %all-to-all-start = ((bf16[16,384,128]{2,1,0:T(8,128)(2,1)}), bf16[16,384,128]{2,1,0:T(8,128)(2,1)S(1)}, u32[]{:S(2)}, u32[]{:S(2)}) async-start(bf16[16,384,128]{2,1,0:T(8,128)(2,1)} %get-tuple-element.14), calls=%async_computation | async-start | bytes 3145728 | tf_op jit(solution)/shard_map/all_to_all | solution.py:628
  9.1 6.6 %collective-permute-start = (f32[8,128]{1,0:T(8,128)S(1)}, f32[8,128]{1,0:T(8,128)S(1)}, u32[]{:S(2)}, u32[]{:S(2)}) collective-permute-start(f32[8,128]{1,0:T(8,128)S(1)} %get-tuple-element.13), channel_id=1, source_target_pairs={{0,1},{1,2},{2,3},{3,0},{4,5},{5,6},{6,7},{7,4},{8,9},{9,10},{10,1... | collective-permute-start | bytes 12296 | tf_op jit(solution)/shard_map/ppermute | solution.py:136
  11.1 5.2 %collective-permute-start.1 = (f32[8,128]{1,0:T(8,128)S(1)}, f32[8,128]{1,0:T(8,128)S(1)}, u32[]{:S(2)}, u32[]{:S(2)}) collective-permute-start(f32[8,128]{1,0:T(8,128)S(1)} %get-tuple-element.13), channel_id=1, source_target_pairs={{0,2},{1,3},{2,0},{3,1},{4,6},{5,7},{6,4},{7,5},{8,10},{9,11},{10,... | collective-permute-start | bytes 12296 | tf_op jit(solution)/shard_map/ppermute | solution.py:136
  14.7 3.6 %collective-permute-start.2 = (f32[8,128]{1,0:T(8,128)S(1)}, f32[8,128]{1,0:T(8,128)S(1)}, u32[]{:S(2)}, u32[]{:S(2)}) collective-permute-start(f32[8,128]{1,0:T(8,128)S(1)} %get-tuple-element.13), channel_id=1, source_target_pairs={{0,3},{1,0},{2,1},{3,2},{4,7},{5,4},{6,5},{7,6},{8,11},{9,8},{10,9... | collective-permute-start | bytes 12296 | tf_op jit(solution)/shard_map/ppermute | solution.py:136
  18.3 1.2 %collective-permute-start.3 = (f32[2,128]{1,0:T(2,128)S(1)}, f32[2,128]{1,0:T(2,128)S(1)}, u32[]{:S(2)}, u32[]{:S(2)}) collective-permute-start(f32[2,128]{1,0:T(2,128)S(1)} %slice.12), channel_id=1, source_target_pairs={{0,4},{4,0},{8,12},{12,8},{16,20},{20,16},{24,28},{28,24},{32,36},... | collective-permute-start | bytes 3080 | tf_op jit(solution)/shard_map/ppermute | solution.py:143
  19.5 8.8 %collective-permute-start.4 = (f32[4,128]{1,0:T(4,128)S(1)}, f32[4,128]{1,0:T(4,128)S(1)}, u32[]{:S(2)}, u32[]{:S(2)}) collective-permute-start(f32[4,128]{1,0:T(4,128)S(1)} %pad_maximum_fusion.1), channel_id=1, source_target_pairs={{0,8},{4,12},{8,16},{12,20},{16,24},{20,28},{24,0},{28,4},{32,40},... | collective-permute-start | bytes 6152 | tf_op jit(solution)/shard_map/ppermute | solution.py:149
  21.3 7.3 %collective-permute-start.5 = (f32[4,128]{1,0:T(4,128)S(1)}, f32[4,128]{1,0:T(4,128)S(1)}, u32[]{:S(2)}, u32[]{:S(2)}) collective-permute-start(f32[4,128]{1,0:T(4,128)S(1)} %pad_maximum_fusion.1), channel_id=1, source_target_pairs={{0,16},{4,20},{8,24},{12,28},{16,0},{20,4},{24,8},{28,12},{32,48},... | collective-permute-start | bytes 6152 | tf_op jit(solution)/shard_map/ppermute | solution.py:149
  24.0 4.6 %collective-permute-start.6 = (f32[4,128]{1,0:T(4,128)S(1)}, f32[4,128]{1,0:T(4,128)S(1)}, u32[]{:S(2)}, u32[]{:S(2)}) collective-permute-start(f32[4,128]{1,0:T(4,128)S(1)} %pad_maximum_fusion.1), channel_id=1, source_target_pairs={{0,24},{4,28},{8,0},{12,4},{16,8},{20,12},{24,16},{28,20},{32,56},... | collective-permute-start | bytes 6152 | tf_op jit(solution)/shard_map/ppermute | solution.py:149
  28.6 7.3 %collective-permute-start.7 = (f32[16,128]{1,0:T(8,128)S(1)}, f32[16,128]{1,0:T(8,128)S(1)}, u32[]{:S(2)}, u32[]{:S(2)}) collective-permute-start(f32[16,128]{1,0:T(8,128)S(1)} %concatenate.15), channel_id=1, source_target_pairs={{0,32},{4,36},{8,40},{12,44},{16,48},{20,52},{24,56},{28,60},{32,0... | collective-permute-start | bytes 24584 | tf_op jit(solution)/shard_map/ppermute | solution.py:143
  33.2 3.9 %copy-start.3 = (s32[16]{0:T(128)S(1)}, s32[16]{0:T(128)}, u32[]{:S(2)}) copy-start(s32[16]{0:T(128)} %order_ref.1) | copy-start | bytes 196
  36.0 1.1 %copy-start.4 = (bf16[16,384,128]{2,1,0:T(8,128)(2,1)}, bf16[16,384,128]{2,1,0:T(8,128)(2,1)S(1)}, u32[]{:S(2)}) copy-start(bf16[16,384,128]{2,1,0:T(8,128)(2,1)S(1)} %all-to-all-done.raw_hbm) | copy-start | bytes 4718596
  45.1 5.2 %copy-start = (bf16[1,128,2048]{2,1,0:T(8,128)(2,1)S(1)}, bf16[1,128,2048]{2,1,0:T(8,128)(2,1)}, u32[]{:S(2)}) copy-start(bf16[1,128,2048]{2,1,0:T(8,128)(2,1)} %saved_ref.5) | copy-start | bytes 1572868
  45.1 23.9 %copy-start.1 = (bf16[1,128,2048]{2,1,0:T(8,128)(2,1)S(1)}, bf16[1,128,2048]{2,1,0:T(8,128)(2,1)}, u32[]{:S(2)}) copy-start(bf16[1,128,2048]{2,1,0:T(8,128)(2,1)} %cot_ref.3) | copy-start | bytes 1572868
  45.1 23.9 %copy-start.2 = (bf16[1,128,2048]{2,1,0:T(8,128)(2,1)S(1)}, bf16[1,128,2048]{2,1,0:T(8,128)(2,1)}, u32[]{:S(2)}) copy-start(bf16[1,128,2048]{2,1,0:T(8,128)(2,1)} %sconv_ref.3) | copy-start | bytes 1572868
  45.1 23.9 %all-to-all-start.1 = ((bf16[16,152,256]{2,1,0:T(8,128)(2,1)}), bf16[16,152,256]{2,1,0:T(8,128)(2,1)S(1)}, u32[]{:S(2)}, u32[]{:S(2)}) async-start(bf16[16,152,256]{2,1,0:T(8,128)(2,1)} %convolve.1), calls=%async_computation.1 | async-start | bytes 2490368 | tf_op jit(solution)/shard_map/all_to_all | solution.py:638
  50.3 47.7 %collective-permute-start.12 = (bf16[1,128,2048]{2,1,0:T(8,128)(2,1)S(1)}, bf16[1,128,2048]{2,1,0:T(8,128)(2,1)S(1)}, u32[]{:S(2)}, u32[]{:S(2)}) collective-permute-start(bf16[1,128,2048]{2,1,0:T(8,128)(2,1)S(1)} %copy-done), channel_id=1, source_target_pairs={{64,0},{65,1},{66,2},{67,3},{68,4},{69,5},{70,6},{71,7},{72,8},{73... | collective-permute-start | bytes 1572872 | tf_op jit(solution)/shard_map/ppermute | solution.py:634
  70.6 31.4 %collective-permute-start.13 = (bf16[1,128,2048]{2,1,0:T(8,128)(2,1)S(1)}, bf16[1,128,2048]{2,1,0:T(8,128)(2,1)S(1)}, u32[]{:S(2)}, u32[]{:S(2)}) collective-permute-start(bf16[1,128,2048]{2,1,0:T(8,128)(2,1)S(1)} %get-tuple-element.15.send_ref), channel_id=1, source_target_pairs={{0,64},{64,0},{1,65},{65,1},{2,66},{66,2},{3,67},{67,3},{4,68},{68... | collective-permute-start | bytes 1572872 | tf_op jit(solution)/shard_map/ppermute | solution.py:643
  74.0 16.5 %collective-permute-start.8 = (f32[8,128]{1,0:T(8,128)S(1)}, f32[8,128]{1,0:T(8,128)S(1)}, u32[]{:S(2)}, u32[]{:S(2)}) collective-permute-start(f32[8,128]{1,0:T(8,128)S(1)} %get-tuple-element.18), channel_id=1, source_target_pairs={{64,0},{65,1},{66,2},{67,3},{68,4},{69,5},{70,6},{71,7},{72,8},{73... | collective-permute-start | bytes 12296 | tf_op jit(solution)/shard_map/ppermute | solution.py:642
  90.5 7.5 %collective-permute-start.10 = (f32[8,128]{1,0:T(8,128)S(1)}, f32[8,128]{1,0:T(8,128)S(1)}, u32[]{:S(2)}, u32[]{:S(2)}) collective-permute-start(f32[8,128]{1,0:T(8,128)S(1)} %pad_maximum_fusion.s0), channel_id=1, source_target_pairs={{0,2},{1,3},{2,0},{3,1},{4,6},{5,7},{6,4},{7,5},{8,10},{9,11},{10,... | collective-permute-start | bytes 12296 | tf_op jit(solution)/shard_map/ppermute | solution.py:136
  94.4 3.6 %collective-permute-start.11 = (f32[8,128]{1,0:T(8,128)S(1)}, f32[8,128]{1,0:T(8,128)S(1)}, u32[]{:S(2)}, u32[]{:S(2)}) collective-permute-start(f32[8,128]{1,0:T(8,128)S(1)} %pad_maximum_fusion.s0), channel_id=1, source_target_pairs={{0,3},{1,0},{2,1},{3,2},{4,7},{5,4},{6,5},{7,6},{8,11},{9,8},{10,9... | collective-permute-start | bytes 12296 | tf_op jit(solution)/shard_map/ppermute | solution.py:136
  95.2 4.8 %collective-permute-start.9 = (f32[8,128]{1,0:T(8,128)S(1)}, f32[8,128]{1,0:T(8,128)S(1)}, u32[]{:S(2)}, u32[]{:S(2)}) collective-permute-start(f32[8,128]{1,0:T(8,128)S(1)} %pad_maximum_fusion.s0), channel_id=1, source_target_pairs={{0,1},{1,2},{2,3},{3,0},{4,5},{5,6},{6,7},{7,4},{8,9},{9,10},{10,1... | collective-permute-start | bytes 12296 | tf_op jit(solution)/shard_map/ppermute | solution.py:136

commit v7 on v6

--- a/solution.py
+++ b/solution.py
@@ -79,27 +79,25 @@
                 held.at[index, :, pl.ds(step * wide, wide)],
                 in_sem.at[index, step],
             )
-            for index, source in enumerate(sources)
+            for index, source in enumerate(sources[:2])
         ]
         for step in range(steps)
     ]
-    for copies in arriving:
-        for copy in copies:
-            copy.start()
-    leaving = []
+    leaving = [
+        pltpu.make_async_copy(
+            source.at[0, :, pl.ds(group * LANES, LANES)],
+            out_hbm.at[group, pl.ds(index * rows, rows), :],
+            out_sem.at[index, group],
+        )
+        for group in range(width // LANES)
+        for index, source in enumerate(sources)
+    ]
+    for copy in sum(arriving, []) + leaving:
+        copy.start()
     totals = [jnp.zeros((rows, LANES), jnp.float32)] * 2
     for step, copies in enumerate(arriving):
         for index, copy in enumerate(copies):
             copy.wait()
-            for group in range(step * wide // LANES, (step + 1) * wide // LANES):
-                out = pltpu.make_async_copy(
-                    held.at[index, :, pl.ds(group * LANES, LANES)],
-                    out_hbm.at[group, pl.ds(index * rows, rows), :],
-                    out_sem.at[index, group],
-                )
-                out.start()
-                leaving.append(out)
-        for index in range(2):
             for group in range(step * wide // LANES, (step + 1) * wide // LANES):
                 value = held[index, :, group * LANES : (group + 1) * LANES].astype(jnp.float32)
                 totals[index] = totals[index] + value * value
@@ -119,8 +117,8 @@
         in_specs=[HBM] * 3,
         out_specs=(HBM, VMEM),
         scratch_shapes=[
-            pltpu.VMEM((3, rows, width), jnp.bfloat16),
-            pltpu.SemaphoreType.DMA((3, 4)),
+            pltpu.VMEM((2, rows, width), jnp.bfloat16),
+            pltpu.SemaphoreType.DMA((2, 4)),
             pltpu.SemaphoreType.DMA((3, width // LANES)),
         ],
         name="pack",
@@ -155,7 +153,7 @@
     core = (block ^ own) & 1
     back = (own // 2 - block // 2) % 4
     side = (block // 8) ^ (own // 8)
-    return side * 8 + back * 2 + core
+    return back * 4 + side * 2 + core
 
 
 def early_kernel(sums_ref, saved_ref, sconv_ref, cot_ref, out_ref, inv):
@@ -598,24 +596,36 @@
     )(pipe, *scales, in_vmem(send), in_vmem(keep), in_vmem(saved_in), in_vmem(peer_saved))
 
 
-def received_kernel(value_ref, term_ref, out_ref):
-    wide = out_ref.shape[2]
-    for at in range(0, wide, LANES):
-        own = pl.ds(at, LANES)
-        source = pl.ds(pl.multiple_of(pl.program_id(0) * wide + at, LANES), LANES)
-        value = value_ref[0, :, source].astype(jnp.float32)
-        out_ref[0, :, own] = (value - term_ref[:, source]).astype(jnp.bfloat16)
+def received_kernel(value_ref, term_ref, out_hbm, out_ref, out_sem):
+    steps = out_sem.shape[0]
+    wide = out_ref.shape[1] // steps
+    copies = []
+    for step in range(steps):
+        for at in range(step * wide, (step + 1) * wide, LANES):
+            own = pl.ds(at, LANES)
+            value = value_ref[0, :, own].astype(jnp.float32)
+            out_ref[:, own] = (value - term_ref[:, own]).astype(jnp.bfloat16)
+        chunk = pl.ds(step * wide, wide)
+        copy = pltpu.make_async_copy(
+            out_ref.at[:, chunk], out_hbm.at[0, :, chunk], out_sem.at[step]
+        )
+        copy.start()
+        copies.append(copy)
+    for copy in copies:
+        copy.wait()
 
 
 def finish_received(value, term):
     rows, width = term.shape
-    wide = 512
     return pl.pallas_call(
         received_kernel,
-        out_shape=jax.ShapeDtypeStruct(value.shape, jnp.bfloat16),
-        grid=(width // wide,),
+        out_shape=pltpu.HBM(value.shape, jnp.bfloat16),
         in_specs=[VMEM, VMEM],
-        out_specs=lane_spec(rows, wide),
+        out_specs=HBM,
+        scratch_shapes=[
+            pltpu.VMEM((rows, width), jnp.bfloat16),
+            pltpu.SemaphoreType.DMA((8,)),
+        ],
         name="received",
         compiler_params=pltpu.CompilerParams(vmem_limit_bytes=8 << 20),
     )(in_vmem(value), in_vmem(term))
@@ -629,8 +639,9 @@
     own_sums = sum(over_chan(sums))
     sums = own_sums[:2]
     sums = jnp.concatenate([sums, across(sums, 1)], axis=0)
+    sums = jnp.concatenate([sums, across(sums, 8)], axis=0)
     sums = jnp.concatenate([sums] + [round_ring(sums, apart) for apart in (1, 2, 3)], axis=0)
-    inv = lax.rsqrt(jnp.concatenate([sums, across(sums, 8)], axis=0) / D + EPSILON)
+    inv = lax.rsqrt(sums / D + EPSILON)
     peer_saved = lax.ppermute(saved_in, "pipe", [(1, 0)])
     spectra = filter_spectra(where, filters, tables)
     known = early(own_sums, saved_in, saved_conv, grad_out)

time: 104 us -> 154 us (1.48)
  Pallas kernels: 22.2 us -> 68.1 us
  waiting for transfers between devices: 41.4 us -> 46.1 us
    pallas_call x1, Pallas kernels: 2.69 us -> 49.3 us  [pack(): pl.pallas_call(pack_kernel, out_shape=(pltpu.HBM((width // LANES, 3 * row...]
    ppermute x2, waiting for transfers between devices: 1.16 us -> 9.02 us  [across(): lax.ppermute(rows, 'seq', [(low, low ^ flip) for low in range(count)])]
    ppermute x3, waiting for transfers between devices: 3.13 us -> 0.01 us  [round_ring(): lax.ppermute(rows, 'seq', [(low, place(low)) for low in range(count)])]
  transfers between devices with their start and end apart: 16 -> 16, of which waited for: 9 -> 8; matrix products, arithmetic and copies ran while one was open for 1% -> 1% of each run, Pallas kernels for 10% -> 7%
where the time goes in v7:
time: 154 us; the launch traced here: 153 us
  Pallas kernels  68.1 us (44%)
  waiting for transfers between devices  46.1 us (30%)
  starting transfers between devices  36.2 us (24%)
  local copies, waits for them, and re-layouts  1.89 us (1%)
    pallas_call x1, Pallas kernels, pack(): pl.pallas_call(pack_kernel, out_shape=(pltpu.HBM((width // LANES, 3 * row...  49.3 us
    all_to_all x1, waiting for transfers between devices, per_device(): back = lax.all_to_all(back, 'seq', 0, 0)  17.3 us
    ppermute x1, waiting for transfers between devices, per_device(): peer_cross = lax.ppermute(cross, 'pipe', [(1, 0)])  15.1 us
    ppermute x6, starting transfers between devices, over_chan(): lax.ppermute(rows, 'chan', [(low, (low + apart) % count) for low in range...  12.6 us
    ppermute x2, waiting for transfers between devices, across(): lax.ppermute(rows, 'seq', [(low, low ^ flip) for low in range(count)])  9.02 us
    pallas_call x1, Pallas kernels, convolve(): pl.pallas_call(conv_kernel, out_shape=pltpu.HBM((stored, rows + 24, 2 * L...  7.95 us
    ppermute x3, starting transfers between devices, round_ring(): lax.ppermute(rows, 'seq', [(low, place(low)) for low in range(count)])  6.22 us
    all_to_all x1, starting transfers between devices, per_device(): raw = lax.all_to_all(raw, 'seq', 0, 0)  5.76 us
  transfers between devices with their start and end apart: 16, of which 8 were waited for; matrix products, arithmetic and copies ran while one was open for 1% of the time, Pallas kernels for 7%

profile of v7, /device:TPU:0, one launch (start us, length us, event | category | flops | bytes accessed | tf_op | source)
XLA Modules:
  0.0 153.2 jit_solution(10464350547652291532)
XLA Ops:
  0.6 49.3 %pack.1 = (bf16[16,384,128]{2,1,0:T(8,128)(2,1)}, f32[8,128]{1,0:T(8,128)S(1)}) custom-call(bf16[1,128,2048]{2,1,0:T(8,128)(2,1)} %fwd_hbm.3, bf16[1,128,2048]{2,1,0:T(8,128)(2,1)} %saved_ref.5, bf16[1,128,2048]{2,1,0:T(8,128)(2,1)} %cot_ref.3), custom_call_target="tpu_custom_call" | custom-call | tf_op jit(solution)/shard_map/pack/pallas_call | solution.py:111
  49.9 0.0 copy-start.5
  49.9 5.8 %all-to-all-start = ((bf16[16,384,128]{2,1,0:T(8,128)(2,1)}), bf16[16,384,128]{2,1,0:T(8,128)(2,1)S(1)}, u32[]{:S(2)}, u32[]{:S(2)}) async-start(bf16[16,384,128]{2,1,0:T(8,128)(2,1)} %get-tuple-element.14), calls=%async_computation | async-start | bytes 3145728 | tf_op jit(solution)/shard_map/all_to_all | solution.py:638
  55.7 2.0 %collective-permute-start = (f32[8,128]{1,0:T(8,128)S(1)}, f32[8,128]{1,0:T(8,128)S(1)}, u32[]{:S(2)}, u32[]{:S(2)}) collective-permute-start(f32[8,128]{1,0:T(8,128)S(1)} %get-tuple-element.13), channel_id=1, source_target_pairs={{0,1},{1,2},{2,3},{3,0},{4,5},{5,6},{6,7},{7,4},{8,9},{9,10},{10,1... | collective-permute-start | bytes 12296 | tf_op jit(solution)/shard_map/ppermute | solution.py:134
  57.7 3.6 %collective-permute-start.1 = (f32[8,128]{1,0:T(8,128)S(1)}, f32[8,128]{1,0:T(8,128)S(1)}, u32[]{:S(2)}, u32[]{:S(2)}) collective-permute-start(f32[8,128]{1,0:T(8,128)S(1)} %get-tuple-element.13), channel_id=1, source_target_pairs={{0,2},{1,3},{2,0},{3,1},{4,6},{5,7},{6,4},{7,5},{8,10},{9,11},{10,... | collective-permute-start | bytes 12296 | tf_op jit(solution)/shard_map/ppermute | solution.py:134
  61.2 1.0 collective-permute-start.2
  62.3 0.0 collective-permute-done
  62.3 0.6 collective-permute-done.1
  62.9 2.0 %collective-permute-done.2 = f32[8,128]{1,0:T(8,128)S(1)} collective-permute-done((f32[8,128]{1,0:T(8,128)S(1)}, f32[8,128]{1,0:T(8,128)S(1)}, u32[]{:S(2)}, u32[]{:S(2)}) %collective-permute-start.2) | collective-permute-done | bytes 4128 | tf_op jit(solution)/shard_map/ppermute | solution.py:134
  64.9 0.0 collective-permute-start.3
  64.9 1.2 collective-permute-done.3
  66.0 1.9 %collective-permute-start.4 = (f32[4,128]{1,0:T(4,128)S(1)}, f32[4,128]{1,0:T(4,128)S(1)}, u32[]{:S(2)}, u32[]{:S(2)}) collective-permute-start(f32[4,128]{1,0:T(4,128)S(1)} %pad_maximum_fusion.2), channel_id=1, source_target_pairs={{0,32},{4,36},{8,40},{12,44},{16,48},{20,52},{24,56},{28,60},{32,0... | collective-permute-start | bytes 6152 | tf_op jit(solution)/shard_map/ppermute | solution.py:141
  67.9 7.9 %collective-permute-done.4 = f32[4,128]{1,0:T(4,128)S(1)} collective-permute-done((f32[4,128]{1,0:T(4,128)S(1)}, f32[4,128]{1,0:T(4,128)S(1)}, u32[]{:S(2)}, u32[]{:S(2)}) %collective-permute-start.4) | collective-permute-done | bytes 2080 | tf_op jit(solution)/shard_map/ppermute | solution.py:141
  75.8 3.1 %collective-permute-start.5 = (f32[8,128]{1,0:T(8,128)S(1)}, f32[8,128]{1,0:T(8,128)S(1)}, u32[]{:S(2)}, u32[]{:S(2)}) collective-permute-start(f32[8,128]{1,0:T(8,128)S(1)} %pad_maximum_fusion), channel_id=1, source_target_pairs={{0,8},{4,12},{8,16},{12,20},{16,24},{20,28},{24,0},{28,4},{32,40},... | collective-permute-start | bytes 12296 | tf_op jit(solution)/shard_map/ppermute | solution.py:147
  78.8 1.2 collective-permute-start.6
  80.1 1.9 %collective-permute-start.7 = (f32[8,128]{1,0:T(8,128)S(1)}, f32[8,128]{1,0:T(8,128)S(1)}, u32[]{:S(2)}, u32[]{:S(2)}) collective-permute-start(f32[8,128]{1,0:T(8,128)S(1)} %pad_maximum_fusion), channel_id=1, source_target_pairs={{0,24},{4,28},{8,0},{12,4},{16,8},{20,12},{24,16},{28,20},{32,56},... | collective-permute-start | bytes 12296 | tf_op jit(solution)/shard_map/ppermute | solution.py:147
  82.0 0.0 copy-done.5
  82.0 2.9 %filter_spectra.1.filt_hbm = f32[8,2,256,128]{3,2,1,0:T(8,128)} custom-call(s32[1]{0:T(128)} %bitcast.1.where_ref, bf16[1,2048,2048]{2,1,0:T(8,128)(2,1)} %taps_ref.1, bf16[512,256]{1,0:T(8,128)(2,1)} %constant.83.clone.enter.enter_hbm), custom_call_target="tpu_custom_call" | custom-call | tf_op jit(solution)/shard_map/filter_spectra/pallas_call | solution.py:220
  84.9 0.0 copy-start.3
  85.0 2.6 %early.1.known_ref = f32[16,256]{1,0:T(8,128)S(1)} custom-call(f32[8,128]{1,0:T(8,128)S(1)} %add_add_fusion.sums_ref, bf16[1,128,2048]{2,1,0:T(8,128)(2,1)} %saved_ref.5, bf16[1,128,2048]{2,1,0:T(8,128)(2,1)} %sconv_ref.3, bf16[1,128,2048]{2,1,0:T(8,128)(2,1)} %cot_ref.3), custom_call_target="tpu_custom_call" | custom-call | tf_op jit(solution)/shard_map/early/pallas_call | solution.py:181
  87.6 0.0 collective-permute-done.5
  87.6 0.0 collective-permute-done.6
  87.6 0.0 collective-permute-done.7
  87.7 0.0 all-to-all-done.raw_hbm
  87.7 0.0 copy-start.4
  87.7 1.1 copy-done.4
  88.8 0.0 copy-done.3
  88.8 7.9 %convolve.1 = bf16[16,152,256]{2,1,0:T(8,128)(2,1)} custom-call(s32[1]{0:T(128)} %bitcast.1.where_ref, s32[16]{0:T(128)S(1)} %copy-done.3, s32[16]{0:T(128)S(1)} %fusion.3.gathered_ref, f32[32,128]{1,0:T(8,128)S(1)} %add_rsqrt_fusion.inv_ref, f32[16,256]{1,0:T(8,128)S(1)} %early.1.known_ref, f32[1,7,2048]{2,1,0:T(8,128)S(1)} %copy.13.params_ref, ...), custom_call_target="tpu_custom_call" | custom-call | tf_op jit(solution)/shard_map/convolve/pallas_call | solution.py:387
  96.8 0.0 copy-start
  96.8 0.0 copy-start.1
  96.8 0.0 copy-start.2
  96.8 3.8 %all-to-all-start.1 = ((bf16[16,152,256]{2,1,0:T(8,128)(2,1)}), bf16[16,152,256]{2,1,0:T(8,128)(2,1)S(1)}, u32[]{:S(2)}, u32[]{:S(2)}) async-start(bf16[16,152,256]{2,1,0:T(8,128)(2,1)} %convolve.1), calls=%async_computation.1 | async-start | bytes 2490368 | tf_op jit(solution)/shard_map/all_to_all | solution.py:649
  100.7 0.0 copy-done
  100.7 1.3 collective-permute-start.12
  102.0 17.3 %all-to-all-done.1.back_ref = bf16[16,152,256]{2,1,0:T(8,128)(2,1)S(1)} async-done(((bf16[16,152,256]{2,1,0:T(8,128)(2,1)}), bf16[16,152,256]{2,1,0:T(8,128)(2,1)S(1)}, u32[]{:S(2)}, u32[]{:S(2)}) %all-to-all-start.1) | async-done | bytes 1245216 | tf_op jit(solution)/shard_map/all_to_all | solution.py:649
  119.3 0.0 copy-done.1
  119.3 0.0 copy-done.2
  119.3 1.6 %leave.1 = (bf16[1,128,2048]{2,1,0:T(8,128)(2,1)S(1)}, bf16[1,128,2048]{2,1,0:T(8,128)(2,1)S(1)}, f32[8,128]{1,0:T(8,128)S(1)}) custom-call(s32[1]{0:T(128)} %bitcast.pipe_ref, f32[32,128]{1,0:T(8,128)S(1)} %add_rsqrt_fusion.inv_ref, bf16[16,152,256]{2,1,0:T(8,128)(2,1)S(1)} %all-to-all-done.1.back_ref, bf16[1,128,2048]{2,1,0:T(8,128)(2,1)} %fwd_hbm.3, ...), custom_call_target="tpu_custom_call" | custom-call | tf_op jit(solution)/shard_map/leave/pallas_call | solution.py:477
  121.0 3.4 %collective-permute-start.13 = (bf16[1,128,2048]{2,1,0:T(8,128)(2,1)S(1)}, bf16[1,128,2048]{2,1,0:T(8,128)(2,1)S(1)}, u32[]{:S(2)}, u32[]{:S(2)}) collective-permute-start(bf16[1,128,2048]{2,1,0:T(8,128)(2,1)S(1)} %get-tuple-element.15.send_ref), channel_id=1, source_target_pairs={{0,64},{64,0},{1,65},{65,1},{2,66},{66,2},{3,67},{67,3},{4,68},{68... | collective-permute-start | bytes 1572872 | tf_op jit(solution)/shard_map/ppermute | solution.py:654
  124.3 1.3 collective-permute-start.8
  125.6 15.1 %collective-permute-done.8 = f32[8,128]{1,0:T(8,128)S(1)} collective-permute-done((f32[8,128]{1,0:T(8,128)S(1)}, f32[8,128]{1,0:T(8,128)S(1)}, u32[]{:S(2)}, u32[]{:S(2)}) %collective-permute-start.8) | collective-permute-done | bytes 4128 | tf_op jit(solution)/shard_map/ppermute | solution.py:653
  140.7 4.0 %collective-permute-start.10 = (f32[8,128]{1,0:T(8,128)S(1)}, f32[8,128]{1,0:T(8,128)S(1)}, u32[]{:S(2)}, u32[]{:S(2)}) collective-permute-start(f32[8,128]{1,0:T(8,128)S(1)} %pad_maximum_fusion.1.s0), channel_id=1, source_target_pairs={{0,2},{1,3},{2,0},{3,1},{4,6},{5,7},{6,4},{7,5},{8,10},{9,11},{10,... | collective-permute-start | bytes 12296 | tf_op jit(solution)/shard_map/ppermute | solution.py:134
  144.7 0.7 collective-permute-start.11
  145.4 1.3 collective-permute-start.9
  146.7 0.8 finish_rows.1
  147.5 0.7 copy.16
  148.2 0.0 collective-permute-done.12.peer_ref
  148.2 0.0 collective-permute-done.10.s2
  148.2 0.1 collective-permute-done.11.s3
  148.3 1.9 %collective-permute-done.9.s1 = f32[8,128]{1,0:T(8,128)S(1)} collective-permute-done((f32[8,128]{1,0:T(8,128)S(1)}, f32[8,128]{1,0:T(8,128)S(1)}, u32[]{:S(2)}, u32[]{:S(2)}) %collective-permute-start.9) | collective-permute-done | bytes 4128 | tf_op jit(solution)/shard_map/ppermute | solution.py:134
  150.2 2.1 %finish_cross.1 = (bf16[1,128,2048]{2,1,0:T(8,128)(2,1)}, f32[128,2048]{1,0:T(8,128)S(1)}) custom-call(s32[1]{0:T(128)} %bitcast.pipe_ref, f32[8,128]{1,0:T(8,128)S(1)} %pad_maximum_fusion.1.s0, f32[8,128]{1,0:T(8,128)S(1)} %collective-permute-done.9.s1, f32[8,128]{1,0:T(8,128)S(1)} %collective-permute-done.10.s2, f32[8,128]{1,0:T(8,128)S(1)} %collective-permute-done.11.s3, ...), custom_call_target="tpu_custom_call" | custom-call | tf_op jit(solution)/shard_map/finish_cross/pallas_call | solution.py:584
  152.3 0.0 collective-permute-done.13.value_ref
  152.3 0.9 received.1
  (11 shorter events, 0.1 us)
Async XLA Ops:
  49.9 32.1 %copy-start.5 = (f32[1,7,2048]{2,0,1:T(1,128)S(1)}, f32[1,7,2048]{2,0,1:T(1,128)}, u32[]{:S(2)}) copy-start(f32[1,7,2048]{2,0,1:T(1,128)} %param.14) | copy-start | bytes 172036
  49.9 37.8 %all-to-all-start = ((bf16[16,384,128]{2,1,0:T(8,128)(2,1)}), bf16[16,384,128]{2,1,0:T(8,128)(2,1)S(1)}, u32[]{:S(2)}, u32[]{:S(2)}) async-start(bf16[16,384,128]{2,1,0:T(8,128)(2,1)} %get-tuple-element.14), calls=%async_computation | async-start | bytes 3145728 | tf_op jit(solution)/shard_map/all_to_all | solution.py:638
  55.7 6.6 %collective-permute-start = (f32[8,128]{1,0:T(8,128)S(1)}, f32[8,128]{1,0:T(8,128)S(1)}, u32[]{:S(2)}, u32[]{:S(2)}) collective-permute-start(f32[8,128]{1,0:T(8,128)S(1)} %get-tuple-element.13), channel_id=1, source_target_pairs={{0,1},{1,2},{2,3},{3,0},{4,5},{5,6},{6,7},{7,4},{8,9},{9,10},{10,1... | collective-permute-start | bytes 12296 | tf_op jit(solution)/shard_map/ppermute | solution.py:134
  57.7 5.2 %collective-permute-start.1 = (f32[8,128]{1,0:T(8,128)S(1)}, f32[8,128]{1,0:T(8,128)S(1)}, u32[]{:S(2)}, u32[]{:S(2)}) collective-permute-start(f32[8,128]{1,0:T(8,128)S(1)} %get-tuple-element.13), channel_id=1, source_target_pairs={{0,2},{1,3},{2,0},{3,1},{4,6},{5,7},{6,4},{7,5},{8,10},{9,11},{10,... | collective-permute-start | bytes 12296 | tf_op jit(solution)/shard_map/ppermute | solution.py:134
  61.2 3.6 %collective-permute-start.2 = (f32[8,128]{1,0:T(8,128)S(1)}, f32[8,128]{1,0:T(8,128)S(1)}, u32[]{:S(2)}, u32[]{:S(2)}) collective-permute-start(f32[8,128]{1,0:T(8,128)S(1)} %get-tuple-element.13), channel_id=1, source_target_pairs={{0,3},{1,0},{2,1},{3,2},{4,7},{5,4},{6,5},{7,6},{8,11},{9,8},{10,9... | collective-permute-start | bytes 12296 | tf_op jit(solution)/shard_map/ppermute | solution.py:134
  64.9 1.2 collective-permute-start.3
  66.0 9.7 %collective-permute-start.4 = (f32[4,128]{1,0:T(4,128)S(1)}, f32[4,128]{1,0:T(4,128)S(1)}, u32[]{:S(2)}, u32[]{:S(2)}) collective-permute-start(f32[4,128]{1,0:T(4,128)S(1)} %pad_maximum_fusion.2), channel_id=1, source_target_pairs={{0,32},{4,36},{8,40},{12,44},{16,48},{20,52},{24,56},{28,60},{32,0... | collective-permute-start | bytes 6152 | tf_op jit(solution)/shard_map/ppermute | solution.py:141
  75.8 11.8 %collective-permute-start.5 = (f32[8,128]{1,0:T(8,128)S(1)}, f32[8,128]{1,0:T(8,128)S(1)}, u32[]{:S(2)}, u32[]{:S(2)}) collective-permute-start(f32[8,128]{1,0:T(8,128)S(1)} %pad_maximum_fusion), channel_id=1, source_target_pairs={{0,8},{4,12},{8,16},{12,20},{16,24},{20,28},{24,0},{28,4},{32,40},... | collective-permute-start | bytes 12296 | tf_op jit(solution)/shard_map/ppermute | solution.py:147
  78.8 8.8 %collective-permute-start.6 = (f32[8,128]{1,0:T(8,128)S(1)}, f32[8,128]{1,0:T(8,128)S(1)}, u32[]{:S(2)}, u32[]{:S(2)}) collective-permute-start(f32[8,128]{1,0:T(8,128)S(1)} %pad_maximum_fusion), channel_id=1, source_target_pairs={{0,16},{4,20},{8,24},{12,28},{16,0},{20,4},{24,8},{28,12},{32,48},... | collective-permute-start | bytes 12296 | tf_op jit(solution)/shard_map/ppermute | solution.py:147
  80.1 7.6 %collective-permute-start.7 = (f32[8,128]{1,0:T(8,128)S(1)}, f32[8,128]{1,0:T(8,128)S(1)}, u32[]{:S(2)}, u32[]{:S(2)}) collective-permute-start(f32[8,128]{1,0:T(8,128)S(1)} %pad_maximum_fusion), channel_id=1, source_target_pairs={{0,24},{4,28},{8,0},{12,4},{16,8},{20,12},{24,16},{28,20},{32,56},... | collective-permute-start | bytes 12296 | tf_op jit(solution)/shard_map/ppermute | solution.py:147
  84.9 3.9 %copy-start.3 = (s32[16]{0:T(128)S(1)}, s32[16]{0:T(128)}, u32[]{:S(2)}) copy-start(s32[16]{0:T(128)} %order_ref.1) | copy-start | bytes 196
  87.7 1.1 copy-start.4
  96.8 3.9 %copy-start = (bf16[1,128,2048]{2,1,0:T(8,128)(2,1)S(1)}, bf16[1,128,2048]{2,1,0:T(8,128)(2,1)}, u32[]{:S(2)}) copy-start(bf16[1,128,2048]{2,1,0:T(8,128)(2,1)} %saved_ref.5) | copy-start | bytes 1572868
  96.8 22.5 %copy-start.1 = (bf16[1,128,2048]{2,1,0:T(8,128)(2,1)S(1)}, bf16[1,128,2048]{2,1,0:T(8,128)(2,1)}, u32[]{:S(2)}) copy-start(bf16[1,128,2048]{2,1,0:T(8,128)(2,1)} %cot_ref.3) | copy-start | bytes 1572868
  96.8 22.5 %copy-start.2 = (bf16[1,128,2048]{2,1,0:T(8,128)(2,1)S(1)}, bf16[1,128,2048]{2,1,0:T(8,128)(2,1)}, u32[]{:S(2)}) copy-start(bf16[1,128,2048]{2,1,0:T(8,128)(2,1)} %sconv_ref.3) | copy-start | bytes 1572868
  96.8 22.5 %all-to-all-start.1 = ((bf16[16,152,256]{2,1,0:T(8,128)(2,1)}), bf16[16,152,256]{2,1,0:T(8,128)(2,1)S(1)}, u32[]{:S(2)}, u32[]{:S(2)}) async-start(bf16[16,152,256]{2,1,0:T(8,128)(2,1)} %convolve.1), calls=%async_computation.1 | async-start | bytes 2490368 | tf_op jit(solution)/shard_map/all_to_all | solution.py:649
  100.7 47.5 %collective-permute-start.12 = (bf16[1,128,2048]{2,1,0:T(8,128)(2,1)S(1)}, bf16[1,128,2048]{2,1,0:T(8,128)(2,1)S(1)}, u32[]{:S(2)}, u32[]{:S(2)}) collective-permute-start(bf16[1,128,2048]{2,1,0:T(8,128)(2,1)S(1)} %copy-done), channel_id=1, source_target_pairs={{64,0},{65,1},{66,2},{67,3},{68,4},{69,5},{70,6},{71,7},{72,8},{73... | collective-permute-start | bytes 1572872 | tf_op jit(solution)/shard_map/ppermute | solution.py:645
  121.0 31.3 %collective-permute-start.13 = (bf16[1,128,2048]{2,1,0:T(8,128)(2,1)S(1)}, bf16[1,128,2048]{2,1,0:T(8,128)(2,1)S(1)}, u32[]{:S(2)}, u32[]{:S(2)}) collective-permute-start(bf16[1,128,2048]{2,1,0:T(8,128)(2,1)S(1)} %get-tuple-element.15.send_ref), channel_id=1, source_target_pairs={{0,64},{64,0},{1,65},{65,1},{2,66},{66,2},{3,67},{67,3},{4,68},{68... | collective-permute-start | bytes 1572872 | tf_op jit(solution)/shard_map/ppermute | solution.py:654
  124.3 16.4 %collective-permute-start.8 = (f32[8,128]{1,0:T(8,128)S(1)}, f32[8,128]{1,0:T(8,128)S(1)}, u32[]{:S(2)}, u32[]{:S(2)}) collective-permute-start(f32[8,128]{1,0:T(8,128)S(1)} %get-tuple-element.18), channel_id=1, source_target_pairs={{64,0},{65,1},{66,2},{67,3},{68,4},{69,5},{70,6},{71,7},{72,8},{73... | collective-permute-start | bytes 12296 | tf_op jit(solution)/shard_map/ppermute | solution.py:653
  140.7 7.5 %collective-permute-start.10 = (f32[8,128]{1,0:T(8,128)S(1)}, f32[8,128]{1,0:T(8,128)S(1)}, u32[]{:S(2)}, u32[]{:S(2)}) collective-permute-start(f32[8,128]{1,0:T(8,128)S(1)} %pad_maximum_fusion.1.s0), channel_id=1, source_target_pairs={{0,2},{1,3},{2,0},{3,1},{4,6},{5,7},{6,4},{7,5},{8,10},{9,11},{10,... | collective-permute-start | bytes 12296 | tf_op jit(solution)/shard_map/ppermute | solution.py:134
  144.7 3.6 %collective-permute-start.11 = (f32[8,128]{1,0:T(8,128)S(1)}, f32[8,128]{1,0:T(8,128)S(1)}, u32[]{:S(2)}, u32[]{:S(2)}) collective-permute-start(f32[8,128]{1,0:T(8,128)S(1)} %pad_maximum_fusion.1.s0), channel_id=1, source_target_pairs={{0,3},{1,0},{2,1},{3,2},{4,7},{5,4},{6,5},{7,6},{8,11},{9,8},{10,9... | collective-permute-start | bytes 12296 | tf_op jit(solution)/shard_map/ppermute | solution.py:134
  145.4 4.8 %collective-permute-start.9 = (f32[8,128]{1,0:T(8,128)S(1)}, f32[8,128]{1,0:T(8,128)S(1)}, u32[]{:S(2)}, u32[]{:S(2)}) collective-permute-start(f32[8,128]{1,0:T(8,128)S(1)} %pad_maximum_fusion.1.s0), channel_id=1, source_target_pairs={{0,1},{1,2},{2,3},{3,0},{4,5},{5,6},{6,7},{7,4},{8,9},{9,10},{10,1... | collective-permute-start | bytes 12296 | tf_op jit(solution)/shard_map/ppermute | solution.py:134

commit v8 on v6

--- a/solution.py
+++ b/solution.py
@@ -560,62 +560,83 @@
 
 
 def cross_kernel(
-    pipe_ref, s0, s1, s2, s3, send_ref, keep_ref, saved_ref, peer_ref, grad_ref, term_ref, scale
+    pipe_ref, s0, s1, s2, s3, send_ref, keep_ref, saved_ref, peer_ref, grad_hbm, term_ref,
+    grad_ref, scale, grad_sem,
 ):
-    step = pl.program_id(0)
     first = pipe_ref[0] == 0
-
-    @pl.when(step == 0)
-    def _():
-        scale[...] = rows_to_columns(s0[...] + s1[...] + s2[...] + s3[...])
-
-    wide = grad_ref.shape[2]
-    for group in range(wide // LANES):
-        own = pl.ds(group * LANES, LANES)
-        at = pl.ds(pl.multiple_of(step * wide + group * LANES, LANES), LANES)
-        partial = jnp.where(first, keep_ref[0, :, at], send_ref[0, :, at]).astype(jnp.float32)
-        saved = saved_ref[0, :, at].astype(jnp.float32)
-        grad_ref[0, :, own] = (partial - saved * scale[:, 0:1]).astype(jnp.bfloat16)
+    steps = grad_sem.shape[0]
+    wide = grad_ref.shape[1] // steps
+    scale[...] = rows_to_columns(s0[...] + s1[...] + s2[...] + s3[...])
+    copies = []
+    for step in range(steps):
+        for group in range(step * wide, (step + 1) * wide, LANES):
+            at = pl.ds(group, LANES)
+            partial = jnp.where(first, keep_ref[0, :, at], send_ref[0, :, at]).astype(jnp.float32)
+            saved = saved_ref[0, :, at].astype(jnp.float32)
+            grad_ref[:, at] = (partial - saved * scale[:, 0:1]).astype(jnp.bfloat16)
+        chunk = pl.ds(step * wide, wide)
+        copy = pltpu.make_async_copy(
+            grad_ref.at[:, chunk], grad_hbm.at[0, :, chunk], grad_sem.at[step]
+        )
+        copy.start()
+        copies.append(copy)
+    for group in range(0, grad_ref.shape[1], LANES):
+        at = pl.ds(group, LANES)
         term_ref[:, at] = peer_ref[0, :, at].astype(jnp.float32) * scale[:, 1:2]
+    for copy in copies:
+        copy.wait()
 
 
 def finish_cross(pipe, scales, send, keep, saved_in, peer_saved):
     rows, width = saved_in.shape[1:]
-    wide = 512
-    spec = lane_spec(rows, wide)
     return pl.pallas_call(
         cross_kernel,
         out_shape=(
-            jax.ShapeDtypeStruct(saved_in.shape, jnp.bfloat16),
+            pltpu.HBM(saved_in.shape, jnp.bfloat16),
             pltpu.VMEM((rows, width), jnp.float32),
         ),
-        grid=(width // wide,),
         in_specs=[SMEM] + [VMEM] * 8,
-        out_specs=(spec, VMEM),
-        scratch_shapes=[pltpu.VMEM((rows, 128), jnp.float32)],
+        out_specs=(HBM, VMEM),
+        scratch_shapes=[
+            pltpu.VMEM((rows, width), jnp.bfloat16),
+            pltpu.VMEM((rows, 128), jnp.float32),
+            pltpu.SemaphoreType.DMA((4,)),
+        ],
         name="finish_cross",
         compiler_params=pltpu.CompilerParams(vmem_limit_bytes=8 << 20),
     )(pipe, *scales, in_vmem(send), in_vmem(keep), in_vmem(saved_in), in_vmem(peer_saved))
 
 
-def received_kernel(value_ref, term_ref, out_ref):
-    wide = out_ref.shape[2]
-    for at in range(0, wide, LANES):
-        own = pl.ds(at, LANES)
-        source = pl.ds(pl.multiple_of(pl.program_id(0) * wide + at, LANES), LANES)
-        value = value_ref[0, :, source].astype(jnp.float32)
-        out_ref[0, :, own] = (value - term_ref[:, source]).astype(jnp.bfloat16)
+def received_kernel(value_ref, term_ref, out_hbm, out_ref, out_sem):
+    steps = out_sem.shape[0]
+    wide = out_ref.shape[1] // steps
+    copies = []
+    for step in range(steps):
+        for at in range(step * wide, (step + 1) * wide, LANES):
+            own = pl.ds(at, LANES)
+            value = value_ref[0, :, own].astype(jnp.float32)
+            out_ref[:, own] = (value - term_ref[:, own]).astype(jnp.bfloat16)
+        chunk = pl.ds(step * wide, wide)
+        copy = pltpu.make_async_copy(
+            out_ref.at[:, chunk], out_hbm.at[0, :, chunk], out_sem.at[step]
+        )
+        copy.start()
+        copies.append(copy)
+    for copy in copies:
+        copy.wait()
 
 
 def finish_received(value, term):
     rows, width = term.shape
-    wide = 512
     return pl.pallas_call(
         received_kernel,
-        out_shape=jax.ShapeDtypeStruct(value.shape, jnp.bfloat16),
-        grid=(width // wide,),
+        out_shape=pltpu.HBM(value.shape, jnp.bfloat16),
         in_specs=[VMEM, VMEM],
-        out_specs=lane_spec(rows, wide),
+        out_specs=HBM,
+        scratch_shapes=[
+            pltpu.VMEM((rows, width), jnp.bfloat16),
+            pltpu.SemaphoreType.DMA((8,)),
+        ],
         name="received",
         compiler_params=pltpu.CompilerParams(vmem_limit_bytes=8 << 20),
     )(in_vmem(value), in_vmem(term))

time: 104 us -> 102 us (0.981)
  Pallas kernels: 22.2 us -> 20.6 us
    pallas_call x2, Pallas kernels: 3.59 us -> 2.03 us  [the longest x1 1.15 us: finish_cross(): pl.pallas_call(cross_kernel, out_shape=(pltpu.HBM(saved_in.shape, jnp.bfl...]
  transfers between devices with their start and end apart: 16 -> 16, of which waited for: 9 -> 9; matrix products, arithmetic and copies ran while one was open for 1% -> 1% of each run, Pallas kernels for 10% -> 9%
where the time goes in v8:
time: 102 us
  waiting for transfers between devices  41.4 us (41%)
  starting transfers between devices  37.1 us (36%)
  Pallas kernels  20.6 us (20%)
  local copies, waits for them, and re-layouts  1.95 us (2%)
    all_to_all x1, waiting for transfers between devices, per_device(): back = lax.all_to_all(back, 'seq', 0, 0)  17.4 us
    ppermute x1, waiting for transfers between devices, per_device(): peer_cross = lax.ppermute(cross, 'pipe', [(1, 0)])  15.2 us
    ppermute x6, starting transfers between devices, over_chan(): lax.ppermute(rows, 'chan', [(low, (low + apart) % count) for low in range...  12.6 us
    pallas_call x1, Pallas kernels, convolve(): pl.pallas_call(conv_kernel, out_shape=pltpu.HBM((stored, rows + 24, 2 * L...  7.95 us
    ppermute x3, starting transfers between devices, round_ring(): lax.ppermute(rows, 'seq', [(low, place(low)) for low in range(count)])  5.99 us
    all_to_all x1, starting transfers between devices, per_device(): raw = lax.all_to_all(raw, 'seq', 0, 0)  5.76 us
    all_to_all x1, starting transfers between devices, per_device(): back = lax.all_to_all(back, 'seq', 0, 0)  5.18 us
    ppermute x6, waiting for transfers between devices, over_chan(): lax.ppermute(rows, 'chan', [(low, (low + apart) % count) for low in range...  4.61 us
  transfers between devices with their start and end apart: 16, of which 9 were waited for; matrix products, arithmetic and copies ran while one was open for 1% of the time, Pallas kernels for 9%

profile of v8, /device:TPU:0, one launch (start us, length us, event | category | flops | bytes accessed | tf_op | source)
XLA Modules:
  0.0 102.0 jit_solution(6284153529571563109)
XLA Ops:
  0.6 2.7 %pack.1 = (bf16[16,384,128]{2,1,0:T(8,128)(2,1)}, f32[8,128]{1,0:T(8,128)S(1)}) custom-call(bf16[1,128,2048]{2,1,0:T(8,128)(2,1)} %fwd_hbm.3, bf16[1,128,2048]{2,1,0:T(8,128)(2,1)} %saved_ref.5, bf16[1,128,2048]{2,1,0:T(8,128)(2,1)} %cot_ref.3), custom_call_target="tpu_custom_call" | custom-call | tf_op jit(solution)/shard_map/pack/pallas_call | solution.py:113
  3.3 0.0 copy-start.5
  3.3 5.8 %all-to-all-start = ((bf16[16,384,128]{2,1,0:T(8,128)(2,1)}), bf16[16,384,128]{2,1,0:T(8,128)(2,1)S(1)}, u32[]{:S(2)}, u32[]{:S(2)}) async-start(bf16[16,384,128]{2,1,0:T(8,128)(2,1)} %get-tuple-element.14), calls=%async_computation | async-start | bytes 3145728 | tf_op jit(solution)/shard_map/all_to_all | solution.py:649
  9.1 2.0 %collective-permute-start = (f32[8,128]{1,0:T(8,128)S(1)}, f32[8,128]{1,0:T(8,128)S(1)}, u32[]{:S(2)}, u32[]{:S(2)}) collective-permute-start(f32[8,128]{1,0:T(8,128)S(1)} %get-tuple-element.13), channel_id=1, source_target_pairs={{0,1},{1,2},{2,3},{3,0},{4,5},{5,6},{6,7},{7,4},{8,9},{9,10},{10,1... | collective-permute-start | bytes 12296 | tf_op jit(solution)/shard_map/ppermute | solution.py:136
  11.1 3.6 %collective-permute-start.1 = (f32[8,128]{1,0:T(8,128)S(1)}, f32[8,128]{1,0:T(8,128)S(1)}, u32[]{:S(2)}, u32[]{:S(2)}) collective-permute-start(f32[8,128]{1,0:T(8,128)S(1)} %get-tuple-element.13), channel_id=1, source_target_pairs={{0,2},{1,3},{2,0},{3,1},{4,6},{5,7},{6,4},{7,5},{8,10},{9,11},{10,... | collective-permute-start | bytes 12296 | tf_op jit(solution)/shard_map/ppermute | solution.py:136
  14.7 1.0 collective-permute-start.2
  15.7 0.0 collective-permute-done
  15.7 0.6 collective-permute-done.1
  16.3 2.0 %collective-permute-done.2 = f32[8,128]{1,0:T(8,128)S(1)} collective-permute-done((f32[8,128]{1,0:T(8,128)S(1)}, f32[8,128]{1,0:T(8,128)S(1)}, u32[]{:S(2)}, u32[]{:S(2)}) %collective-permute-start.2) | collective-permute-done | bytes 4128 | tf_op jit(solution)/shard_map/ppermute | solution.py:136
  18.3 0.0 collective-permute-start.3
  18.3 1.2 %collective-permute-done.3 = f32[2,128]{1,0:T(2,128)S(1)} collective-permute-done((f32[2,128]{1,0:T(2,128)S(1)}, f32[2,128]{1,0:T(2,128)S(1)}, u32[]{:S(2)}, u32[]{:S(2)}) %collective-permute-start.3) | collective-permute-done | bytes 1056 | tf_op jit(solution)/shard_map/ppermute | solution.py:143
  19.5 1.9 %collective-permute-start.4 = (f32[4,128]{1,0:T(4,128)S(1)}, f32[4,128]{1,0:T(4,128)S(1)}, u32[]{:S(2)}, u32[]{:S(2)}) collective-permute-start(f32[4,128]{1,0:T(4,128)S(1)} %pad_maximum_fusion.1), channel_id=1, source_target_pairs={{0,8},{4,12},{8,16},{12,20},{16,24},{20,28},{24,0},{28,4},{32,40},... | collective-permute-start | bytes 6152 | tf_op jit(solution)/shard_map/ppermute | solution.py:149
  21.3 2.7 %collective-permute-start.5 = (f32[4,128]{1,0:T(4,128)S(1)}, f32[4,128]{1,0:T(4,128)S(1)}, u32[]{:S(2)}, u32[]{:S(2)}) collective-permute-start(f32[4,128]{1,0:T(4,128)S(1)} %pad_maximum_fusion.1), channel_id=1, source_target_pairs={{0,16},{4,20},{8,24},{12,28},{16,0},{20,4},{24,8},{28,12},{32,48},... | collective-permute-start | bytes 6152 | tf_op jit(solution)/shard_map/ppermute | solution.py:149
  24.0 1.5 %collective-permute-start.6 = (f32[4,128]{1,0:T(4,128)S(1)}, f32[4,128]{1,0:T(4,128)S(1)}, u32[]{:S(2)}, u32[]{:S(2)}) collective-permute-start(f32[4,128]{1,0:T(4,128)S(1)} %pad_maximum_fusion.1), channel_id=1, source_target_pairs={{0,24},{4,28},{8,0},{12,4},{16,8},{20,12},{24,16},{28,20},{32,56},... | collective-permute-start | bytes 6152 | tf_op jit(solution)/shard_map/ppermute | solution.py:149
  25.5 2.8 %collective-permute-done.4 = f32[4,128]{1,0:T(4,128)S(1)} collective-permute-done((f32[4,128]{1,0:T(4,128)S(1)}, f32[4,128]{1,0:T(4,128)S(1)}, u32[]{:S(2)}, u32[]{:S(2)}) %collective-permute-start.4) | collective-permute-done | bytes 2080 | tf_op jit(solution)/shard_map/ppermute | solution.py:149
  28.2 0.4 collective-permute-done.5
  28.6 0.0 collective-permute-done.6
  28.6 1.7 %collective-permute-start.7 = (f32[16,128]{1,0:T(8,128)S(1)}, f32[16,128]{1,0:T(8,128)S(1)}, u32[]{:S(2)}, u32[]{:S(2)}) collective-permute-start(f32[16,128]{1,0:T(8,128)S(1)} %concatenate.15), channel_id=1, source_target_pairs={{0,32},{4,36},{8,40},{12,44},{16,48},{20,52},{24,56},{28,60},{32,0... | collective-permute-start | bytes 24584 | tf_op jit(solution)/shard_map/ppermute | solution.py:143
  30.3 0.0 copy-done.5
  30.3 2.9 %filter_spectra.1.filt_hbm = f32[8,2,256,128]{3,2,1,0:T(8,128)} custom-call(s32[1]{0:T(128)} %bitcast.1.where_ref, bf16[1,2048,2048]{2,1,0:T(8,128)(2,1)} %taps_ref.1, bf16[512,256]{1,0:T(8,128)(2,1)} %constant.84.clone.enter.enter_hbm), custom_call_target="tpu_custom_call" | custom-call | tf_op jit(solution)/shard_map/filter_spectra/pallas_call | solution.py:222
  33.2 0.0 copy-start.3
  33.2 2.6 %early.1.known_ref = f32[16,256]{1,0:T(8,128)S(1)} custom-call(f32[8,128]{1,0:T(8,128)S(1)} %add_add_fusion.sums_ref, bf16[1,128,2048]{2,1,0:T(8,128)(2,1)} %saved_ref.5, bf16[1,128,2048]{2,1,0:T(8,128)(2,1)} %sconv_ref.3, bf16[1,128,2048]{2,1,0:T(8,128)(2,1)} %cot_ref.3), custom_call_target="tpu_custom_call" | custom-call | tf_op jit(solution)/shard_map/early/pallas_call | solution.py:183
  35.9 0.0 collective-permute-done.7
  36.0 0.0 all-to-all-done.raw_hbm
  36.0 0.0 copy-start.4
  36.0 1.1 %copy-done.4 = bf16[16,384,128]{2,1,0:T(8,128)(2,1)} copy-done((bf16[16,384,128]{2,1,0:T(8,128)(2,1)}, bf16[16,384,128]{2,1,0:T(8,128)(2,1)S(1)}, u32[]{:S(2)}) %copy-start.4) | copy-done | bytes 1572888
  37.1 0.0 copy-done.3
  37.1 7.9 %convolve.1 = bf16[16,152,256]{2,1,0:T(8,128)(2,1)} custom-call(s32[1]{0:T(128)} %bitcast.1.where_ref, s32[16]{0:T(128)S(1)} %copy-done.3, s32[16]{0:T(128)S(1)} %fusion.4.gathered_ref, f32[32,128]{1,0:T(8,128)S(1)} %add_rsqrt_fusion.inv_ref, f32[16,256]{1,0:T(8,128)S(1)} %early.1.known_ref, f32[1,7,2048]{2,1,0:T(8,128)S(1)} %copy.13.params_ref, ...), custom_call_target="tpu_custom_call" | custom-call | tf_op jit(solution)/shard_map/convolve/pallas_call | solution.py:389
  45.1 0.0 copy-start
  45.1 0.0 copy-start.1
  45.1 0.0 copy-start.2
  45.1 5.2 %all-to-all-start.1 = ((bf16[16,152,256]{2,1,0:T(8,128)(2,1)}), bf16[16,152,256]{2,1,0:T(8,128)(2,1)S(1)}, u32[]{:S(2)}, u32[]{:S(2)}) async-start(bf16[16,152,256]{2,1,0:T(8,128)(2,1)} %convolve.1), calls=%async_computation.1 | async-start | bytes 2490368 | tf_op jit(solution)/shard_map/all_to_all | solution.py:659
  50.3 0.0 copy-done
  50.3 1.3 %collective-permute-start.12 = (bf16[1,128,2048]{2,1,0:T(8,128)(2,1)S(1)}, bf16[1,128,2048]{2,1,0:T(8,128)(2,1)S(1)}, u32[]{:S(2)}, u32[]{:S(2)}) collective-permute-start(bf16[1,128,2048]{2,1,0:T(8,128)(2,1)S(1)} %copy-done), channel_id=1, source_target_pairs={{64,0},{65,1},{66,2},{67,3},{68,4},{69,5},{70,6},{71,7},{72,8},{73... | collective-permute-start | bytes 1572872 | tf_op jit(solution)/shard_map/ppermute | solution.py:655
  51.6 17.4 %all-to-all-done.1.back_ref = bf16[16,152,256]{2,1,0:T(8,128)(2,1)S(1)} async-done(((bf16[16,152,256]{2,1,0:T(8,128)(2,1)}), bf16[16,152,256]{2,1,0:T(8,128)(2,1)S(1)}, u32[]{:S(2)}, u32[]{:S(2)}) %all-to-all-start.1) | async-done | bytes 1245216 | tf_op jit(solution)/shard_map/all_to_all | solution.py:659
  69.0 0.0 copy-done.1
  69.0 0.0 copy-done.2
  69.0 1.6 %leave.1 = (bf16[1,128,2048]{2,1,0:T(8,128)(2,1)S(1)}, bf16[1,128,2048]{2,1,0:T(8,128)(2,1)S(1)}, f32[8,128]{1,0:T(8,128)S(1)}) custom-call(s32[1]{0:T(128)} %bitcast.pipe_ref, f32[32,128]{1,0:T(8,128)S(1)} %add_rsqrt_fusion.inv_ref, bf16[16,152,256]{2,1,0:T(8,128)(2,1)S(1)} %all-to-all-done.1.back_ref, bf16[1,128,2048]{2,1,0:T(8,128)(2,1)} %fwd_hbm.3, ...), custom_call_target="tpu_custom_call" | custom-call | tf_op jit(solution)/shard_map/leave/pallas_call | solution.py:479
  70.6 3.4 %collective-permute-start.13 = (bf16[1,128,2048]{2,1,0:T(8,128)(2,1)S(1)}, bf16[1,128,2048]{2,1,0:T(8,128)(2,1)S(1)}, u32[]{:S(2)}, u32[]{:S(2)}) collective-permute-start(bf16[1,128,2048]{2,1,0:T(8,128)(2,1)S(1)} %get-tuple-element.15.send_ref), channel_id=1, source_target_pairs={{0,64},{64,0},{1,65},{65,1},{2,66},{66,2},{3,67},{67,3},{4,68},{68... | collective-permute-start | bytes 1572872 | tf_op jit(solution)/shard_map/ppermute | solution.py:664
  74.0 1.3 %collective-permute-start.8 = (f32[8,128]{1,0:T(8,128)S(1)}, f32[8,128]{1,0:T(8,128)S(1)}, u32[]{:S(2)}, u32[]{:S(2)}) collective-permute-start(f32[8,128]{1,0:T(8,128)S(1)} %get-tuple-element.18), channel_id=1, source_target_pairs={{64,0},{65,1},{66,2},{67,3},{68,4},{69,5},{70,6},{71,7},{72,8},{73... | collective-permute-start | bytes 12296 | tf_op jit(solution)/shard_map/ppermute | solution.py:663
  75.3 15.2 %collective-permute-done.8 = f32[8,128]{1,0:T(8,128)S(1)} collective-permute-done((f32[8,128]{1,0:T(8,128)S(1)}, f32[8,128]{1,0:T(8,128)S(1)}, u32[]{:S(2)}, u32[]{:S(2)}) %collective-permute-start.8) | collective-permute-done | bytes 4128 | tf_op jit(solution)/shard_map/ppermute | solution.py:663
  90.5 4.0 %collective-permute-start.10 = (f32[8,128]{1,0:T(8,128)S(1)}, f32[8,128]{1,0:T(8,128)S(1)}, u32[]{:S(2)}, u32[]{:S(2)}) collective-permute-start(f32[8,128]{1,0:T(8,128)S(1)} %pad_maximum_fusion.s0), channel_id=1, source_target_pairs={{0,2},{1,3},{2,0},{3,1},{4,6},{5,7},{6,4},{7,5},{8,10},{9,11},{10,... | collective-permute-start | bytes 12296 | tf_op jit(solution)/shard_map/ppermute | solution.py:136
  94.4 0.7 collective-permute-start.11
  95.2 1.3 %collective-permute-start.9 = (f32[8,128]{1,0:T(8,128)S(1)}, f32[8,128]{1,0:T(8,128)S(1)}, u32[]{:S(2)}, u32[]{:S(2)}) collective-permute-start(f32[8,128]{1,0:T(8,128)S(1)} %pad_maximum_fusion.s0), channel_id=1, source_target_pairs={{0,1},{1,2},{2,3},{3,0},{4,5},{5,6},{6,7},{7,4},{8,9},{9,10},{10,1... | collective-permute-start | bytes 12296 | tf_op jit(solution)/shard_map/ppermute | solution.py:136
  96.5 0.8 finish_rows.1
  97.3 0.7 copy.16
  98.0 0.0 collective-permute-done.12.peer_ref
  98.0 0.0 collective-permute-done.10.s2
  98.0 0.1 collective-permute-done.11.s3
  98.0 1.9 %collective-permute-done.9.s1 = f32[8,128]{1,0:T(8,128)S(1)} collective-permute-done((f32[8,128]{1,0:T(8,128)S(1)}, f32[8,128]{1,0:T(8,128)S(1)}, u32[]{:S(2)}, u32[]{:S(2)}) %collective-permute-start.9) | collective-permute-done | bytes 4128 | tf_op jit(solution)/shard_map/ppermute | solution.py:136
  100.0 1.2 %finish_cross.1 = (bf16[1,128,2048]{2,1,0:T(8,128)(2,1)}, f32[128,2048]{1,0:T(8,128)S(1)}) custom-call(s32[1]{0:T(128)} %bitcast.pipe_ref, f32[8,128]{1,0:T(8,128)S(1)} %pad_maximum_fusion.s0, f32[8,128]{1,0:T(8,128)S(1)} %collective-permute-done.9.s1, f32[8,128]{1,0:T(8,128)S(1)} %collective-permute-done.10.s2, f32[8,128]{1,0:T(8,128)S(1)} %collective-permute-done.11.s3, ...), custom_call_target="tpu_custom_call" | custom-call | tf_op jit(solution)/shard_map/finish_cross/pallas_call | solution.py:592
  101.1 0.0 collective-permute-done.13.value_ref
  101.1 0.9 received.1
  (11 shorter events, 0.2 us)
Async XLA Ops:
  3.3 27.0 %copy-start.5 = (f32[1,7,2048]{2,0,1:T(1,128)S(1)}, f32[1,7,2048]{2,0,1:T(1,128)}, u32[]{:S(2)}) copy-start(f32[1,7,2048]{2,0,1:T(1,128)} %param.14) | copy-start | bytes 172036
  3.3 32.6 %all-to-all-start = ((bf16[16,384,128]{2,1,0:T(8,128)(2,1)}), bf16[16,384,128]{2,1,0:T(8,128)(2,1)S(1)}, u32[]{:S(2)}, u32[]{:S(2)}) async-start(bf16[16,384,128]{2,1,0:T(8,128)(2,1)} %get-tuple-element.14), calls=%async_computation | async-start | bytes 3145728 | tf_op jit(solution)/shard_map/all_to_all | solution.py:649
  9.1 6.6 %collective-permute-start = (f32[8,128]{1,0:T(8,128)S(1)}, f32[8,128]{1,0:T(8,128)S(1)}, u32[]{:S(2)}, u32[]{:S(2)}) collective-permute-start(f32[8,128]{1,0:T(8,128)S(1)} %get-tuple-element.13), channel_id=1, source_target_pairs={{0,1},{1,2},{2,3},{3,0},{4,5},{5,6},{6,7},{7,4},{8,9},{9,10},{10,1... | collective-permute-start | bytes 12296 | tf_op jit(solution)/shard_map/ppermute | solution.py:136
  11.1 5.2 %collective-permute-start.1 = (f32[8,128]{1,0:T(8,128)S(1)}, f32[8,128]{1,0:T(8,128)S(1)}, u32[]{:S(2)}, u32[]{:S(2)}) collective-permute-start(f32[8,128]{1,0:T(8,128)S(1)} %get-tuple-element.13), channel_id=1, source_target_pairs={{0,2},{1,3},{2,0},{3,1},{4,6},{5,7},{6,4},{7,5},{8,10},{9,11},{10,... | collective-permute-start | bytes 12296 | tf_op jit(solution)/shard_map/ppermute | solution.py:136
  14.7 3.6 %collective-permute-start.2 = (f32[8,128]{1,0:T(8,128)S(1)}, f32[8,128]{1,0:T(8,128)S(1)}, u32[]{:S(2)}, u32[]{:S(2)}) collective-permute-start(f32[8,128]{1,0:T(8,128)S(1)} %get-tuple-element.13), channel_id=1, source_target_pairs={{0,3},{1,0},{2,1},{3,2},{4,7},{5,4},{6,5},{7,6},{8,11},{9,8},{10,9... | collective-permute-start | bytes 12296 | tf_op jit(solution)/shard_map/ppermute | solution.py:136
  18.3 1.2 %collective-permute-start.3 = (f32[2,128]{1,0:T(2,128)S(1)}, f32[2,128]{1,0:T(2,128)S(1)}, u32[]{:S(2)}, u32[]{:S(2)}) collective-permute-start(f32[2,128]{1,0:T(2,128)S(1)} %slice.12), channel_id=1, source_target_pairs={{0,4},{4,0},{8,12},{12,8},{16,20},{20,16},{24,28},{28,24},{32,36},... | collective-permute-start | bytes 3080 | tf_op jit(solution)/shard_map/ppermute | solution.py:143
  19.5 8.8 %collective-permute-start.4 = (f32[4,128]{1,0:T(4,128)S(1)}, f32[4,128]{1,0:T(4,128)S(1)}, u32[]{:S(2)}, u32[]{:S(2)}) collective-permute-start(f32[4,128]{1,0:T(4,128)S(1)} %pad_maximum_fusion.1), channel_id=1, source_target_pairs={{0,8},{4,12},{8,16},{12,20},{16,24},{20,28},{24,0},{28,4},{32,40},... | collective-permute-start | bytes 6152 | tf_op jit(solution)/shard_map/ppermute | solution.py:149
  21.3 7.3 %collective-permute-start.5 = (f32[4,128]{1,0:T(4,128)S(1)}, f32[4,128]{1,0:T(4,128)S(1)}, u32[]{:S(2)}, u32[]{:S(2)}) collective-permute-start(f32[4,128]{1,0:T(4,128)S(1)} %pad_maximum_fusion.1), channel_id=1, source_target_pairs={{0,16},{4,20},{8,24},{12,28},{16,0},{20,4},{24,8},{28,12},{32,48},... | collective-permute-start | bytes 6152 | tf_op jit(solution)/shard_map/ppermute | solution.py:149
  24.0 4.6 %collective-permute-start.6 = (f32[4,128]{1,0:T(4,128)S(1)}, f32[4,128]{1,0:T(4,128)S(1)}, u32[]{:S(2)}, u32[]{:S(2)}) collective-permute-start(f32[4,128]{1,0:T(4,128)S(1)} %pad_maximum_fusion.1), channel_id=1, source_target_pairs={{0,24},{4,28},{8,0},{12,4},{16,8},{20,12},{24,16},{28,20},{32,56},... | collective-permute-start | bytes 6152 | tf_op jit(solution)/shard_map/ppermute | solution.py:149
  28.6 7.3 %collective-permute-start.7 = (f32[16,128]{1,0:T(8,128)S(1)}, f32[16,128]{1,0:T(8,128)S(1)}, u32[]{:S(2)}, u32[]{:S(2)}) collective-permute-start(f32[16,128]{1,0:T(8,128)S(1)} %concatenate.15), channel_id=1, source_target_pairs={{0,32},{4,36},{8,40},{12,44},{16,48},{20,52},{24,56},{28,60},{32,0... | collective-permute-start | bytes 24584 | tf_op jit(solution)/shard_map/ppermute | solution.py:143
  33.2 3.9 %copy-start.3 = (s32[16]{0:T(128)S(1)}, s32[16]{0:T(128)}, u32[]{:S(2)}) copy-start(s32[16]{0:T(128)} %order_ref.1) | copy-start | bytes 196
  36.0 1.1 %copy-start.4 = (bf16[16,384,128]{2,1,0:T(8,128)(2,1)}, bf16[16,384,128]{2,1,0:T(8,128)(2,1)S(1)}, u32[]{:S(2)}) copy-start(bf16[16,384,128]{2,1,0:T(8,128)(2,1)S(1)} %all-to-all-done.raw_hbm) | copy-start | bytes 4718596
  45.1 5.2 %copy-start = (bf16[1,128,2048]{2,1,0:T(8,128)(2,1)S(1)}, bf16[1,128,2048]{2,1,0:T(8,128)(2,1)}, u32[]{:S(2)}) copy-start(bf16[1,128,2048]{2,1,0:T(8,128)(2,1)} %saved_ref.5) | copy-start | bytes 1572868
  45.1 23.9 %copy-start.1 = (bf16[1,128,2048]{2,1,0:T(8,128)(2,1)S(1)}, bf16[1,128,2048]{2,1,0:T(8,128)(2,1)}, u32[]{:S(2)}) copy-start(bf16[1,128,2048]{2,1,0:T(8,128)(2,1)} %cot_ref.3) | copy-start | bytes 1572868
  45.1 23.9 %copy-start.2 = (bf16[1,128,2048]{2,1,0:T(8,128)(2,1)S(1)}, bf16[1,128,2048]{2,1,0:T(8,128)(2,1)}, u32[]{:S(2)}) copy-start(bf16[1,128,2048]{2,1,0:T(8,128)(2,1)} %sconv_ref.3) | copy-start | bytes 1572868
  45.1 23.9 %all-to-all-start.1 = ((bf16[16,152,256]{2,1,0:T(8,128)(2,1)}), bf16[16,152,256]{2,1,0:T(8,128)(2,1)S(1)}, u32[]{:S(2)}, u32[]{:S(2)}) async-start(bf16[16,152,256]{2,1,0:T(8,128)(2,1)} %convolve.1), calls=%async_computation.1 | async-start | bytes 2490368 | tf_op jit(solution)/shard_map/all_to_all | solution.py:659
  50.3 47.7 %collective-permute-start.12 = (bf16[1,128,2048]{2,1,0:T(8,128)(2,1)S(1)}, bf16[1,128,2048]{2,1,0:T(8,128)(2,1)S(1)}, u32[]{:S(2)}, u32[]{:S(2)}) collective-permute-start(bf16[1,128,2048]{2,1,0:T(8,128)(2,1)S(1)} %copy-done), channel_id=1, source_target_pairs={{64,0},{65,1},{66,2},{67,3},{68,4},{69,5},{70,6},{71,7},{72,8},{73... | collective-permute-start | bytes 1572872 | tf_op jit(solution)/shard_map/ppermute | solution.py:655
  70.6 30.5 %collective-permute-start.13 = (bf16[1,128,2048]{2,1,0:T(8,128)(2,1)S(1)}, bf16[1,128,2048]{2,1,0:T(8,128)(2,1)S(1)}, u32[]{:S(2)}, u32[]{:S(2)}) collective-permute-start(bf16[1,128,2048]{2,1,0:T(8,128)(2,1)S(1)} %get-tuple-element.15.send_ref), channel_id=1, source_target_pairs={{0,64},{64,0},{1,65},{65,1},{2,66},{66,2},{3,67},{67,3},{4,68},{68... | collective-permute-start | bytes 1572872 | tf_op jit(solution)/shard_map/ppermute | solution.py:664
  74.0 16.5 %collective-permute-start.8 = (f32[8,128]{1,0:T(8,128)S(1)}, f32[8,128]{1,0:T(8,128)S(1)}, u32[]{:S(2)}, u32[]{:S(2)}) collective-permute-start(f32[8,128]{1,0:T(8,128)S(1)} %get-tuple-element.18), channel_id=1, source_target_pairs={{64,0},{65,1},{66,2},{67,3},{68,4},{69,5},{70,6},{71,7},{72,8},{73... | collective-permute-start | bytes 12296 | tf_op jit(solution)/shard_map/ppermute | solution.py:663
  90.5 7.5 %collective-permute-start.10 = (f32[8,128]{1,0:T(8,128)S(1)}, f32[8,128]{1,0:T(8,128)S(1)}, u32[]{:S(2)}, u32[]{:S(2)}) collective-permute-start(f32[8,128]{1,0:T(8,128)S(1)} %pad_maximum_fusion.s0), channel_id=1, source_target_pairs={{0,2},{1,3},{2,0},{3,1},{4,6},{5,7},{6,4},{7,5},{8,10},{9,11},{10,... | collective-permute-start | bytes 12296 | tf_op jit(solution)/shard_map/ppermute | solution.py:136
  94.4 3.6 %collective-permute-start.11 = (f32[8,128]{1,0:T(8,128)S(1)}, f32[8,128]{1,0:T(8,128)S(1)}, u32[]{:S(2)}, u32[]{:S(2)}) collective-permute-start(f32[8,128]{1,0:T(8,128)S(1)} %pad_maximum_fusion.s0), channel_id=1, source_target_pairs={{0,3},{1,0},{2,1},{3,2},{4,7},{5,4},{6,5},{7,6},{8,11},{9,8},{10,9... | collective-permute-start | bytes 12296 | tf_op jit(solution)/shard_map/ppermute | solution.py:136
  95.2 4.8 %collective-permute-start.9 = (f32[8,128]{1,0:T(8,128)S(1)}, f32[8,128]{1,0:T(8,128)S(1)}, u32[]{:S(2)}, u32[]{:S(2)}) collective-permute-start(f32[8,128]{1,0:T(8,128)S(1)} %pad_maximum_fusion.s0), channel_id=1, source_target_pairs={{0,1},{1,2},{2,3},{3,0},{4,5},{5,6},{6,7},{7,4},{8,9},{9,10},{10,1... | collective-permute-start | bytes 12296 | tf_op jit(solution)/shard_map/ppermute | solution.py:136

commit v9 on v8

--- a/solution.py
+++ b/solution.py
@@ -533,7 +533,8 @@
             p[0] * value_normed,
             p[0] * p[3] * m1 + p[4] * m0,
         ]
-        grads_ref[0, :, own] = jnp.concatenate(grads, axis=0)
+        for index, value in enumerate(grads):
+            grads_ref[index, :, own] = value
 
     @pl.when(first)
     def _():
@@ -549,7 +550,7 @@
         rows_kernel,
         out_shape=(
             pltpu.HBM(send.shape, jnp.bfloat16),
-            jax.ShapeDtypeStruct(mix_params.shape, jnp.float32),
+            jax.ShapeDtypeStruct((7, 1, send.shape[2]), jnp.float32),
         ),
         in_specs=[SMEM] + [VMEM] * 4,
         out_specs=(HBM, VMEM),
@@ -666,7 +667,7 @@
     layer_out, param_grad = finish_rows(pipe, back, outgoing, keep, mix_params)
     input_grad, term = finish_cross(pipe, scales, outgoing, keep, saved_in, peer_saved)
     received = finish_received(incoming, term)
-    return (layer_out, input_grad, param_grad, received)
+    return (layer_out, input_grad, param_grad.transpose(1, 0, 2), received)
 
 
 def solution(mesh):

time: 102 us -> 102 us (level)
  transfers between devices with their start and end apart: 16 -> 16, of which waited for: 9 -> 9; matrix products, arithmetic and copies ran while one was open for 1% -> 0% of each run, Pallas kernels for 9% -> 10%
where the time goes in v9:
time: 102 us
  waiting for transfers between devices  41.5 us (41%)
  starting transfers between devices  37.1 us (36%)
  Pallas kernels  21.3 us (21%)
  local copies, waits for them, and re-layouts  1.27 us (1%)
    all_to_all x1, waiting for transfers between devices, per_device(): back = lax.all_to_all(back, 'seq', 0, 0)  17.4 us
    ppermute x1, waiting for transfers between devices, per_device(): peer_cross = lax.ppermute(cross, 'pipe', [(1, 0)])  15.2 us
    ppermute x6, starting transfers between devices, over_chan(): lax.ppermute(rows, 'chan', [(low, (low + apart) % count) for low in range...  12.6 us
    pallas_call x1, Pallas kernels, convolve(): pl.pallas_call(conv_kernel, out_shape=pltpu.HBM((stored, rows + 24, 2 * L...  7.95 us
    ppermute x3, starting transfers between devices, round_ring(): lax.ppermute(rows, 'seq', [(low, place(low)) for low in range(count)])  5.99 us
    all_to_all x1, starting transfers between devices, per_device(): raw = lax.all_to_all(raw, 'seq', 0, 0)  5.76 us
    all_to_all x1, starting transfers between devices, per_device(): back = lax.all_to_all(back, 'seq', 0, 0)  5.18 us
    ppermute x6, waiting for transfers between devices, over_chan(): lax.ppermute(rows, 'chan', [(low, (low + apart) % count) for low in range...  4.65 us
  transfers between devices with their start and end apart: 16, of which 9 were waited for; matrix products, arithmetic and copies ran while one was open for 0% of the time, Pallas kernels for 10%

profile of v9, /device:TPU:0, one launch (start us, length us, event | category | flops | bytes accessed | tf_op | source)
XLA Modules:
  0.0 102.0 jit_solution(348951198252078555)
XLA Ops:
  0.6 2.7 %pack.1 = (bf16[16,384,128]{2,1,0:T(8,128)(2,1)}, f32[8,128]{1,0:T(8,128)S(1)}) custom-call(bf16[1,128,2048]{2,1,0:T(8,128)(2,1)} %fwd_hbm.3, bf16[1,128,2048]{2,1,0:T(8,128)(2,1)} %saved_ref.5, bf16[1,128,2048]{2,1,0:T(8,128)(2,1)} %cot_ref.3), custom_call_target="tpu_custom_call" | custom-call | tf_op jit(solution)/shard_map/pack/pallas_call | solution.py:113
  3.3 0.0 copy-start.5
  3.3 5.8 %all-to-all-start = ((bf16[16,384,128]{2,1,0:T(8,128)(2,1)}), bf16[16,384,128]{2,1,0:T(8,128)(2,1)S(1)}, u32[]{:S(2)}, u32[]{:S(2)}) async-start(bf16[16,384,128]{2,1,0:T(8,128)(2,1)} %get-tuple-element.14), calls=%async_computation | async-start | bytes 3145728 | tf_op jit(solution)/shard_map/all_to_all | solution.py:650
  9.1 2.0 %collective-permute-start = (f32[8,128]{1,0:T(8,128)S(1)}, f32[8,128]{1,0:T(8,128)S(1)}, u32[]{:S(2)}, u32[]{:S(2)}) collective-permute-start(f32[8,128]{1,0:T(8,128)S(1)} %get-tuple-element.13), channel_id=1, source_target_pairs={{0,1},{1,2},{2,3},{3,0},{4,5},{5,6},{6,7},{7,4},{8,9},{9,10},{10,1... | collective-permute-start | bytes 12296 | tf_op jit(solution)/shard_map/ppermute | solution.py:136
  11.1 3.6 %collective-permute-start.1 = (f32[8,128]{1,0:T(8,128)S(1)}, f32[8,128]{1,0:T(8,128)S(1)}, u32[]{:S(2)}, u32[]{:S(2)}) collective-permute-start(f32[8,128]{1,0:T(8,128)S(1)} %get-tuple-element.13), channel_id=1, source_target_pairs={{0,2},{1,3},{2,0},{3,1},{4,6},{5,7},{6,4},{7,5},{8,10},{9,11},{10,... | collective-permute-start | bytes 12296 | tf_op jit(solution)/shard_map/ppermute | solution.py:136
  14.7 1.0 collective-permute-start.2
  15.7 0.0 collective-permute-done
  15.7 0.6 collective-permute-done.1
  16.3 2.0 %collective-permute-done.2 = f32[8,128]{1,0:T(8,128)S(1)} collective-permute-done((f32[8,128]{1,0:T(8,128)S(1)}, f32[8,128]{1,0:T(8,128)S(1)}, u32[]{:S(2)}, u32[]{:S(2)}) %collective-permute-start.2) | collective-permute-done | bytes 4128 | tf_op jit(solution)/shard_map/ppermute | solution.py:136
  18.3 0.0 collective-permute-start.3
  18.3 1.2 %collective-permute-done.3 = f32[2,128]{1,0:T(2,128)S(1)} collective-permute-done((f32[2,128]{1,0:T(2,128)S(1)}, f32[2,128]{1,0:T(2,128)S(1)}, u32[]{:S(2)}, u32[]{:S(2)}) %collective-permute-start.3) | collective-permute-done | bytes 1056 | tf_op jit(solution)/shard_map/ppermute | solution.py:143
  19.5 1.9 %collective-permute-start.4 = (f32[4,128]{1,0:T(4,128)S(1)}, f32[4,128]{1,0:T(4,128)S(1)}, u32[]{:S(2)}, u32[]{:S(2)}) collective-permute-start(f32[4,128]{1,0:T(4,128)S(1)} %pad_maximum_fusion.1), channel_id=1, source_target_pairs={{0,8},{4,12},{8,16},{12,20},{16,24},{20,28},{24,0},{28,4},{32,40},... | collective-permute-start | bytes 6152 | tf_op jit(solution)/shard_map/ppermute | solution.py:149
  21.3 2.7 %collective-permute-start.5 = (f32[4,128]{1,0:T(4,128)S(1)}, f32[4,128]{1,0:T(4,128)S(1)}, u32[]{:S(2)}, u32[]{:S(2)}) collective-permute-start(f32[4,128]{1,0:T(4,128)S(1)} %pad_maximum_fusion.1), channel_id=1, source_target_pairs={{0,16},{4,20},{8,24},{12,28},{16,0},{20,4},{24,8},{28,12},{32,48},... | collective-permute-start | bytes 6152 | tf_op jit(solution)/shard_map/ppermute | solution.py:149
  24.0 1.5 %collective-permute-start.6 = (f32[4,128]{1,0:T(4,128)S(1)}, f32[4,128]{1,0:T(4,128)S(1)}, u32[]{:S(2)}, u32[]{:S(2)}) collective-permute-start(f32[4,128]{1,0:T(4,128)S(1)} %pad_maximum_fusion.1), channel_id=1, source_target_pairs={{0,24},{4,28},{8,0},{12,4},{16,8},{20,12},{24,16},{28,20},{32,56},... | collective-permute-start | bytes 6152 | tf_op jit(solution)/shard_map/ppermute | solution.py:149
  25.5 2.8 %collective-permute-done.4 = f32[4,128]{1,0:T(4,128)S(1)} collective-permute-done((f32[4,128]{1,0:T(4,128)S(1)}, f32[4,128]{1,0:T(4,128)S(1)}, u32[]{:S(2)}, u32[]{:S(2)}) %collective-permute-start.4) | collective-permute-done | bytes 2080 | tf_op jit(solution)/shard_map/ppermute | solution.py:149
  28.2 0.4 collective-permute-done.5
  28.6 0.0 collective-permute-done.6
  28.6 1.7 %collective-permute-start.7 = (f32[16,128]{1,0:T(8,128)S(1)}, f32[16,128]{1,0:T(8,128)S(1)}, u32[]{:S(2)}, u32[]{:S(2)}) collective-permute-start(f32[16,128]{1,0:T(8,128)S(1)} %concatenate.15), channel_id=1, source_target_pairs={{0,32},{4,36},{8,40},{12,44},{16,48},{20,52},{24,56},{28,60},{32,0... | collective-permute-start | bytes 24584 | tf_op jit(solution)/shard_map/ppermute | solution.py:143
  30.3 0.0 copy-done.5
  30.3 2.9 %filter_spectra.1.filt_hbm = f32[8,2,256,128]{3,2,1,0:T(8,128)} custom-call(s32[1]{0:T(128)} %bitcast.1.where_ref, bf16[1,2048,2048]{2,1,0:T(8,128)(2,1)} %taps_ref.1, bf16[512,256]{1,0:T(8,128)(2,1)} %constant.84.clone.enter.enter_hbm), custom_call_target="tpu_custom_call" | custom-call | tf_op jit(solution)/shard_map/filter_spectra/pallas_call | solution.py:222
  33.2 0.0 copy-start.3
  33.2 2.6 %early.1.known_ref = f32[16,256]{1,0:T(8,128)S(1)} custom-call(f32[8,128]{1,0:T(8,128)S(1)} %add_add_fusion.sums_ref, bf16[1,128,2048]{2,1,0:T(8,128)(2,1)} %saved_ref.5, bf16[1,128,2048]{2,1,0:T(8,128)(2,1)} %sconv_ref.3, bf16[1,128,2048]{2,1,0:T(8,128)(2,1)} %cot_ref.3), custom_call_target="tpu_custom_call" | custom-call | tf_op jit(solution)/shard_map/early/pallas_call | solution.py:183
  35.9 0.0 collective-permute-done.7
  36.0 0.0 all-to-all-done.raw_hbm
  36.0 0.0 copy-start.4
  36.0 1.1 %copy-done.4 = bf16[16,384,128]{2,1,0:T(8,128)(2,1)} copy-done((bf16[16,384,128]{2,1,0:T(8,128)(2,1)}, bf16[16,384,128]{2,1,0:T(8,128)(2,1)S(1)}, u32[]{:S(2)}) %copy-start.4) | copy-done | bytes 1572888
  37.1 0.0 copy-done.3
  37.1 7.9 %convolve.1 = bf16[16,152,256]{2,1,0:T(8,128)(2,1)} custom-call(s32[1]{0:T(128)} %bitcast.1.where_ref, s32[16]{0:T(128)S(1)} %copy-done.3, s32[16]{0:T(128)S(1)} %fusion.4.gathered_ref, f32[32,128]{1,0:T(8,128)S(1)} %add_rsqrt_fusion.inv_ref, f32[16,256]{1,0:T(8,128)S(1)} %early.1.known_ref, f32[1,7,2048]{2,1,0:T(8,128)S(1)} %copy.13.params_ref, ...), custom_call_target="tpu_custom_call" | custom-call | tf_op jit(solution)/shard_map/convolve/pallas_call | solution.py:389
  45.1 0.0 copy-start
  45.1 0.0 copy-start.1
  45.1 0.0 copy-start.2
  45.1 5.2 %all-to-all-start.1 = ((bf16[16,152,256]{2,1,0:T(8,128)(2,1)}), bf16[16,152,256]{2,1,0:T(8,128)(2,1)S(1)}, u32[]{:S(2)}, u32[]{:S(2)}) async-start(bf16[16,152,256]{2,1,0:T(8,128)(2,1)} %convolve.1), calls=%async_computation.1 | async-start | bytes 2490368 | tf_op jit(solution)/shard_map/all_to_all | solution.py:660
  50.3 0.0 copy-done
  50.3 1.3 %collective-permute-start.12 = (bf16[1,128,2048]{2,1,0:T(8,128)(2,1)S(1)}, bf16[1,128,2048]{2,1,0:T(8,128)(2,1)S(1)}, u32[]{:S(2)}, u32[]{:S(2)}) collective-permute-start(bf16[1,128,2048]{2,1,0:T(8,128)(2,1)S(1)} %copy-done), channel_id=1, source_target_pairs={{64,0},{65,1},{66,2},{67,3},{68,4},{69,5},{70,6},{71,7},{72,8},{73... | collective-permute-start | bytes 1572872 | tf_op jit(solution)/shard_map/ppermute | solution.py:656
  51.6 17.4 %all-to-all-done.1.back_ref = bf16[16,152,256]{2,1,0:T(8,128)(2,1)S(1)} async-done(((bf16[16,152,256]{2,1,0:T(8,128)(2,1)}), bf16[16,152,256]{2,1,0:T(8,128)(2,1)S(1)}, u32[]{:S(2)}, u32[]{:S(2)}) %all-to-all-start.1) | async-done | bytes 1245216 | tf_op jit(solution)/shard_map/all_to_all | solution.py:660
  69.0 0.0 copy-done.1
  69.0 0.0 copy-done.2
  69.0 1.6 %leave.1 = (bf16[1,128,2048]{2,1,0:T(8,128)(2,1)S(1)}, bf16[1,128,2048]{2,1,0:T(8,128)(2,1)S(1)}, f32[8,128]{1,0:T(8,128)S(1)}) custom-call(s32[1]{0:T(128)} %bitcast.pipe_ref, f32[32,128]{1,0:T(8,128)S(1)} %add_rsqrt_fusion.inv_ref, bf16[16,152,256]{2,1,0:T(8,128)(2,1)S(1)} %all-to-all-done.1.back_ref, bf16[1,128,2048]{2,1,0:T(8,128)(2,1)} %fwd_hbm.3, ...), custom_call_target="tpu_custom_call" | custom-call | tf_op jit(solution)/shard_map/leave/pallas_call | solution.py:479
  70.6 3.4 %collective-permute-start.13 = (bf16[1,128,2048]{2,1,0:T(8,128)(2,1)S(1)}, bf16[1,128,2048]{2,1,0:T(8,128)(2,1)S(1)}, u32[]{:S(2)}, u32[]{:S(2)}) collective-permute-start(bf16[1,128,2048]{2,1,0:T(8,128)(2,1)S(1)} %get-tuple-element.15.send_ref), channel_id=1, source_target_pairs={{0,64},{64,0},{1,65},{65,1},{2,66},{66,2},{3,67},{67,3},{4,68},{68... | collective-permute-start | bytes 1572872 | tf_op jit(solution)/shard_map/ppermute | solution.py:665
  74.0 1.3 %collective-permute-start.8 = (f32[8,128]{1,0:T(8,128)S(1)}, f32[8,128]{1,0:T(8,128)S(1)}, u32[]{:S(2)}, u32[]{:S(2)}) collective-permute-start(f32[8,128]{1,0:T(8,128)S(1)} %get-tuple-element.18), channel_id=1, source_target_pairs={{64,0},{65,1},{66,2},{67,3},{68,4},{69,5},{70,6},{71,7},{72,8},{73... | collective-permute-start | bytes 12296 | tf_op jit(solution)/shard_map/ppermute | solution.py:664
  75.3 15.2 %collective-permute-done.8 = f32[8,128]{1,0:T(8,128)S(1)} collective-permute-done((f32[8,128]{1,0:T(8,128)S(1)}, f32[8,128]{1,0:T(8,128)S(1)}, u32[]{:S(2)}, u32[]{:S(2)}) %collective-permute-start.8) | collective-permute-done | bytes 4128 | tf_op jit(solution)/shard_map/ppermute | solution.py:664
  90.5 4.0 %collective-permute-start.10 = (f32[8,128]{1,0:T(8,128)S(1)}, f32[8,128]{1,0:T(8,128)S(1)}, u32[]{:S(2)}, u32[]{:S(2)}) collective-permute-start(f32[8,128]{1,0:T(8,128)S(1)} %pad_maximum_fusion.s0), channel_id=1, source_target_pairs={{0,2},{1,3},{2,0},{3,1},{4,6},{5,7},{6,4},{7,5},{8,10},{9,11},{10,... | collective-permute-start | bytes 12296 | tf_op jit(solution)/shard_map/ppermute | solution.py:136
  94.4 0.7 collective-permute-start.11
  95.2 1.3 %collective-permute-start.9 = (f32[8,128]{1,0:T(8,128)S(1)}, f32[8,128]{1,0:T(8,128)S(1)}, u32[]{:S(2)}, u32[]{:S(2)}) collective-permute-start(f32[8,128]{1,0:T(8,128)S(1)} %pad_maximum_fusion.s0), channel_id=1, source_target_pairs={{0,1},{1,2},{2,3},{3,0},{4,5},{5,6},{6,7},{7,4},{8,9},{9,10},{10,1... | collective-permute-start | bytes 12296 | tf_op jit(solution)/shard_map/ppermute | solution.py:136
  96.5 1.4 %finish_rows.1 = (bf16[1,128,2048]{2,1,0:T(8,128)(2,1)}, f32[7,1,2048]{2,1,0:T(1,128)}) custom-call(s32[1]{0:T(128)} %bitcast.pipe_ref, bf16[16,152,256]{2,1,0:T(8,128)(2,1)S(1)} %all-to-all-done.1.back_ref, bf16[1,128,2048]{2,1,0:T(8,128)(2,1)S(1)} %get-tuple-element.15.send_ref, bf16[1,128,2048]{2,1,0:T(8,128)(2,1)S(1)} %get-tuple-element.16.keep_ref, ...), custom_call_target="tpu_custom_call" | custom-call | tf_op jit(solution)/shard_map/finish_rows/pallas_call | solution.py:549
  97.9 0.0 collective-permute-done.12.peer_ref
  97.9 0.0 collective-permute-done.10.s2
  97.9 0.1 collective-permute-done.11.s3
  98.0 1.9 %collective-permute-done.9.s1 = f32[8,128]{1,0:T(8,128)S(1)} collective-permute-done((f32[8,128]{1,0:T(8,128)S(1)}, f32[8,128]{1,0:T(8,128)S(1)}, u32[]{:S(2)}, u32[]{:S(2)}) %collective-permute-start.9) | collective-permute-done | bytes 4128 | tf_op jit(solution)/shard_map/ppermute | solution.py:136
  100.0 1.2 %finish_cross.1 = (bf16[1,128,2048]{2,1,0:T(8,128)(2,1)}, f32[128,2048]{1,0:T(8,128)S(1)}) custom-call(s32[1]{0:T(128)} %bitcast.pipe_ref, f32[8,128]{1,0:T(8,128)S(1)} %pad_maximum_fusion.s0, f32[8,128]{1,0:T(8,128)S(1)} %collective-permute-done.9.s1, f32[8,128]{1,0:T(8,128)S(1)} %collective-permute-done.10.s2, f32[8,128]{1,0:T(8,128)S(1)} %collective-permute-done.11.s3, ...), custom_call_target="tpu_custom_call" | custom-call | tf_op jit(solution)/shard_map/finish_cross/pallas_call | solution.py:593
  101.1 0.0 collective-permute-done.13.value_ref
  101.1 0.9 received.1
  (11 shorter events, 0.2 us)
Async XLA Ops:
  3.3 27.0 %copy-start.5 = (f32[1,7,2048]{2,0,1:T(1,128)S(1)}, f32[1,7,2048]{2,0,1:T(1,128)}, u32[]{:S(2)}) copy-start(f32[1,7,2048]{2,0,1:T(1,128)} %param.14) | copy-start | bytes 172036
  3.3 32.6 %all-to-all-start = ((bf16[16,384,128]{2,1,0:T(8,128)(2,1)}), bf16[16,384,128]{2,1,0:T(8,128)(2,1)S(1)}, u32[]{:S(2)}, u32[]{:S(2)}) async-start(bf16[16,384,128]{2,1,0:T(8,128)(2,1)} %get-tuple-element.14), calls=%async_computation | async-start | bytes 3145728 | tf_op jit(solution)/shard_map/all_to_all | solution.py:650
  9.1 6.6 %collective-permute-start = (f32[8,128]{1,0:T(8,128)S(1)}, f32[8,128]{1,0:T(8,128)S(1)}, u32[]{:S(2)}, u32[]{:S(2)}) collective-permute-start(f32[8,128]{1,0:T(8,128)S(1)} %get-tuple-element.13), channel_id=1, source_target_pairs={{0,1},{1,2},{2,3},{3,0},{4,5},{5,6},{6,7},{7,4},{8,9},{9,10},{10,1... | collective-permute-start | bytes 12296 | tf_op jit(solution)/shard_map/ppermute | solution.py:136
  11.1 5.2 %collective-permute-start.1 = (f32[8,128]{1,0:T(8,128)S(1)}, f32[8,128]{1,0:T(8,128)S(1)}, u32[]{:S(2)}, u32[]{:S(2)}) collective-permute-start(f32[8,128]{1,0:T(8,128)S(1)} %get-tuple-element.13), channel_id=1, source_target_pairs={{0,2},{1,3},{2,0},{3,1},{4,6},{5,7},{6,4},{7,5},{8,10},{9,11},{10,... | collective-permute-start | bytes 12296 | tf_op jit(solution)/shard_map/ppermute | solution.py:136
  14.7 3.6 %collective-permute-start.2 = (f32[8,128]{1,0:T(8,128)S(1)}, f32[8,128]{1,0:T(8,128)S(1)}, u32[]{:S(2)}, u32[]{:S(2)}) collective-permute-start(f32[8,128]{1,0:T(8,128)S(1)} %get-tuple-element.13), channel_id=1, source_target_pairs={{0,3},{1,0},{2,1},{3,2},{4,7},{5,4},{6,5},{7,6},{8,11},{9,8},{10,9... | collective-permute-start | bytes 12296 | tf_op jit(solution)/shard_map/ppermute | solution.py:136
  18.3 1.2 %collective-permute-start.3 = (f32[2,128]{1,0:T(2,128)S(1)}, f32[2,128]{1,0:T(2,128)S(1)}, u32[]{:S(2)}, u32[]{:S(2)}) collective-permute-start(f32[2,128]{1,0:T(2,128)S(1)} %slice.12), channel_id=1, source_target_pairs={{0,4},{4,0},{8,12},{12,8},{16,20},{20,16},{24,28},{28,24},{32,36},... | collective-permute-start | bytes 3080 | tf_op jit(solution)/shard_map/ppermute | solution.py:143
  19.5 8.8 %collective-permute-start.4 = (f32[4,128]{1,0:T(4,128)S(1)}, f32[4,128]{1,0:T(4,128)S(1)}, u32[]{:S(2)}, u32[]{:S(2)}) collective-permute-start(f32[4,128]{1,0:T(4,128)S(1)} %pad_maximum_fusion.1), channel_id=1, source_target_pairs={{0,8},{4,12},{8,16},{12,20},{16,24},{20,28},{24,0},{28,4},{32,40},... | collective-permute-start | bytes 6152 | tf_op jit(solution)/shard_map/ppermute | solution.py:149
  21.3 7.3 %collective-permute-start.5 = (f32[4,128]{1,0:T(4,128)S(1)}, f32[4,128]{1,0:T(4,128)S(1)}, u32[]{:S(2)}, u32[]{:S(2)}) collective-permute-start(f32[4,128]{1,0:T(4,128)S(1)} %pad_maximum_fusion.1), channel_id=1, source_target_pairs={{0,16},{4,20},{8,24},{12,28},{16,0},{20,4},{24,8},{28,12},{32,48},... | collective-permute-start | bytes 6152 | tf_op jit(solution)/shard_map/ppermute | solution.py:149
  24.0 4.6 %collective-permute-start.6 = (f32[4,128]{1,0:T(4,128)S(1)}, f32[4,128]{1,0:T(4,128)S(1)}, u32[]{:S(2)}, u32[]{:S(2)}) collective-permute-start(f32[4,128]{1,0:T(4,128)S(1)} %pad_maximum_fusion.1), channel_id=1, source_target_pairs={{0,24},{4,28},{8,0},{12,4},{16,8},{20,12},{24,16},{28,20},{32,56},... | collective-permute-start | bytes 6152 | tf_op jit(solution)/shard_map/ppermute | solution.py:149
  28.6 7.3 %collective-permute-start.7 = (f32[16,128]{1,0:T(8,128)S(1)}, f32[16,128]{1,0:T(8,128)S(1)}, u32[]{:S(2)}, u32[]{:S(2)}) collective-permute-start(f32[16,128]{1,0:T(8,128)S(1)} %concatenate.15), channel_id=1, source_target_pairs={{0,32},{4,36},{8,40},{12,44},{16,48},{20,52},{24,56},{28,60},{32,0... | collective-permute-start | bytes 24584 | tf_op jit(solution)/shard_map/ppermute | solution.py:143
  33.2 3.9 %copy-start.3 = (s32[16]{0:T(128)S(1)}, s32[16]{0:T(128)}, u32[]{:S(2)}) copy-start(s32[16]{0:T(128)} %order_ref.1) | copy-start | bytes 196
  36.0 1.1 %copy-start.4 = (bf16[16,384,128]{2,1,0:T(8,128)(2,1)}, bf16[16,384,128]{2,1,0:T(8,128)(2,1)S(1)}, u32[]{:S(2)}) copy-start(bf16[16,384,128]{2,1,0:T(8,128)(2,1)S(1)} %all-to-all-done.raw_hbm) | copy-start | bytes 4718596
  45.1 5.2 %copy-start = (bf16[1,128,2048]{2,1,0:T(8,128)(2,1)S(1)}, bf16[1,128,2048]{2,1,0:T(8,128)(2,1)}, u32[]{:S(2)}) copy-start(bf16[1,128,2048]{2,1,0:T(8,128)(2,1)} %saved_ref.5) | copy-start | bytes 1572868
  45.1 23.9 %copy-start.1 = (bf16[1,128,2048]{2,1,0:T(8,128)(2,1)S(1)}, bf16[1,128,2048]{2,1,0:T(8,128)(2,1)}, u32[]{:S(2)}) copy-start(bf16[1,128,2048]{2,1,0:T(8,128)(2,1)} %cot_ref.3) | copy-start | bytes 1572868
  45.1 23.9 %copy-start.2 = (bf16[1,128,2048]{2,1,0:T(8,128)(2,1)S(1)}, bf16[1,128,2048]{2,1,0:T(8,128)(2,1)}, u32[]{:S(2)}) copy-start(bf16[1,128,2048]{2,1,0:T(8,128)(2,1)} %sconv_ref.3) | copy-start | bytes 1572868
  45.1 23.9 %all-to-all-start.1 = ((bf16[16,152,256]{2,1,0:T(8,128)(2,1)}), bf16[16,152,256]{2,1,0:T(8,128)(2,1)S(1)}, u32[]{:S(2)}, u32[]{:S(2)}) async-start(bf16[16,152,256]{2,1,0:T(8,128)(2,1)} %convolve.1), calls=%async_computation.1 | async-start | bytes 2490368 | tf_op jit(solution)/shard_map/all_to_all | solution.py:660
  50.3 47.6 %collective-permute-start.12 = (bf16[1,128,2048]{2,1,0:T(8,128)(2,1)S(1)}, bf16[1,128,2048]{2,1,0:T(8,128)(2,1)S(1)}, u32[]{:S(2)}, u32[]{:S(2)}) collective-permute-start(bf16[1,128,2048]{2,1,0:T(8,128)(2,1)S(1)} %copy-done), channel_id=1, source_target_pairs={{64,0},{65,1},{66,2},{67,3},{68,4},{69,5},{70,6},{71,7},{72,8},{73... | collective-permute-start | bytes 1572872 | tf_op jit(solution)/shard_map/ppermute | solution.py:656
  70.6 30.5 %collective-permute-start.13 = (bf16[1,128,2048]{2,1,0:T(8,128)(2,1)S(1)}, bf16[1,128,2048]{2,1,0:T(8,128)(2,1)S(1)}, u32[]{:S(2)}, u32[]{:S(2)}) collective-permute-start(bf16[1,128,2048]{2,1,0:T(8,128)(2,1)S(1)} %get-tuple-element.15.send_ref), channel_id=1, source_target_pairs={{0,64},{64,0},{1,65},{65,1},{2,66},{66,2},{3,67},{67,3},{4,68},{68... | collective-permute-start | bytes 1572872 | tf_op jit(solution)/shard_map/ppermute | solution.py:665
  74.0 16.5 %collective-permute-start.8 = (f32[8,128]{1,0:T(8,128)S(1)}, f32[8,128]{1,0:T(8,128)S(1)}, u32[]{:S(2)}, u32[]{:S(2)}) collective-permute-start(f32[8,128]{1,0:T(8,128)S(1)} %get-tuple-element.18), channel_id=1, source_target_pairs={{64,0},{65,1},{66,2},{67,3},{68,4},{69,5},{70,6},{71,7},{72,8},{73... | collective-permute-start | bytes 12296 | tf_op jit(solution)/shard_map/ppermute | solution.py:664
  90.5 7.4 %collective-permute-start.10 = (f32[8,128]{1,0:T(8,128)S(1)}, f32[8,128]{1,0:T(8,128)S(1)}, u32[]{:S(2)}, u32[]{:S(2)}) collective-permute-start(f32[8,128]{1,0:T(8,128)S(1)} %pad_maximum_fusion.s0), channel_id=1, source_target_pairs={{0,2},{1,3},{2,0},{3,1},{4,6},{5,7},{6,4},{7,5},{8,10},{9,11},{10,... | collective-permute-start | bytes 12296 | tf_op jit(solution)/shard_map/ppermute | solution.py:136
  94.4 3.6 %collective-permute-start.11 = (f32[8,128]{1,0:T(8,128)S(1)}, f32[8,128]{1,0:T(8,128)S(1)}, u32[]{:S(2)}, u32[]{:S(2)}) collective-permute-start(f32[8,128]{1,0:T(8,128)S(1)} %pad_maximum_fusion.s0), channel_id=1, source_target_pairs={{0,3},{1,0},{2,1},{3,2},{4,7},{5,4},{6,5},{7,6},{8,11},{9,8},{10,9... | collective-permute-start | bytes 12296 | tf_op jit(solution)/shard_map/ppermute | solution.py:136
  95.2 4.8 %collective-permute-start.9 = (f32[8,128]{1,0:T(8,128)S(1)}, f32[8,128]{1,0:T(8,128)S(1)}, u32[]{:S(2)}, u32[]{:S(2)}) collective-permute-start(f32[8,128]{1,0:T(8,128)S(1)} %pad_maximum_fusion.s0), channel_id=1, source_target_pairs={{0,1},{1,2},{2,3},{3,0},{4,5},{5,6},{6,7},{7,4},{8,9},{9,10},{10,1... | collective-permute-start | bytes 12296 | tf_op jit(solution)/shard_map/ppermute | solution.py:136

commit v10 on v9

--- a/solution.py
+++ b/solution.py
@@ -166,13 +166,13 @@
         inv[...] = rows_to_columns(lax.rsqrt(sums_ref[...] / D + EPSILON))
 
     inv_saved = inv[:, 1:2]
-    pairs = saved_ref.shape[2] // (2 * LANES)
+    groups = saved_ref.shape[2] // LANES
     half = out_ref.shape[0] // 2
-    for pair in range(pairs):
-        at = pl.ds(pair * 2 * LANES, 2 * LANES)
+    for group in range(groups):
+        at = pl.ds(group * LANES, LANES)
         normed = saved_ref[0, :, at].astype(jnp.float32) * inv_saved
         grad_query = cot_ref[0, :, at].astype(jnp.float32) * sconv_ref[0, :, at].astype(jnp.float32)
-        row = step * pairs + pair
+        row = step * groups + group
         out_ref[pl.ds(row, 1), :] = jnp.sum(grad_query, axis=0, keepdims=True)
         out_ref[pl.ds(row + half, 1), :] = jnp.sum(grad_query * normed, axis=0, keepdims=True)
 
@@ -180,16 +180,17 @@
 def early(sums, saved_in, saved_conv, grad_out):
     rows, width = saved_in.shape[1:]
     wide = 512
+    shape = (2 * width // LANES, LANES)
     return pl.pallas_call(
         early_kernel,
-        out_shape=jax.ShapeDtypeStruct((width // LANES, 2 * LANES), jnp.float32),
+        out_shape=jax.ShapeDtypeStruct(shape, jnp.float32),
         grid=(width // wide,),
         in_specs=[VMEM] + [lane_spec(rows, wide)] * 3,
-        out_specs=whole((width // LANES, 2 * LANES)),
+        out_specs=whole(shape),
         scratch_shapes=[pltpu.VMEM((rows, 128), jnp.float32)],
         name="early",
         compiler_params=pltpu.CompilerParams(vmem_limit_bytes=12 << 20),
-    )(sums, in_hbm(saved_in), in_hbm(saved_conv), in_hbm(grad_out))
+    )(sums, in_vmem(saved_in), in_vmem(saved_conv), in_vmem(grad_out))
 
 
 def side_by_side(ref, index):
@@ -239,7 +240,7 @@
 
 
 def conv_kernel(
-    where_ref, order_ref, gathered_ref, inv_ref, known_ref, params_ref, filt_hbm, raw_hbm, enter_hbm,
+    where_ref, order_ref, gathered_ref, inv_ref, params_ref, filt_hbm, raw_hbm, enter_hbm,
     leave_hbm, out_hbm, raw_ref, filt, enter, leave, out_ref, ordered, spectra, product, inv_rows, inv, raw_sem, table_sem, out_sem,
 ):
     stored = raw_ref.shape[0]
@@ -369,34 +370,32 @@
         + [jnp.zeros((5, LANES), jnp.float32)],
         axis=0,
     )
-    known = known_ref[...].astype(jnp.bfloat16)
     top = sums.astype(jnp.bfloat16)
     rest = (sums - top.astype(jnp.float32)).astype(jnp.bfloat16)
     for index in range(stored):
-        out_ref[index, rows : rows + 16, :] = known
-        out_ref[index, rows + 16 :, :LANES] = top
-        out_ref[index, rows + 16 :, LANES:] = rest
+        out_ref[index, rows:, :LANES] = top
+        out_ref[index, rows:, LANES:] = rest
         out_copies[index].start()
     for copy in out_copies:
         copy.wait()
 
 
-def convolve(where, order, gathered, raw, inv, known, params, spectra, tables):
+def convolve(where, order, gathered, raw, inv, params, spectra, tables):
     stored = raw.shape[0]
     rows = raw.shape[1] // 3
     length = stored * rows
     blocks = length // BLOCK
     return pl.pallas_call(
         conv_kernel,
-        out_shape=pltpu.HBM((stored, rows + 24, 2 * LANES), jnp.bfloat16),
-        in_specs=[SMEM] * 3 + [VMEM] * 3 + [HBM] * 4,
+        out_shape=pltpu.HBM((stored, rows + 8, 2 * LANES), jnp.bfloat16),
+        in_specs=[SMEM] * 3 + [VMEM] * 2 + [HBM] * 4,
         out_specs=HBM,
         scratch_shapes=[
             pltpu.VMEM(raw.shape, jnp.bfloat16),
             pltpu.VMEM(spectra.shape, jnp.float32),
             pltpu.VMEM((2 * BLOCK, BLOCK), jnp.bfloat16),
             pltpu.VMEM((BLOCK, 2 * BLOCK), jnp.bfloat16),
-            pltpu.VMEM((stored, rows + 24, 2 * LANES), jnp.bfloat16),
+            pltpu.VMEM((stored, rows + 8, 2 * LANES), jnp.bfloat16),
             pltpu.VMEM((length, 2 * LANES), jnp.bfloat16),
             pltpu.VMEM((blocks, 2 * BLOCK, 2 * LANES), jnp.float32),
             pltpu.VMEM((blocks, 2 * BLOCK, 2 * LANES), jnp.float32),
@@ -409,7 +408,7 @@
         name="convolve",
         compiler_params=pltpu.CompilerParams(vmem_limit_bytes=28 << 20),
     )(
-        where, order, gathered, inv, known, params, in_hbm(spectra), in_hbm(raw),
+        where, order, gathered, inv, params, in_hbm(spectra), in_hbm(raw),
         *[in_hbm(table) for table in tables],
     )
 
@@ -496,7 +495,7 @@
 
 
 def rows_kernel(
-    pipe_ref, back_ref, send_ref, keep_ref, params_ref, layer_hbm, grads_ref, layer_sem
+    pipe_ref, known_ref, back_ref, send_ref, keep_ref, params_ref, layer_hbm, grads_ref, layer_sem
 ):
     first = pipe_ref[0] == 0
     stored, rows = back_ref.shape[0], send_ref.shape[1]
@@ -511,17 +510,14 @@
     def _():
         kept.start()
 
-    known = back_ref[0, rows : rows + 16, :].astype(jnp.float32)
-    for index in range(1, stored):
-        known = known + back_ref[index, rows : rows + 16, :].astype(jnp.float32)
     for group in range(stored):
         own = pl.ds(group * LANES, LANES)
         p = [params_ref[0, row : row + 1, own] for row in range(7)]
-        extra = back_ref[group, rows + 16 :, :].astype(jnp.float32)
+        extra = back_ref[group, rows:, :].astype(jnp.float32)
         extra = extra[:, :LANES] + extra[:, LANES:]
         m0, m1, m2 = extra[0:1], extra[1:2], extra[2:3]
-        row, side = group // 2, slice(group % 2 * LANES, (group % 2 + 1) * LANES)
-        q0, q1 = known[row : row + 1, side], known[row + 8 : row + 9, side]
+        q0 = known_ref[group : group + 1, :]
+        q1 = known_ref[stored + group : stored + group + 1, :]
         key_normed = p[0] * p[5] * m2 + p[6] * m1
         value_normed = p[0] * p[3] * m2 + p[4] * m1
         grads = [
@@ -545,19 +541,19 @@
         kept.wait()
 
 
-def finish_rows(pipe, back, send, keep, mix_params):
+def finish_rows(pipe, known, back, send, keep, mix_params):
     return pl.pallas_call(
         rows_kernel,
         out_shape=(
             pltpu.HBM(send.shape, jnp.bfloat16),
             jax.ShapeDtypeStruct((7, 1, send.shape[2]), jnp.float32),
         ),
-        in_specs=[SMEM] + [VMEM] * 4,
+        in_specs=[SMEM] + [VMEM] * 5,
         out_specs=(HBM, VMEM),
         scratch_shapes=[pltpu.SemaphoreType.DMA],
         name="finish_rows",
         compiler_params=pltpu.CompilerParams(vmem_limit_bytes=8 << 20),
-    )(pipe, in_vmem(back), in_vmem(send), in_vmem(keep), mix_params)
+    )(pipe, known, in_vmem(back), in_vmem(send), in_vmem(keep), mix_params)
 
 
 def cross_kernel(
@@ -650,13 +646,21 @@
     raw = lax.all_to_all(raw, "seq", 0, 0)
     own_sums = sum(over_chan(sums))
     sums = own_sums[:2]
-    sums = jnp.concatenate([sums, across(sums, 1)], axis=0)
-    sums = jnp.concatenate([sums] + [round_ring(sums, apart) for apart in (1, 2, 3)], axis=0)
-    inv = lax.rsqrt(jnp.concatenate([sums, across(sums, 8)], axis=0) / D + EPSILON)
+    known = early(own_sums, saved_in, saved_conv, grad_out)
+    got = across(jnp.concatenate([sums, known], axis=0), 1)
+    sums = jnp.concatenate([sums, got[:2]], axis=0)
+    known = known + got[2:]
+    message = jnp.concatenate([sums, known], axis=0)
+    got = [message] + [round_ring(message, apart) for apart in (1, 2, 3)]
+    sums = jnp.concatenate([rows[:4] for rows in got], axis=0)
+    got = [rows[4:] for rows in got]
+    known = (got[0] + got[2]) + (got[1] + got[3])
+    got = across(jnp.concatenate([sums, known], axis=0), 8)
+    inv = lax.rsqrt(jnp.concatenate([sums, got[:16]], axis=0) / D + EPSILON)
+    known = known + got[16:]
     peer_saved = lax.ppermute(saved_in, "pipe", [(1, 0)])
     spectra = filter_spectra(where, filters, tables)
-    known = early(own_sums, saved_in, saved_conv, grad_out)
-    back = convolve(where, span_order, gather_order(), raw, inv, known, mix_params, spectra, tables)
+    back = convolve(where, span_order, gather_order(), raw, inv, mix_params, spectra, tables)
     back = lax.all_to_all(back, "seq", 0, 0)
     outgoing, keep, cross = leave(
         pipe, inv, back, fwd_in, saved_in, saved_conv, grad_out, mix_params
@@ -664,7 +668,7 @@
     peer_cross = lax.ppermute(cross, "pipe", [(1, 0)])
     incoming = lax.ppermute(outgoing, "pipe", [(0, 1), (1, 0)])
     scales = over_chan(jnp.concatenate([cross[:1], peer_cross[:1], cross[:6]], axis=0))
-    layer_out, param_grad = finish_rows(pipe, back, outgoing, keep, mix_params)
+    layer_out, param_grad = finish_rows(pipe, known, back, outgoing, keep, mix_params)
     input_grad, term = finish_cross(pipe, scales, outgoing, keep, saved_in, peer_saved)
     received = finish_received(incoming, term)
     return (layer_out, input_grad, param_grad.transpose(1, 0, 2), received)

time: 102 us -> 98.1 us (0.962)
  Pallas kernels: 21.3 us -> 19.4 us
  starting transfers between devices: 37.1 us -> 35.6 us
  local copies, waits for them, and re-layouts: 1.27 us -> 0.16 us
    pallas_call x2, Pallas kernels: 10.6 us -> 8.68 us  [the longest x1 7.93 us: convolve(): pl.pallas_call(conv_kernel, out_shape=pltpu.HBM((stored, rows + 8, 2 * LA...]
    all_to_all x1, waiting for transfers between devices: 17.4 us -> 15.9 us  [per_device(): back = lax.all_to_all(back, 'seq', 0, 0)]
    ppermute x6, starting transfers between devices: 12.6 us -> 11.1 us  [over_chan(): lax.ppermute(rows, 'chan', [(low, (low + apart) % count) for low in range...]
    ppermute x3, waiting for transfers between devices: 3.13 us -> 4.4 us  [round_ring(): lax.ppermute(rows, 'seq', [(low, place(low)) for low in range(count)])]
    unnamed x13 -> x11, local copies, waits for them, and re-layouts: 1.18 us -> 0.06 us
  transfers between devices with their start and end apart: 16 -> 16, of which waited for: 9 -> 9; matrix products, arithmetic and copies ran while one was open for 0% -> 0% of each run, Pallas kernels for 10% -> 8%
where the time goes in v10:
time: 98.1 us; the launch traced here: 97.7 us
  waiting for transfers between devices  41.6 us (42%)
  starting transfers between devices  35.6 us (36%)
  Pallas kernels  19.4 us (20%)
    all_to_all x1, waiting for transfers between devices, per_device(): back = lax.all_to_all(back, 'seq', 0, 0)  15.9 us
    ppermute x1, waiting for transfers between devices, per_device(): peer_cross = lax.ppermute(cross, 'pipe', [(1, 0)])  15.2 us
    ppermute x6, starting transfers between devices, over_chan(): lax.ppermute(rows, 'chan', [(low, (low + apart) % count) for low in range...  11.1 us
    pallas_call x1, Pallas kernels, convolve(): pl.pallas_call(conv_kernel, out_shape=pltpu.HBM((stored, rows + 8, 2 * LA...  7.93 us
    ppermute x3, starting transfers between devices, round_ring(): lax.ppermute(rows, 'seq', [(low, place(low)) for low in range(count)])  6.08 us
    all_to_all x1, starting transfers between devices, per_device(): raw = lax.all_to_all(raw, 'seq', 0, 0)  5.8 us
    ppermute x6, waiting for transfers between devices, over_chan(): lax.ppermute(rows, 'chan', [(low, (low + apart) % count) for low in range...  4.82 us
    all_to_all x1, starting transfers between devices, per_device(): back = lax.all_to_all(back, 'seq', 0, 0)  4.56 us
  transfers between devices with their start and end apart: 16, of which 9 were waited for; matrix products, arithmetic and copies ran while one was open for 0% of the time, Pallas kernels for 8%

profile of v10, /device:TPU:0, one launch (start us, length us, event | category | flops | bytes accessed | tf_op | source)
XLA Modules:
  0.0 97.7 jit_solution(7994199280733884415)
XLA Ops:
  0.6 2.7 %pack.1 = (bf16[16,384,128]{2,1,0:T(8,128)(2,1)}, f32[8,128]{1,0:T(8,128)S(1)}) custom-call(bf16[1,128,2048]{2,1,0:T(8,128)(2,1)} %fwd_hbm.3, bf16[1,128,2048]{2,1,0:T(8,128)(2,1)} %saved_ref.5, bf16[1,128,2048]{2,1,0:T(8,128)(2,1)} %cot_ref.3), custom_call_target="tpu_custom_call" | custom-call | tf_op jit(solution)/shard_map/pack/pallas_call | solution.py:113
  3.4 0.0 copy-start
  3.4 0.0 copy-start.1
  3.4 0.0 copy-start.2
  3.4 5.8 %all-to-all-start = ((bf16[16,384,128]{2,1,0:T(8,128)(2,1)}), bf16[16,384,128]{2,1,0:T(8,128)(2,1)}, u32[]{:S(2)}, u32[]{:S(2)}) async-start(bf16[16,384,128]{2,1,0:T(8,128)(2,1)} %get-tuple-element.14), calls=%async_computation | async-start | bytes 3145728 | tf_op jit(solution)/shard_map/all_to_all | solution.py:646
  9.2 0.0 copy-start.4
  9.2 4.1 %collective-permute-start.2 = (f32[8,128]{1,0:T(8,128)S(1)}, f32[8,128]{1,0:T(8,128)S(1)}, u32[]{:S(2)}, u32[]{:S(2)}) collective-permute-start(f32[8,128]{1,0:T(8,128)S(1)} %get-tuple-element.13), channel_id=1, source_target_pairs={{0,3},{1,0},{2,1},{3,2},{4,7},{5,4},{6,5},{7,6},{8,11},{9,8},{10,9... | collective-permute-start | bytes 12296 | tf_op jit(solution)/shard_map/ppermute | solution.py:136
  13.3 0.0 collective-permute-start.1
  13.3 1.3 %collective-permute-start = (f32[8,128]{1,0:T(8,128)S(1)}, f32[8,128]{1,0:T(8,128)S(1)}, u32[]{:S(2)}, u32[]{:S(2)}) collective-permute-start(f32[8,128]{1,0:T(8,128)S(1)} %get-tuple-element.13), channel_id=1, source_target_pairs={{0,1},{1,2},{2,3},{3,0},{4,5},{5,6},{6,7},{7,4},{8,9},{9,10},{10,1... | collective-permute-start | bytes 12296 | tf_op jit(solution)/shard_map/ppermute | solution.py:136
  14.6 0.1 collective-permute-done.2
  14.7 3.8 %collective-permute-done.1 = f32[8,128]{1,0:T(8,128)S(1)} collective-permute-done((f32[8,128]{1,0:T(8,128)S(1)}, f32[8,128]{1,0:T(8,128)S(1)}, u32[]{:S(2)}, u32[]{:S(2)}) %collective-permute-start.1) | collective-permute-done | bytes 4128 | tf_op jit(solution)/shard_map/ppermute | solution.py:136
  18.4 0.0 collective-permute-done
  18.5 0.0 copy-done
  18.5 0.0 copy-done.1
  18.5 0.0 copy-done.2
  18.5 0.8 early.1
  19.3 0.1 collective-permute-start.3
  19.4 1.2 %collective-permute-done.3 = f32[34,128]{1,0:T(8,128)S(1)} collective-permute-done((f32[34,128]{1,0:T(8,128)S(1)}, f32[34,128]{1,0:T(8,128)S(1)}, u32[]{:S(2)}, u32[]{:S(2)}) %collective-permute-start.3) | collective-permute-done | bytes 17440 | tf_op jit(solution)/shard_map/ppermute | solution.py:143
  20.6 1.9 %collective-permute-start.5 = (f32[36,128]{1,0:T(8,128)S(1)}, f32[36,128]{1,0:T(8,128)S(1)}, u32[]{:S(2)}, u32[]{:S(2)}) collective-permute-start(f32[36,128]{1,0:T(8,128)S(1)} %pad_maximum_fusion.1), channel_id=1, source_target_pairs={{0,8},{4,12},{8,16},{12,20},{16,24},{20,28},{24,0},{28,4},{32,40},... | collective-permute-start | bytes 55304 | tf_op jit(solution)/shard_map/ppermute | solution.py:149
  22.5 2.7 %collective-permute-start.4 = (f32[36,128]{1,0:T(8,128)S(1)}, f32[36,128]{1,0:T(8,128)S(1)}, u32[]{:S(2)}, u32[]{:S(2)}) collective-permute-start(f32[36,128]{1,0:T(8,128)S(1)} %pad_maximum_fusion.1), channel_id=1, source_target_pairs={{0,16},{4,20},{8,24},{12,28},{16,0},{20,4},{24,8},{28,12},{32,48},... | collective-permute-start | bytes 55304 | tf_op jit(solution)/shard_map/ppermute | solution.py:149
  25.2 1.5 %collective-permute-start.6 = (f32[36,128]{1,0:T(8,128)S(1)}, f32[36,128]{1,0:T(8,128)S(1)}, u32[]{:S(2)}, u32[]{:S(2)}) collective-permute-start(f32[36,128]{1,0:T(8,128)S(1)} %pad_maximum_fusion.1), channel_id=1, source_target_pairs={{0,24},{4,28},{8,0},{12,4},{16,8},{20,12},{24,16},{28,20},{32,56},... | collective-permute-start | bytes 55304 | tf_op jit(solution)/shard_map/ppermute | solution.py:149
  26.6 2.2 %collective-permute-done.5 = f32[36,128]{1,0:T(8,128)S(1)} collective-permute-done((f32[36,128]{1,0:T(8,128)S(1)}, f32[36,128]{1,0:T(8,128)S(1)}, u32[]{:S(2)}, u32[]{:S(2)}) %collective-permute-start.5) | collective-permute-done | bytes 18464 | tf_op jit(solution)/shard_map/ppermute | solution.py:149
  28.8 0.7 collective-permute-done.4
  29.5 1.5 %collective-permute-done.6 = f32[36,128]{1,0:T(8,128)S(1)} collective-permute-done((f32[36,128]{1,0:T(8,128)S(1)}, f32[36,128]{1,0:T(8,128)S(1)}, u32[]{:S(2)}, u32[]{:S(2)}) %collective-permute-start.6) | collective-permute-done | bytes 18464 | tf_op jit(solution)/shard_map/ppermute | solution.py:149
  31.1 2.0 %collective-permute-start.7 = (f32[48,128]{1,0:T(8,128)S(1)}, f32[48,128]{1,0:T(8,128)S(1)}, u32[]{:S(2)}, u32[]{:S(2)}) collective-permute-start(f32[48,128]{1,0:T(8,128)S(1)} %concatenate.23), channel_id=1, source_target_pairs={{0,32},{4,36},{8,40},{12,44},{16,48},{20,52},{24,56},{28,60},{32,0... | collective-permute-start | bytes 73736 | tf_op jit(solution)/shard_map/ppermute | solution.py:143
  33.1 0.0 copy-done.4
  33.2 0.0 copy-start.3
  33.2 2.9 %filter_spectra.1.filt_hbm = f32[8,2,256,128]{3,2,1,0:T(8,128)} custom-call(s32[1]{0:T(128)} %bitcast.1.where_ref, bf16[1,2048,2048]{2,1,0:T(8,128)(2,1)} %taps_ref.1, bf16[512,256]{1,0:T(8,128)(2,1)} %constant.84.clone.enter.enter_hbm), custom_call_target="tpu_custom_call" | custom-call | tf_op jit(solution)/shard_map/filter_spectra/pallas_call | solution.py:223
  36.1 0.0 collective-permute-done.7
  36.2 0.0 all-to-all-done.raw_hbm
  36.2 0.0 copy-done.3
  36.2 7.9 %convolve.1 = bf16[16,136,256]{2,1,0:T(8,128)(2,1)} custom-call(s32[1]{0:T(128)} %bitcast.1.where_ref, s32[16]{0:T(128)S(1)} %copy-done.3, s32[16]{0:T(128)S(1)} %fusion.5.gathered_ref, f32[32,128]{1,0:T(8,128)S(1)} %add_rsqrt_fusion.inv_ref, f32[1,7,2048]{2,1,0:T(8,128)S(1)} %copy.13.params_ref, f32[8,2,256,128]{3,2,1,0:T(8,128)} %filter_spectra.1.filt_hbm, ...), custom_call_target="tpu_custom_call" | custom-call | tf_op jit(solution)/shard_map/convolve/pallas_call | solution.py:388
  44.1 4.6 %all-to-all-start.1 = ((bf16[16,136,256]{2,1,0:T(8,128)(2,1)}), bf16[16,136,256]{2,1,0:T(8,128)(2,1)S(1)}, u32[]{:S(2)}, u32[]{:S(2)}) async-start(bf16[16,136,256]{2,1,0:T(8,128)(2,1)} %convolve.1), calls=%async_computation.1 | async-start | bytes 2228224 | tf_op jit(solution)/shard_map/all_to_all | solution.py:664
  48.7 1.3 %collective-permute-start.12 = (bf16[1,128,2048]{2,1,0:T(8,128)(2,1)S(1)}, bf16[1,128,2048]{2,1,0:T(8,128)(2,1)S(1)}, u32[]{:S(2)}, u32[]{:S(2)}) collective-permute-start(bf16[1,128,2048]{2,1,0:T(8,128)(2,1)S(1)} %copy-done), channel_id=1, source_target_pairs={{64,0},{65,1},{66,2},{67,3},{68,4},{69,5},{70,6},{71,7},{72,8},{73... | collective-permute-start | bytes 1572872 | tf_op jit(solution)/shard_map/ppermute | solution.py:661
  50.0 15.9 %all-to-all-done.1.back_ref = bf16[16,136,256]{2,1,0:T(8,128)(2,1)S(1)} async-done(((bf16[16,136,256]{2,1,0:T(8,128)(2,1)}), bf16[16,136,256]{2,1,0:T(8,128)(2,1)S(1)}, u32[]{:S(2)}, u32[]{:S(2)}) %all-to-all-start.1) | async-done | bytes 1114144 | tf_op jit(solution)/shard_map/all_to_all | solution.py:664
  65.9 1.6 %leave.1 = (bf16[1,128,2048]{2,1,0:T(8,128)(2,1)S(1)}, bf16[1,128,2048]{2,1,0:T(8,128)(2,1)S(1)}, f32[8,128]{1,0:T(8,128)S(1)}) custom-call(s32[1]{0:T(128)} %bitcast.pipe_ref, f32[32,128]{1,0:T(8,128)S(1)} %add_rsqrt_fusion.inv_ref, bf16[16,136,256]{2,1,0:T(8,128)(2,1)S(1)} %all-to-all-done.1.back_ref, bf16[1,128,2048]{2,1,0:T(8,128)(2,1)} %fwd_hbm.3, ...), custom_call_target="tpu_custom_call" | custom-call | tf_op jit(solution)/shard_map/leave/pallas_call | solution.py:478
  67.6 3.4 %collective-permute-start.13 = (bf16[1,128,2048]{2,1,0:T(8,128)(2,1)S(1)}, bf16[1,128,2048]{2,1,0:T(8,128)(2,1)S(1)}, u32[]{:S(2)}, u32[]{:S(2)}) collective-permute-start(bf16[1,128,2048]{2,1,0:T(8,128)(2,1)S(1)} %get-tuple-element.15.send_ref), channel_id=1, source_target_pairs={{0,64},{64,0},{1,65},{65,1},{2,66},{66,2},{3,67},{67,3},{4,68},{68... | collective-permute-start | bytes 1572872 | tf_op jit(solution)/shard_map/ppermute | solution.py:669
  70.9 1.3 %collective-permute-start.8 = (f32[8,128]{1,0:T(8,128)S(1)}, f32[8,128]{1,0:T(8,128)S(1)}, u32[]{:S(2)}, u32[]{:S(2)}) collective-permute-start(f32[8,128]{1,0:T(8,128)S(1)} %get-tuple-element.18), channel_id=1, source_target_pairs={{64,0},{65,1},{66,2},{67,3},{68,4},{69,5},{70,6},{71,7},{72,8},{73... | collective-permute-start | bytes 12296 | tf_op jit(solution)/shard_map/ppermute | solution.py:668
  72.2 15.2 %collective-permute-done.8 = f32[8,128]{1,0:T(8,128)S(1)} collective-permute-done((f32[8,128]{1,0:T(8,128)S(1)}, f32[8,128]{1,0:T(8,128)S(1)}, u32[]{:S(2)}, u32[]{:S(2)}) %collective-permute-start.8) | collective-permute-done | bytes 4128 | tf_op jit(solution)/shard_map/ppermute | solution.py:668
  87.5 1.2 %collective-permute-start.9 = (f32[8,128]{1,0:T(8,128)S(1)}, f32[8,128]{1,0:T(8,128)S(1)}, u32[]{:S(2)}, u32[]{:S(2)}) collective-permute-start(f32[8,128]{1,0:T(8,128)S(1)} %pad_maximum_fusion.2.s0), channel_id=1, source_target_pairs={{0,1},{1,2},{2,3},{3,0},{4,5},{5,6},{6,7},{7,4},{8,9},{9,10},{10,1... | collective-permute-start | bytes 12296 | tf_op jit(solution)/shard_map/ppermute | solution.py:136
  88.6 3.4 %collective-permute-start.10 = (f32[8,128]{1,0:T(8,128)S(1)}, f32[8,128]{1,0:T(8,128)S(1)}, u32[]{:S(2)}, u32[]{:S(2)}) collective-permute-start(f32[8,128]{1,0:T(8,128)S(1)} %pad_maximum_fusion.2.s0), channel_id=1, source_target_pairs={{0,2},{1,3},{2,0},{3,1},{4,6},{5,7},{6,4},{7,5},{8,10},{9,11},{10,... | collective-permute-start | bytes 12296 | tf_op jit(solution)/shard_map/ppermute | solution.py:136
  92.1 1.2 %collective-permute-start.11 = (f32[8,128]{1,0:T(8,128)S(1)}, f32[8,128]{1,0:T(8,128)S(1)}, u32[]{:S(2)}, u32[]{:S(2)}) collective-permute-start(f32[8,128]{1,0:T(8,128)S(1)} %pad_maximum_fusion.2.s0), channel_id=1, source_target_pairs={{0,3},{1,0},{2,1},{3,2},{4,7},{5,4},{6,5},{7,6},{8,11},{9,8},{10,9... | collective-permute-start | bytes 12296 | tf_op jit(solution)/shard_map/ppermute | solution.py:136
  93.2 1.4 %finish_rows.1 = (bf16[1,128,2048]{2,1,0:T(8,128)(2,1)}, f32[7,1,2048]{2,1,0:T(1,128)}) custom-call(s32[1]{0:T(128)} %bitcast.pipe_ref, f32[32,128]{1,0:T(8,128)S(1)} %slice_add_fusion.known_ref, bf16[16,136,256]{2,1,0:T(8,128)(2,1)S(1)} %all-to-all-done.1.back_ref, bf16[1,128,2048]{2,1,0:T(8,128)(2,1)S(1)} %get-tuple-element.15.send_ref, ...), custom_call_target="tpu_custom_call" | custom-call | tf_op jit(solution)/shard_map/finish_rows/pallas_call | solution.py:545
  94.7 0.0 collective-permute-done.12.peer_ref
  94.7 0.0 collective-permute-done.9.s1
  94.7 0.0 collective-permute-done.10.s2
  94.7 1.0 collective-permute-done.11.s3
  95.7 1.2 %finish_cross.1 = (bf16[1,128,2048]{2,1,0:T(8,128)(2,1)}, f32[128,2048]{1,0:T(8,128)S(1)}) custom-call(s32[1]{0:T(128)} %bitcast.pipe_ref, f32[8,128]{1,0:T(8,128)S(1)} %pad_maximum_fusion.2.s0, f32[8,128]{1,0:T(8,128)S(1)} %collective-permute-done.9.s1, f32[8,128]{1,0:T(8,128)S(1)} %collective-permute-done.10.s2, f32[8,128]{1,0:T(8,128)S(1)} %collective-permute-done.11.s3, ...), custom_call_target="tpu_custom_call" | custom-call | tf_op jit(solution)/shard_map/finish_cross/pallas_call | solution.py:589
  96.8 0.0 collective-permute-done.13.value_ref
  96.8 0.9 received.1
  (20 shorter events, 0.2 us)
Async XLA Ops:
  3.4 15.1 %copy-start = (bf16[1,128,2048]{2,1,0:T(8,128)(2,1)S(1)}, bf16[1,128,2048]{2,1,0:T(8,128)(2,1)}, u32[]{:S(2)}) copy-start(bf16[1,128,2048]{2,1,0:T(8,128)(2,1)} %saved_ref.5) | copy-start | bytes 1572868
  3.4 15.1 %copy-start.1 = (bf16[1,128,2048]{2,1,0:T(8,128)(2,1)S(1)}, bf16[1,128,2048]{2,1,0:T(8,128)(2,1)}, u32[]{:S(2)}) copy-start(bf16[1,128,2048]{2,1,0:T(8,128)(2,1)} %cot_ref.3) | copy-start | bytes 1572868
  3.4 15.1 %copy-start.2 = (bf16[1,128,2048]{2,1,0:T(8,128)(2,1)S(1)}, bf16[1,128,2048]{2,1,0:T(8,128)(2,1)}, u32[]{:S(2)}) copy-start(bf16[1,128,2048]{2,1,0:T(8,128)(2,1)} %sconv_ref.3) | copy-start | bytes 1572868
  3.4 32.8 %all-to-all-start = ((bf16[16,384,128]{2,1,0:T(8,128)(2,1)}), bf16[16,384,128]{2,1,0:T(8,128)(2,1)}, u32[]{:S(2)}, u32[]{:S(2)}) async-start(bf16[16,384,128]{2,1,0:T(8,128)(2,1)} %get-tuple-element.14), calls=%async_computation | async-start | bytes 3145728 | tf_op jit(solution)/shard_map/all_to_all | solution.py:646
  9.2 23.9 %copy-start.4 = (f32[1,7,2048]{2,0,1:T(1,128)S(1)}, f32[1,7,2048]{2,0,1:T(1,128)}, u32[]{:S(2)}) copy-start(f32[1,7,2048]{2,0,1:T(1,128)} %param.14) | copy-start | bytes 172036
  9.2 5.4 %collective-permute-start.2 = (f32[8,128]{1,0:T(8,128)S(1)}, f32[8,128]{1,0:T(8,128)S(1)}, u32[]{:S(2)}, u32[]{:S(2)}) collective-permute-start(f32[8,128]{1,0:T(8,128)S(1)} %get-tuple-element.13), channel_id=1, source_target_pairs={{0,3},{1,0},{2,1},{3,2},{4,7},{5,4},{6,5},{7,6},{8,11},{9,8},{10,9... | collective-permute-start | bytes 12296 | tf_op jit(solution)/shard_map/ppermute | solution.py:136
  13.3 5.1 %collective-permute-start.1 = (f32[8,128]{1,0:T(8,128)S(1)}, f32[8,128]{1,0:T(8,128)S(1)}, u32[]{:S(2)}, u32[]{:S(2)}) collective-permute-start(f32[8,128]{1,0:T(8,128)S(1)} %get-tuple-element.13), channel_id=1, source_target_pairs={{0,2},{1,3},{2,0},{3,1},{4,6},{5,7},{6,4},{7,5},{8,10},{9,11},{10,... | collective-permute-start | bytes 12296 | tf_op jit(solution)/shard_map/ppermute | solution.py:136
  13.3 5.1 %collective-permute-start = (f32[8,128]{1,0:T(8,128)S(1)}, f32[8,128]{1,0:T(8,128)S(1)}, u32[]{:S(2)}, u32[]{:S(2)}) collective-permute-start(f32[8,128]{1,0:T(8,128)S(1)} %get-tuple-element.13), channel_id=1, source_target_pairs={{0,1},{1,2},{2,3},{3,0},{4,5},{5,6},{6,7},{7,4},{8,9},{9,10},{10,1... | collective-permute-start | bytes 12296 | tf_op jit(solution)/shard_map/ppermute | solution.py:136
  19.3 1.3 %collective-permute-start.3 = (f32[34,128]{1,0:T(8,128)S(1)}, f32[34,128]{1,0:T(8,128)S(1)}, u32[]{:S(2)}, u32[]{:S(2)}) collective-permute-start(f32[34,128]{1,0:T(8,128)S(1)} %pad_maximum_fusion), channel_id=1, source_target_pairs={{0,4},{4,0},{8,12},{12,8},{16,20},{20,16},{24,28},{28,24},{32,36},... | collective-permute-start | bytes 52232 | tf_op jit(solution)/shard_map/ppermute | solution.py:143
  20.6 8.3 %collective-permute-start.5 = (f32[36,128]{1,0:T(8,128)S(1)}, f32[36,128]{1,0:T(8,128)S(1)}, u32[]{:S(2)}, u32[]{:S(2)}) collective-permute-start(f32[36,128]{1,0:T(8,128)S(1)} %pad_maximum_fusion.1), channel_id=1, source_target_pairs={{0,8},{4,12},{8,16},{12,20},{16,24},{20,28},{24,0},{28,4},{32,40},... | collective-permute-start | bytes 55304 | tf_op jit(solution)/shard_map/ppermute | solution.py:149
  22.5 7.0 %collective-permute-start.4 = (f32[36,128]{1,0:T(8,128)S(1)}, f32[36,128]{1,0:T(8,128)S(1)}, u32[]{:S(2)}, u32[]{:S(2)}) collective-permute-start(f32[36,128]{1,0:T(8,128)S(1)} %pad_maximum_fusion.1), channel_id=1, source_target_pairs={{0,16},{4,20},{8,24},{12,28},{16,0},{20,4},{24,8},{28,12},{32,48},... | collective-permute-start | bytes 55304 | tf_op jit(solution)/shard_map/ppermute | solution.py:149
  25.2 5.9 %collective-permute-start.6 = (f32[36,128]{1,0:T(8,128)S(1)}, f32[36,128]{1,0:T(8,128)S(1)}, u32[]{:S(2)}, u32[]{:S(2)}) collective-permute-start(f32[36,128]{1,0:T(8,128)S(1)} %pad_maximum_fusion.1), channel_id=1, source_target_pairs={{0,24},{4,28},{8,0},{12,4},{16,8},{20,12},{24,16},{28,20},{32,56},... | collective-permute-start | bytes 55304 | tf_op jit(solution)/shard_map/ppermute | solution.py:149
  31.1 5.0 %collective-permute-start.7 = (f32[48,128]{1,0:T(8,128)S(1)}, f32[48,128]{1,0:T(8,128)S(1)}, u32[]{:S(2)}, u32[]{:S(2)}) collective-permute-start(f32[48,128]{1,0:T(8,128)S(1)} %concatenate.23), channel_id=1, source_target_pairs={{0,32},{4,36},{8,40},{12,44},{16,48},{20,52},{24,56},{28,60},{32,0... | collective-permute-start | bytes 73736 | tf_op jit(solution)/shard_map/ppermute | solution.py:143
  33.2 3.0 %copy-start.3 = (s32[16]{0:T(128)S(1)}, s32[16]{0:T(128)}, u32[]{:S(2)}) copy-start(s32[16]{0:T(128)} %order_ref.1) | copy-start | bytes 196
  44.1 21.8 %all-to-all-start.1 = ((bf16[16,136,256]{2,1,0:T(8,128)(2,1)}), bf16[16,136,256]{2,1,0:T(8,128)(2,1)S(1)}, u32[]{:S(2)}, u32[]{:S(2)}) async-start(bf16[16,136,256]{2,1,0:T(8,128)(2,1)} %convolve.1), calls=%async_computation.1 | async-start | bytes 2228224 | tf_op jit(solution)/shard_map/all_to_all | solution.py:664
  48.7 46.0 %collective-permute-start.12 = (bf16[1,128,2048]{2,1,0:T(8,128)(2,1)S(1)}, bf16[1,128,2048]{2,1,0:T(8,128)(2,1)S(1)}, u32[]{:S(2)}, u32[]{:S(2)}) collective-permute-start(bf16[1,128,2048]{2,1,0:T(8,128)(2,1)S(1)} %copy-done), channel_id=1, source_target_pairs={{64,0},{65,1},{66,2},{67,3},{68,4},{69,5},{70,6},{71,7},{72,8},{73... | collective-permute-start | bytes 1572872 | tf_op jit(solution)/shard_map/ppermute | solution.py:661
  67.6 29.3 %collective-permute-start.13 = (bf16[1,128,2048]{2,1,0:T(8,128)(2,1)S(1)}, bf16[1,128,2048]{2,1,0:T(8,128)(2,1)S(1)}, u32[]{:S(2)}, u32[]{:S(2)}) collective-permute-start(bf16[1,128,2048]{2,1,0:T(8,128)(2,1)S(1)} %get-tuple-element.15.send_ref), channel_id=1, source_target_pairs={{0,64},{64,0},{1,65},{65,1},{2,66},{66,2},{3,67},{67,3},{4,68},{68... | collective-permute-start | bytes 1572872 | tf_op jit(solution)/shard_map/ppermute | solution.py:669
  70.9 16.5 %collective-permute-start.8 = (f32[8,128]{1,0:T(8,128)S(1)}, f32[8,128]{1,0:T(8,128)S(1)}, u32[]{:S(2)}, u32[]{:S(2)}) collective-permute-start(f32[8,128]{1,0:T(8,128)S(1)} %get-tuple-element.18), channel_id=1, source_target_pairs={{64,0},{65,1},{66,2},{67,3},{68,4},{69,5},{70,6},{71,7},{72,8},{73... | collective-permute-start | bytes 12296 | tf_op jit(solution)/shard_map/ppermute | solution.py:668
  87.5 7.2 %collective-permute-start.9 = (f32[8,128]{1,0:T(8,128)S(1)}, f32[8,128]{1,0:T(8,128)S(1)}, u32[]{:S(2)}, u32[]{:S(2)}) collective-permute-start(f32[8,128]{1,0:T(8,128)S(1)} %pad_maximum_fusion.2.s0), channel_id=1, source_target_pairs={{0,1},{1,2},{2,3},{3,0},{4,5},{5,6},{6,7},{7,4},{8,9},{9,10},{10,1... | collective-permute-start | bytes 12296 | tf_op jit(solution)/shard_map/ppermute | solution.py:136
  88.6 6.1 %collective-permute-start.10 = (f32[8,128]{1,0:T(8,128)S(1)}, f32[8,128]{1,0:T(8,128)S(1)}, u32[]{:S(2)}, u32[]{:S(2)}) collective-permute-start(f32[8,128]{1,0:T(8,128)S(1)} %pad_maximum_fusion.2.s0), channel_id=1, source_target_pairs={{0,2},{1,3},{2,0},{3,1},{4,6},{5,7},{6,4},{7,5},{8,10},{9,11},{10,... | collective-permute-start | bytes 12296 | tf_op jit(solution)/shard_map/ppermute | solution.py:136
  92.1 3.6 %collective-permute-start.11 = (f32[8,128]{1,0:T(8,128)S(1)}, f32[8,128]{1,0:T(8,128)S(1)}, u32[]{:S(2)}, u32[]{:S(2)}) collective-permute-start(f32[8,128]{1,0:T(8,128)S(1)} %pad_maximum_fusion.2.s0), channel_id=1, source_target_pairs={{0,3},{1,0},{2,1},{3,2},{4,7},{5,4},{6,5},{7,6},{8,11},{9,8},{10,9... | collective-permute-start | bytes 12296 | tf_op jit(solution)/shard_map/ppermute | solution.py:136
